TPU v7x, 32 devices: a whole 2x2x4 slice. The times are simulated.
32 devices in a mesh: fsdp: 4 (over y, core), ctx: 8 (over z, x).
Axes of the slice: x: 2, y: 2, z: 4, core: 2. Of those that a mesh axis runs over, the one named last changes fastest.
Arguments:
- tokens: bfloat16 [4, 2048, 768], P('fsdp', 'ctx'), may hold values from -6 to 6
- segment_ids: int32 [4, 2048], P('fsdp', 'ctx'), may hold values from 0 to 15, as said below
- positions: int32 [4, 2048], P('fsdp', 'ctx'), may hold values from 0 to 1023, as said below
- gain_attn: bfloat16 [768], P(('fsdp', 'ctx')), may hold values from 0.5 to 1.5
- w_qkv: bfloat16 [768, 2304], P(('fsdp', 'ctx')), may hold values from -0.21875 to 0.21875
- w_out: bfloat16 [768, 768], P(('fsdp', 'ctx')), may hold values from -3 to 3
- gain_mlp: bfloat16 [768], P(('fsdp', 'ctx')), may hold values from 0.5 to 1.5
- w_in: bfloat16 [768, 2304], P(('fsdp', 'ctx')), may hold values from -0.21875 to 0.21875
- w_down: bfloat16 [1152, 768], P(None, ('fsdp', 'ctx')), may hold values from -0.1875 to 0.1875
- cotangent: bfloat16 [4, 2048, 768], P('fsdp', 'ctx'), may hold values from -6 to 6
Outputs:
- output: bfloat16 [4, 2048, 768], P('fsdp', 'ctx')
- input_grad: bfloat16 [4, 2048, 768], P('fsdp', 'ctx')
- grad_gain_attn: float32 [768], P(('fsdp', 'ctx'))
- grad_w_qkv: float32 [768, 2304], P(('fsdp', 'ctx'))
- grad_w_out: float32 [768, 768], P(('fsdp', 'ctx'))
- grad_gain_mlp: float32 [768], P(('fsdp', 'ctx'))
- grad_w_in: float32 [768, 2304], P(('fsdp', 'ctx'))
- grad_w_down: float32 [1152, 768], P(None, ('fsdp', 'ctx'))
Inputs may be any that keep to these rules, and one draw needn't show every extreme that they name: `segment_ids`: along each sequence the ids never fall and every id is used; one document holds exactly 1024 tokens, the others share the rest. `positions`: A token's place within its document, counting from 0.
All inputs are finite; a program needn't handle non-finite values.
Results may differ from a plain program's by a relative error of at most 0.019.
Values may be sent and summed in bfloat16 or wider, within the bound.
No kernel may reach another device: no remote copies, remote signals or barrier semaphores. Data moves between devices by JAX's collectives and lax.ppermute only.
A program may use at most 192 MiB of HBM per device.

v0:
```python
import math

import jax
import jax.numpy as jnp
from jax import lax
from jax.sharding import PartitionSpec as P

HD = 64


EPS = 1e-05
THETA = 160000.0
NEG = -1e30
ROOT_HALF = 0.7071067811865476
INV_ROOT_TWO_PI = 0.3989422804014327


def norm_rows(values):
    center = values - jnp.mean(values, axis=-1, keepdims=True)
    spread = jnp.mean(center * center, axis=-1, keepdims=True)
    inverse = lax.rsqrt(spread + EPS)
    return (center * inverse, inverse)


def norm_back(grad_normed, normed, inverse):
    return inverse * (
        grad_normed
        - jnp.mean(grad_normed, axis=-1, keepdims=True)
        - normed * jnp.mean(grad_normed * normed, axis=-1, keepdims=True)
    )


def rotary_tables(places, head_size):
    rates = THETA ** (-jnp.arange(0, head_size, 2).astype(jnp.float32) / head_size)
    freqs = places.astype(jnp.float32)[:, None] * rates[None, :]
    angles = jnp.concatenate([freqs, freqs], axis=-1)[:, None, :]
    return (jnp.cos(angles), jnp.sin(angles))


def rotate_half(values):
    half = values.shape[-1] // 2
    return jnp.concatenate([-values[..., half:], values[..., :half]], axis=-1)


def rotary(values, cosine, sine):
    return values * cosine + rotate_half(values) * sine


def rotary_back(grads, cosine, sine):
    return grads * cosine - rotate_half(grads * sine)


def scores_of(queries, keys, query_docs, key_docs, scale):
    scores = jnp.einsum("thd,khd->htk", queries, keys, preferred_element_type=jnp.float32) * scale
    mask = (query_docs[:, None] == key_docs[None, :])[None]
    return (scores, mask)


def pair_terms(queries, query_docs, grads, log_sum, delta, keys, values, key_docs, scale):
    scores, mask = scores_of(queries, keys, query_docs, key_docs, scale)
    probs = jnp.where(mask, jnp.exp(scores - log_sum[..., None]), 0.0)
    grad_probs = jnp.einsum("thd,khd->htk", grads, values, preferred_element_type=jnp.float32)
    grad_scores = (probs * (grad_probs - delta[..., None])).astype(jnp.bfloat16)
    return (probs.astype(jnp.bfloat16), grad_scores)


def on_device(
    tokens, segment_ids, positions, gain_attn, w_qkv, w_out, gain_mlp, w_in, w_down, cotangent
):
    f32 = jnp.float32
    bf16 = jnp.bfloat16
    inputs = tokens[0].astype(f32)
    local_rows, width = inputs.shape
    head_size = HD
    heads = width // head_size
    scale = head_size ** (-0.5)
    hidden_units = w_in.shape[1] // 2
    doc_ids = segment_ids[0].astype(bf16)
    cosine, sine = rotary_tables(positions[0], head_size)
    gain_one, w_joined, w_proj = (
        lax.all_gather(gain_attn, ("fsdp", "ctx"), axis=0, tiled=True),
        lax.all_gather(w_qkv, ("fsdp", "ctx"), axis=0, tiled=True),
        lax.all_gather(w_out, ("fsdp", "ctx"), axis=0, tiled=True),
    )
    normed_one, inverse_one = norm_rows(inputs)
    hidden_one = (normed_one * gain_one.astype(f32)).astype(bf16)
    joined = jnp.dot(hidden_one, w_joined, preferred_element_type=f32)
    query = rotary(joined[:, :width].reshape(local_rows, heads, head_size), cosine, sine).astype(
        bf16
    )
    keys = rotary(
        joined[:, width : 2 * width].reshape(local_rows, heads, head_size), cosine, sine
    ).astype(bf16)
    values = joined[:, 2 * width :].astype(bf16)
    key_all, value_all, doc_all = (
        lax.all_gather(keys.reshape(local_rows, width), "ctx", axis=0, tiled=True),
        lax.all_gather(values, "ctx", axis=0, tiled=True),
        lax.all_gather(doc_ids, "ctx", axis=0, tiled=True),
    )
    total = key_all.shape[0]
    block_rows = math.gcd(total, 1024)
    count = total // block_rows
    key_blocks = key_all.reshape(count, block_rows, heads, head_size)
    value_blocks = value_all.reshape(count, block_rows, heads, head_size)
    doc_blocks = doc_all.reshape(count, block_rows)

    def forward_step(carry, block):
        run_max, run_sum, accum = carry
        key_block, value_block, doc_block = block
        scores, mask = scores_of(query, key_block, doc_ids, doc_block, scale)
        scores = jnp.where(mask, scores, NEG)
        new_max = jnp.maximum(run_max, jnp.max(scores, axis=-1))
        expo = jnp.where(mask, jnp.exp(scores - new_max[..., None]), 0.0)
        factor = jnp.exp(run_max - new_max)
        run_sum = run_sum * factor + jnp.sum(expo, axis=-1)
        accum = accum * factor[..., None] + jnp.einsum(
            "htk,khd->htd", expo.astype(bf16), value_block, preferred_element_type=f32
        )
        return ((new_max, run_sum, accum), None)

    start = (
        jnp.full((heads, local_rows), NEG, f32),
        jnp.zeros((heads, local_rows), f32),
        jnp.zeros((heads, local_rows, head_size), f32),
    )
    (row_max, row_sum, accum), unused = lax.scan(
        forward_step, start, (key_blocks, value_blocks, doc_blocks)
    )
    attended = jnp.transpose(accum / row_sum[..., None], (1, 0, 2)).reshape(local_rows, width)
    log_sum = row_max + jnp.log(row_sum)
    attended_low = attended.astype(bf16)
    middle = inputs + jnp.dot(attended_low, w_proj, preferred_element_type=f32)
    gain_two, w_up, w_back = (
        lax.all_gather(gain_mlp, ("fsdp", "ctx"), axis=0, tiled=True),
        lax.all_gather(w_in, ("fsdp", "ctx"), axis=0, tiled=True),
        lax.all_gather(w_down, ("fsdp", "ctx"), axis=1, tiled=True),
    )
    normed_two, inverse_two = norm_rows(middle)
    hidden_two = (normed_two * gain_two.astype(f32)).astype(bf16)
    upward = jnp.dot(hidden_two, w_up, preferred_element_type=f32)
    inner = upward[:, :hidden_units]
    gate = upward[:, hidden_units:]
    cdf = 0.5 * (1.0 + jax.scipy.special.erf(inner * ROOT_HALF))
    gelu_value = inner * cdf
    product = (gelu_value * gate).astype(bf16)
    result = middle + jnp.dot(product, w_back, preferred_element_type=f32)
    output = result.astype(bf16)[None]
    grad_low = cotangent[0]
    grad_result = grad_low.astype(f32)
    grad_w_back_part = jnp.dot(product.T, grad_low, preferred_element_type=f32)
    grad_product = jnp.dot(grad_low, w_back.T, preferred_element_type=f32)
    grad_inner = (
        grad_product * gate * (cdf + inner * jnp.exp(-0.5 * inner * inner) * INV_ROOT_TWO_PI)
    )
    grad_gate = grad_product * gelu_value
    grad_up = jnp.concatenate([grad_inner, grad_gate], axis=1).astype(bf16)
    grad_w_up_part = jnp.dot(hidden_two.T, grad_up, preferred_element_type=f32)
    grad_hidden_two = jnp.dot(grad_up, w_up.T, preferred_element_type=f32)
    grad_gain_two_part = jnp.sum(grad_hidden_two * normed_two, axis=0)
    grad_middle = grad_result + norm_back(
        grad_hidden_two * gain_two.astype(f32), normed_two, inverse_two
    )
    sum_gain_two, sum_w_up, sum_w_back = (
        lax.psum_scatter(grad_gain_two_part, ("fsdp", "ctx"), scatter_dimension=0, tiled=True),
        lax.psum_scatter(grad_w_up_part, ("fsdp", "ctx"), scatter_dimension=0, tiled=True),
        lax.psum_scatter(grad_w_back_part, ("fsdp", "ctx"), scatter_dimension=1, tiled=True),
    )
    grad_branch = grad_middle.astype(bf16)
    grad_w_proj_part = jnp.dot(attended_low.T, grad_branch, preferred_element_type=f32)
    grad_attended = jnp.dot(grad_branch, w_proj.T, preferred_element_type=f32).astype(bf16)
    grad_heads = grad_attended.reshape(local_rows, heads, head_size)
    delta = jnp.sum(
        grad_heads.astype(f32) * attended.reshape(local_rows, heads, head_size), axis=-1
    ).T

    def back_step(grad_query, block):
        key_block, value_block, doc_block = block
        probs_low, grad_scores = pair_terms(
            query, doc_ids, grad_heads, log_sum, delta, key_block, value_block, doc_block, scale
        )
        grad_query = (
            grad_query
            + jnp.einsum("htk,khd->thd", grad_scores, key_block, preferred_element_type=f32) * scale
        )
        grad_key = (
            jnp.einsum("htk,thd->khd", grad_scores, query, preferred_element_type=f32) * scale
        )
        grad_value = jnp.einsum("htk,thd->khd", probs_low, grad_heads, preferred_element_type=f32)
        return (grad_query, (grad_key, grad_value))

    grad_query, (key_terms, value_terms) = lax.scan(
        back_step,
        jnp.zeros((local_rows, heads, head_size), f32),
        (key_blocks, value_blocks, doc_blocks),
    )
    grad_keys, grad_values = (
        lax.psum_scatter(
            key_terms.reshape(total, width).astype(jnp.bfloat16),
            "ctx",
            scatter_dimension=0,
            tiled=True,
        ).astype(jnp.float32),
        lax.psum_scatter(
            value_terms.reshape(total, width).astype(jnp.bfloat16),
            "ctx",
            scatter_dimension=0,
            tiled=True,
        ).astype(jnp.float32),
    )
    grad_query_rot = rotary_back(grad_query, cosine, sine).reshape(local_rows, width)
    grad_key_rot = rotary_back(
        grad_keys.reshape(local_rows, heads, head_size), cosine, sine
    ).reshape(local_rows, width)
    grad_joined = jnp.concatenate([grad_query_rot, grad_key_rot, grad_values], axis=1).astype(bf16)
    grad_w_joined_part = jnp.dot(hidden_one.T, grad_joined, preferred_element_type=f32)
    grad_hidden_one = jnp.dot(grad_joined, w_joined.T, preferred_element_type=f32)
    grad_gain_one_part = jnp.sum(grad_hidden_one * normed_one, axis=0)
    grad_inputs = grad_middle + norm_back(
        grad_hidden_one * gain_one.astype(f32), normed_one, inverse_one
    )
    sum_gain_one, sum_w_joined, sum_w_proj = (
        lax.psum_scatter(grad_gain_one_part, ("fsdp", "ctx"), scatter_dimension=0, tiled=True),
        lax.psum_scatter(grad_w_joined_part, ("fsdp", "ctx"), scatter_dimension=0, tiled=True),
        lax.psum_scatter(grad_w_proj_part, ("fsdp", "ctx"), scatter_dimension=0, tiled=True),
    )
    return (
        output,
        grad_inputs.astype(bf16)[None],
        sum_gain_one,
        sum_w_joined,
        sum_w_proj,
        sum_gain_two,
        sum_w_up,
        sum_w_back,
    )


def solution(mesh):
    return jax.shard_map(
        on_device,
        mesh=mesh,
        in_specs=(
            P("fsdp", "ctx", None),
            P("fsdp", "ctx"),
            P("fsdp", "ctx"),
            P(("fsdp", "ctx")),
            P(("fsdp", "ctx"), None),
            P(("fsdp", "ctx"), None),
            P(("fsdp", "ctx")),
            P(("fsdp", "ctx"), None),
            P(None, ("fsdp", "ctx")),
            P("fsdp", "ctx", None),
        ),
        out_specs=(
            P("fsdp", "ctx", None),
            P("fsdp", "ctx", None),
            P(("fsdp", "ctx")),
            P(("fsdp", "ctx"), None),
            P(("fsdp", "ctx"), None),
            P(("fsdp", "ctx")),
            P(("fsdp", "ctx"), None),
            P(None, ("fsdp", "ctx")),
        ),
        check_vma=False,
    )
```

profile of v0, /device:TPU:0, one launch (start us, length us, event | category | flops | bytes accessed | tf_op | source)
XLA Modules:
  0.0 1075.4 jit_solution(16776251409051863482)
XLA Ops:
  9.6 42.3 %all-reduce.6 = (bf16[768]{0:T(1024)(128)(2,1)S(1)}, bf16[768]{0:T(1024)(128)(2,1)S(1)}) all-reduce(bf16[768]{0:T(1024)(128)(2,1)S(1)} %dynamic-update-slice, bf16[768]{0:T(1024)(128)(2,1)S(1)} %dynamic-update-slice.1), channel_id=1, replica_groups=mesh['fsdp'=4,'ctx'=8] {'fsdp','ctx'}, use_global_device_ids=true, to_apply=%add | all-reduce | flops 1536 | bytes 6144
  54.4 19.7 %all-gather.8.cloned.1.call-done = bf16[768,2304]{1,0:T(8,128)(2,1)} async-done(((bf16[24,2304]{1,0:T(8,128)(2,1)}), bf16[768,2304]{1,0:T(8,128)(2,1)}) %all-gather.8.cloned.1.call-update) | async-done | bytes 3538960 | tf_op jit(solution)/shard_map/all_gather | solution.py:82
  74.1 3.3 fusion.98
  88.7 19.4 %all-gather = bf16[1,2048]{1,0:T(2,128)(2,1)S(1)} all-gather(bf16[1,256]{1,0:T(2,128)(2,1)S(1)} %convert_element_type.107), channel_id=2, replica_groups=mesh['fsdp'=4,'ctx'=8] {'ctx'}, dimensions={1}, use_global_device_ids=true | all-gather | bytes 4608 | tf_op jit(solution)/shard_map/all_gather | solution.py:98
  109.2 28.4 %all-gather.12.cloned.1.call-done = bf16[2048,768]{1,0:T(8,128)(2,1)} async-done(((bf16[256,768]{1,0:T(8,128)(2,1)}), bf16[2048,768]{1,0:T(8,128)(2,1)}) %all-gather.12.cloned.1.call-update) | async-done | bytes 3145744 | tf_op jit(solution)/shard_map/all_gather | solution.py:97
  140.9 4.0 reshape.230
  144.8 4.6 copy.68
  149.4 50.1 %all-gather.10.cloned.1.call-done = bf16[2048,768]{1,0:T(8,128)(2,1)} async-done(((bf16[256,768]{1,0:T(8,128)(2,1)}), bf16[2048,768]{1,0:T(8,128)(2,1)}) %all-gather.10.cloned.1.call-update) | async-done | bytes 3145744 | tf_op jit(solution)/shard_map/all_gather | solution.py:96
  202.7 4.0 reshape.228
  209.6 22.4 %while.30 = (s32[]{:T(128)}, f32[12,256]{1,0:T(8,128)S(1)}, f32[12,256]{1,0:T(8,128)}, f32[12,256,64]{1,2,0:T(8,128)}, bf16[256]{0:T(256)(128)(2,1)}, /*index=5*...) while((s32[]{:T(128)}, f32[12,256]{1,0:T(8,128)S(1)}, ...), condition=%wide.region_5.6_spmd.clone, body=%wide.region_2.5_spmd.clone.sunk | while | flops 847068160 | bytes 63093528 | solution.py:126
  234.0 21.2 %all-gather.14.cloned.1.call-done = bf16[768,768]{1,0:T(8,128)(2,1)} async-done(((bf16[24,768]{1,0:T(8,128)(2,1)}), bf16[768,768]{1,0:T(8,128)(2,1)}) %all-gather.14.cloned.1.call-update) | async-done | bytes 1179664 | tf_op jit(solution)/shard_map/all_gather | solution.py:83
  259.6 57.6 %all-gather.16.cloned.1.call-done = bf16[768,2304]{1,0:T(8,128)(2,1)} async-done(((bf16[24,2304]{1,0:T(8,128)(2,1)}), bf16[768,2304]{1,0:T(8,128)(2,1)}) %all-gather.16.cloned.1.call-update) | async-done | bytes 3538960 | tf_op jit(solution)/shard_map/all_gather | solution.py:135
  317.2 4.9 fusion.100
  322.1 52.3 %all-gather.18.cloned.1.call-done = bf16[1152,768]{0,1:T(8,128)(2,1)} async-done(((bf16[1152,24]{0,1:T(8,128)(2,1)}), bf16[1152,768]{0,1:T(8,128)(2,1)}) %all-gather.18.cloned.1.call-update) | async-done | bytes 1769488 | tf_op jit(solution)/shard_map/all_gather | solution.py:136
  374.4 4.2 fusion.58
  386.9 58.7 %while.31 = (s32[]{:T(128)}, f32[256,12,64]{0,2,1:T(8,128)}, bf16[2,1024,12,64]{1,3,2,0:T(8,128)(2,1)}, bf16[2,1024,12,64]{1,3,2,0:T(8,128)(2,1)}, bf16[2,1024,1...) while((s32[]{:T(128)}, f32[256,12,64]{0,2,1:T(8,128)}, ...), condition=%wide.region_12.13_spmd.clone, body=%wide.region_11.12_spmd.clone.sunk | while | flops 2046361600 | bytes 117328776 | solution.py:191
  388.5 6.4 fusion.159
  395.0 8.5 bitcast_dynamic-update-slice_fusion.5
  403.4 7.0 fusion.160
  417.7 6.4 fusion.159
  424.1 8.5 bitcast_dynamic-update-slice_fusion.5
  432.6 7.0 fusion.160
  445.6 5.1 copy.72
  467.4 5.2 fusion.79
  472.8 54.9 %reduce-scatter.9.cloned.1.call-done = bf16[256,768]{0,1:T(8,128)(2,1)} async-done(((bf16[2048,768]{0,1:T(8,128)(2,1)}), bf16[256,768]{0,1:T(8,128)(2,1)}) %reduce-scatter.9.cloned.1.call-update) | async-done | bytes 393232 | tf_op jit(solution)/shard_map/reduce_scatter | solution.py:197
  531.0 74.5 %reduce-scatter.11.cloned.1.call-done = bf16[256,768]{0,1:T(8,128)(2,1)} async-done(((bf16[2048,768]{0,1:T(8,128)(2,1)}), bf16[256,768]{0,1:T(8,128)(2,1)}) %reduce-scatter.11.cloned.1.call-update) | async-done | bytes 393232 | tf_op jit(solution)/shard_map/reduce_scatter | solution.py:203
  605.6 5.5 fusion.81
  616.5 39.8 %all-reduce.5 = (f32[768]{0:T(1024)S(1)}, f32[768]{0:T(1024)S(1)}) all-reduce(f32[768]{0:T(1024)S(1)} %get-tuple-element.261, f32[768]{0:T(1024)S(1)} %copy-done.56), channel_id=5, replica_groups=mesh['fsdp'=4,'ctx'=8] {'fsdp','ctx'}, use_global_device_ids=true, to_apply=%region_18.19.clone | all-reduce | flops 1536 | bytes 12288
  658.6 51.1 %reduce-scatter.15.cloned.1.call-done = f32[24,768]{1,0:T(8,128)} async-done(((f32[768,768]{1,0:T(8,128)}), f32[24,768]{1,0:T(8,128)}) %reduce-scatter.15.cloned.1.call-update) | async-done | bytes 73744 | tf_op jit(solution)/shard_map/reduce_scatter | solution.py:224
  709.6 108.9 %reduce-scatter.19.cloned.1.call-done = f32[1152,24]{0,1:T(8,128)} async-done(((f32[1152,768]{0,1:T(8,128)}), f32[1152,24]{0,1:T(8,128)}) %reduce-scatter.19.cloned.1.call-update) | async-done | bytes 110608
  818.6 125.3 %reduce-scatter.17.cloned.1.call-done = f32[24,2304]{1,0:T(8,128)} async-done(((f32[768,2304]{1,0:T(8,128)}), f32[24,2304]{1,0:T(8,128)}) %reduce-scatter.17.cloned.1.call-update) | async-done | bytes 221200 | tf_op jit(solution)/shard_map/reduce_scatter | solution.py:165
  943.9 124.5 %reduce-scatter.13.cloned.1.call-done = f32[24,2304]{1,0:T(8,128)} async-done(((f32[768,2304]{1,0:T(8,128)}), f32[24,2304]{1,0:T(8,128)}) %reduce-scatter.13.cloned.1.call-update) | async-done | bytes 221200 | tf_op jit(solution)/shard_map/reduce_scatter | solution.py:223
  (261 shorter events, 104.8 us)
Async XLA Ops:
  7.2 66.9 %all-gather.8.cloned.1.call-start = ((), (), s32[]{:S(2)}) async-start(), calls=%async_computation.6 | async-start | bytes 3649536 | tf_op jit(solution)/shard_map/all_gather | solution.py:82
  7.9 129.8 %all-gather.12.cloned.1.call-start = ((), (), s32[]{:S(2)}) async-start(), calls=%async_computation.8 | async-start | bytes 3538944 | tf_op jit(solution)/shard_map/all_gather | solution.py:97
  51.9 25.4 %copy-start.38 = (f32[768]{0:T(1024)}, f32[768]{0:T(1024)S(1)}, u32[]{:S(2)}) copy-start(f32[768]{0:T(1024)S(1)} %convert_element_type.109) | copy-start | bytes 9220
  53.1 24.3 %copy-start.43 = (f32[256]{0:T(256)}, f32[256]{0:T(256)S(1)}, u32[]{:S(2)}) copy-start(f32[256]{0:T(256)S(1)} %broadcast_multiply_fusion.8) | copy-start | bytes 3076
  54.3 23.0 %copy-start.49 = (f32[256]{0:T(256)}, f32[256]{0:T(256)S(1)}, u32[]{:S(2)}) copy-start(f32[256]{0:T(256)S(1)} %add_rsqrt_fusion.1) | copy-start | bytes 3076
  54.3 23.9 %copy-start.57 = (s32[1,256]{1,0:T(1,128)S(1)}, s32[1,256]{1,0:T(1,128)}, u32[]{:S(2)}) copy-start(s32[1,256]{1,0:T(1,128)} %param.16) | copy-start | bytes 3076
  78.2 121.4 %all-gather.10.cloned.1.call-start = ((), (), s32[]{:S(2)}) async-start(), calls=%async_computation.7 | async-start | bytes 3538944 | tf_op jit(solution)/shard_map/all_gather | solution.py:96
  78.5 30.6 %copy-start.21 = (f32[256,64]{0,1:T(8,128)}, f32[256,64]{0,1:T(8,128)S(1)}, u32[]{:S(2)}) copy-start(f32[256,64]{0,1:T(8,128)S(1)} %get-tuple-element.330) | copy-start | bytes 196612
  78.5 30.6 %copy-start.33 = (f32[256,64]{0,1:T(8,128)}, f32[256,64]{0,1:T(8,128)S(1)}, u32[]{:S(2)}) copy-start(f32[256,64]{0,1:T(8,128)S(1)} %get-tuple-element.331) | copy-start | bytes 196612
  85.8 169.4 %all-gather.14.cloned.1.call-start = ((), (), s32[]{:S(2)}) async-start(), calls=%async_computation.9 | async-start | bytes 1216512 | tf_op jit(solution)/shard_map/all_gather | solution.py:83
  86.4 230.8 %all-gather.16.cloned.1.call-start = ((), (), s32[]{:S(2)}) async-start(), calls=%async_computation.10 | async-start | bytes 3649536 | tf_op jit(solution)/shard_map/all_gather | solution.py:135
  86.9 287.4 %all-gather.18.cloned.1.call-start = ((), (), s32[]{:S(2)}) async-start(), calls=%async_computation.11 | async-start | bytes 1824768 | tf_op jit(solution)/shard_map/all_gather | solution.py:136
  87.5 440.3 %reduce-scatter.9.cloned.1.call-start = ((), (), s32[]{:S(2)}) async-start(), calls=%async_computation.12 | async-start | bytes 3538944 | tf_op jit(solution)/shard_map/reduce_scatter | solution.py:197
  322.1 56.5 %copy-start.40 = (f32[768]{0:T(1024)S(1)}, f32[768]{0:T(1024)}, u32[]{:S(2)}) copy-start(f32[768]{0:T(1024)} %convert_element_type.118) | copy-start | bytes 9220
  322.1 56.5 %copy-start.46 = (f32[256]{0:T(256)S(1)}, f32[256]{0:T(256)}, u32[]{:S(2)}) copy-start(f32[256]{0:T(256)} %copy-done.45) | copy-start | bytes 3076
  322.1 56.5 %copy-start.51 = (f32[256]{0:T(256)S(1)}, f32[256]{0:T(256)}, u32[]{:S(2)}) copy-start(f32[256]{0:T(256)} %add_rsqrt_fusion) | copy-start | bytes 3076
  395.0 8.5 copy-start.14
  395.0 8.5 copy-start.54
  424.1 8.5 copy-start.14
  424.1 8.5 copy-start.54
  453.6 152.0 %reduce-scatter.11.cloned.1.call-start = ((), (), s32[]{:S(2)}) async-start(), calls=%async_computation.13 | async-start | bytes 3538944 | tf_op jit(solution)/shard_map/reduce_scatter | solution.py:203
  461.6 248.1 %reduce-scatter.15.cloned.1.call-start = ((), (), s32[]{:S(2)}) async-start(), calls=%async_computation.15 | async-start | bytes 2433024 | tf_op jit(solution)/shard_map/reduce_scatter | solution.py:224
  464.6 354.0 %reduce-scatter.19.cloned.1.call-start = ((), (), s32[]{:S(2)}) async-start(), calls=%async_computation.17 | async-start | bytes 3649536
  467.3 476.6 %reduce-scatter.17.cloned.1.call-start = ((), (), s32[]{:S(2)}) async-start(), calls=%async_computation.16 | async-start | bytes 7299072 | tf_op jit(solution)/shard_map/reduce_scatter | solution.py:165
  472.6 55.2 %copy-start.2 = (f32[256,12,64]{0,2,1:T(8,128)S(1)}, f32[256,12,64]{0,2,1:T(8,128)}, u32[]{:S(2)}) copy-start(f32[256,12,64]{0,2,1:T(8,128)} %get-tuple-element.124) | copy-start | bytes 2359300
  472.6 55.2 %copy-start.34 = (f32[256,64]{0,1:T(8,128)S(1)}, f32[256,64]{0,1:T(8,128)}, u32[]{:S(2)}) copy-start(f32[256,64]{0,1:T(8,128)} %copy-done.33) | copy-start | bytes 196612
  472.6 56.6 %copy-start.22 = (f32[256,64]{0,1:T(8,128)S(1)}, f32[256,64]{0,1:T(8,128)}, u32[]{:S(2)}) copy-start(f32[256,64]{0,1:T(8,128)} %copy-done.21) | copy-start | bytes 196612
  472.6 595.8 %reduce-scatter.13.cloned.1.call-start = ((), (), s32[]{:S(2)}) async-start(), calls=%async_computation.14 | async-start | bytes 7299072 | tf_op jit(solution)/shard_map/reduce_scatter | solution.py:223
  529.1 76.5 %copy-start.6 = (bf16[1,256,768]{2,1,0:T(8,128)(2,1)S(1)}, bf16[1,256,768]{2,1,0:T(8,128)(2,1)}, u32[]{:S(2)}) copy-start(bf16[1,256,768]{2,1,0:T(8,128)(2,1)} %param.14) | copy-start | bytes 1179652
  529.1 76.5 %copy-start.39 = (f32[768]{0:T(1024)S(1)}, f32[768]{0:T(1024)}, u32[]{:S(2)}) copy-start(f32[768]{0:T(1024)} %copy-done.38) | copy-start | bytes 9220
  529.1 76.5 %copy-start.44 = (f32[256]{0:T(256)S(1)}, f32[256]{0:T(256)}, u32[]{:S(2)}) copy-start(f32[256]{0:T(256)} %copy-done.43) | copy-start | bytes 3076
  529.1 76.5 %copy-start.50 = (f32[256]{0:T(256)S(1)}, f32[256]{0:T(256)}, u32[]{:S(2)}) copy-start(f32[256]{0:T(256)} %copy-done.49) | copy-start | bytes 3076
  (52 other events, 152.9 us)
Sparse Core Ops, SparseCore 0:
  11.0 63.0 all-gather.7
  78.3 59.3 all-gather.11
  140.4 59.0 all-gather.9
  202.4 52.7 all-gather.13
  258.0 59.1 all-gather.15
  319.9 54.4 all-gather.17
  453.7 74.0 reduce-scatter.8
  531.4 74.1 reduce-scatter.10
  611.4 98.1 reduce-scatter.14
  716.4 102.1 reduce-scatter.18
  825.8 118.0 reduce-scatter.16
  950.0 118.3 reduce-scatter.12
where the time goes:
time: 1080 us
  waiting for transfers between devices  771 us (71%)
  blocking collectives  101 us (9%)
  matrix products  99 us (9%)
  local copies, waits for them, and re-layouts  61.1 us (6%)
  other arithmetic  26.2 us (2%)
  between operations  15.1 us (1%)
    reduce_scatter x1, waiting for transfers between devices, on_device(): lax.psum_scatter(grad_w_up_part, ('fsdp', 'ctx'), scatter_dimension=0, ti...  125 us
    reduce_scatter x1, waiting for transfers between devices, on_device(): lax.psum_scatter(grad_w_joined_part, ('fsdp', 'ctx'), scatter_dimension=0...  125 us
    unnamed x13, waiting for transfers between devices  111 us
    unnamed x2, blocking collectives  82.1 us
    reduce_scatter x1, waiting for transfers between devices, on_device(): lax.psum_scatter(value_terms.reshape(total, width).astype(jnp.bfloat16),...  74.5 us
    all_gather x1, waiting for transfers between devices, on_device(): lax.all_gather(w_in, ('fsdp', 'ctx'), axis=0, tiled=True)  57.6 us
    reduce_scatter x1, waiting for transfers between devices, on_device(): lax.psum_scatter(key_terms.reshape(total, width).astype(jnp.bfloat16), 'c...  54.9 us
    all_gather x1, waiting for transfers between devices, on_device(): lax.all_gather(w_down, ('fsdp', 'ctx'), axis=1, tiled=True)  52.3 us
  transfers between devices with their start and end apart: 12, of which 12 were waited for; matrix products, arithmetic and copies ran while one was open for 9% of the time, Pallas kernels for 0%

commit v1 on v0

v1 whole, which is shorter than its diff:
```python
import math

import jax
import jax.numpy as jnp
from jax import lax
from jax.experimental import pallas as pl
from jax.experimental.pallas import tpu as pltpu
from jax.sharding import PartitionSpec as P

HD = 64
SLOTS = 2
LANES = SLOTS * HD
EPS = 1e-05
THETA = 160000.0
NEG = -1e30
ROOT_HALF = 0.7071067811865476
INV_ROOT_TWO_PI = 0.3989422804014327
VMEM_BYTES = 50 * 1024 * 1024
AXES = ("fsdp", "ctx")

f32 = jnp.float32
bf16 = jnp.bfloat16


def norm_rows(values):
    center = values - jnp.mean(values, axis=-1, keepdims=True)
    spread = jnp.mean(center * center, axis=-1, keepdims=True)
    inverse = lax.rsqrt(spread + EPS)
    return (center * inverse, inverse)


def norm_back(grad_normed, normed, inverse):
    return inverse * (
        grad_normed
        - jnp.mean(grad_normed, axis=-1, keepdims=True)
        - normed * jnp.mean(grad_normed * normed, axis=-1, keepdims=True)
    )


def rotate_half(values):
    lane = lax.broadcasted_iota(jnp.int32, values.shape, 1)
    ahead = pltpu.roll(values, LANES - HD // 2, 1)
    behind = pltpu.roll(values, HD // 2, 1)
    return jnp.where(lane % HD < HD // 2, -ahead, behind)


def dot_tt(left, right):
    return lax.dot_general(left, right, (((1,), (1,)), ((), ())), preferred_element_type=f32)


def dot_rows(left, right):
    return lax.dot_general(left, right, (((0,), (0,)), ((), ())), preferred_element_type=f32)


def params():
    return pltpu.CompilerParams(
        dimension_semantics=("arbitrary",), vmem_limit_bytes=VMEM_BYTES
    )


def project_kernel(order_ref, x_ref, gain_ref, w_ref, cos_ref, sin_ref, hidden_ref, qkv_ref):
    rows = hidden_ref.shape[0]
    normed, _ = norm_rows(x_ref[0, :rows, :].astype(f32))
    hidden = (normed * gain_ref[...].astype(f32)).astype(bf16)
    hidden_ref[...] = hidden
    joined = jnp.dot(hidden, w_ref[:, : 3 * LANES], preferred_element_type=f32)
    cosine = cos_ref[...]
    sine = sin_ref[...]
    query = joined[:, :LANES]
    keys = joined[:, LANES : 2 * LANES]
    query = (query * cosine + rotate_half(query) * sine).astype(bf16)
    keys = (keys * cosine + rotate_half(keys) * sine).astype(bf16)
    qkv_ref[:, :LANES] = query * bf16(HD**-0.5)
    qkv_ref[:, LANES : 2 * LANES] = keys
    qkv_ref[:, 2 * LANES :] = joined[:, 2 * LANES :].astype(bf16)


def project(order, arrived, gain, w_heads, cosine, sine, rows):
    count, held, width = arrived.shape
    total = count * rows
    sorted_block = lambda i, order: (order[i], 0)
    fixed = lambda i, order: (0, 0)
    return pl.pallas_call(
        project_kernel,
        grid_spec=pltpu.PrefetchScalarGridSpec(
            num_scalar_prefetch=1,
            grid=(count,),
            in_specs=[
                pl.BlockSpec((1, held, width), lambda i, order: (i, 0, 0)),
                pl.BlockSpec((1, width), fixed),
                pl.BlockSpec(w_heads.shape, fixed),
                pl.BlockSpec((rows, LANES), sorted_block),
                pl.BlockSpec((rows, LANES), sorted_block),
            ],
            out_specs=[
                pl.BlockSpec((rows, width), sorted_block),
                pl.BlockSpec((rows, 3 * LANES), sorted_block),
            ],
        ),
        out_shape=[
            jax.ShapeDtypeStruct((total, width), bf16),
            jax.ShapeDtypeStruct((total, 3 * LANES), bf16),
        ],
        compiler_params=params(),
        name="project",
    )(order, arrived, gain, w_heads, cosine, sine)


def attend_kernel(lo_ref, hi_ref, ok_ref, q_ref, k_ref, v_ref, doc_col_ref, doc_row_ref,
                  low_ref, att_ref, lse_ref):
    block = pl.program_id(0)
    rows = q_ref.shape[0]
    lane = lax.broadcasted_iota(jnp.int32, (rows, LANES), 1)
    docs = doc_col_ref[...]
    query = q_ref[...]
    att_ref[...] = jnp.zeros((rows, LANES), f32)
    lse_ref[...] = jnp.zeros((rows, LANES), f32)
    for slot in range(SLOTS):
        mine = lane // HD == slot

        @pl.when(ok_ref[block * SLOTS + slot] == 1)
        def _():
            q_slot = jnp.where(mine, query, bf16(0))

            def step(at, carry):
                run_max, run_sum, accum = carry
                span = pl.ds(pl.multiple_of(at * rows, rows), rows)
                scores = dot_tt(q_slot, k_ref[span, :])
                same = docs == doc_row_ref[pl.ds(at, 1), :]
                scores = jnp.where(same, scores, NEG)
                new_max = jnp.maximum(run_max, jnp.max(scores, axis=1, keepdims=True))
                expo = jnp.where(same, jnp.exp(scores - new_max), 0.0)
                factor = jnp.exp(run_max - new_max)
                run_sum = run_sum * factor + jnp.sum(expo, axis=1, keepdims=True)
                accum = accum * factor + jnp.dot(
                    expo.astype(bf16), v_ref[span, :], preferred_element_type=f32
                )
                return (new_max, run_sum, accum)

            start = (
                jnp.full((rows, 1), NEG, f32),
                jnp.zeros((rows, 1), f32),
                jnp.zeros((rows, LANES), f32),
            )
            top, total, accum = lax.fori_loop(lo_ref[block], hi_ref[block], step, start)
            att_ref[...] = jnp.where(mine, accum / total, att_ref[...])
            lse_ref[...] = jnp.where(mine, top + jnp.log(total), lse_ref[...])

    low_ref[0] = att_ref[...].astype(bf16)


def attend(lo, hi, ok, qkv, doc_col, doc_row, rows):
    total = qkv.shape[0]
    count = total // rows
    whole = lambda part: pl.BlockSpec((total, LANES), lambda i, *s: (0, part))
    mine = pl.BlockSpec((rows, LANES), lambda i, *s: (i, 0))
    return pl.pallas_call(
        attend_kernel,
        grid_spec=pltpu.PrefetchScalarGridSpec(
            num_scalar_prefetch=3,
            grid=(count,),
            in_specs=[
                mine,
                whole(1),
                whole(2),
                pl.BlockSpec((rows, 1), lambda i, *s: (i, 0)),
                pl.BlockSpec((count, rows), lambda i, *s: (0, 0)),
            ],
            out_specs=[
                pl.BlockSpec((1, rows, LANES), lambda i, *s: (i, 0, 0)),
                mine,
                mine,
            ],
        ),
        out_shape=[
            jax.ShapeDtypeStruct((count, rows, LANES), bf16),
            jax.ShapeDtypeStruct((total, LANES), f32),
            jax.ShapeDtypeStruct((total, LANES), f32),
        ],
        compiler_params=params(),
        name="attend",
    )(lo, hi, ok, qkv, qkv, qkv, doc_col, doc_row)


def attend_back_kernel(lo_ref, hi_ref, ok_ref, q_ref, k_ref, v_ref, doc_col_ref, doc_row_ref,
                       grad_ref, att_ref, lse_ref, cos_ref, sin_ref, out_ref, dk_ref, dv_ref):
    block = pl.program_id(0)
    count = pl.num_programs(0)
    rows = q_ref.shape[0]
    lane = lax.broadcasted_iota(jnp.int32, (rows, LANES), 1)

    @pl.when(block == 0)
    def _():
        dk_ref[...] = jnp.zeros(dk_ref.shape, f32)
        dv_ref[...] = jnp.zeros(dv_ref.shape, f32)

    docs = doc_col_ref[...]
    query = q_ref[...]
    grads = grad_ref[0]
    spread = grads.astype(f32) * att_ref[...]
    log_sums = lse_ref[...]
    here = pl.ds(pl.multiple_of(block * rows, rows), rows)

    def turn_back(values, span):
        return values * cos_ref[span, :] - rotate_half(values * sin_ref[span, :])

    out_ref[block, :, :LANES] = jnp.zeros((rows, LANES), bf16)
    for slot in range(SLOTS):
        mine = lane // HD == slot

        @pl.when(ok_ref[block * SLOTS + slot] == 1)
        def _():
            q_slot = jnp.where(mine, query, bf16(0))
            g_slot = jnp.where(mine, grads, bf16(0))
            delta = jnp.sum(jnp.where(mine, spread, 0.0), axis=1, keepdims=True)
            log_sum = log_sums[:, slot * HD : slot * HD + 1]

            def step(at, grad_query):
                span = pl.ds(pl.multiple_of(at * rows, rows), rows)
                keys = k_ref[span, :]
                scores = dot_tt(q_slot, keys)
                same = docs == doc_row_ref[pl.ds(at, 1), :]
                probs = jnp.exp(jnp.where(same, scores, NEG) - log_sum)
                dv_ref[span, :] += dot_rows(probs.astype(bf16), g_slot)
                grad_probs = dot_tt(g_slot, v_ref[span, :])
                grad_scores = (probs * (grad_probs - delta)).astype(bf16)
                dk_ref[span, :] += dot_rows(grad_scores, q_slot)
                return grad_query + jnp.dot(grad_scores, keys, preferred_element_type=f32)

            grad_query = lax.fori_loop(
                lo_ref[block], hi_ref[block], step, jnp.zeros((rows, LANES), f32)
            )
            turned = turn_back(grad_query * HD**-0.5, here).astype(bf16)
            out_ref[block, :, :LANES] = jnp.where(mine, turned, out_ref[block, :, :LANES])

    @pl.when(block == count - 1)
    def _():
        def finish(at, carry):
            span = pl.ds(pl.multiple_of(at * rows, rows), rows)
            out_ref[at, :, LANES : 2 * LANES] = turn_back(dk_ref[span, :], span).astype(bf16)
            out_ref[at, :, 2 * LANES :] = dv_ref[span, :].astype(bf16)
            return carry

        lax.fori_loop(0, count, finish, 0)


def attend_back(lo, hi, ok, qkv, doc_col, doc_row, grads, att, lse, cosine, sine, rows):
    total = qkv.shape[0]
    count = total // rows
    whole = lambda part: pl.BlockSpec((total, LANES), lambda i, *s: (0, part))
    mine = pl.BlockSpec((rows, LANES), lambda i, *s: (i, 0))
    return pl.pallas_call(
        attend_back_kernel,
        grid_spec=pltpu.PrefetchScalarGridSpec(
            num_scalar_prefetch=3,
            grid=(count,),
            in_specs=[
                mine,
                whole(1),
                whole(2),
                pl.BlockSpec((rows, 1), lambda i, *s: (i, 0)),
                pl.BlockSpec((count, rows), lambda i, *s: (0, 0)),
                pl.BlockSpec((1, rows, LANES), lambda i, *s: (i, 0, 0)),
                mine,
                mine,
                whole(0),
                whole(0),
            ],
            out_specs=pl.BlockSpec((count, rows, 3 * LANES), lambda i, *s: (0, 0, 0)),
            scratch_shapes=[pltpu.VMEM((total, LANES), f32), pltpu.VMEM((total, LANES), f32)],
        ),
        out_shape=jax.ShapeDtypeStruct((count, rows, 3 * LANES), bf16),
        compiler_params=params(),
        name="attend_back",
    )(lo, hi, ok, qkv, qkv, qkv, doc_col, doc_row, grads, att, lse, cosine, sine)


def program(fsdp, ctx):
    def on_device(tokens, segment_ids, positions, gain_attn, w_qkv, w_out, gain_mlp, w_in, w_down,
                  cotangent):
        rows, width = tokens.shape[1:]
        shard = w_qkv.shape[0]
        heads = width // HD
        common = math.gcd(heads, ctx)
        splits = ctx // common
        units = heads // common
        first = [min(units * c // splits, heads - SLOTS) for c in range(ctx)]
        owners = [
            [
                (c, slot)
                for c in range(ctx)
                for slot in range(SLOTS)
                if first[c] + slot == head
                and max(units * c, head * splits) < min(units * (c + 1), (head + 1) * splits)
            ]
            for head in range(heads)
        ]
        me = lax.axis_index("ctx")
        blocks = jnp.arange(ctx, dtype=jnp.int32)

        packed = jnp.concatenate([w_out, w_in, w_down.T], axis=1)
        mlp_all = lax.all_gather(packed, AXES, axis=0, tiled=True)

        gains = jnp.concatenate(
            [gain_attn[:, None], gain_mlp[:, None], jnp.zeros((shard, LANES - 2), bf16)], axis=1
        )
        head_cols = jnp.stack(
            [
                jnp.concatenate(
                    [
                        w_qkv[:, part * width + first[c] * HD : part * width + first[c] * HD + LANES]
                        for part in range(3)
                    ]
                    + [gains],
                    axis=1,
                )
                for c in range(ctx)
            ]
        )
        w_heads = lax.all_to_all(head_cols, "ctx", 0, 0, tiled=True).reshape(ctx * shard, 4 * LANES)
        w_heads = lax.all_gather(w_heads, "fsdp", axis=0, tiled=True)
        gain_one = w_heads[:, 3 * LANES].reshape(1, width)
        gain_two = w_heads[:, 3 * LANES + 1].reshape(1, width).astype(f32)

        places = jnp.concatenate(
            [segment_ids, positions // 64, positions % 64], axis=1
        ).astype(bf16)
        places = places.reshape(-1, width)
        places = jnp.concatenate([places, jnp.zeros((8 - places.shape[0], width), bf16)], axis=0)
        block = jnp.concatenate([tokens[0], places], axis=0)
        outer = ctx // 2
        ring = [(o * 2 + i, (o + 1) % outer * 2 + i) for o in range(outer) for i in range(2)]
        swap = [(c, c ^ 1) for c in range(ctx)]
        arrived = []
        order = []
        for step in range(outer):
            if step > 0:
                block = lax.ppermute(block, "ctx", ring)
            arrived += [block, lax.ppermute(block, "ctx", swap)]
            source = (me // 2 + outer - step) % outer * 2 + me % 2
            order += [source, source ^ 1]
        arrived = jnp.stack(arrived)
        order = jnp.stack(order).astype(jnp.int32)
        infos = arrived[:, rows : rows + 3 * rows // width, :].reshape(ctx, 3, rows).astype(f32)
        pick = (blocks[:, None] == order[None, :]).astype(f32)
        infos = jnp.sum(pick[:, :, None, None] * infos[None], axis=1)
        docs = infos[:, 0].astype(jnp.int32)
        spots = (infos[:, 1] * 64 + infos[:, 2]).reshape(ctx * rows, 1)
        first_doc = docs[:, 0]
        last_doc = docs[:, rows - 1]
        lo = jnp.sum((last_doc[None, :] < first_doc[:, None]).astype(jnp.int32), axis=1)
        hi = jnp.sum((first_doc[None, :] <= last_doc[:, None]).astype(jnp.int32), axis=1)
        unit = (
            (jnp.asarray(first, jnp.int32)[me] + jnp.arange(SLOTS, dtype=jnp.int32))[None, :] * splits
            + (blocks % splits)[:, None]
        )
        ok = ((unit >= units * me) & (unit < units * (me + 1))).astype(jnp.int32).reshape(-1)
        half = jnp.arange(LANES) % (HD // 2)
        rates = THETA ** (-2.0 * half.astype(f32) / HD)
        angles = spots * rates[None, :]
        cosine = jnp.cos(angles)
        sine = jnp.sin(angles)
        doc_col = docs.reshape(ctx * rows, 1)

        hidden_one, qkv = project(order, arrived, gain_one, w_heads, cosine, sine, rows)
        att_low, att, lse = attend(lo, hi, ok, qkv, doc_col, docs, rows)
        att_in = lax.all_to_all(att_low, "ctx", 0, 0, tiled=True)

        def join(parts, at):
            pieces = []
            for head in range(heads):
                terms = [
                    parts[c, :, at + slot * HD : at + (slot + 1) * HD] for c, slot in owners[head]
                ]
                total = terms[0].astype(f32)
                for term in terms[1:]:
                    total = total + term.astype(f32)
                pieces.append(total.astype(bf16))
            return jnp.concatenate(pieces, axis=1)

        attended = join(att_in, 0)

        inputs = tokens[0].astype(f32)
        w_proj = mlp_all[:, :width]
        w_up = mlp_all[:, width : width + w_in.shape[1]]
        w_back_t = mlp_all[:, width + w_in.shape[1] :]
        hidden_units = w_down.shape[0]
        middle = inputs + jnp.dot(attended, w_proj, preferred_element_type=f32)
        normed_two, inverse_two = norm_rows(middle)
        hidden_two = (normed_two * gain_two).astype(bf16)
        upward = jnp.dot(hidden_two, w_up, preferred_element_type=f32)
        inner = upward[:, :hidden_units]
        gate = upward[:, hidden_units:]
        cdf = 0.5 * (1.0 + jax.scipy.special.erf(inner * ROOT_HALF))
        gelu_value = inner * cdf
        product = (gelu_value * gate).astype(bf16)
        output = (middle + dot_tt(product, w_back_t)).astype(bf16)[None]
        grad_low = cotangent[0]
        grad_product = jnp.dot(grad_low, w_back_t, preferred_element_type=f32)
        grad_inner = (
            grad_product * gate * (cdf + inner * jnp.exp(-0.5 * inner * inner) * INV_ROOT_TWO_PI)
        )
        grad_gate = grad_product * gelu_value
        grad_up = jnp.concatenate([grad_inner, grad_gate], axis=1).astype(bf16)
        grad_hidden_two = dot_tt(grad_up, w_up)
        grad_middle = grad_low.astype(f32) + norm_back(
            grad_hidden_two * gain_two, normed_two, inverse_two
        )
        grad_branch = grad_middle.astype(bf16)
        grad_attended = dot_tt(grad_branch, w_proj).astype(bf16)
        grad_heads = jnp.stack(
            [grad_attended[:, first[c] * HD : first[c] * HD + LANES] for c in range(ctx)]
        )
        grad_heads = lax.all_to_all(grad_heads, "ctx", 0, 0, tiled=True)

        grad_packed = jnp.concatenate(
            [
                dot_rows(attended, grad_branch),
                dot_rows(hidden_two, grad_up),
                dot_rows(grad_low, product),
            ],
            axis=1,
        ).astype(bf16)
        grad_packed = lax.psum_scatter(grad_packed, "fsdp", scatter_dimension=0, tiled=True)
        grad_packed = lax.psum_scatter(grad_packed, "ctx", scatter_dimension=0, tiled=True)
        grad_packed = grad_packed.astype(f32)
        sum_w_out = grad_packed[:, :width]
        sum_w_in = grad_packed[:, width : width + w_in.shape[1]]
        sum_w_down = grad_packed[:, width + w_in.shape[1] :].T
        sum_gain_mlp = jnp.sum(w_in.astype(f32) * sum_w_in, axis=1) / gain_mlp.astype(f32)

        w_joined = lax.all_gather(w_qkv, AXES, axis=0, tiled=True)
        grad_joined = attend_back(
            lo, hi, ok, qkv, doc_col, docs, grad_heads, att, lse, cosine, sine, rows
        )
        grad_cols = dot_rows(hidden_one, grad_joined.reshape(ctx * rows, 3 * LANES)).astype(bf16)
        grad_joined = lax.all_to_all(grad_joined, "ctx", 0, 0, tiled=True)
        grad_joined = jnp.concatenate([join(grad_joined, part * LANES) for part in range(3)], axis=1)
        grad_hidden_one = dot_tt(grad_joined, w_joined)
        normed_one, inverse_one = norm_rows(inputs)
        input_grad = grad_middle + norm_back(
            grad_hidden_one * gain_one.astype(f32), normed_one, inverse_one
        )

        grad_cols = grad_cols.reshape(fsdp, ctx * shard, 3 * LANES)
        grad_cols = lax.all_to_all(grad_cols, "fsdp", 0, 0, tiled=True)
        grad_cols = jnp.sum(grad_cols.astype(f32), axis=0).astype(bf16)
        grad_cols = lax.all_to_all(grad_cols.reshape(ctx, shard, 3 * LANES), "ctx", 0, 0, tiled=True)
        grad_cols = grad_cols.astype(f32)
        pieces = []
        for part in range(3):
            for head in range(heads):
                total = 0.0
                for c, slot in owners[head]:
                    at = part * LANES + slot * HD
                    total = total + grad_cols[c, :, at : at + HD]
                pieces.append(total)
        sum_w_qkv = jnp.concatenate(pieces, axis=1)
        sum_gain_attn = jnp.sum(w_qkv.astype(f32) * sum_w_qkv, axis=1) / gain_attn.astype(f32)
        return (
            output,
            input_grad.astype(bf16)[None],
            sum_gain_attn,
            sum_w_qkv,
            sum_w_out,
            sum_gain_mlp,
            sum_w_in,
            sum_w_down,
        )

    return on_device


def solution(mesh):
    rows = P(AXES, None)
    tokens = P("fsdp", "ctx", None)
    return jax.shard_map(
        program(mesh.shape["fsdp"], mesh.shape["ctx"]),
        mesh=mesh,
        in_specs=(
            tokens,
            P("fsdp", "ctx"),
            P("fsdp", "ctx"),
            P(AXES),
            rows,
            rows,
            P(AXES),
            rows,
            P(None, AXES),
            tokens,
        ),
        out_specs=(tokens, tokens, P(AXES), rows, rows, P(AXES), rows, P(None, AXES)),
        check_vma=False,
    )
```

time: 1080 us -> 411 us (0.38)
  waiting for transfers between devices: 771 us -> 145 us
  Pallas kernels: 0 us -> 82.9 us
  matrix products: 99 us -> 25.7 us
  blocking collectives: 101 us -> 59.6 us
  local copies, waits for them, and re-layouts: 61.1 us -> 35.1 us
  starting transfers between devices: 0.66 us -> 20.8 us
    reduce_scatter x5 -> x1, waiting for transfers between devices: 430 us -> 0.02 us  [on_device(): lax.psum_scatter(grad_packed, 'fsdp', scatter_dimension=0, tiled=True)]
    all_gather x6 -> x2, waiting for transfers between devices: 229 us -> 0.04 us  [the longest x1 0.02 us: on_device(): mlp_all = lax.all_gather(packed, AXES, axis=0, tiled=True)]
    pallas_call x0 -> x3, Pallas kernels: none -> 82.9 us  [the longest x1 45 us: attend_back(): pl.pallas_call(attend_back_kernel, grid_spec=pltpu.PrefetchScalarGridSpec...]
    unnamed x2 -> x0, blocking collectives: 82.1 us -> none
    dot_general x25 -> x10, matrix products: 94.1 us -> 22.1 us  [the longest x4 9.7 us: dot_rows(): lax.dot_general(left, right, (((0,), (0,)), ((), ())), preferred_element_...]
    unnamed x13 -> x5, waiting for transfers between devices: 111 us -> 50.5 us
    all_to_all x0 -> x3, waiting for transfers between devices: none -> 54.5 us  [the longest x1 38.2 us: on_device(): grad_joined = lax.all_to_all(grad_joined, 'ctx', 0, 0, tiled=True)]
    all_to_all x0 -> x3, blocking collectives: none -> 48.9 us  [the longest x1 19.5 us: on_device(): grad_cols = lax.all_to_all(grad_cols, 'fsdp', 0, 0, tiled=True)]
  transfers between devices with their start and end apart: 12 -> 14, of which waited for: 12 -> 7; matrix products, arithmetic and copies ran while one was open for 9% -> 13% of each run, Pallas kernels for 0% -> 20%
where the time goes in v1:
time: 411 us
  waiting for transfers between devices  145 us (35%)
  Pallas kernels  82.9 us (20%)
  blocking collectives  59.6 us (15%)
  local copies, waits for them, and re-layouts  35.1 us (9%)
  other arithmetic  27.5 us (7%)
  matrix products  25.7 us (6%)
  starting transfers between devices  20.8 us (5%)
  between operations  14.3 us (3%)
    unnamed x5, waiting for transfers between devices  50.5 us
    pallas_call x1, Pallas kernels, attend_back(): pl.pallas_call(attend_back_kernel, grid_spec=pltpu.PrefetchScalarGridSpec...  45 us
    all_to_all x1, waiting for transfers between devices, on_device(): grad_joined = lax.all_to_all(grad_joined, 'ctx', 0, 0, tiled=True)  38.2 us
    ppermute x3, waiting for transfers between devices, on_device(): block = lax.ppermute(block, 'ctx', ring)  32.7 us
    pallas_call x1, Pallas kernels, attend(): pl.pallas_call(attend_kernel, grid_spec=pltpu.PrefetchScalarGridSpec(num_...  28.2 us
    all_to_all x1, blocking collectives, on_device(): grad_cols = lax.all_to_all(grad_cols, 'fsdp', 0, 0, tiled=True)  19.5 us
    unnamed x66, local copies, waits for them, and re-layouts  15.9 us
    all_to_all x1, blocking collectives, on_device(): lax.all_to_all(grad_cols.reshape(ctx, shard, 3 * LANES), 'ctx', 0, 0, til...  15.7 us
  transfers between devices with their start and end apart: 14, of which 7 were waited for; matrix products, arithmetic and copies ran while one was open for 13% of the time, Pallas kernels for 20%

profile of v1, /device:TPU:0, one launch (start us, length us, event | category | flops | bytes accessed | tf_op | source)
XLA Modules:
  0.0 411.0 jit_solution(9658045526562160982)
XLA Ops:
  11.5 3.0 collective-permute-start
  25.1 3.9 all-to-all-start
  31.2 6.4 %all-to-all-done = bf16[8,24,512]{2,1,0:T(8,128)(2,1)S(1)} async-done(((bf16[8,24,512]{2,1,0:T(8,128)(2,1)}), bf16[8,24,512]{2,1,0:T(8,128)(2,1)S(1)}, u32[]{:S(2)}, u32[]{:S(2)}) %all-to-all-start) | async-done | bytes 196640 | tf_op jit(solution)/shard_map/all_to_all | solution.py:320
  37.7 10.7 %all_gather.9.w_ref = bf16[768,512]{1,0:T(8,128)(2,1)S(1)} all-gather(bf16[192,512]{1,0:T(8,128)(2,1)S(1)} %bitcast.295), channel_id=1, replica_groups=mesh['fsdp'=4,'ctx'=8] {'fsdp'}, dimensions={0}, use_global_device_ids=true | all-gather | bytes 983040 | tf_op jit(solution)/shard_map/all_gather | solution.py:321
  52.1 14.2 %collective-permute-done.3 = bf16[264,768]{1,0:T(8,128)(2,1)S(1)} collective-permute-done((bf16[264,768]{1,0:T(8,128)(2,1)S(1)}, bf16[264,768]{1,0:T(8,128)(2,1)S(1)}, u32[]{:S(2)}, u32[]{:S(2)}) %collective-permute-start.3) | collective-permute-done | bytes 405536 | tf_op jit(solution)/shard_map/ppermute | solution.py:338
  68.0 18.5 %collective-permute-done.5 = bf16[264,768]{1,0:T(8,128)(2,1)S(1)} collective-permute-done((bf16[264,768]{1,0:T(8,128)(2,1)S(1)}, bf16[264,768]{1,0:T(8,128)(2,1)S(1)}, u32[]{:S(2)}, u32[]{:S(2)}) %collective-permute-start.5) | collective-permute-done | bytes 405536 | tf_op jit(solution)/shard_map/ppermute | solution.py:338
  86.5 1.9 collective-permute-start.6
  90.0 7.4 %collective-permute-done.6 = bf16[264,768]{1,0:T(8,128)(2,1)S(1)} collective-permute-done((bf16[264,768]{1,0:T(8,128)(2,1)S(1)}, bf16[264,768]{1,0:T(8,128)(2,1)S(1)}, u32[]{:S(2)}, u32[]{:S(2)}) %collective-permute-start.6) | collective-permute-done | bytes 405536 | tf_op jit(solution)/shard_map/ppermute | solution.py:339
  99.7 3.7 multiply_sine_fusion
  105.1 9.7 %project.1 = (bf16[2048,768]{1,0:T(8,128)(2,1)}, bf16[2048,384]{1,0:T(8,128)(2,1)}) custom-call(s32[8]{0:T(128)S(1)} %stack.116.order_ref, bf16[8,264,768]{2,1,0:T(8,128)(2,1)} %bitcast_dynamic-update-slice_fusion.x_ref, bf16[1,768]{1,0:T(2,128)(2,1)S(1)} %reshape_squeeze.4.gain_ref, bf16[768,512]{1,0:T(8,128)(2,1)S(1)} %copy-done.3, ...), custom_call_target="tpu_custom_call" | custom-call | tf_op jit(solution)/shard_map/project/pallas_call | solution.py:83
  115.2 28.2 %attend.1 = (bf16[8,256,128]{2,1,0:T(8,128)(2,1)}, f32[2048,128]{1,0:T(8,128)S(1)}, f32[2048,128]{1,0:T(8,128)S(1)}) custom-call(s32[8]{0:T(128)S(1)} %get-tuple-element.27.lo_ref, s32[8]{0:T(128)S(1)} %get-tuple-element.26.hi_ref, s32[16]{0:T(128)S(1)} %reshape.301.ok_ref, bf16[2048,384]{1,0:T(8,128)(2,1)} %get-tuple-element.13.q_ref.k_ref.v_ref, ...), custom_call_target="tpu_custom_call" | custom-call | tf_op jit(solution)/shard_map/attend/pallas_call | solution.py:157
  144.5 4.9 %all-to-all-start.1 = ((bf16[8,256,128]{2,1,0:T(8,128)(2,1)}), bf16[8,256,128]{2,1,0:T(8,128)(2,1)}, u32[]{:S(2)}, u32[]{:S(2)}) async-start(bf16[8,256,128]{2,1,0:T(8,128)(2,1)} %get-tuple-element.14), calls=%async_computation.1 | async-start | bytes 1048576 | tf_op jit(solution)/shard_map/all_to_all | solution.py:367
  149.8 9.9 %all-to-all-done.1 = bf16[8,256,128]{2,1,0:T(8,128)(2,1)} async-done(((bf16[8,256,128]{2,1,0:T(8,128)(2,1)}), bf16[8,256,128]{2,1,0:T(8,128)(2,1)}, u32[]{:S(2)}, u32[]{:S(2)}) %all-to-all-start.1) | async-done | bytes 524320 | tf_op jit(solution)/shard_map/all_to_all | solution.py:367
  160.9 1.8 slice_bitcast_fusion.33
  163.9 2.0 fusion.96
  166.2 3.5 fusion.2
  171.2 1.9 fusion.4
  173.1 3.0 convolution_convert_fusion
  179.9 2.4 copy.104
  182.3 6.4 %pad_maximum_fusion = bf16[768,4224]{1,0:T(8,128)(2,1)} fusion(bf16[768,1152]{1,0:T(8,128)(2,1)} %fusion.4, bf16[768,2304]{1,0:T(8,128)(2,1)} %convolution_convert_fusion, bf16[768,768]{1,0:T(8,128)(2,1)} %copy.104), kind=kLoop, calls=%fused_computation | loop fusion | flops 19464192 | bytes 12976128 | tf_op jit(solution)/shard_map/concatenate | solution.py:416
  189.5 1.8 convolution_convert_fusion.4
  191.7 13.8 %all_to_all.30.grad_ref = bf16[8,256,128]{2,1,0:T(8,128)(2,1)S(1)} all-to-all(bf16[8,256,128]{2,1,0:T(8,128)(2,1)S(1)} %fusion.59), channel_id=1, replica_groups=mesh['fsdp'=4,'ctx'=8] {'ctx'}, dimensions={0} | all-to-all | bytes 1048576 | tf_op jit(solution)/shard_map/all_to_all | solution.py:414
  206.7 45.0 %attend_back.1 = bf16[8,256,384]{2,1,0:T(8,128)(2,1)} custom-call(s32[8]{0:T(128)S(1)} %get-tuple-element.27.lo_ref, s32[8]{0:T(128)S(1)} %get-tuple-element.26.hi_ref, s32[16]{0:T(128)S(1)} %reshape.301.ok_ref, bf16[2048,384]{1,0:T(8,128)(2,1)} %get-tuple-element.13.q_ref.k_ref.v_ref, bf16[2048,384]{1,0:T(8,128)(2,1)} %get-tuple-element.13.q_ref.k_ref.v_ref, ...), custom_call_target="tpu_custom_call" | custom-call | tf_op jit(solution)/shard_map/attend_back/pallas_call | solution.py:252
  251.7 3.2 convolution_convert_fusion.3
  255.0 19.5 %all_to_all.31 = bf16[4,192,384]{2,1,0:T(8,128)(2,1)S(1)} all-to-all(bf16[4,192,384]{2,1,0:T(8,128)(2,1)S(1)} %bitcast.294), channel_id=1, replica_groups=mesh['fsdp'=4,'ctx'=8] {'fsdp'}, dimensions={0} | all-to-all | bytes 1179648 | tf_op jit(solution)/shard_map/all_to_all | solution.py:446
  274.5 15.7 %all_to_all.32 = bf16[8,24,384]{2,1,0:T(8,128)(2,1)} all-to-all(bf16[8,24,384]{2,1,0:T(8,128)(2,1)S(1)} %bitcast.296), channel_id=1, replica_groups=mesh['fsdp'=4,'ctx'=8] {'ctx'}, dimensions={0} | all-to-all | bytes 294912 | tf_op jit(solution)/shard_map/all_to_all | solution.py:448
  290.2 3.7 all-to-all-start.3
  294.7 3.2 fusion.17
  300.0 38.2 %all-to-all-done.3 = bf16[8,256,384]{2,1,0:T(8,128)(2,1)S(1)} async-done(((bf16[8,256,384]{2,1,0:T(8,128)(2,1)}), bf16[8,256,384]{2,1,0:T(8,128)(2,1)S(1)}, u32[]{:S(2)}, u32[]{:S(2)}) %all-to-all-start.3) | async-done | bytes 1572896 | tf_op jit(solution)/shard_map/all_to_all | solution.py:437
  342.0 3.0 concatenate.81
  345.0 3.3 fusion.92
  349.4 49.8 %reduce-scatter.7.cloned.1.call-done = bf16[24,4224]{1,0:T(8,128)(2,1)} async-done(((bf16[192,4224]{1,0:T(8,128)(2,1)}), bf16[24,4224]{1,0:T(8,128)(2,1)}) %reduce-scatter.7.cloned.1.call-update) | async-done | bytes 202768
  (161 shorter events, 53.3 us)
Async XLA Ops:
  7.2 21.8 %copy-start.21 = (s32[8]{0:T(128)S(1)}, s32[8]{0:T(128)}, u32[]{:S(2)}) copy-start(s32[8]{0:T(128)} %constant.162.clone) | copy-start | bytes 100
  7.2 23.2 %copy-start.7 = (bf16[1,256,768]{2,1,0:T(8,128)(2,1)S(1)}, bf16[1,256,768]{2,1,0:T(8,128)(2,1)}, u32[]{:S(2)}) copy-start(bf16[1,256,768]{2,1,0:T(8,128)(2,1)} %param.11) | copy-start | bytes 1179652
  7.2 156.7 %all-gather.3.cloned.1.call-start = ((), (), s32[]{:S(2)}) async-start(), calls=%async_computation.8 | async-start | bytes 6690816 | tf_op jit(solution)/shard_map/all_gather | solution.py:302
  11.5 39.0 %collective-permute-start = (bf16[264,768]{1,0:T(8,128)(2,1)S(1)}, bf16[264,768]{1,0:T(8,128)(2,1)S(1)}, u32[]{:S(2)}, u32[]{:S(2)}) collective-permute-start(bf16[264,768]{1,0:T(8,128)(2,1)S(1)} %maximum_maximum_fusion), channel_id=1, source_target_pairs={{0,1},{1,0},{2,3},{3,2},{4,5},{5,4},{6,7},{7,6},{8,9},{9,8},{10,11... | collective-permute-start | bytes 1216520 | tf_op jit(solution)/shard_map/ppermute | solution.py:339
  14.5 34.8 %collective-permute-start.1 = (bf16[264,768]{1,0:T(8,128)(2,1)S(1)}, bf16[264,768]{1,0:T(8,128)(2,1)S(1)}, u32[]{:S(2)}, u32[]{:S(2)}) collective-permute-start(bf16[264,768]{1,0:T(8,128)(2,1)S(1)} %maximum_maximum_fusion), channel_id=1, source_target_pairs={{0,2},{1,3},{2,4},{3,5},{4,6},{5,7},{6,0},{7,1},{8,10},{9,11},{10,... | collective-permute-start | bytes 1216520 | tf_op jit(solution)/shard_map/ppermute | solution.py:338
  25.1 12.6 %all-to-all-start = ((bf16[8,24,512]{2,1,0:T(8,128)(2,1)}), bf16[8,24,512]{2,1,0:T(8,128)(2,1)S(1)}, u32[]{:S(2)}, u32[]{:S(2)}) async-start(bf16[8,24,512]{2,1,0:T(8,128)(2,1)} %constant_dynamic-update-slice_fusion), calls=%async_computation | async-start | bytes 393216 | tf_op jit(solution)/shard_map/all_to_all | solution.py:320
  49.4 17.0 %collective-permute-start.2 = (bf16[264,768]{1,0:T(8,128)(2,1)S(1)}, bf16[264,768]{1,0:T(8,128)(2,1)S(1)}, u32[]{:S(2)}, u32[]{:S(2)}) collective-permute-start(bf16[264,768]{1,0:T(8,128)(2,1)S(1)} %collective-permute-done.1), channel_id=1, source_target_pairs={{0,1},{1,0},{2,3},{3,2},{4,5},{5,4},{6,7},{7,6},{8,9},{9,8},{10,11... | collective-permute-start | bytes 1216520 | tf_op jit(solution)/shard_map/ppermute | solution.py:339
  50.6 15.8 %collective-permute-start.3 = (bf16[264,768]{1,0:T(8,128)(2,1)S(1)}, bf16[264,768]{1,0:T(8,128)(2,1)S(1)}, u32[]{:S(2)}, u32[]{:S(2)}) collective-permute-start(bf16[264,768]{1,0:T(8,128)(2,1)S(1)} %collective-permute-done.1), channel_id=1, source_target_pairs={{0,2},{1,3},{2,4},{3,5},{4,6},{5,7},{6,0},{7,1},{8,10},{9,11},{10,... | collective-permute-start | bytes 1216520 | tf_op jit(solution)/shard_map/ppermute | solution.py:338
  66.3 22.1 %collective-permute-start.4 = (bf16[264,768]{1,0:T(8,128)(2,1)S(1)}, bf16[264,768]{1,0:T(8,128)(2,1)S(1)}, u32[]{:S(2)}, u32[]{:S(2)}) collective-permute-start(bf16[264,768]{1,0:T(8,128)(2,1)S(1)} %collective-permute-done.3), channel_id=1, source_target_pairs={{0,1},{1,0},{2,3},{3,2},{4,5},{5,4},{6,7},{7,6},{8,9},{9,8},{10,11... | collective-permute-start | bytes 1216520 | tf_op jit(solution)/shard_map/ppermute | solution.py:339
  66.4 20.2 %collective-permute-start.5 = (bf16[264,768]{1,0:T(8,128)(2,1)S(1)}, bf16[264,768]{1,0:T(8,128)(2,1)S(1)}, u32[]{:S(2)}, u32[]{:S(2)}) collective-permute-start(bf16[264,768]{1,0:T(8,128)(2,1)S(1)} %collective-permute-done.3), channel_id=1, source_target_pairs={{0,2},{1,3},{2,4},{3,5},{4,6},{5,7},{6,0},{7,1},{8,10},{9,11},{10,... | collective-permute-start | bytes 1216520 | tf_op jit(solution)/shard_map/ppermute | solution.py:338
  86.5 10.9 %collective-permute-start.6 = (bf16[264,768]{1,0:T(8,128)(2,1)S(1)}, bf16[264,768]{1,0:T(8,128)(2,1)S(1)}, u32[]{:S(2)}, u32[]{:S(2)}) collective-permute-start(bf16[264,768]{1,0:T(8,128)(2,1)S(1)} %collective-permute-done.5), channel_id=1, source_target_pairs={{0,1},{1,0},{2,3},{3,2},{4,5},{5,4},{6,7},{7,6},{8,9},{9,8},{10,11... | collective-permute-start | bytes 1216520 | tf_op jit(solution)/shard_map/ppermute | solution.py:339
  103.4 11.4 %copy-start = (f32[2048,128]{1,0:T(8,128)}, f32[2048,128]{1,0:T(8,128)S(1)}, u32[]{:S(2)}) copy-start(f32[2048,128]{1,0:T(8,128)S(1)} %get-tuple-element.145.sin_ref) | copy-start | bytes 3145732
  103.4 11.4 %copy-start.1 = (f32[2048,128]{1,0:T(8,128)}, f32[2048,128]{1,0:T(8,128)S(1)}, u32[]{:S(2)}) copy-start(f32[2048,128]{1,0:T(8,128)S(1)} %get-tuple-element.146.cos_ref) | copy-start | bytes 3145732
  103.4 1.7 copy-start.3
  115.2 34.4 %copy-start.4 = (bf16[768,512]{1,0:T(8,128)(2,1)S(1)}, bf16[768,512]{1,0:T(8,128)(2,1)}, u32[]{:S(2)}) copy-start(bf16[768,512]{1,0:T(8,128)(2,1)} %copy-done.2) | copy-start | bytes 2359300
  144.5 15.3 %all-to-all-start.1 = ((bf16[8,256,128]{2,1,0:T(8,128)(2,1)}), bf16[8,256,128]{2,1,0:T(8,128)(2,1)}, u32[]{:S(2)}, u32[]{:S(2)}) async-start(bf16[8,256,128]{2,1,0:T(8,128)(2,1)} %get-tuple-element.14), calls=%async_computation.1 | async-start | bytes 1048576 | tf_op jit(solution)/shard_map/all_to_all | solution.py:367
  149.4 145.3 %reduce-scatter.5.cloned.1.call-start = ((), (), s32[]{:S(2)}) async-start(), calls=%async_computation.10 | async-start | bytes 8110080 | tf_op jit(solution)/shard_map/reduce_scatter | solution.py:424
  163.9 5.8 %copy-start.11 = (bf16[256,768]{1,0:T(8,128)(2,1)}, bf16[256,768]{1,0:T(8,128)(2,1)S(1)}, u32[]{:S(2)}) copy-start(bf16[256,768]{1,0:T(8,128)(2,1)S(1)} %concatenate.78) | copy-start | bytes 1179652
  165.9 11.5 %copy-start.8 = (f32[256,768]{1,0:T(8,128)}, f32[256,768]{1,0:T(8,128)S(1)}, u32[]{:S(2)}) copy-start(f32[256,768]{1,0:T(8,128)S(1)} %get-tuple-element.150) | copy-start | bytes 2359300
  165.9 4.2 %copy-start.18 = (bf16[768,4224]{1,0:T(8,128)(2,1)S(1)}, bf16[768,4224]{1,0:T(8,128)(2,1)}, u32[]{:S(2)}) copy-start(bf16[768,4224]{1,0:T(8,128)(2,1)} %all-gather.3.cloned.1.call-done) | copy-start | bytes 19464196
  166.2 4.0 copy-start.13
  171.1 2.0 copy-start.16
  188.7 156.3 %all-gather.5.cloned.1.call-start = ((), (), s32[]{:S(2)}) async-start(), calls=%async_computation.9 | async-start | bytes 3649536 | tf_op jit(solution)/shard_map/all_gather | solution.py:432
  206.7 45.0 %copy-start.10 = (bf16[2048,768]{1,0:T(8,128)(2,1)S(1)}, bf16[2048,768]{1,0:T(8,128)(2,1)}, u32[]{:S(2)}) copy-start(bf16[2048,768]{1,0:T(8,128)(2,1)} %get-tuple-element.17) | copy-start | bytes 9437188
  290.2 4.4 %copy-start.9 = (f32[256,768]{1,0:T(8,128)S(1)}, f32[256,768]{1,0:T(8,128)}, u32[]{:S(2)}) copy-start(f32[256,768]{1,0:T(8,128)} %copy-done.8) | copy-start | bytes 2359300
  290.2 48.0 %all-to-all-start.3 = ((bf16[8,256,384]{2,1,0:T(8,128)(2,1)}), bf16[8,256,384]{2,1,0:T(8,128)(2,1)S(1)}, u32[]{:S(2)}, u32[]{:S(2)}) async-start(bf16[8,256,384]{2,1,0:T(8,128)(2,1)} %attend_back.1), calls=%async_computation.3 | async-start | bytes 3145728 | tf_op jit(solution)/shard_map/all_to_all | solution.py:437
  294.0 105.2 %reduce-scatter.7.cloned.1.call-start = ((), (), s32[]{:S(2)}) async-start(), calls=%async_computation.11 | async-start | bytes 1824768
  294.7 3.2 copy-start.15
  294.7 4.8 %copy-start.19 = (bf16[24]{0:T(256)(128)(2,1)S(1)}, bf16[24]{0:T(256)(128)(2,1)}, u32[]{:S(2)}) copy-start(bf16[24]{0:T(256)(128)(2,1)} %param.14) | copy-start | bytes 148
  298.3 43.6 %copy-start.14 = (f32[24,2304]{1,0:T(8,128)}, f32[24,2304]{1,0:T(8,128)S(1)}, u32[]{:S(2)}) copy-start(f32[24,2304]{1,0:T(8,128)S(1)} %concatenate.82) | copy-start | bytes 663556
  348.3 50.9 %copy-start.17 = (bf16[24,2304]{1,0:T(8,128)(2,1)S(1)}, bf16[24,2304]{1,0:T(8,128)(2,1)}, u32[]{:S(2)}) copy-start(bf16[24,2304]{1,0:T(8,128)(2,1)} %param.18) | copy-start | bytes 331780
  348.3 52.6 %copy-start.20 = (bf16[24]{0:T(256)(128)(2,1)S(1)}, bf16[24]{0:T(256)(128)(2,1)}, u32[]{:S(2)}) copy-start(bf16[24]{0:T(256)(128)(2,1)} %param.17) | copy-start | bytes 148
  (4 other events, 4.1 us)
Sparse Core Ops, SparseCore 0:
  11.4 85.4 all-gather.2
  188.8 62.2 reduce-scatter.4
  254.6 78.3 all-gather.4
  336.7 62.3 reduce-scatter.6

commit v2 on v1

v2 whole, which is shorter than its diff:
```python
import functools
import math

import jax
import jax.numpy as jnp
from jax import lax
from jax.experimental import pallas as pl
from jax.experimental.pallas import tpu as pltpu
from jax.sharding import PartitionSpec as P

HD = 64
SLOTS = 2
LANES = SLOTS * HD
GRAIN = 128
KEY_TILE = 512
CHUNK = 384
EPS = 1e-05
THETA = 160000.0
NEG = -1e30
ROOT_HALF = 0.7071067811865476
INV_ROOT_TWO_PI = 0.3989422804014327
VMEM_BYTES = 50 * 1024 * 1024
AXES = ("fsdp", "ctx")

f32 = jnp.float32
bf16 = jnp.bfloat16


def norm_rows(values):
    center = values - jnp.mean(values, axis=-1, keepdims=True)
    spread = jnp.mean(center * center, axis=-1, keepdims=True)
    inverse = lax.rsqrt(spread + EPS)
    return (center * inverse, inverse)


def norm_back(grad_normed, normed, inverse):
    return inverse * (
        grad_normed
        - jnp.mean(grad_normed, axis=-1, keepdims=True)
        - normed * jnp.mean(grad_normed * normed, axis=-1, keepdims=True)
    )


def rotate_half(values):
    lane = lax.broadcasted_iota(jnp.int32, values.shape, 1)
    ahead = pltpu.roll(values, LANES - HD // 2, 1)
    behind = pltpu.roll(values, HD // 2, 1)
    return jnp.where(lane % HD < HD // 2, -ahead, behind)


def dot_tt(left, right):
    return lax.dot_general(left, right, (((1,), (1,)), ((), ())), preferred_element_type=f32)


def dot_rows(left, right):
    return lax.dot_general(left, right, (((0,), (0,)), ((), ())), preferred_element_type=f32)


def params():
    return pltpu.CompilerParams(
        dimension_semantics=("arbitrary",), vmem_limit_bytes=VMEM_BYTES
    )


def spread_kernel(first, w_ref, gain_one_ref, gain_two_ref, doc_ref, place_ref, out_ref):
    shard, columns = w_ref.shape
    width = columns // 3
    rows = doc_ref.shape[1]
    square = (shard, shard)
    eye = lax.broadcasted_iota(jnp.int32, square, 0) == lax.broadcasted_iota(jnp.int32, square, 1)

    def upright(ref):
        spread = jnp.where(eye, ref[...].astype(f32), 0.0)
        return jnp.sum(spread, axis=1, keepdims=True).astype(bf16)

    lane = lax.broadcasted_iota(jnp.int32, (shard, LANES), 1)
    gains = jnp.where(
        lane == 0, upright(gain_one_ref), jnp.where(lane == 1, upright(gain_two_ref), bf16(0))
    )
    place = place_ref[...]
    top = jnp.concatenate([doc_ref[...], place >> 6], axis=1).astype(f32)
    low = jnp.concatenate([place & 63, jnp.zeros_like(place)], axis=1).astype(f32)
    row = lax.broadcasted_iota(jnp.int32, (8, 2 * rows), 0)
    places = jnp.where(row == 0, top, jnp.where(row == 1, low, 0.0)).astype(bf16)
    for c, head in enumerate(first):
        for part in range(3):
            at = part * width + head * HD
            out_ref[c, :shard, part * LANES : (part + 1) * LANES] = w_ref[:, at : at + LANES]
        out_ref[c, :shard, 3 * LANES :] = gains
        out_ref[c, shard:, :] = places


def spread(first, w_qkv, gain_one, gain_two, docs, places):
    shard = w_qkv.shape[0]
    return pl.pallas_call(
        functools.partial(spread_kernel, first),
        out_shape=jax.ShapeDtypeStruct((len(first), shard + 8, 4 * LANES), bf16),
        compiler_params=pltpu.CompilerParams(vmem_limit_bytes=VMEM_BYTES),
        name="spread",
    )(w_qkv, gain_one[None], gain_two[None], docs, places)


def project_kernel(masks, at_ref, own_ref, other_ref, w_ref, cos_ref, sin_ref, *refs):
    hidden_ref, qkv_ref, turned_ref, gains_ref, w_all = refs[-5:]
    rows = own_ref.shape[0]
    share = w_ref.shape[1]
    for i, mask in enumerate(masks):
        start = pl.multiple_of((at_ref[2] ^ mask) * share, share)
        w_all[pl.ds(start, share), :] = w_ref[i]
    gains = jnp.transpose(w_all[:, 3 * LANES :].astype(f32))
    gains_ref[...] = gains[:8]
    gain = gains[:1]
    for flip, x_ref in enumerate((own_ref, other_ref)):
        span = pl.ds(pl.multiple_of((at_ref[1] ^ flip) * rows, rows), rows)
        normed, _ = norm_rows(x_ref[...].astype(f32))
        hidden = (normed * gain).astype(bf16)
        hidden_ref[span, :] = hidden
        joined = jnp.dot(hidden, w_all[:, : 3 * LANES], preferred_element_type=f32)
        cosine = cos_ref[span, :]
        sine = sin_ref[span, :]
        query = joined[:, :LANES]
        keys = joined[:, LANES : 2 * LANES]
        values = joined[:, 2 * LANES :]
        query = (query * cosine + rotate_half(query) * sine).astype(bf16)
        keys = keys * cosine + rotate_half(keys) * sine
        qkv_ref[span, :LANES] = query * bf16(HD**-0.5)
        qkv_ref[span, LANES : 2 * LANES] = keys.astype(bf16)
        qkv_ref[span, 2 * LANES :] = values.astype(bf16)
        turned_ref[:LANES, span] = jnp.transpose(keys).astype(bf16)
        turned_ref[LANES:, span] = jnp.transpose(values).astype(bf16)


def project(masks, at, own, other, w_parts, cosine, sine, total, held):
    rows, width = own.shape
    fixed = lambda shape: pl.BlockSpec(shape, lambda i, at: (0,) * len(shape))
    pair = lambda width: pl.BlockSpec((2 * rows, width), lambda i, at: (at[0], 0))
    shapes = [
        jax.ShapeDtypeStruct((total, width), bf16),
        jax.ShapeDtypeStruct((total, 3 * LANES), bf16),
        jax.ShapeDtypeStruct((2 * LANES, total), bf16),
    ]
    return pl.pallas_call(
        functools.partial(project_kernel, masks),
        grid_spec=pltpu.PrefetchScalarGridSpec(
            num_scalar_prefetch=1,
            grid=(1,),
            in_specs=[
                fixed((rows, width)),
                fixed((rows, width)),
                fixed(w_parts.shape),
                pair(LANES),
                pair(LANES),
            ]
            + [pl.BlockSpec(memory_space=pl.ANY) for _ in held],
            out_specs=[
                pair(width),
                pair(3 * LANES),
                pl.BlockSpec((2 * LANES, 2 * rows), lambda i, at: (0, at[0])),
                fixed((8, width)),
            ],
            scratch_shapes=[pltpu.VMEM((width, 4 * LANES), bf16)],
        ),
        out_shape=shapes + [jax.ShapeDtypeStruct((8, width), f32)],
        input_output_aliases={6 + i: i for i in range(len(held))},
        compiler_params=params(),
        cost_estimate=pl.CostEstimate(
            flops=2 * 2 * rows * width * 3 * LANES, bytes_accessed=6 << 20, transcendentals=0
        ),
        name="project",
    )(at, own, other, w_parts, cosine, sine, *held)


def gather_rows(units_ref, ref, units, part):
    lane = lax.broadcasted_iota(jnp.int32, (part, LANES), 1)
    chunks = []
    for i in range(units):
        start = pl.multiple_of(units_ref[units + i] * part, part)
        chunk = ref[pl.ds(start, part), :]
        chunks.append(jnp.where(lane // HD == units_ref[i], chunk, jnp.zeros_like(chunk)))
    return jnp.concatenate(chunks, axis=0)


def scatter_rows(units_ref, acc_ref, values, units, part):
    lane = lax.broadcasted_iota(jnp.int32, (part, LANES), 1)
    acc_ref[...] = jnp.zeros(acc_ref.shape, f32)
    for i in range(units):
        start = pl.multiple_of(units_ref[units + i] * part, part)
        chunk = values[i * part : (i + 1) * part]
        acc_ref[pl.ds(start, part), :] += jnp.where(lane // HD == units_ref[i], chunk, 0.0)


def across(slab, wide):
    if wide <= LANES:
        return slab[:, :wide]
    return jnp.concatenate([slab] * (wide // LANES), axis=1)


def fold(values, reduce):
    rows, wide = values.shape
    return reduce(values.reshape(rows // 8, 8, wide), axis=0)


def tile_span(base_ref, block, at, tile):
    return pl.ds(pl.multiple_of(base_ref[block] * GRAIN + at * tile, GRAIN), tile)


def attend_kernel(units, tile, base_ref, count_ref, units_ref, q_ref, k_ref, vt_ref, doc_ref, doc_q_ref,
                  low_ref, att_ref, lse_ref, s_ref, acc_ref):
    block = pl.program_id(0)
    wide = s_ref.shape[1]
    part = wide // units
    queries = gather_rows(units_ref, q_ref, units, part)
    doc_q = doc_q_ref[0]

    def score(at, top):
        span = tile_span(base_ref, block, at, tile)
        scores = dot_tt(k_ref[span, :], queries)
        scores = jnp.where(across(doc_ref[span, :], wide) == doc_q, scores, NEG)
        s_ref[span, :] = scores
        return jnp.maximum(top, fold(scores, jnp.max))

    count = count_ref[block]
    top = lax.fori_loop(0, count, score, jnp.full((8, wide), NEG, f32))
    top = jnp.max(top, axis=0, keepdims=True)

    def weigh(at, carry):
        total, accum = carry
        span = tile_span(base_ref, block, at, tile)
        expo = jnp.exp(s_ref[span, :] - top)
        total = total + fold(expo, jnp.sum)
        accum = accum + jnp.dot(vt_ref[:, span], expo.astype(bf16), preferred_element_type=f32)
        return (total, accum)

    total, accum = lax.fori_loop(
        0, count, weigh, (jnp.zeros((8, wide), f32), jnp.zeros((LANES, wide), f32))
    )
    total = jnp.sum(total, axis=0, keepdims=True)
    att = accum / total
    att_ref[0] = att
    lse_ref[0] = top + jnp.log(total)
    scatter_rows(units_ref, acc_ref, jnp.transpose(att), units, part)
    low_ref[0] = acc_ref[...].astype(bf16)


def attend(base, tiles, unit_places, qkv, turned, doc_slab, doc_q, rows, tile):
    total = qkv.shape[0]
    count = total // rows
    units = unit_places.shape[0] // 2
    wide = doc_q.shape[2]
    return pl.pallas_call(
        functools.partial(attend_kernel, units, tile),
        grid_spec=pltpu.PrefetchScalarGridSpec(
            num_scalar_prefetch=3,
            grid=(count,),
            in_specs=[
                pl.BlockSpec((rows, LANES), lambda i, *s: (i, 0)),
                pl.BlockSpec((total, LANES), lambda i, *s: (0, 1)),
                pl.BlockSpec((LANES, total), lambda i, *s: (1, 0)),
                pl.BlockSpec((total, LANES), lambda i, *s: (0, 0)),
                pl.BlockSpec((1, 1, wide), lambda i, *s: (i, 0, 0)),
            ],
            out_specs=[
                pl.BlockSpec((1, rows, LANES), lambda i, *s: (i, 0, 0)),
                pl.BlockSpec((1, LANES, wide), lambda i, *s: (i, 0, 0)),
                pl.BlockSpec((1, 1, wide), lambda i, *s: (i, 0, 0)),
            ],
            scratch_shapes=[pltpu.VMEM((total, wide), f32), pltpu.VMEM((rows, LANES), f32)],
        ),
        out_shape=[
            jax.ShapeDtypeStruct((count, rows, LANES), bf16),
            jax.ShapeDtypeStruct((count, LANES, wide), f32),
            jax.ShapeDtypeStruct((count, 1, wide), f32),
        ],
        compiler_params=params(),
        cost_estimate=pl.CostEstimate(
            flops=4 * count * wide * total * LANES,
            bytes_accessed=8 << 20,
            transcendentals=count * wide * total,
        ),
        name="attend",
    )(base, tiles, unit_places, qkv, qkv, turned, doc_slab, doc_q)


def attend_back_kernel(units, tile, base_ref, count_ref, units_ref, q_ref, k_ref, v_ref, kt_ref, doc_ref,
                       doc_q_ref, grad_ref, att_ref, lse_ref, cos_ref, sin_ref,
                       out_ref, dk_ref, dv_ref, acc_ref):
    block = pl.program_id(0)
    count = pl.num_programs(0)
    rows = acc_ref.shape[0]
    wide = att_ref.shape[2]
    part = wide // units

    @pl.when(block == 0)
    def _():
        dk_ref[...] = jnp.zeros(dk_ref.shape, f32)
        dv_ref[...] = jnp.zeros(dv_ref.shape, f32)

    def turn_back(values, span):
        return values * cos_ref[span, :] - rotate_half(values * sin_ref[span, :])

    queries = gather_rows(units_ref, q_ref, units, part)
    grads = gather_rows(units_ref, grad_ref.at[0], units, part)
    delta = jnp.sum(jnp.transpose(grads.astype(f32)) * att_ref[0], axis=0, keepdims=True)
    log_sum = lse_ref[0]
    doc_q = doc_q_ref[0]

    def step(at, grad_query):
        span = tile_span(base_ref, block, at, tile)
        scores = dot_tt(k_ref[span, :], queries)
        grad_probs = dot_tt(v_ref[span, :], grads)
        scores = jnp.where(across(doc_ref[span, :], wide) == doc_q, scores, NEG)
        probs = jnp.exp(scores - log_sum)
        dv_ref[span, :] += jnp.dot(probs.astype(bf16), grads, preferred_element_type=f32)
        grad_scores = (probs * (grad_probs - delta)).astype(bf16)
        dk_ref[span, :] += jnp.dot(grad_scores, queries, preferred_element_type=f32)
        return grad_query + jnp.dot(kt_ref[:, span], grad_scores, preferred_element_type=f32)

    grad_query = lax.fori_loop(
        0, count_ref[block], step, jnp.zeros((LANES, wide), f32)
    )
    scatter_rows(units_ref, acc_ref, jnp.transpose(grad_query) * HD**-0.5, units, part)
    here = pl.ds(pl.multiple_of(block * rows, rows), rows)
    out_ref[block, :, :LANES] = turn_back(acc_ref[...], here).astype(bf16)

    @pl.when(block == count - 1)
    def _():
        def finish(at, carry):
            span = pl.ds(pl.multiple_of(at * rows, rows), rows)
            out_ref[at, :, LANES : 2 * LANES] = turn_back(dk_ref[span, :], span).astype(bf16)
            out_ref[at, :, 2 * LANES :] = dv_ref[span, :].astype(bf16)
            return carry

        lax.fori_loop(0, count, finish, 0)


def attend_back(base, tiles, unit_places, qkv, turned, doc_slab, doc_q, grads, att, lse, cosine, sine,
                rows, tile):
    total = qkv.shape[0]
    count = total // rows
    units = unit_places.shape[0] // 2
    wide = doc_q.shape[2]
    whole = lambda part: pl.BlockSpec((total, LANES), lambda i, *s: (0, part))
    each = lambda *shape: pl.BlockSpec((1,) + shape, lambda i, *s: (i, 0, 0))
    return pl.pallas_call(
        functools.partial(attend_back_kernel, units, tile),
        grid_spec=pltpu.PrefetchScalarGridSpec(
            num_scalar_prefetch=3,
            grid=(count,),
            in_specs=[
                pl.BlockSpec((rows, LANES), lambda i, *s: (i, 0)),
                whole(1),
                whole(2),
                pl.BlockSpec((LANES, total), lambda i, *s: (0, 0)),
                whole(0),
                each(1, wide),
                each(rows, LANES),
                each(LANES, wide),
                each(1, wide),
                whole(0),
                whole(0),
            ],
            out_specs=pl.BlockSpec((count, rows, 3 * LANES), lambda i, *s: (0, 0, 0)),
            scratch_shapes=[
                pltpu.VMEM((total, LANES), f32),
                pltpu.VMEM((total, LANES), f32),
                pltpu.VMEM((rows, LANES), f32),
            ],
        ),
        out_shape=jax.ShapeDtypeStruct((count, rows, 3 * LANES), bf16),
        compiler_params=params(),
        cost_estimate=pl.CostEstimate(
            flops=10 * count * wide * total * LANES,
            bytes_accessed=12 << 20,
            transcendentals=count * wide * total,
        ),
        name="attend_back",
    )(base, tiles, unit_places, qkv, qkv, qkv, turned, doc_slab, doc_q, grads, att, lse, cosine, sine)


def join_heads(parts_ref, at, owners):
    rows = parts_ref.shape[1]
    side = lax.broadcasted_iota(jnp.int32, (rows, LANES), 1) // HD
    tiles = []
    for tile in range(len(owners) // SLOTS):
        column = jnp.zeros((rows, LANES), f32)
        for half in range(SLOTS):
            for c, slot in owners[tile * SLOTS + half]:
                slab = parts_ref[c, :, at : at + LANES].astype(f32)
                if slot != half:
                    slab = pltpu.roll(slab, HD, 1)
                column = column + jnp.where(side == half, slab, 0.0)
        tiles.append(column.astype(bf16))
    return jnp.concatenate(tiles, axis=1)


def middle_kernel(owners, first, att_ref, tokens_ref, gain_ref, cot_ref, weights_ref,
                  output_ref, grad_heads_ref, grad_middle_ref, attended_ref, branch_ref,
                  hidden_ref, grad_up_ref, product_ref,
                  proj_ref, up_ref, down_ref, sems):
    width = tokens_ref.shape[1]
    units = product_ref.shape[1]
    copies = []
    at = 0
    for i, ref in enumerate((proj_ref, up_ref, down_ref)):
        span = weights_ref.at[:, at : at + ref.shape[1]]
        copies.append(pltpu.make_async_copy(span, ref, sems.at[i]))
        copies[-1].start()
        at += ref.shape[1]
    gain = gain_ref[1:2, :]
    cot = cot_ref[...]
    attended = join_heads(att_ref, 0, owners)
    attended_ref[...] = attended
    copies[0].wait()
    middle = tokens_ref[...].astype(f32) + jnp.dot(
        attended, proj_ref[...], preferred_element_type=f32
    )
    normed, inverse = norm_rows(middle)
    hidden = (normed * gain).astype(bf16)
    hidden_ref[...] = hidden
    copies[1].wait()
    copies[2].wait()
    result = middle
    grad_hidden = jnp.zeros(middle.shape, f32)
    for at in range(0, units, CHUNK):
        one = slice(at, at + CHUNK)
        two = slice(units + at, units + at + CHUNK)
        inner = jnp.dot(hidden, up_ref[:, one], preferred_element_type=f32)
        gate = jnp.dot(hidden, up_ref[:, two], preferred_element_type=f32)
        grad_product = jnp.dot(cot, down_ref[:, one], preferred_element_type=f32)
        cdf = 0.5 * (1.0 + lax.erf(inner * ROOT_HALF))
        gelu_value = inner * cdf
        product = (gelu_value * gate).astype(bf16)
        product_ref[:, one] = product
        slope = cdf + inner * jnp.exp(-0.5 * inner * inner) * INV_ROOT_TWO_PI
        grad_inner = (grad_product * gate * slope).astype(bf16)
        grad_gate = (grad_product * gelu_value).astype(bf16)
        grad_up_ref[:, one] = grad_inner
        grad_up_ref[:, two] = grad_gate
        result = result + dot_tt(product, down_ref[:, one])
        grad_hidden = grad_hidden + dot_tt(grad_inner, up_ref[:, one])
        grad_hidden = grad_hidden + dot_tt(grad_gate, up_ref[:, two])
    output_ref[...] = result.astype(bf16)
    grad_middle = cot.astype(f32) + norm_back(grad_hidden * gain, normed, inverse)
    grad_middle_ref[...] = grad_middle
    grad_branch = grad_middle.astype(bf16)
    branch_ref[...] = grad_branch
    grad_attended = dot_tt(grad_branch, proj_ref[...])
    for c, head in enumerate(first):
        grad_heads_ref[c] = grad_attended[:, head * HD : head * HD + LANES].astype(bf16)


def middle_stage(owners, first, att_in, tokens, gains, cot, weights, units):
    rows, width = tokens.shape
    vmem = pl.BlockSpec(memory_space=pltpu.VMEM)
    shape = jax.ShapeDtypeStruct
    return pl.pallas_call(
        functools.partial(middle_kernel, owners, first),
        in_specs=[vmem] * 4 + [pl.BlockSpec(memory_space=pl.ANY)],
        out_specs=[vmem] * 8,
        out_shape=[
            shape((rows, width), bf16),
            shape((len(first), rows, LANES), bf16),
            shape((rows, width), f32),
            shape((rows, width), bf16),
            shape((rows, width), bf16),
            shape((rows, width), bf16),
            shape((rows, 2 * units), bf16),
            shape((rows, units), bf16),
        ],
        scratch_shapes=[
            pltpu.VMEM((width, width), bf16),
            pltpu.VMEM((width, 2 * units), bf16),
            pltpu.VMEM((width, units), bf16),
            pltpu.SemaphoreType.DMA((3,)),
        ],
        compiler_params=pltpu.CompilerParams(vmem_limit_bytes=VMEM_BYTES),
        cost_estimate=pl.CostEstimate(
            flops=4 * rows * width * (width + 3 * units),
            bytes_accessed=10 << 20,
            transcendentals=2 * rows * units,
        ),
        name="middle_stage",
    )(att_in, tokens, gains, cot, weights)


def finish_kernel(owners, at, parts_ref, tokens_ref, gain_ref, grad_ref, weights_ref, out_ref,
                  w_ref, sem):
    copy = pltpu.make_async_copy(weights_ref.at[:, at : at + w_ref.shape[1]], w_ref, sem)
    copy.start()
    joined = jnp.concatenate(
        [join_heads(parts_ref, part * LANES, owners) for part in range(3)], axis=1
    )
    normed, inverse = norm_rows(tokens_ref[...].astype(f32))
    copy.wait()
    grad_hidden = dot_tt(joined, w_ref[...])
    back = norm_back(grad_hidden * gain_ref[:1, :], normed, inverse)
    out_ref[...] = (grad_ref[...] + back).astype(bf16)


def finish(owners, at, parts, tokens, gains, grad_middle, weights):
    rows, width = tokens.shape
    vmem = pl.BlockSpec(memory_space=pltpu.VMEM)
    return pl.pallas_call(
        functools.partial(finish_kernel, owners, at),
        in_specs=[vmem] * 4 + [pl.BlockSpec(memory_space=pl.ANY)],
        out_specs=vmem,
        out_shape=jax.ShapeDtypeStruct((rows, width), bf16),
        scratch_shapes=[pltpu.VMEM((width, 3 * width), bf16), pltpu.SemaphoreType.DMA],
        compiler_params=pltpu.CompilerParams(vmem_limit_bytes=VMEM_BYTES),
        cost_estimate=pl.CostEstimate(
            flops=6 * rows * width * width, bytes_accessed=6 << 20, transcendentals=0
        ),
        name="finish",
    )(parts, tokens, gains, grad_middle, weights)


def split_rows(side, value, at, kept_ref, gone_ref):
    halves, share = kept_ref.shape[:2]
    span = slice(at, at + value.shape[1])
    for f in range(2 * halves):
        block = value[f * share : (f + 1) * share].astype(bf16)

        @pl.when(side == f % 2)
        def _():
            kept_ref[f // 2, :, span] = block

        @pl.when(side != f % 2)
        def _():
            gone_ref[f // 2, :, span] = block


def weight_grads_kernel(side_ref, *refs):
    kept_ref, gone_ref = refs[-2:]
    at = 0
    for left_ref, right_ref in zip(refs[0:-2:2], refs[1:-2:2]):
        left = jnp.transpose(left_ref[...])
        columns = right_ref.shape[1]
        for start in range(0, columns, CHUNK):
            value = jnp.dot(
                left, right_ref[:, start : start + CHUNK], preferred_element_type=f32
            )
            split_rows(side_ref[0], value, at + start, kept_ref, gone_ref)
        at += columns


def head_grads_kernel(side_ref, left_ref, right_ref, kept_ref, gone_ref, acc_ref):
    acc_ref[...] = jnp.zeros(acc_ref.shape, f32)
    count, rows, _ = right_ref.shape

    def step(at, carry):
        span = pl.ds(pl.multiple_of(at * rows, rows), rows)
        left = jnp.transpose(left_ref[span, :])
        acc_ref[...] += jnp.dot(left, right_ref[at], preferred_element_type=f32)
        return carry

    lax.fori_loop(0, count, step, 0)
    split_rows(side_ref[0], acc_ref[...], 0, kept_ref, gone_ref)


def split_grads(kernel, fsdp, side, operands, width, columns, scratch, name):
    vmem = pl.BlockSpec(memory_space=pltpu.VMEM)
    half = jax.ShapeDtypeStruct((fsdp // 2, width // fsdp, columns), bf16)
    rows = operands[0].shape[0]
    return pl.pallas_call(
        kernel,
        in_specs=[pl.BlockSpec(memory_space=pltpu.SMEM)] + [vmem] * len(operands),
        out_specs=[vmem, vmem],
        out_shape=[half, half],
        scratch_shapes=scratch,
        compiler_params=pltpu.CompilerParams(vmem_limit_bytes=VMEM_BYTES),
        cost_estimate=pl.CostEstimate(
            flops=2 * rows * width * columns, bytes_accessed=4 * width * columns, transcendentals=0
        ),
        name=name,
    )(side, *operands)


def halvings(count):
    return [1 << i for i in range(count.bit_length() - 1)]


def flips(count, bit):
    return [(i, i ^ bit) for i in range(count)]


def halve(blocks, index, bit):
    pairs = blocks.reshape((-1, 2) + blocks.shape[1:])
    side = index // bit % 2
    kept = lax.dynamic_index_in_dim(pairs, side, 1, keepdims=False)
    gone = lax.dynamic_index_in_dim(pairs, 1 - side, 1, keepdims=False)
    return kept, gone.astype(bf16)


def sum_rest(blocks, axis, count, index):
    while blocks.shape[0] > 1:
        bit = count // blocks.shape[0]
        kept, gone = halve(blocks, index // bit, 1)
        got = lax.ppermute(gone, axis, flips(count, bit))
        blocks = kept.astype(f32) + got.astype(f32)
    return blocks[0]


def exchange(blocks, axis, index):
    count = blocks.shape[0]
    held = blocks[:, None]
    masks = [0]
    for bit in halvings(count):
        pairs = held.reshape((-1, 2) + held.shape[1:])
        side = index // bit % 2
        kept = lax.dynamic_index_in_dim(pairs, side, 1, keepdims=False)
        gone = lax.dynamic_index_in_dim(pairs, 1 - side, 1, keepdims=False)
        got = lax.ppermute(gone, axis, flips(count, bit))
        held = jnp.concatenate([kept, got], axis=1)
        masks += [mask ^ bit for mask in masks]
    source = index ^ jnp.asarray(masks, jnp.int32)
    pick = jnp.arange(count, dtype=jnp.int32)[:, None] == source[None, :]
    return jnp.sum(jnp.where(pick[:, :, None, None], held.astype(f32), 0.0), axis=1)


def program(fsdp, ctx):
    def on_device(tokens, segment_ids, positions, gain_attn, w_qkv, w_out, gain_mlp, w_in, w_down,
                  cotangent):
        rows, width = tokens.shape[1:]
        shard = w_qkv.shape[0]
        heads = width // HD
        common = math.gcd(heads, ctx)
        splits = ctx // common
        units = heads // common
        part = rows // splits
        tile = KEY_TILE
        first = [min(units * c // splits, heads - SLOTS) for c in range(ctx)]
        owners = [
            [
                (c, slot)
                for c in range(ctx)
                for slot in range(SLOTS)
                if first[c] + slot == head
                and max(units * c, head * splits) < min(units * (c + 1), (head + 1) * splits)
            ]
            for head in range(heads)
        ]
        me = lax.axis_index("ctx")
        mine = lax.axis_index("fsdp")
        total = ctx * rows

        outer = ctx // 2
        ring = [(o * 2 + i, (o + 1) % outer * 2 + i) for o in range(outer) for i in range(2)]
        swap = [(c, c ^ 1) for c in range(ctx)]
        bits = halvings(fsdp)[::-1]
        masks = [0]
        own = [tokens[0]]
        other = []
        step = 0
        while step < outer or bits:
            if step > 0 and bits:
                bit = bits.pop(0)
                got = lax.ppermute(w_parts, "fsdp", flips(fsdp, bit))
                w_parts = jnp.concatenate([w_parts, got], axis=0)
                masks += [mask ^ bit for mask in masks]
            if step < outer:
                other.append(lax.ppermute(own[step], "ctx", swap))
            if step < outer - 1:
                own.append(lax.ppermute(own[step], "ctx", ring))
            if step == 0:
                sent = spread(first, w_qkv, gain_attn, gain_mlp, segment_ids, positions)
                sent = lax.all_to_all(sent, "ctx", 0, 0, tiled=True)
                w_parts = sent[:, :shard, :].reshape(1, ctx * shard, 4 * LANES)
            if step < outer - 1:
                own[-1], other[-1], w_parts = lax.optimization_barrier(
                    (own[-1], other[-1], w_parts)
                )
            step += 1
        infos = sent[:, shard : shard + 2, :].astype(f32)
        docs = infos[:, 0, :rows].astype(jnp.int32)
        spots = (infos[:, 0, rows:] * 64 + infos[:, 1, :rows]).reshape(total, 1)
        half = jnp.arange(LANES) % (HD // 2)
        rates = THETA ** (-2.0 * half.astype(f32) / HD)
        angles = spots * rates[None, :]
        cosine = jnp.cos(angles)
        sine = jnp.sin(angles)
        doc_slab = jnp.broadcast_to(docs.reshape(total, 1), (total, LANES))
        edges = docs.reshape(total // GRAIN, GRAIN)
        lo = jnp.sum((edges[None, :, -1] < docs[:, :1]).astype(jnp.int32), axis=1)
        hi = jnp.sum((edges[None, :, 0] <= docs[:, rows - 1 :]).astype(jnp.int32), axis=1)
        count = (hi - lo + tile // GRAIN - 1) // (tile // GRAIN)
        base = jnp.minimum(lo, total // GRAIN - count * (tile // GRAIN))
        unit = units * me + jnp.arange(units, dtype=jnp.int32)
        first_head = jnp.minimum(units * me // splits, heads - SLOTS)
        unit_slot = unit // splits - first_head
        unit_part = unit % splits
        unit_places = jnp.concatenate([unit_slot, unit_part]).astype(jnp.int32)
        pick = unit_part[:, None] == jnp.arange(splits, dtype=jnp.int32)[None, :]
        doc_q = jnp.sum(
            jnp.where(pick[None, :, :, None], docs.reshape(ctx, 1, splits, part), 0), axis=2
        ).reshape(ctx, 1, units * part)

        held = []
        for step in range(outer):
            at = jnp.stack([(me // 2 + outer - step) % outer, me % 2, mine]).astype(jnp.int32)
            *held, gains = project(
                masks, at, own[step], other[step], w_parts, cosine, sine, total, held
            )
        hidden_one, qkv, turned = held
        att_low, att, lse = attend(base, count, unit_places, qkv, turned, doc_slab, doc_q, rows, tile)
        att_in = lax.all_to_all(att_low, "ctx", 0, 0, tiled=True)

        packed = jnp.concatenate([w_out, w_in, w_down.T, w_qkv], axis=1)
        weights = lax.all_gather(packed, AXES, axis=0, tiled=True)

        cot = cotangent[0]
        output, grad_heads, grad_middle, attended, grad_branch, hidden_two, grad_up, product = (
            middle_stage(
                owners, first, att_in, tokens[0], gains, cot, weights, w_down.shape[0]
            )
        )
        grad_heads = lax.all_to_all(grad_heads, "ctx", 0, 0, tiled=True)

        side = (mine % 2).astype(jnp.int32).reshape(1)
        columns = packed.shape[1] - w_qkv.shape[1]
        kept, gone = split_grads(
            weight_grads_kernel, fsdp, side,
            [attended, grad_branch, hidden_two, grad_up, cot, product],
            width, columns, [], "weight_grads",
        )
        got = lax.ppermute(gone, "fsdp", flips(fsdp, 1))
        grad_heads, kept, got = lax.optimization_barrier((grad_heads, kept, got))
        grad_packed = kept.astype(f32) + got.astype(f32)
        grad_packed = sum_rest(grad_packed, "fsdp", fsdp, mine).reshape(ctx, shard, columns)
        kept, gone = halve(grad_packed, me, 1)
        got = lax.ppermute(gone, "ctx", flips(ctx, 1))

        grad_joined = attend_back(
            base, count, unit_places, qkv, turned, doc_slab, doc_q, grad_heads, att, lse, cosine,
            sine, rows, tile,
        )
        kept_cols, gone_cols = split_grads(
            head_grads_kernel, fsdp, side, [hidden_one, grad_joined], width, 3 * LANES,
            [pltpu.VMEM((width, 3 * LANES), f32)], "head_grads",
        )
        got_cols = lax.ppermute(gone_cols, "fsdp", flips(fsdp, 1))
        grad_cols = kept_cols.astype(f32) + got_cols.astype(f32)
        grad_cols = sum_rest(grad_cols, "fsdp", fsdp, mine)
        grad_joined = lax.all_to_all(grad_joined, "ctx", 0, 0, tiled=True)
        grad_joined, grad_cols, kept, got = lax.optimization_barrier(
            (grad_joined, grad_cols, kept, got)
        )
        input_grad = finish(
            owners, columns, grad_joined, tokens[0], gains, grad_middle, weights
        )
        grad_packed = sum_rest(kept.astype(f32) + got.astype(f32), "ctx", ctx, me)
        sum_w_out = grad_packed[:, :width]
        sum_w_in = grad_packed[:, width : width + w_in.shape[1]]
        sum_w_down = grad_packed[:, width + w_in.shape[1] :].T
        sum_gain_mlp = jnp.sum(w_in.astype(f32) * sum_w_in, axis=1) / gain_mlp.astype(f32)

        grad_cols = exchange(grad_cols.astype(bf16).reshape(ctx, shard, 3 * LANES), "ctx", me)
        pieces = []
        for part in range(3):
            for head in range(heads):
                column = 0.0
                for c, slot in owners[head]:
                    at = part * LANES + slot * HD
                    column = column + grad_cols[c, :, at : at + HD]
                pieces.append(column)
        sum_w_qkv = jnp.concatenate(pieces, axis=1)
        sum_gain_attn = jnp.sum(w_qkv.astype(f32) * sum_w_qkv, axis=1) / gain_attn.astype(f32)
        return (
            output[None],
            input_grad[None],
            sum_gain_attn,
            sum_w_qkv,
            sum_w_out,
            sum_gain_mlp,
            sum_w_in,
            sum_w_down,
        )

    return on_device


def solution(mesh):
    rows = P(AXES, None)
    tokens = P("fsdp", "ctx", None)
    return jax.shard_map(
        program(mesh.shape["fsdp"], mesh.shape["ctx"]),
        mesh=mesh,
        in_specs=(
            tokens,
            P("fsdp", "ctx"),
            P("fsdp", "ctx"),
            P(AXES),
            rows,
            rows,
            P(AXES),
            rows,
            P(None, AXES),
            tokens,
        ),
        out_specs=(tokens, tokens, P(AXES), rows, rows, P(AXES), rows, P(None, AXES)),
        check_vma=False,
    )
```

time: 411 us -> 282 us (0.69)
  blocking collectives: 59.6 us -> 0 us
  waiting for transfers between devices: 145 us -> 107 us
  matrix products: 25.7 us -> 0 us
  starting transfers between devices: 20.8 us -> 37.9 us
  local copies, waits for them, and re-layouts: 35.1 us -> 20.4 us
  Pallas kernels: 82.9 us -> 78 us
    unnamed x5 -> x1, waiting for transfers between devices: 50.5 us -> 0.02 us
    all_to_all x3 -> x0, blocking collectives: 48.9 us -> none  [the longest x1 19.5 us: on_device(): grad_cols = lax.all_to_all(grad_cols, 'fsdp', 0, 0, tiled=True)]
    all_to_all x1, waiting for transfers between devices: 38.2 us -> 0.48 us  [on_device(): grad_joined = lax.all_to_all(grad_joined, 'ctx', 0, 0, tiled=True)]
    ppermute x7 -> x19, waiting for transfers between devices: 40.1 us -> 67.8 us  [the longest x1 28.3 us: on_device(): got = lax.ppermute(gone, 'ctx', flips(ctx, 1))]
    dot_general x11 -> x0, matrix products: 25.7 us -> none  [the longest x4 9.7 us: dot_rows(): lax.dot_general(left, right, (((0,), (0,)), ((), ())), preferred_element_...]
    all_to_all x1 -> x2, waiting for transfers between devices: 6.43 us -> 28.2 us  [the longest x1 15.2 us: on_device(): grad_heads = lax.all_to_all(grad_heads, 'ctx', 0, 0, tiled=True)]
    ppermute x7 -> x19, starting transfers between devices: 7.72 us -> 21.6 us  [the longest x4 6.37 us: on_device(): other.append(lax.ppermute(own[step], 'ctx', swap))]
    all_gather x1 -> x0, blocking collectives: 10.7 us -> none  [on_device(): w_heads = lax.all_gather(w_heads, 'fsdp', axis=0, tiled=True)]
  transfers between devices with their start and end apart: 14 -> 24, of which waited for: 7 -> 16; matrix products, arithmetic and copies ran while one was open for 13% -> 6% of each run, Pallas kernels for 20% -> 22%
where the time goes in v2:
time: 282 us; the launch traced here: 281 us
  waiting for transfers between devices  107 us (38%)
  Pallas kernels  78 us (28%)
  starting transfers between devices  37.9 us (13%)
  other arithmetic  23.5 us (8%)
  local copies, waits for them, and re-layouts  20.4 us (7%)
  between operations  14.5 us (5%)
    ppermute x1, waiting for transfers between devices, on_device(): got = lax.ppermute(gone, 'ctx', flips(ctx, 1))  28.3 us
    pallas_call x1, Pallas kernels, attend_back(): pl.pallas_call(functools.partial(attend_back_kernel, units, tile), grid_s...  21 us
    all_to_all x1, waiting for transfers between devices, on_device(): grad_heads = lax.all_to_all(grad_heads, 'ctx', 0, 0, tiled=True)  15.2 us
    pallas_call x4, Pallas kernels, project(): pl.pallas_call(functools.partial(project_kernel, masks), grid_spec=pltpu....  14.6 us
    pallas_call x1, Pallas kernels, attend(): pl.pallas_call(functools.partial(attend_kernel, units, tile), grid_spec=p...  14.5 us
    ppermute x4, waiting for transfers between devices, on_device(): other.append(lax.ppermute(own[step], 'ctx', swap))  14.2 us
    unnamed x75, local copies, waits for them, and re-layouts  13.5 us
    pallas_call x2, Pallas kernels, split_grads(): pl.pallas_call(kernel, in_specs=[pl.BlockSpec(memory_space=pltpu.SMEM)] +...  13.4 us
  transfers between devices with their start and end apart: 24, of which 16 were waited for; matrix products, arithmetic and copies ran while one was open for 6% of the time, Pallas kernels for 22%

profile of v2, /device:TPU:0, one launch (start us, length us, event | category | flops | bytes accessed | tf_op | source)
XLA Modules:
  0.0 280.9 jit_solution(1325388429637045254)
XLA Ops:
  9.0 3.0 %collective-permute-start.1 = (bf16[256,768]{1,0:T(8,128)(2,1)}, bf16[256,768]{1,0:T(8,128)(2,1)S(1)}, u32[]{:S(2)}, u32[]{:S(2)}) collective-permute-start(bf16[256,768]{1,0:T(8,128)(2,1)} %bitcast.133), channel_id=1, source_target_pairs={{0,1},{1,0},{2,3},{3,2},{4,5},{5,4},{6,7},{7,6},{8,9},{9,8},{10,11... | collective-permute-start | bytes 1179656 | tf_op jit(solution)/shard_map/ppermute | solution.py:661
  18.0 3.9 %all-to-all-start = ((bf16[8,32,512]{2,1,0:T(8,128)(2,1)}), bf16[8,32,512]{2,1,0:T(8,128)(2,1)S(1)}, u32[]{:S(2)}, u32[]{:S(2)}) async-start(bf16[8,32,512]{2,1,0:T(8,128)(2,1)} %spread.1), calls=%async_computation | async-start | bytes 524288 | tf_op jit(solution)/shard_map/all_to_all | solution.py:666
  22.7 13.0 %all-to-all-done = bf16[8,32,512]{2,1,0:T(8,128)(2,1)S(1)} async-done(((bf16[8,32,512]{2,1,0:T(8,128)(2,1)}), bf16[8,32,512]{2,1,0:T(8,128)(2,1)S(1)}, u32[]{:S(2)}, u32[]{:S(2)}) %all-to-all-start) | async-done | bytes 262176 | tf_op jit(solution)/shard_map/all_to_all | solution.py:666
  39.5 5.3 %multiply_sine_fusion = (f32[2048,128]{1,0:T(8,128)}, f32[2048,128]{1,0:T(8,128)S(1)}) fusion(f32[128]{0:T(128)S(1)} %fusion.21, f32[2048]{0:T(1024)S(1)} %bitcast.160), kind=kLoop, calls=%fused_computation.7 | loop fusion | flops 262144 | bytes 2105856 | tf_op jit(solution)/shard_map/sin | solution.py:680
  45.6 3.0 %collective-permute-done.2.own_ref = bf16[256,768]{1,0:T(8,128)(2,1)S(1)} collective-permute-done((bf16[256,768]{1,0:T(8,128)(2,1)S(1)}, bf16[256,768]{1,0:T(8,128)(2,1)S(1)}, u32[]{:S(2)}, u32[]{:S(2)}) %collective-permute-start.2) | collective-permute-done | bytes 393248 | tf_op jit(solution)/shard_map/ppermute | solution.py:663
  51.9 10.5 %collective-permute-done.6.other_ref = bf16[256,768]{1,0:T(8,128)(2,1)S(1)} collective-permute-done((bf16[256,768]{1,0:T(8,128)(2,1)S(1)}, bf16[256,768]{1,0:T(8,128)(2,1)S(1)}, u32[]{:S(2)}, u32[]{:S(2)}) %collective-permute-start.6) | collective-permute-done | bytes 393248 | tf_op jit(solution)/shard_map/ppermute | solution.py:661
  63.2 5.3 %collective-permute-done.5.own_ref = bf16[256,768]{1,0:T(8,128)(2,1)} collective-permute-done((bf16[256,768]{1,0:T(8,128)(2,1)S(1)}, bf16[256,768]{1,0:T(8,128)(2,1)}, u32[]{:S(2)}, u32[]{:S(2)}) %collective-permute-start.5) | collective-permute-done | bytes 393248 | tf_op jit(solution)/shard_map/ppermute | solution.py:663
  68.4 2.0 collective-permute-start.8
  71.7 3.7 %project.4 = (bf16[2048,768]{1,0:T(8,128)(2,1)}, bf16[2048,384]{1,0:T(8,128)(2,1)}, bf16[256,2048]{1,0:T(8,128)(2,1)S(1)}, f32[8,768]{1,0:T(8,128)}) custom-call(s32[3]{0:T(128)S(1)} %add_add_fusion.3.at_ref, bf16[256,768]{1,0:T(8,128)(2,1)S(1)} %bitcast.135, bf16[256,768]{1,0:T(8,128)(2,1)S(1)} %copy-done.11, ...), custom_call_target="tpu_custom_call" | custom-call | flops 301989888 | bytes 6291456 | tf_op jit(solution)/shard_map/project/pallas_call | solution.py:142
  75.3 3.6 %project.5 = (bf16[2048,768]{1,0:T(8,128)(2,1)}, bf16[2048,384]{1,0:T(8,128)(2,1)}, bf16[256,2048]{1,0:T(8,128)(2,1)S(1)}, f32[8,768]{1,0:T(8,128)}) custom-call(s32[3]{0:T(128)S(1)} %get-tuple-element.155.at_ref, bf16[256,768]{1,0:T(8,128)(2,1)S(1)} %collective-permute-done.own_ref, ...), custom_call_target="tpu_custom_call", output_to_operand_aliasing={{0}: (6, {}), {1}: (7, {}), {2}: (8, {})} | custom-call | flops 301989888 | bytes 6291456 | tf_op jit(solution)/shard_map/project/pallas_call | solution.py:142
  79.0 3.6 %project.6 = (bf16[2048,768]{1,0:T(8,128)(2,1)}, bf16[2048,384]{1,0:T(8,128)(2,1)}, bf16[256,2048]{1,0:T(8,128)(2,1)S(1)}, f32[8,768]{1,0:T(8,128)}) custom-call(s32[3]{0:T(128)S(1)} %get-tuple-element.154.at_ref, bf16[256,768]{1,0:T(8,128)(2,1)S(1)} %collective-permute-done.2.own_ref, ...), custom_call_target="tpu_custom_call", output_to_operand_aliasing={{0}: (6, {}), {1}: (7, {}), {2}: (8, {})} | custom-call | flops 301989888 | bytes 6291456 | tf_op jit(solution)/shard_map/project/pallas_call | solution.py:142
  82.6 3.7 %collective-permute-done.8.other_ref = bf16[256,768]{1,0:T(8,128)(2,1)S(1)} collective-permute-done((bf16[256,768]{1,0:T(8,128)(2,1)}, bf16[256,768]{1,0:T(8,128)(2,1)S(1)}, u32[]{:S(2)}, u32[]{:S(2)}) %collective-permute-start.8) | collective-permute-done | bytes 393248 | tf_op jit(solution)/shard_map/ppermute | solution.py:661
  86.3 3.7 %project.7 = (bf16[2048,768]{1,0:T(8,128)(2,1)}, bf16[2048,384]{1,0:T(8,128)(2,1)}, bf16[256,2048]{1,0:T(8,128)(2,1)S(1)}, f32[8,768]{1,0:T(8,128)S(1)}) custom-call(s32[3]{0:T(128)S(1)} %get-tuple-element.153.at_ref, bf16[256,768]{1,0:T(8,128)(2,1)} %collective-permute-done.5.own_ref, ...), custom_call_target="tpu_custom_call", output_to_operand_aliasing={{0}: (6, {}), {1}: (7, {}), {2}: (8, {})} | custom-call | flops 301989888 | bytes 6291456 | tf_op jit(solution)/shard_map/project/pallas_call | solution.py:142
  90.4 14.5 %attend.1 = (bf16[8,256,128]{2,1,0:T(8,128)(2,1)S(1)}, f32[8,128,384]{2,1,0:T(8,128)}, f32[8,1,384]{2,1,0:T(1,128)S(1)}) custom-call(s32[8]{0:T(128)S(1)} %get-tuple-element.100.base_ref, s32[8]{0:T(128)S(1)} %get-tuple-element.101.count_ref, s32[6]{0:T(128)S(1)} %copy-done.25, bf16[2048,384]{1,0:T(8,128)(2,1)} %get-tuple-element.70.q_ref.k_ref.v_ref, ...), custom_call_target="tpu_custom_call" | custom-call | flops 3221225472 | bytes 8388608 | tf_op jit(solution)/shard_map/attend/pallas_call | solution.py:250
  106.2 4.3 %all-to-all-start.1 = ((bf16[8,256,128]{2,1,0:T(8,128)(2,1)}), bf16[8,256,128]{2,1,0:T(8,128)(2,1)}, u32[]{:S(2)}, u32[]{:S(2)}) async-start(bf16[8,256,128]{2,1,0:T(8,128)(2,1)} %copy-done.5), calls=%async_computation.1 | async-start | bytes 1048576 | tf_op jit(solution)/shard_map/all_to_all | solution.py:705
  110.6 10.1 %all-to-all-done.1.att_ref = bf16[8,256,128]{2,1,0:T(8,128)(2,1)} async-done(((bf16[8,256,128]{2,1,0:T(8,128)(2,1)}), bf16[8,256,128]{2,1,0:T(8,128)(2,1)}, u32[]{:S(2)}, u32[]{:S(2)}) %all-to-all-start.1) | async-done | bytes 524320 | tf_op jit(solution)/shard_map/all_to_all | solution.py:705
  122.4 9.6 %middle_stage.1 = (bf16[256,768]{1,0:T(8,128)(2,1)}, bf16[8,256,128]{2,1,0:T(8,128)(2,1)S(1)}, f32[256,768]{1,0:T(8,128)}, bf16[256,768]{1,0:T(8,128)(2,1)S(1)},...) custom-call(bf16[8,256,128]{2,1,0:T(8,128)(2,1)} %all-to-all-done.1., ...), custom_call_target="tpu_custom_call" | custom-call | flops 3321888768 | bytes 10485760 | tf_op jit(solution)/shard_map/middle_stage/pallas_call | solution.py:456
  134.0 7.7 %weight_grads.1 = (bf16[2,192,4224]{2,1,0:T(8,128)(2,1)}, bf16[2,192,4224]{2,1,0:T(8,128)(2,1)}) custom-call(s32[1]{0:T(128)} %bitcast.20.side_ref, bf16[256,768]{1,0:T(8,128)(2,1)S(1)} %get-tuple-element.76.refs_0_, bf16[256,768]{1,0:T(8,128)(2,1)S(1)} %get-tuple-element.77.refs_1_, bf16[256,768]{1,0:T(8,128)(2,1)S(1)} %get-tuple-element.78.refs_2_, ...), custom_call_target="tpu_custom_call" | custom-call | flops 1660944384 | bytes 12976128 | tf_op jit(solution)/shard_map/weight_grads/pallas_call | solution.py:564
  141.7 4.4 %all-to-all-start.2 = ((bf16[8,256,128]{2,1,0:T(8,128)(2,1)}), bf16[8,256,128]{2,1,0:T(8,128)(2,1)}, u32[]{:S(2)}, u32[]{:S(2)}) async-start(bf16[8,256,128]{2,1,0:T(8,128)(2,1)} %copy-done.4), calls=%async_computation.2 | async-start | bytes 1048576 | tf_op jit(solution)/shard_map/all_to_all | solution.py:716
  146.1 15.2 %all-to-all-done.2.grad_ref = bf16[8,256,128]{2,1,0:T(8,128)(2,1)} async-done(((bf16[8,256,128]{2,1,0:T(8,128)(2,1)}), bf16[8,256,128]{2,1,0:T(8,128)(2,1)}, u32[]{:S(2)}, u32[]{:S(2)}) %all-to-all-start.2) | async-done | bytes 524320 | tf_op jit(solution)/shard_map/all_to_all | solution.py:716
  161.3 6.2 %convert_add_fusion = f32[2,192,4224]{2,1,0:T(8,128)} fusion(bf16[2,192,4224]{2,1,0:T(8,128)(2,1)} %collective-permute-done.9, bf16[2,192,4224]{2,1,0:T(8,128)(2,1)} %get-tuple-element.89), kind=kLoop, calls=%fused_computation | loop fusion | flops 4866048 | bytes 12976128 | tf_op jit(solution)/shard_map/add | solution.py:727
  167.5 3.3 %dynamic-slice_convert_fusion = bf16[1,192,4224]{2,1,0:T(8,128)(2,1)} fusion(f32[2,192,4224]{2,1,0:T(8,128)} %convert_add_fusion, s32[]{:T(128)S(6)} %select_n.175), kind=kLoop, calls=%fused_computation.2 | loop fusion | bytes 3244036 | tf_op jit(solution)/shard_map/convert_element_type | solution.py:591
  174.5 21.0 %attend_back.1.right_ref = bf16[8,256,384]{2,1,0:T(8,128)(2,1)} custom-call(s32[8]{0:T(128)S(1)} %get-tuple-element.100.base_ref, s32[8]{0:T(128)S(1)} %copy-done.22, s32[6]{0:T(128)S(1)} %copy-done.26, bf16[2048,384]{1,0:T(8,128)(2,1)} %get-tuple-element.70.q_ref.k_ref.v_ref, bf16[2048,384]{1,0:T(8,128)(2,1)} %get-tuple-element.70.q_ref.k_ref.v_ref, ...), custom_call_target="tpu_custom_call" | custom-call | flops 8053063680 | bytes 12582912 | tf_op jit(solution)/shard_map/attend_back/pallas_call | solution.py:344
  195.5 5.7 %head_grads.1 = (bf16[2,192,384]{2,1,0:T(8,128)(2,1)S(1)}, bf16[2,192,384]{2,1,0:T(8,128)(2,1)S(1)}) custom-call(s32[1]{0:T(128)} %bitcast.20.side_ref, bf16[2048,768]{1,0:T(8,128)(2,1)} %get-tuple-element.86.left_ref, bf16[8,256,384]{2,1,0:T(8,128)(2,1)} %attend_back.1.right_ref), custom_call_target="tpu_custom_call" | custom-call | flops 1207959552 | bytes 1179648 | tf_op jit(solution)/shard_map/head_grads/pallas_call | solution.py:564
  201.3 3.6 %all-to-all-start.3 = ((bf16[8,256,384]{2,1,0:T(8,128)(2,1)}), bf16[8,256,384]{2,1,0:T(8,128)(2,1)S(1)}, u32[]{:S(2)}, u32[]{:S(2)}) async-start(bf16[8,256,384]{2,1,0:T(8,128)(2,1)} %attend_back.1.right_ref), calls=%async_computation.3 | async-start | bytes 3145728 | tf_op jit(solution)/shard_map/all_to_all | solution.py:743
  205.1 3.5 %collective-permute-done.12 = bf16[1,192,4224]{2,1,0:T(8,128)(2,1)} collective-permute-done((bf16[1,192,4224]{2,1,0:T(8,128)(2,1)}, bf16[1,192,4224]{2,1,0:T(8,128)(2,1)}, u32[]{:S(2)}, u32[]{:S(2)}) %collective-permute-start.12) | collective-permute-done | bytes 1622048 | tf_op jit(solution)/shard_map/ppermute | solution.py:598
  208.7 2.7 convert_add_fusion.1
  214.0 28.3 %collective-permute-done.13 = bf16[4,24,4224]{2,1,0:T(8,128)(2,1)S(1)} collective-permute-done((bf16[4,24,4224]{2,1,0:T(8,128)(2,1)S(1)}, bf16[4,24,4224]{2,1,0:T(8,128)(2,1)S(1)}, u32[]{:S(2)}, u32[]{:S(2)}) %collective-permute-start.13) | collective-permute-done | bytes 811040 | tf_op jit(solution)/shard_map/ppermute | solution.py:730
  249.5 3.1 %collective-permute-done.15 = bf16[2,2,24,384]{3,2,1,0:T(8,128)(2,1)S(1)} collective-permute-done((bf16[2,2,24,384]{3,2,1,0:T(8,128)(2,1)S(1)}, bf16[2,2,24,384]{3,2,1,0:T(8,128)(2,1)S(1)}, u32[]{:S(2)}, u32[]{:S(2)}) %collective-permute-start.15) | collective-permute-done | bytes 73760 | tf_op jit(solution)/shard_map/ppermute | solution.py:612
  254.6 4.1 %finish.1 = bf16[256,768]{1,0:T(8,128)(2,1)} custom-call(bf16[8,256,384]{2,1,0:T(8,128)(2,1)S(1)} %all-to-all-done.3.parts_ref, bf16[256,768]{1,0:T(8,128)(2,1)S(1)} %bitcast.137, f32[8,768]{1,0:T(8,128)S(1)} %copy-done.14, f32[256,768]{1,0:T(8,128)S(1)} %copy-done.3, bf16[768,6528]{1,0:T(8,128)(2,1)} %all-gather.2.cloned.1.call-done.weights_ref), custom_call_target="tpu_custom_call" | custom-call | flops 905969664 | bytes 6291456 | tf_op jit(solution)/shard_map/finish/pallas_call | solution.py:503
  260.4 3.4 %collective-permute-start.18 = (bf16[1,24,4224]{2,1,0:T(8,128)(2,1)S(1)}, bf16[1,24,4224]{2,1,0:T(8,128)(2,1)S(1)}, u32[]{:S(2)}, u32[]{:S(2)}) collective-permute-start(bf16[1,24,4224]{2,1,0:T(8,128)(2,1)S(1)} %dynamic-slice_convert_fusion.2), channel_id=1, source_target_pairs={{0,4},{1,5},{2,6},{3,7},{4,0},{5,1},{6,2},{7,3},{8,12},{9,13},{10,... | collective-permute-start | bytes 608264 | tf_op jit(solution)/shard_map/ppermute | solution.py:598
  264.3 7.1 %collective-permute-done.18 = bf16[1,24,4224]{2,1,0:T(8,128)(2,1)S(1)} collective-permute-done((bf16[1,24,4224]{2,1,0:T(8,128)(2,1)S(1)}, bf16[1,24,4224]{2,1,0:T(8,128)(2,1)S(1)}, u32[]{:S(2)}, u32[]{:S(2)}) %collective-permute-start.18) | collective-permute-done | bytes 202784 | tf_op jit(solution)/shard_map/ppermute | solution.py:598
  (157 shorter events, 44.4 us)
Async XLA Ops:
  7.2 113.5 %all-gather.2.cloned.1.call-start = ((), (), s32[]{:S(2)}) async-start(), calls=%async_computation.4 | async-start | bytes 10340352 | tf_op jit(solution)/shard_map/all_gather | solution.py:708
  9.0 26.8 %collective-permute-start.1 = (bf16[256,768]{1,0:T(8,128)(2,1)}, bf16[256,768]{1,0:T(8,128)(2,1)S(1)}, u32[]{:S(2)}, u32[]{:S(2)}) collective-permute-start(bf16[256,768]{1,0:T(8,128)(2,1)} %bitcast.133), channel_id=1, source_target_pairs={{0,1},{1,0},{2,3},{3,2},{4,5},{5,4},{6,7},{7,6},{8,9},{9,8},{10,11... | collective-permute-start | bytes 1179656 | tf_op jit(solution)/shard_map/ppermute | solution.py:661
  12.0 24.6 %collective-permute-start = (bf16[256,768]{1,0:T(8,128)(2,1)}, bf16[256,768]{1,0:T(8,128)(2,1)S(1)}, u32[]{:S(2)}, u32[]{:S(2)}) collective-permute-start(bf16[256,768]{1,0:T(8,128)(2,1)} %bitcast.134), channel_id=1, source_target_pairs={{0,2},{1,3},{2,4},{3,5},{4,6},{5,7},{6,0},{7,1},{8,10},{9,11},{10,... | collective-permute-start | bytes 1179656 | tf_op jit(solution)/shard_map/ppermute | solution.py:663
  18.0 17.8 %all-to-all-start = ((bf16[8,32,512]{2,1,0:T(8,128)(2,1)}), bf16[8,32,512]{2,1,0:T(8,128)(2,1)S(1)}, u32[]{:S(2)}, u32[]{:S(2)}) async-start(bf16[8,32,512]{2,1,0:T(8,128)(2,1)} %spread.1), calls=%async_computation | async-start | bytes 524288 | tf_op jit(solution)/shard_map/all_to_all | solution.py:666
  36.5 34.1 %copy-start = (bf16[1,256,768]{2,1,0:T(8,128)(2,1)S(1)}, bf16[1,256,768]{2,1,0:T(8,128)(2,1)}, u32[]{:S(2)}) copy-start(bf16[1,256,768]{2,1,0:T(8,128)(2,1)} %param.11) | copy-start | bytes 1179652
  36.5 9.1 %collective-permute-start.3 = (bf16[256,768]{1,0:T(8,128)(2,1)S(1)}, bf16[256,768]{1,0:T(8,128)(2,1)S(1)}, u32[]{:S(2)}, u32[]{:S(2)}) collective-permute-start(bf16[256,768]{1,0:T(8,128)(2,1)S(1)} %collective-permute-done.own_ref), channel_id=1, source_target_pairs={{0,1},{1,0},{2,3},{3,2},{4,5},{5,4},{6,7},{7,6},{8,9},{9,8},{10,11... | collective-permute-start | bytes 1179656 | tf_op jit(solution)/shard_map/ppermute | solution.py:661
  37.9 10.7 %collective-permute-start.2 = (bf16[256,768]{1,0:T(8,128)(2,1)S(1)}, bf16[256,768]{1,0:T(8,128)(2,1)S(1)}, u32[]{:S(2)}, u32[]{:S(2)}) collective-permute-start(bf16[256,768]{1,0:T(8,128)(2,1)S(1)} %collective-permute-done.own_ref), channel_id=1, source_target_pairs={{0,2},{1,3},{2,4},{3,5},{4,6},{5,7},{6,0},{7,1},{8,10},{9,11},{10,... | collective-permute-start | bytes 1179656 | tf_op jit(solution)/shard_map/ppermute | solution.py:663
  37.9 6.9 %collective-permute-start.4 = (bf16[1,192,512]{2,1,0:T(8,128)(2,1)S(1)}, bf16[1,192,512]{2,1,0:T(8,128)(2,1)S(1)}, u32[]{:S(2)}, u32[]{:S(2)}) collective-permute-start(bf16[1,192,512]{2,1,0:T(8,128)(2,1)S(1)} %bitcast.146), channel_id=1, source_target_pairs={{0,16},{8,24},{16,0},{24,8},{1,17},{9,25},{17,1},{25,9},{2,18},{10... | collective-permute-start | bytes 589832 | tf_op jit(solution)/shard_map/ppermute | solution.py:657
  39.5 35.9 %copy-start.34 = (s32[8,1,256]{2,1,0:T(1,128)}, s32[8,1,256]{2,1,0:T(1,128)S(1)}, u32[]{:S(2)}) copy-start(s32[8,1,256]{2,1,0:T(1,128)S(1)} %get-tuple-element.145) | copy-start | bytes 24580
  45.6 25.1 %copy-start.6 = (bf16[256,768]{1,0:T(8,128)(2,1)}, bf16[256,768]{1,0:T(8,128)(2,1)S(1)}, u32[]{:S(2)}) copy-start(bf16[256,768]{1,0:T(8,128)(2,1)S(1)} %collective-permute-done.3.other_ref) | copy-start | bytes 1179652
  48.6 2.1 collective-permute-start.7
  48.7 13.7 %collective-permute-start.6 = (bf16[256,768]{1,0:T(8,128)(2,1)S(1)}, bf16[256,768]{1,0:T(8,128)(2,1)S(1)}, u32[]{:S(2)}, u32[]{:S(2)}) collective-permute-start(bf16[256,768]{1,0:T(8,128)(2,1)S(1)} %collective-permute-done.2.own_ref), channel_id=1, source_target_pairs={{0,1},{1,0},{2,3},{3,2},{4,5},{5,4},{6,7},{7,6},{8,9},{9,8},{10,11... | collective-permute-start | bytes 1179656 | tf_op jit(solution)/shard_map/ppermute | solution.py:661
  48.8 19.7 %collective-permute-start.5 = (bf16[256,768]{1,0:T(8,128)(2,1)S(1)}, bf16[256,768]{1,0:T(8,128)(2,1)}, u32[]{:S(2)}, u32[]{:S(2)}) collective-permute-start(bf16[256,768]{1,0:T(8,128)(2,1)S(1)} %collective-permute-done.2.own_ref), channel_id=1, source_target_pairs={{0,2},{1,3},{2,4},{3,5},{4,6},{5,7},{6,0},{7,1},{8,10},{9,11},{10,... | collective-permute-start | bytes 1179656 | tf_op jit(solution)/shard_map/ppermute | solution.py:663
  68.4 17.8 %collective-permute-start.8 = (bf16[256,768]{1,0:T(8,128)(2,1)}, bf16[256,768]{1,0:T(8,128)(2,1)S(1)}, u32[]{:S(2)}, u32[]{:S(2)}) collective-permute-start(bf16[256,768]{1,0:T(8,128)(2,1)} %collective-permute-done.5.own_ref), channel_id=1, source_target_pairs={{0,1},{1,0},{2,3},{3,2},{4,5},{5,4},{6,7},{7,6},{8,9},{9,8},{10,11... | collective-permute-start | bytes 1179656 | tf_op jit(solution)/shard_map/ppermute | solution.py:661
  70.6 19.7 %copy-start.21 = (s32[8]{0:T(128)}, s32[8]{0:T(128)S(1)}, u32[]{:S(2)}) copy-start(s32[8]{0:T(128)S(1)} %get-tuple-element.101.count_ref) | copy-start | bytes 100
  90.0 14.8 %copy-start.12 = (f32[8,768]{1,0:T(8,128)}, f32[8,768]{1,0:T(8,128)S(1)}, u32[]{:S(2)}) copy-start(f32[8,768]{1,0:T(8,128)S(1)} %get-tuple-element.73.gain_ref) | copy-start | bytes 73732
  106.2 14.4 %all-to-all-start.1 = ((bf16[8,256,128]{2,1,0:T(8,128)(2,1)}), bf16[8,256,128]{2,1,0:T(8,128)(2,1)}, u32[]{:S(2)}, u32[]{:S(2)}) async-start(bf16[8,256,128]{2,1,0:T(8,128)(2,1)} %copy-done.5), calls=%async_computation.1 | async-start | bytes 1048576 | tf_op jit(solution)/shard_map/all_to_all | solution.py:705
  141.7 19.6 %collective-permute-start.9 = (bf16[2,192,4224]{2,1,0:T(8,128)(2,1)}, bf16[2,192,4224]{2,1,0:T(8,128)(2,1)}, u32[]{:S(2)}, u32[]{:S(2)}) collective-permute-start(bf16[2,192,4224]{2,1,0:T(8,128)(2,1)} %get-tuple-element.82), channel_id=1, source_target_pairs={{0,8},{8,0},{16,24},{24,16},{1,9},{9,1},{17,25},{25,17},{2,10},{10... | collective-permute-start | bytes 9732104 | tf_op jit(solution)/shard_map/ppermute | solution.py:725
  141.7 19.6 %all-to-all-start.2 = ((bf16[8,256,128]{2,1,0:T(8,128)(2,1)}), bf16[8,256,128]{2,1,0:T(8,128)(2,1)}, u32[]{:S(2)}, u32[]{:S(2)}) async-start(bf16[8,256,128]{2,1,0:T(8,128)(2,1)} %copy-done.4), calls=%async_computation.2 | async-start | bytes 1048576 | tf_op jit(solution)/shard_map/all_to_all | solution.py:716
  170.8 37.9 %collective-permute-start.12 = (bf16[1,192,4224]{2,1,0:T(8,128)(2,1)}, bf16[1,192,4224]{2,1,0:T(8,128)(2,1)}, u32[]{:S(2)}, u32[]{:S(2)}) collective-permute-start(bf16[1,192,4224]{2,1,0:T(8,128)(2,1)} %dynamic-slice_convert_fusion), channel_id=1, source_target_pairs={{0,16},{8,24},{16,0},{24,8},{1,17},{9,25},{17,1},{25,9},{2,18},{10... | collective-permute-start | bytes 4866056 | tf_op jit(solution)/shard_map/ppermute | solution.py:598
  201.2 3.7 %collective-permute-start.10 = (bf16[2,192,384]{2,1,0:T(8,128)(2,1)S(1)}, bf16[2,192,384]{2,1,0:T(8,128)(2,1)S(1)}, u32[]{:S(2)}, u32[]{:S(2)}) collective-permute-start(bf16[2,192,384]{2,1,0:T(8,128)(2,1)S(1)} %get-tuple-element.88), channel_id=1, source_target_pairs={{0,8},{8,0},{16,24},{24,16},{1,9},{9,1},{17,25},{25,17},{2,10},{10... | collective-permute-start | bytes 884744 | tf_op jit(solution)/shard_map/ppermute | solution.py:740
  201.3 41.5 %all-to-all-start.3 = ((bf16[8,256,384]{2,1,0:T(8,128)(2,1)}), bf16[8,256,384]{2,1,0:T(8,128)(2,1)S(1)}, u32[]{:S(2)}, u32[]{:S(2)}) async-start(bf16[8,256,384]{2,1,0:T(8,128)(2,1)} %attend_back.1.right_ref), calls=%async_computation.3 | async-start | bytes 3145728 | tf_op jit(solution)/shard_map/all_to_all | solution.py:743
  205.1 7.6 %collective-permute-start.11 = (bf16[1,192,384]{2,1,0:T(8,128)(2,1)S(1)}, bf16[1,192,384]{2,1,0:T(8,128)(2,1)S(1)}, u32[]{:S(2)}, u32[]{:S(2)}) collective-permute-start(bf16[1,192,384]{2,1,0:T(8,128)(2,1)S(1)} %dynamic-slice_convert_fusion.3), channel_id=1, source_target_pairs={{0,16},{8,24},{16,0},{24,8},{1,17},{9,25},{17,1},{25,9},{2,18},{10... | collective-permute-start | bytes 442376 | tf_op jit(solution)/shard_map/ppermute | solution.py:598
  211.4 30.9 %collective-permute-start.13 = (bf16[4,24,4224]{2,1,0:T(8,128)(2,1)S(1)}, bf16[4,24,4224]{2,1,0:T(8,128)(2,1)S(1)}, u32[]{:S(2)}, u32[]{:S(2)}) collective-permute-start(bf16[4,24,4224]{2,1,0:T(8,128)(2,1)S(1)} %fusion), channel_id=1, source_target_pairs={{0,1},{1,0},{2,3},{3,2},{4,5},{5,4},{6,7},{7,6},{8,9},{9,8},{10,11... | collective-permute-start | bytes 2433032 | tf_op jit(solution)/shard_map/ppermute | solution.py:730
  242.8 4.4 %collective-permute-start.14 = (bf16[4,1,24,384]{3,2,0,1:T(8,128)(2,1)S(1)}, bf16[4,1,24,384]{3,2,0,1:T(8,128)(2,1)S(1)}, u32[]{:S(2)}, u32[]{:S(2)}) collective-permute-start(bf16[4,1,24,384]{3,2,0,1:T(8,128)(2,1)S(1)} %get-tuple-element.142), channel_id=1, source_target_pairs={{0,1},{1,0},{2,3},{3,2},{4,5},{5,4},{6,7},{7,6},{8,9},{9,8},{10,11... | collective-permute-start | bytes 221192 | tf_op jit(solution)/shard_map/ppermute | solution.py:612
  247.3 5.3 %collective-permute-start.15 = (bf16[2,2,24,384]{3,2,1,0:T(8,128)(2,1)S(1)}, bf16[2,2,24,384]{3,2,1,0:T(8,128)(2,1)S(1)}, u32[]{:S(2)}, u32[]{:S(2)}) collective-permute-start(bf16[2,2,24,384]{3,2,1,0:T(8,128)(2,1)S(1)} %bitcast.156), channel_id=1, source_target_pairs={{0,2},{1,3},{2,0},{3,1},{4,6},{5,7},{6,4},{7,5},{8,10},{9,11},{10,... | collective-permute-start | bytes 221192 | tf_op jit(solution)/shard_map/ppermute | solution.py:612
  248.4 11.8 %collective-permute-start.17 = (bf16[2,24,4224]{2,1,0:T(8,128)(2,1)S(1)}, bf16[2,24,4224]{2,1,0:T(8,128)(2,1)S(1)}, u32[]{:S(2)}, u32[]{:S(2)}) collective-permute-start(bf16[2,24,4224]{2,1,0:T(8,128)(2,1)S(1)} %fusion.1), channel_id=1, source_target_pairs={{0,2},{1,3},{2,0},{3,1},{4,6},{5,7},{6,4},{7,5},{8,10},{9,11},{10,... | collective-permute-start | bytes 1216520 | tf_op jit(solution)/shard_map/ppermute | solution.py:598
  252.6 6.1 %collective-permute-start.16 = (bf16[1,4,24,384]{3,2,1,0:T(8,128)(2,1)S(1)}, bf16[1,4,24,384]{3,2,1,0:T(8,128)(2,1)S(1)}, u32[]{:S(2)}, u32[]{:S(2)}) collective-permute-start(bf16[1,4,24,384]{3,2,1,0:T(8,128)(2,1)S(1)} %get-tuple-element.139), channel_id=1, source_target_pairs={{0,4},{1,5},{2,6},{3,7},{4,0},{5,1},{6,2},{7,3},{8,12},{9,13},{10,... | collective-permute-start | bytes 221192 | tf_op jit(solution)/shard_map/ppermute | solution.py:612
  259.4 13.3 %copy-start.33 = (bf16[24,2304]{1,0:T(8,128)(2,1)S(1)}, bf16[24,2304]{1,0:T(8,128)(2,1)}, u32[]{:S(2)}) copy-start(bf16[24,2304]{1,0:T(8,128)(2,1)} %param.18) | copy-start | bytes 331780
  259.6 14.4 %copy-start.32 = (f32[24,2304]{1,0:T(8,128)}, f32[24,2304]{1,0:T(8,128)S(1)}, u32[]{:S(2)}) copy-start(f32[24,2304]{1,0:T(8,128)S(1)} %concatenate.49) | copy-start | bytes 663556
  259.6 13.9 %copy-start.20 = (bf16[24]{0:T(256)(128)(2,1)S(1)}, bf16[24]{0:T(256)(128)(2,1)}, u32[]{:S(2)}) copy-start(bf16[24]{0:T(256)(128)(2,1)} %param.17) | copy-start | bytes 148
  260.4 11.0 %collective-permute-start.18 = (bf16[1,24,4224]{2,1,0:T(8,128)(2,1)S(1)}, bf16[1,24,4224]{2,1,0:T(8,128)(2,1)S(1)}, u32[]{:S(2)}, u32[]{:S(2)}) collective-permute-start(bf16[1,24,4224]{2,1,0:T(8,128)(2,1)S(1)} %dynamic-slice_convert_fusion.2), channel_id=1, source_target_pairs={{0,4},{1,5},{2,6},{3,7},{4,0},{5,1},{6,2},{7,3},{8,12},{9,13},{10,... | collective-permute-start | bytes 608264 | tf_op jit(solution)/shard_map/ppermute | solution.py:598
  (28 other events, 82.0 us)
Sparse Core Ops, SparseCore 0:
  10.9 100.2 all-gather.1

commit v3 on v2

v3 whole, which is shorter than its diff:
```python
import functools
import math

import jax
import jax.numpy as jnp
from jax import lax
from jax.experimental import pallas as pl
from jax.experimental.pallas import tpu as pltpu
from jax.sharding import PartitionSpec as P

HD = 64
SLOTS = 2
LANES = SLOTS * HD
GRAIN = 128
KEY_TILE = 512
CHUNK = 384
EPS = 1e-05
THETA = 160000.0
NEG = -1e30
ROOT_HALF = 0.7071067811865476
INV_ROOT_TWO_PI = 0.3989422804014327
VMEM_BYTES = 58 * 1024 * 1024
AXES = ("fsdp", "ctx")

f32 = jnp.float32
bf16 = jnp.bfloat16


def norm_rows(values):
    center = values - jnp.mean(values, axis=-1, keepdims=True)
    spread = jnp.mean(center * center, axis=-1, keepdims=True)
    inverse = lax.rsqrt(spread + EPS)
    return (center * inverse, inverse)


def norm_back(grad_normed, normed, inverse):
    return inverse * (
        grad_normed
        - jnp.mean(grad_normed, axis=-1, keepdims=True)
        - normed * jnp.mean(grad_normed * normed, axis=-1, keepdims=True)
    )


def rotate_half(values):
    lane = lax.broadcasted_iota(jnp.int32, values.shape, 1)
    ahead = pltpu.roll(values, LANES - HD // 2, 1)
    behind = pltpu.roll(values, HD // 2, 1)
    return jnp.where(lane % HD < HD // 2, -ahead, behind)


def dot_tt(left, right):
    return lax.dot_general(left, right, (((1,), (1,)), ((), ())), preferred_element_type=f32)


def dot_rows(left, right):
    return lax.dot_general(left, right, (((0,), (0,)), ((), ())), preferred_element_type=f32)


def params():
    return pltpu.CompilerParams(
        dimension_semantics=("arbitrary",), vmem_limit_bytes=VMEM_BYTES
    )


def spread_kernel(first, *refs):
    sems, out_ref = refs[-1], refs[5]
    copies = [
        pltpu.make_async_copy(refs[i], refs[6 + i], sems.at[i]) for i in range(5)
    ]
    for copy in copies:
        copy.start()
    for copy in copies:
        copy.wait()
    w_ref, gain_one_ref, gain_two_ref, doc_ref, place_ref = refs[6:11]
    shard, columns = w_ref.shape
    width = columns // 3
    rows = doc_ref.shape[1]
    square = (shard, shard)
    eye = lax.broadcasted_iota(jnp.int32, square, 0) == lax.broadcasted_iota(jnp.int32, square, 1)

    def upright(ref):
        spread = jnp.where(eye, ref[...].astype(f32), 0.0)
        return jnp.sum(spread, axis=1, keepdims=True).astype(bf16)

    lane = lax.broadcasted_iota(jnp.int32, (shard, LANES), 1)
    gains = jnp.where(
        lane == 0, upright(gain_one_ref), jnp.where(lane == 1, upright(gain_two_ref), bf16(0))
    )
    place = place_ref[...]
    top = jnp.concatenate([doc_ref[...], place >> 6], axis=1).astype(f32)
    low = jnp.concatenate([place & 63, jnp.zeros_like(place)], axis=1).astype(f32)
    row = lax.broadcasted_iota(jnp.int32, (8, 2 * rows), 0)
    places = jnp.where(row == 0, top, jnp.where(row == 1, low, 0.0)).astype(bf16)
    for c, head in enumerate(first):
        for part in range(3):
            at = part * width + head * HD
            out_ref[c, :shard, part * LANES : (part + 1) * LANES] = w_ref[:, at : at + LANES]
        out_ref[c, :shard, 3 * LANES :] = gains
        out_ref[c, shard:, :] = places


def spread(first, w_qkv, gain_one, gain_two, docs, places):
    shard = w_qkv.shape[0]
    operands = (w_qkv, gain_one[None], gain_two[None], docs, places)
    return pl.pallas_call(
        functools.partial(spread_kernel, first),
        in_specs=[pl.BlockSpec(memory_space=pl.ANY)] * 5,
        out_specs=pl.BlockSpec(memory_space=pltpu.VMEM),
        out_shape=jax.ShapeDtypeStruct((len(first), shard + 8, 4 * LANES), bf16),
        scratch_shapes=[pltpu.VMEM(array.shape, array.dtype) for array in operands]
        + [pltpu.SemaphoreType.DMA((5,))],
        compiler_params=pltpu.CompilerParams(vmem_limit_bytes=VMEM_BYTES),
        name="spread",
    )(*operands)


def ready_kernel(masks, at_ref, w_ref, w_out_ref, gains_ref):
    share = w_ref.shape[1]
    for i, mask in enumerate(masks):
        start = pl.multiple_of((at_ref[0] ^ mask) * share, share)
        w_out_ref[pl.ds(start, share), :] = w_ref[i]
    gains_ref[...] = jnp.transpose(w_out_ref[:, 3 * LANES :].astype(f32))[:8]


def ready(masks, at, w_parts):
    count, share, columns = w_parts.shape
    vmem = pl.BlockSpec(memory_space=pltpu.VMEM)
    return pl.pallas_call(
        functools.partial(ready_kernel, masks),
        in_specs=[pl.BlockSpec(memory_space=pltpu.SMEM), vmem],
        out_specs=[vmem, vmem],
        out_shape=[
            jax.ShapeDtypeStruct((count * share, columns), bf16),
            jax.ShapeDtypeStruct((8, count * share), f32),
        ],
        compiler_params=pltpu.CompilerParams(vmem_limit_bytes=VMEM_BYTES),
        name="ready",
    )(at, w_parts)


def project_kernel(at_ref, own_ref, other_ref, w_ref, gains_ref, cos_ref, sin_ref, *refs):
    hidden_ref, qkv_ref, turned_ref = refs[-3:]
    own = pl.program_id(0) == 0
    x = jnp.where(own, own_ref[...], other_ref[...]).astype(f32)
    normed, _ = norm_rows(x)
    hidden = (normed * gains_ref[:1, :]).astype(bf16)
    hidden_ref[...] = hidden
    joined = jnp.dot(hidden, w_ref[...], preferred_element_type=f32)
    cosine = cos_ref[...]
    sine = sin_ref[...]
    query = joined[:, :LANES]
    keys = joined[:, LANES : 2 * LANES]
    values = joined[:, 2 * LANES :]
    query = (query * cosine + rotate_half(query) * sine).astype(bf16)
    keys = keys * cosine + rotate_half(keys) * sine
    qkv_ref[:, :LANES] = query * bf16(HD**-0.5)
    qkv_ref[:, LANES : 2 * LANES] = keys.astype(bf16)
    qkv_ref[:, 2 * LANES :] = values.astype(bf16)
    turned_ref[:LANES, :] = jnp.transpose(keys).astype(bf16)
    turned_ref[LANES:, :] = jnp.transpose(values).astype(bf16)


def project(at, own, other, w_heads, gains, cosine, sine, total, held):
    rows, width = own.shape
    fixed = lambda *shape: pl.BlockSpec(shape, lambda i, at: (0,) * len(shape))
    block = lambda i, at: at[0] * 2 + (at[1] ^ i)
    tall = lambda width: pl.BlockSpec((rows, width), lambda i, at: (block(i, at), 0))
    shapes = [
        jax.ShapeDtypeStruct((total, width), bf16),
        jax.ShapeDtypeStruct((total, 3 * LANES), bf16),
        jax.ShapeDtypeStruct((2 * LANES, total), bf16),
    ]
    return pl.pallas_call(
        project_kernel,
        grid_spec=pltpu.PrefetchScalarGridSpec(
            num_scalar_prefetch=1,
            grid=(2,),
            in_specs=[
                fixed(rows, width),
                fixed(rows, width),
                fixed(width, 3 * LANES),
                fixed(8, width),
                tall(LANES),
                tall(LANES),
            ]
            + [pl.BlockSpec(memory_space=pl.ANY) for _ in held],
            out_specs=[
                tall(width),
                tall(3 * LANES),
                pl.BlockSpec((2 * LANES, rows), lambda i, at: (0, block(i, at))),
            ],
        ),
        out_shape=shapes,
        input_output_aliases={7 + i: i for i in range(len(held))},
        compiler_params=params(),
        cost_estimate=pl.CostEstimate(
            flops=2 * 2 * rows * width * 3 * LANES, bytes_accessed=6 << 20, transcendentals=0
        ),
        name="project",
    )(at, own, other, w_heads, gains, cosine, sine, *held)


def gather_rows(units_ref, ref, units, part):
    lane = lax.broadcasted_iota(jnp.int32, (part, LANES), 1)
    chunks = []
    for i in range(units):
        start = pl.multiple_of(units_ref[units + i] * part, part)
        chunk = ref[pl.ds(start, part), :]
        chunks.append(jnp.where(lane // HD == units_ref[i], chunk, jnp.zeros_like(chunk)))
    return jnp.concatenate(chunks, axis=0)


def scatter_rows(units_ref, acc_ref, values, units, part):
    lane = lax.broadcasted_iota(jnp.int32, (part, LANES), 1)
    acc_ref[...] = jnp.zeros(acc_ref.shape, f32)
    for i in range(units):
        start = pl.multiple_of(units_ref[units + i] * part, part)
        chunk = values[i * part : (i + 1) * part]
        acc_ref[pl.ds(start, part), :] += jnp.where(lane // HD == units_ref[i], chunk, 0.0)


def across(slab, wide):
    if wide <= LANES:
        return slab[:, :wide]
    return jnp.concatenate([slab] * (wide // LANES), axis=1)


def fold(values, reduce):
    rows, wide = values.shape
    return reduce(values.reshape(rows // 8, 8, wide), axis=0)


def tile_span(base_ref, block, at, tile):
    return pl.ds(pl.multiple_of(base_ref[block] * GRAIN + at * tile, GRAIN), tile)


def attend_kernel(units, tile, base_ref, count_ref, units_ref, q_ref, k_ref, vt_ref, doc_ref, doc_q_ref,
                  low_ref, att_ref, lse_ref, s_ref, acc_ref):
    block = pl.program_id(0)
    wide = s_ref.shape[1]
    part = wide // units
    queries = gather_rows(units_ref, q_ref, units, part)
    doc_q = doc_q_ref[0]

    def score(at, top):
        span = tile_span(base_ref, block, at, tile)
        scores = dot_tt(k_ref[span, :], queries)
        scores = jnp.where(across(doc_ref[span, :], wide) == doc_q, scores, NEG)
        s_ref[span, :] = scores
        return jnp.maximum(top, fold(scores, jnp.max))

    count = count_ref[block]
    top = lax.fori_loop(0, count, score, jnp.full((8, wide), NEG, f32))
    top = jnp.max(top, axis=0, keepdims=True)

    def weigh(at, carry):
        total, accum = carry
        span = tile_span(base_ref, block, at, tile)
        expo = jnp.exp(s_ref[span, :] - top)
        total = total + fold(expo, jnp.sum)
        accum = accum + jnp.dot(vt_ref[:, span], expo.astype(bf16), preferred_element_type=f32)
        return (total, accum)

    total, accum = lax.fori_loop(
        0, count, weigh, (jnp.zeros((8, wide), f32), jnp.zeros((LANES, wide), f32))
    )
    total = jnp.sum(total, axis=0, keepdims=True)
    att = accum / total
    att_ref[0] = att
    lse_ref[0] = top + jnp.log(total)
    scatter_rows(units_ref, acc_ref, jnp.transpose(att), units, part)
    low_ref[0] = acc_ref[...].astype(bf16)


def attend(base, tiles, unit_places, qkv, turned, doc_slab, doc_q, rows, tile):
    total = qkv.shape[0]
    count = total // rows
    units = unit_places.shape[0] // 2
    wide = doc_q.shape[2]
    return pl.pallas_call(
        functools.partial(attend_kernel, units, tile),
        grid_spec=pltpu.PrefetchScalarGridSpec(
            num_scalar_prefetch=3,
            grid=(count,),
            in_specs=[
                pl.BlockSpec((rows, LANES), lambda i, *s: (i, 0)),
                pl.BlockSpec((total, LANES), lambda i, *s: (0, 1)),
                pl.BlockSpec((LANES, total), lambda i, *s: (1, 0)),
                pl.BlockSpec((total, LANES), lambda i, *s: (0, 0)),
                pl.BlockSpec((1, 1, wide), lambda i, *s: (i, 0, 0)),
            ],
            out_specs=[
                pl.BlockSpec((1, rows, LANES), lambda i, *s: (i, 0, 0)),
                pl.BlockSpec((1, LANES, wide), lambda i, *s: (i, 0, 0)),
                pl.BlockSpec((1, 1, wide), lambda i, *s: (i, 0, 0)),
            ],
            scratch_shapes=[pltpu.VMEM((total, wide), f32), pltpu.VMEM((rows, LANES), f32)],
        ),
        out_shape=[
            jax.ShapeDtypeStruct((count, rows, LANES), bf16),
            jax.ShapeDtypeStruct((count, LANES, wide), f32),
            jax.ShapeDtypeStruct((count, 1, wide), f32),
        ],
        compiler_params=params(),
        cost_estimate=pl.CostEstimate(
            flops=4 * count * wide * total * LANES,
            bytes_accessed=8 << 20,
            transcendentals=count * wide * total,
        ),
        name="attend",
    )(base, tiles, unit_places, qkv, qkv, turned, doc_slab, doc_q)


def attend_back_kernel(units, tile, base_ref, count_ref, units_ref, q_ref, k_ref, v_ref, kt_ref, doc_ref,
                       doc_q_ref, grad_ref, att_ref, lse_ref, cos_ref, sin_ref,
                       out_ref, dk_ref, dv_ref, acc_ref):
    block = pl.program_id(0)
    count = pl.num_programs(0)
    rows = acc_ref.shape[0]
    wide = att_ref.shape[2]
    part = wide // units

    @pl.when(block == 0)
    def _():
        dk_ref[...] = jnp.zeros(dk_ref.shape, f32)
        dv_ref[...] = jnp.zeros(dv_ref.shape, f32)

    def turn_back(values, span):
        return values * cos_ref[span, :] - rotate_half(values * sin_ref[span, :])

    queries = gather_rows(units_ref, q_ref, units, part)
    grads = gather_rows(units_ref, grad_ref.at[0], units, part)
    delta = jnp.sum(jnp.transpose(grads.astype(f32)) * att_ref[0], axis=0, keepdims=True)
    log_sum = lse_ref[0]
    doc_q = doc_q_ref[0]

    def step(at, grad_query):
        span = tile_span(base_ref, block, at, tile)
        scores = dot_tt(k_ref[span, :], queries)
        grad_probs = dot_tt(v_ref[span, :], grads)
        scores = jnp.where(across(doc_ref[span, :], wide) == doc_q, scores, NEG)
        probs = jnp.exp(scores - log_sum)
        dv_ref[span, :] += jnp.dot(probs.astype(bf16), grads, preferred_element_type=f32)
        grad_scores = (probs * (grad_probs - delta)).astype(bf16)
        dk_ref[span, :] += jnp.dot(grad_scores, queries, preferred_element_type=f32)
        return grad_query + jnp.dot(kt_ref[:, span], grad_scores, preferred_element_type=f32)

    grad_query = lax.fori_loop(
        0, count_ref[block], step, jnp.zeros((LANES, wide), f32)
    )
    scatter_rows(units_ref, acc_ref, jnp.transpose(grad_query) * HD**-0.5, units, part)
    here = pl.ds(pl.multiple_of(block * rows, rows), rows)
    out_ref[block, :, :LANES] = turn_back(acc_ref[...], here).astype(bf16)

    @pl.when(block == count - 1)
    def _():
        def finish(at, carry):
            span = pl.ds(pl.multiple_of(at * rows, rows), rows)
            out_ref[at, :, LANES : 2 * LANES] = turn_back(dk_ref[span, :], span).astype(bf16)
            out_ref[at, :, 2 * LANES :] = dv_ref[span, :].astype(bf16)
            return carry

        lax.fori_loop(0, count, finish, 0)


def attend_back(base, tiles, unit_places, qkv, turned, doc_slab, doc_q, grads, att, lse, cosine, sine,
                rows, tile):
    total = qkv.shape[0]
    count = total // rows
    units = unit_places.shape[0] // 2
    wide = doc_q.shape[2]
    whole = lambda part: pl.BlockSpec((total, LANES), lambda i, *s: (0, part))
    each = lambda *shape: pl.BlockSpec((1,) + shape, lambda i, *s: (i, 0, 0))
    return pl.pallas_call(
        functools.partial(attend_back_kernel, units, tile),
        grid_spec=pltpu.PrefetchScalarGridSpec(
            num_scalar_prefetch=3,
            grid=(count,),
            in_specs=[
                pl.BlockSpec((rows, LANES), lambda i, *s: (i, 0)),
                whole(1),
                whole(2),
                pl.BlockSpec((LANES, total), lambda i, *s: (0, 0)),
                whole(0),
                each(1, wide),
                each(rows, LANES),
                each(LANES, wide),
                each(1, wide),
                whole(0),
                whole(0),
            ],
            out_specs=pl.BlockSpec((count, rows, 3 * LANES), lambda i, *s: (0, 0, 0)),
            scratch_shapes=[
                pltpu.VMEM((total, LANES), f32),
                pltpu.VMEM((total, LANES), f32),
                pltpu.VMEM((rows, LANES), f32),
            ],
        ),
        out_shape=jax.ShapeDtypeStruct((count, rows, 3 * LANES), bf16),
        compiler_params=params(),
        cost_estimate=pl.CostEstimate(
            flops=10 * count * wide * total * LANES,
            bytes_accessed=12 << 20,
            transcendentals=count * wide * total,
        ),
        name="attend_back",
    )(base, tiles, unit_places, qkv, qkv, qkv, turned, doc_slab, doc_q, grads, att, lse, cosine, sine)


def join_heads(parts_ref, at, owners):
    rows = parts_ref.shape[1]
    side = lax.broadcasted_iota(jnp.int32, (rows, LANES), 1) // HD
    tiles = []
    for tile in range(len(owners) // SLOTS):
        column = jnp.zeros((rows, LANES), f32)
        for half in range(SLOTS):
            for c, slot in owners[tile * SLOTS + half]:
                slab = parts_ref[c, :, at : at + LANES].astype(f32)
                if slot != half:
                    slab = pltpu.roll(slab, HD, 1)
                column = column + jnp.where(side == half, slab, 0.0)
        tiles.append(column.astype(bf16))
    return jnp.concatenate(tiles, axis=1)


def fetch_rows(place_ref, metas, refs, target_ref, at, sems):
    copies = []
    for ref, blocks in zip(refs, metas):
        for index, (flip, back) in enumerate(blocks):
            count = ref.shape[1]
            turn = lax.rem(place_ref[1] + place_ref[2] - back, place_ref[2])
            row = (place_ref[0] ^ flip) * place_ref[3] + turn * count
            row = pl.multiple_of(row, count) if count < target_ref.shape[0] else 0
            target = target_ref.at[pl.ds(row, count), pl.ds(at, ref.shape[2])]
            copies.append(pltpu.make_async_copy(ref.at[index], target, sems.at[len(copies)]))
            copies[-1].start()
    return copies


def middle_kernel(owners, first, metas, cut, place_ref, att_ref, tokens_ref, gain_ref, cot_ref,
                  *refs):
    count = len(metas[0]) + len(metas[1])
    sources = refs[:count]
    (output_ref, grad_heads_ref, grad_middle_ref, attended_ref, branch_ref, hidden_ref,
     grad_up_ref, product_ref, w_ref, sems_a, sems_b) = refs[count:]
    width = tokens_ref.shape[1]
    units = product_ref.shape[1]
    copies_a = fetch_rows(place_ref, metas[0], sources[: len(metas[0])], w_ref, 0, sems_a)
    copies_b = fetch_rows(place_ref, metas[1], sources[len(metas[0]) :], w_ref, cut, sems_b)
    up = width
    down = width + 2 * units
    gain = gain_ref[1:2, :]
    cot = cot_ref[...]
    attended = join_heads(att_ref, 0, owners)
    attended_ref[...] = attended
    for copy in copies_a:
        copy.wait()
    middle = tokens_ref[...].astype(f32) + jnp.dot(
        attended, w_ref[:, :width], preferred_element_type=f32
    )
    normed, inverse = norm_rows(middle)
    hidden = (normed * gain).astype(bf16)
    hidden_ref[...] = hidden
    for copy in copies_b:
        copy.wait()
    result = middle
    grad_hidden = jnp.zeros(middle.shape, f32)
    for at in range(0, units, CHUNK):
        one = slice(at, at + CHUNK)
        two = slice(units + at, units + at + CHUNK)
        w_one = w_ref[:, up + at : up + at + CHUNK]
        w_two = w_ref[:, up + units + at : up + units + at + CHUNK]
        w_down = w_ref[:, down + at : down + at + CHUNK]
        inner = jnp.dot(hidden, w_one, preferred_element_type=f32)
        gate = jnp.dot(hidden, w_two, preferred_element_type=f32)
        grad_product = jnp.dot(cot, w_down, preferred_element_type=f32)
        cdf = 0.5 * (1.0 + lax.erf(inner * ROOT_HALF))
        gelu_value = inner * cdf
        product = (gelu_value * gate).astype(bf16)
        product_ref[:, one] = product
        slope = cdf + inner * jnp.exp(-0.5 * inner * inner) * INV_ROOT_TWO_PI
        grad_inner = (grad_product * gate * slope).astype(bf16)
        grad_gate = (grad_product * gelu_value).astype(bf16)
        grad_up_ref[:, one] = grad_inner
        grad_up_ref[:, two] = grad_gate
        result = result + dot_tt(product, w_down)
        grad_hidden = grad_hidden + dot_tt(grad_inner, w_one)
        grad_hidden = grad_hidden + dot_tt(grad_gate, w_two)
    output_ref[...] = result.astype(bf16)
    grad_middle = cot.astype(f32) + norm_back(grad_hidden * gain, normed, inverse)
    grad_middle_ref[...] = grad_middle
    grad_branch = grad_middle.astype(bf16)
    branch_ref[...] = grad_branch
    grad_attended = dot_tt(grad_branch, w_ref[:, :width])
    for c, head in enumerate(first):
        grad_heads_ref[c] = grad_attended[:, head * HD : head * HD + LANES].astype(bf16)


def middle_stage(owners, first, place, att_in, tokens, gains, cot, parts_a, parts_b, units):
    rows, width = tokens.shape
    arrays = [[array for array, _ in parts] for parts in (parts_a, parts_b)]
    metas = [[blocks for _, blocks in parts] for parts in (parts_a, parts_b)]
    vmem = pl.BlockSpec(memory_space=pltpu.VMEM)
    shape = jax.ShapeDtypeStruct
    return pl.pallas_call(
        functools.partial(middle_kernel, owners, first, metas, arrays[0][0].shape[-1]),
        in_specs=[pl.BlockSpec(memory_space=pltpu.SMEM)]
        + [vmem] * 4
        + [pl.BlockSpec(memory_space=pl.ANY)] * (len(arrays[0]) + len(arrays[1])),
        out_specs=[vmem] * 8,
        out_shape=[
            shape((rows, width), bf16),
            shape((len(first), rows, LANES), bf16),
            shape((rows, width), f32),
            shape((rows, width), bf16),
            shape((rows, width), bf16),
            shape((rows, width), bf16),
            shape((rows, 2 * units), bf16),
            shape((rows, units), bf16),
        ],
        scratch_shapes=[pltpu.VMEM((width, 2 * arrays[0][0].shape[-1]), bf16)]
        + [pltpu.SemaphoreType.DMA((sum(len(b) for b in blocks),)) for blocks in metas],
        compiler_params=pltpu.CompilerParams(vmem_limit_bytes=VMEM_BYTES),
        cost_estimate=pl.CostEstimate(
            flops=6 * rows * width * (width + 3 * units),
            bytes_accessed=10 << 20,
            transcendentals=2 * rows * units,
        ),
        name="middle_stage",
    )(place, att_in, tokens, gains, cot, *arrays[0], *arrays[1])


def settle_kernel(metas, place_ref, *refs):
    out_ref, sems = refs[-2:]
    for copy in fetch_rows(place_ref, metas, refs[:-2], out_ref, 0, sems):
        copy.wait()


def settle(place, parts, width):
    arrays = [array for array, _ in parts]
    metas = [blocks for _, blocks in parts]
    anywhere = pl.BlockSpec(memory_space=pl.ANY)
    return pl.pallas_call(
        functools.partial(settle_kernel, metas),
        in_specs=[pl.BlockSpec(memory_space=pltpu.SMEM)] + [anywhere] * len(arrays),
        out_specs=pl.BlockSpec(memory_space=pltpu.VMEM),
        out_shape=jax.ShapeDtypeStruct((width, arrays[0].shape[-1]), bf16),
        scratch_shapes=[pltpu.SemaphoreType.DMA((sum(len(b) for b in metas),))],
        compiler_params=pltpu.CompilerParams(vmem_limit_bytes=VMEM_BYTES),
        cost_estimate=pl.CostEstimate(flops=0, bytes_accessed=8 << 20, transcendentals=0),
        name="settle",
    )(place, *arrays)


def finish_kernel(owners, parts_ref, tokens_ref, gain_ref, grad_ref, w_ref, out_ref):
    joined = jnp.concatenate(
        [join_heads(parts_ref, part * LANES, owners) for part in range(3)], axis=1
    )
    normed, inverse = norm_rows(tokens_ref[...].astype(f32))
    grad_hidden = dot_tt(joined, w_ref[...])
    back = norm_back(grad_hidden * gain_ref[:1, :], normed, inverse)
    out_ref[...] = (grad_ref[...] + back).astype(bf16)


def finish(owners, joined, tokens, gains, grad_middle, w_joined):
    rows, width = tokens.shape
    vmem = pl.BlockSpec(memory_space=pltpu.VMEM)
    return pl.pallas_call(
        functools.partial(finish_kernel, owners),
        in_specs=[vmem] * 5,
        out_specs=vmem,
        out_shape=jax.ShapeDtypeStruct((rows, width), bf16),
        compiler_params=pltpu.CompilerParams(vmem_limit_bytes=VMEM_BYTES),
        cost_estimate=pl.CostEstimate(
            flops=6 * rows * width * width, bytes_accessed=6 << 20, transcendentals=0
        ),
        name="finish",
    )(joined, tokens, gains, grad_middle, w_joined)


def half_rows(pairs, side, share, refs, lt_ref, emit):
    at = 0
    for pair in range(pairs):
        lt_ref[pair] = jnp.transpose(refs[2 * pair][...])
    for pair in range(pairs):
        right_ref = refs[2 * pair + 1]
        columns = right_ref.shape[1]
        for start in range(0, columns, CHUNK):
            right = right_ref[:, start : start + CHUNK]
            for half in range(lt_ref.shape[1] // share // 2):
                row = pl.multiple_of((2 * half + side) * share, share)
                emit(
                    half,
                    at + start,
                    jnp.dot(lt_ref[pair, pl.ds(row, share), :], right, preferred_element_type=f32),
                )
        at += columns


def pieces_of(cut, at, value):
    end = at + value.shape[1]
    found = []
    if at < cut:
        found.append((0, at, value[:, : min(end, cut) - at]))
    if end > cut:
        found.append((1, max(at, cut) - cut, value[:, max(at, cut) - at :]))
    return found


def gone_grads_kernel(pairs, cut, sides_ref, *refs):
    outs = refs[2 * pairs : 2 * pairs + 2]
    share = outs[0].shape[1]

    def emit(half, at, value):
        for which, start, piece in pieces_of(cut, at, value):
            span = slice(start, start + piece.shape[1])
            outs[which][half, :, span] = piece.astype(bf16)

    half_rows(pairs, 1 - sides_ref[0], share, refs, refs[-1], emit)


def kept_grads_kernel(pairs, cut, sides_ref, *refs):
    gots = refs[2 * pairs : 2 * pairs + 2]
    mine_a, other_a, mine_b, other_b = refs[2 * pairs + 2 : 2 * pairs + 6]
    share = gots[0].shape[1]
    shard = mine_b.shape[1]
    outer = share // shard // 2

    def emit(half, at, value):
        for which, start, piece in pieces_of(cut, at, value):
            span = slice(start, start + piece.shape[1])
            total = (piece + gots[which][half, :, span].astype(f32)).astype(bf16)
            if which == 0:

                @pl.when(sides_ref[1] == half)
                def _():
                    mine_a[0, :, span] = total

                @pl.when(sides_ref[1] != half)
                def _():
                    other_a[0, :, span] = total

            else:
                for x in range(2):
                    to = (mine_b, other_b)

                    @pl.when(sides_ref[2] == x)
                    def _():
                        for z in range(outer):
                            for flip in range(2):
                                row = (z * 2 + (x ^ flip)) * shard
                                to[flip][half * outer + z, :, span] = total[row : row + shard]

    half_rows(pairs, sides_ref[0], share, refs, refs[-1], emit)


def weight_grads(kernel, sides, operands, gots, outs, cut, name):
    vmem = pl.BlockSpec(memory_space=pltpu.VMEM)
    rows, width = operands[0].shape
    columns = sum(array.shape[1] for array in operands[1::2])
    return pl.pallas_call(
        functools.partial(kernel, len(operands) // 2, cut),
        in_specs=[pl.BlockSpec(memory_space=pltpu.SMEM)] + [vmem] * (len(operands) + len(gots)),
        out_specs=[vmem] * len(outs),
        out_shape=[jax.ShapeDtypeStruct(shape, bf16) for shape in outs],
        scratch_shapes=[pltpu.VMEM((len(operands) // 2, width, rows), bf16)],
        compiler_params=pltpu.CompilerParams(vmem_limit_bytes=VMEM_BYTES),
        cost_estimate=pl.CostEstimate(
            flops=rows * width * columns, bytes_accessed=3 * width * columns, transcendentals=0
        ),
        name=name,
    )(sides, *operands, *gots)


def head_grads_kernel(sides_ref, left_ref, right_ref, kept_ref, gone_ref, acc_ref):
    acc_ref[...] = jnp.zeros(acc_ref.shape, f32)
    count, rows, _ = right_ref.shape
    halves, share = kept_ref.shape[:2]

    def step(at, carry):
        span = pl.ds(pl.multiple_of(at * rows, rows), rows)
        left = jnp.transpose(left_ref[span, :])
        acc_ref[...] += jnp.dot(left, right_ref[at], preferred_element_type=f32)
        return carry

    lax.fori_loop(0, count, step, 0)
    for half in range(halves):
        for flip, ref in enumerate((kept_ref, gone_ref)):
            row = pl.multiple_of((2 * half + (sides_ref[0] ^ flip)) * share, share)
            ref[half] = acc_ref[pl.ds(row, share), :].astype(bf16)


def head_grads(fsdp, sides, hidden, grad_joined):
    total, width = hidden.shape
    columns = grad_joined.shape[2]
    vmem = pl.BlockSpec(memory_space=pltpu.VMEM)
    half = jax.ShapeDtypeStruct((fsdp // 2, width // fsdp, columns), bf16)
    return pl.pallas_call(
        head_grads_kernel,
        in_specs=[pl.BlockSpec(memory_space=pltpu.SMEM), vmem, vmem],
        out_specs=[vmem, vmem],
        out_shape=[half, half],
        scratch_shapes=[pltpu.VMEM((width, columns), f32)],
        compiler_params=pltpu.CompilerParams(vmem_limit_bytes=VMEM_BYTES),
        cost_estimate=pl.CostEstimate(
            flops=2 * total * width * columns,
            bytes_accessed=2 * total * (width + columns),
            transcendentals=0,
        ),
        name="head_grads",
    )(sides, hidden, grad_joined)


def add_halves_kernel(picks, joined, sides_ref, *refs):
    pairs = len(picks)
    outs = refs[2 * pairs :]
    begin = 0
    for i, pick in enumerate(picks):
        kept_ref, got_ref = refs[2 * i], refs[2 * i + 1]
        columns = kept_ref.shape[-1]
        for at in range(kept_ref.shape[0]):
            for flip in range(2):
                side = sides_ref[pick] ^ flip
                total = kept_ref[at, side].astype(f32) + got_ref[at, side].astype(f32)
                if joined:
                    outs[flip][at, :, begin : begin + columns] = total.astype(bf16)
                else:
                    outs[2 * i + flip][at] = total.astype(bf16)
        begin += columns


def add_halves(sides, pairs, joined=False):
    flat = []
    shapes = []
    for kept, got, axis, _ in pairs:
        shape = kept.shape
        shape = (
            math.prod(shape[:axis]), 2, math.prod(shape[axis + 1 : -1]), shape[-1]
        )
        flat += [kept.reshape(shape), got.reshape(shape)]
        shapes += [(shape[0], shape[2], shape[3])] * 2
    if joined:
        columns = sum(shape[2] for shape in shapes) // 2
        shapes = [shapes[0][:2] + (columns,)] * 2
    vmem = pl.BlockSpec(memory_space=pltpu.VMEM)
    size = sum(array.size for array in flat)
    return pl.pallas_call(
        functools.partial(add_halves_kernel, [pair[3] for pair in pairs], joined),
        in_specs=[pl.BlockSpec(memory_space=pltpu.SMEM)] + [vmem] * len(flat),
        out_specs=[vmem] * len(shapes),
        out_shape=[jax.ShapeDtypeStruct(shape, bf16) for shape in shapes],
        compiler_params=pltpu.CompilerParams(vmem_limit_bytes=VMEM_BYTES),
        cost_estimate=pl.CostEstimate(flops=size, bytes_accessed=3 * size, transcendentals=0),
        name="add_halves",
    )(sides, *flat)


def flips(count, bit):
    return [(i, i ^ bit) for i in range(count)]


def gate(*values):
    return lax.optimization_barrier(values)


def program(fsdp, ctx):
    def on_device(tokens, segment_ids, positions, gain_attn, w_qkv, w_out, gain_mlp, w_in, w_down,
                  cotangent):
        rows, width = tokens.shape[1:]
        shard = w_qkv.shape[0]
        share = ctx * shard
        heads = width // HD
        common = math.gcd(heads, ctx)
        splits = ctx // common
        units = heads // common
        part = rows // splits
        total = ctx * rows
        outer = ctx // 2
        first = [min(units * c // splits, heads - SLOTS) for c in range(ctx)]
        owners = [
            [
                (c, slot)
                for c in range(ctx)
                for slot in range(SLOTS)
                if first[c] + slot == head
                and max(units * c, head * splits) < min(units * (c + 1), (head + 1) * splits)
            ]
            for head in range(heads)
        ]
        me = lax.axis_index("ctx")
        mine = lax.axis_index("fsdp")
        sides = jnp.stack([mine % 2, mine // 2 % 2, me % 2, me // 2 % 2, me // 4 % 2])
        sides = sides.astype(jnp.int32)
        place = jnp.stack([mine, me // 2, 0 * me + outer, 0 * me + share]).astype(jnp.int32)
        swap = flips(ctx, 1)
        turn = lambda back: [
            (o * 2 + i, (o + back) % outer * 2 + i) for o in range(outer) for i in range(2)
        ]
        by_y = flips(fsdp, 2)
        by_core = flips(fsdp, 1)
        by_hand = (fsdp, ctx) == (4, 8) and shard % 8 == 0
        tile = KEY_TILE
        cot = cotangent[0]
        packed = jnp.concatenate([w_out, w_in, w_down.T], axis=1)
        columns = packed.shape[1]
        cut = (columns // LANES + 1) // 2 * LANES

        def weave(own, got):
            low = jnp.where(me % 2 == 0, own, got)
            high = jnp.where(me % 2 == 0, got, own)
            return jnp.concatenate([low, high], axis=1)

        def tables(sent):
            infos = sent[:, shard : shard + 2, :].astype(f32)
            docs = infos[:, 0, :rows].astype(jnp.int32)
            spots = (infos[:, 0, rows:] * 64 + infos[:, 1, :rows]).reshape(total, 1)
            half = jnp.arange(LANES) % (HD // 2)
            rates = THETA ** (-2.0 * half.astype(f32) / HD)
            angles = spots * rates[None, :]
            doc_slab = jnp.broadcast_to(docs.reshape(total, 1), (total, LANES))
            edges = docs.reshape(total // GRAIN, GRAIN)
            lo = jnp.sum((edges[None, :, -1] < docs[:, :1]).astype(jnp.int32), axis=1)
            hi = jnp.sum((edges[None, :, 0] <= docs[:, rows - 1 :]).astype(jnp.int32), axis=1)
            count = (hi - lo + tile // GRAIN - 1) // (tile // GRAIN)
            base = jnp.minimum(lo, total // GRAIN - count * (tile // GRAIN))
            unit = units * me + jnp.arange(units, dtype=jnp.int32)
            first_head = jnp.minimum(units * me // splits, heads - SLOTS)
            unit_places = jnp.concatenate([unit // splits - first_head, unit % splits])
            pick = (unit % splits)[:, None] == jnp.arange(splits, dtype=jnp.int32)[None, :]
            doc_q = jnp.sum(
                jnp.where(pick[None, :, :, None], docs.reshape(ctx, 1, splits, part), 0), axis=2
            ).reshape(ctx, 1, units * part)
            return (
                jnp.cos(angles), jnp.sin(angles), doc_slab, base, count,
                unit_places.astype(jnp.int32), doc_q,
            )

        sent = spread(first, w_qkv, gain_attn, gain_mlp, segment_ids, positions)
        sent = lax.all_to_all(sent, "ctx", 0, 0, tiled=True)
        masks = [0]
        if by_hand:
            own = [tokens[0]]
            near = [jnp.stack(
                [packed[:, :cut], jnp.pad(packed[:, cut:], ((0, 0), (0, 2 * cut - columns)))]
            )]
            own.append(lax.ppermute(own[0], "ctx", turn(1)))
            other = [lax.ppermute(own[0], "ctx", swap)]
            near.append(lax.ppermute(near[0], "ctx", turn(1)))
            own[1], other[0], near[1], sent = gate(own[1], other[0], near[1], sent)

        w_parts = sent[:, :shard, :].reshape(1, share, 4 * LANES)
        bit = fsdp // 2
        while bit:
            got = lax.ppermute(w_parts, "fsdp", flips(fsdp, bit))
            w_parts = jnp.concatenate([w_parts, got], axis=0)
            masks += [mask ^ bit for mask in masks]
            bit //= 2
        known = tables(sent)
        if by_hand:
            own.append(lax.ppermute(own[1], "ctx", turn(1)))
            other.append(lax.ppermute(own[1], "ctx", swap))
            near.append(lax.ppermute(near[1], "ctx", turn(1)))
            low_a = jnp.stack([near[0][0], near[1][0]])
            low_b = jnp.stack([near[0][1], near[1][1]])
            own[2], other[1], near[2], low_a, low_b, w_parts, known = gate(
                own[2], other[1], near[2], low_a, low_b, w_parts, known
            )
        cosine, sine, doc_slab, base, count, unit_places, doc_q = known

        w_heads, gains = ready(masks, mine.astype(jnp.int32).reshape(1), w_parts)

        def project_pair(step, held):
            at = jnp.stack([(me // 2 + outer - step) % outer, me % 2]).astype(jnp.int32)
            return project(
                at, own[step], other[step], w_heads, gains, cosine, sine, total, held
            )

        if by_hand:
            own.append(lax.ppermute(own[2], "ctx", turn(1)))
            other.append(lax.ppermute(own[2], "ctx", swap))
            near.append(lax.ppermute(near[2], "ctx", turn(1)))
            next_a = lax.ppermute(low_a, "ctx", swap)
            next_b = lax.ppermute(low_b, "fsdp", by_y)
            held = project_pair(1, project_pair(0, []))
            own[3], other[2], near[3], next_a, next_b, held = gate(
                own[3], other[2], near[3], next_a, next_b, held
            )

            other.append(lax.ppermute(own[3], "ctx", swap))
            high_a = jnp.stack([near[2][0], near[3][0]])
            high_b = jnp.stack([near[2][1], near[3][1]])
            past_a = lax.ppermute(high_a, "ctx", swap)
            past_b = lax.ppermute(high_b, "fsdp", by_y)
            ring_c = [w_qkv] + [lax.ppermute(w_qkv, "ctx", turn(back)) for back in range(1, outer)]
            held = project_pair(2, held)
            other[3], past_a, past_b, ring_c, held = gate(other[3], past_a, past_b, ring_c, held)

            pair_a = jnp.concatenate([weave(low_a, next_a), weave(high_a, past_a)])
            pair_b = jnp.concatenate([low_b, next_b, high_b, past_b])
            far_a = lax.ppermute(pair_a, "fsdp", by_y)
            far_b = lax.ppermute(pair_b, "ctx", swap)
            held = project_pair(3, held)
        else:
            blocks = lax.all_gather(tokens[0], "ctx", axis=0, tiled=True)
            blocks = blocks.reshape(outer, 2, rows, width)
            held = []
            for step in range(outer):
                at = jnp.asarray([step, 0], jnp.int32)
                held = project(
                    at, blocks[step, 0], blocks[step, 1], w_heads, gains, cosine, sine, total, held
                )
        hidden_one, qkv, turned = held
        att_low, att, lse = attend(
            base, count, unit_places, qkv, turned, doc_slab, doc_q, rows, tile
        )
        if by_hand:
            att_low, far_a, far_b = gate(att_low, far_a, far_b)
            pair_b = weave(pair_b, far_b)
            arrays = [pair_a, far_a, lax.ppermute(pair_a, "fsdp", by_core),
                      lax.ppermute(far_a, "fsdp", by_core),
                      pair_b, lax.ppermute(pair_b, "fsdp", by_core)]
            metas_a = [[(flip + 2 * far, back) for back in range(outer)]
                       for flip in range(2) for far in range(2)]
            metas_b = [[(flip + 2 * near, back) for near in (0, 1) for back in (0, 1)]
                       + [(flip + 2 * near, back) for near in (0, 1) for back in (2, 3)]
                       for flip in range(2)]
            att_in = lax.all_to_all(att_low, "ctx", 0, 0, tiled=True)
            pair_c = jnp.stack(ring_c)
            att_in, arrays, pair_c = gate(att_in, arrays, pair_c)
            near_c = lax.ppermute(pair_c, "ctx", swap)
        else:
            att_in = lax.all_to_all(att_low, "ctx", 0, 0, tiled=True)
            every = lax.all_gather(packed, AXES, axis=0, tiled=True)
            arrays = [every[None, :, :cut], every[None, :, cut:]]
            metas_a = metas_b = [[(0, 0)]]
            place = jnp.stack([0 * me, 0 * me, 0 * me + 1, 0 * me]).astype(jnp.int32)
            w_joined = lax.all_gather(w_qkv, AXES, axis=0, tiled=True)
        parts_a = list(zip(arrays, metas_a))
        parts_b = list(zip(arrays[len(metas_a) :], metas_b))

        output, grad_heads, grad_middle, attended, grad_branch, hidden_two, grad_up, product = (
            middle_stage(
                owners, first, place, att_in, tokens[0], gains, cot, parts_a, parts_b,
                w_down.shape[0],
            )
        )
        operands = [attended, grad_branch, hidden_two, grad_up, cot, product]
        grad_heads = lax.all_to_all(grad_heads, "ctx", 0, 0, tiled=True)
        if by_hand:
            rest = columns - cut
            gone_a, gone_b = weight_grads(
                gone_grads_kernel, sides, operands, [], [(2, share, cut), (2, share, rest)], cut,
                "gone_grads",
            )
            got_a = lax.ppermute(gone_a, "fsdp", by_core)
            got_b = lax.ppermute(gone_b, "fsdp", by_core)
            mine_a, other_a, mine_b, other_b = weight_grads(
                kept_grads_kernel, sides, operands, [got_a, got_b],
                [(1, share, cut)] * 2 + [(2 * outer, shard, rest)] * 2, cut, "kept_grads",
            )
            grad_heads, mine_a, other_a, mine_b, other_b, near_c = gate(
                grad_heads, mine_a, other_a, mine_b, other_b, near_c
            )
            got_a = lax.ppermute(other_a, "fsdp", by_y)
            got_b = lax.ppermute(other_b, "ctx", swap)
        else:
            grad_packed = jnp.concatenate(
                [dot_rows(left, right) for left, right in zip(operands[::2], operands[1::2])],
                axis=1,
            ).astype(bf16)
            grad_packed = lax.psum_scatter(grad_packed, "fsdp", scatter_dimension=0, tiled=True)
            grad_packed = lax.psum_scatter(grad_packed, "ctx", scatter_dimension=0, tiled=True)
            grad_packed = grad_packed.astype(f32)

        grad_joined = attend_back(
            base, count, unit_places, qkv, turned, doc_slab, doc_q, grad_heads, att, lse, cosine,
            sine, rows, tile,
        )
        if by_hand:
            grad_joined, mine_a, got_a, mine_b, got_b = gate(
                grad_joined, mine_a, got_a, mine_b, got_b
            )
            pair_c = weave(pair_c, near_c)
            far_c = lax.ppermute(pair_c, "fsdp", by_y)
            joined_in = lax.all_to_all(grad_joined, "ctx", 0, 0, tiled=True)
            by_x = lambda array: array.reshape(outer, 2, shard, array.shape[-1])
            mine_a, other_a, mine_b, other_b = add_halves(
                sides,
                [(by_x(mine_a), by_x(got_a), 1, 2),
                 (mine_b.reshape(2, share // 2, rest), got_b.reshape(2, share // 2, rest), 0, 1)],
            )
            sides_late, other_a, other_b = gate(sides, other_a, other_b)
            got_a = lax.ppermute(other_a, "ctx", swap)
            got_b = lax.ppermute(other_b, "fsdp", by_y)
            kept_cols, gone_cols = head_grads(fsdp, sides_late, hidden_one, grad_joined)
            mine_a, got_a, mine_b, got_b, kept_cols, gone_cols = gate(
                mine_a, got_a, mine_b, got_b, kept_cols, gone_cols
            )
            pairs = lambda array: array.reshape(outer // 2, 2, shard, array.shape[-1])
            kept, gone = add_halves(
                sides,
                [(pairs(mine_a), pairs(got_a), 1, 3), (pairs(mine_b), pairs(got_b), 1, 3)],
                joined=True,
            )
            got = lax.ppermute(gone, "ctx", flips(ctx, 2))
            got_cols = lax.ppermute(gone_cols, "fsdp", by_core)
            kept, got, kept_cols, got_cols, far_c = gate(kept, got, kept_cols, got_cols, far_c)
            kept, gone = add_halves(sides, [(kept, got, 0, 4)])
            got = lax.ppermute(gone, "ctx", flips(ctx, 4))
            kept_cols, gone_cols = add_halves(sides, [(kept_cols, got_cols, 0, 1)])
            got_cols = lax.ppermute(gone_cols, "fsdp", by_y)
            arrays = [pair_c, far_c, lax.ppermute(pair_c, "fsdp", by_core),
                      lax.ppermute(far_c, "fsdp", by_core)]
            w_joined = settle(place, list(zip(arrays, metas_a)), width)
            joined_in, kept, got, kept_cols, got_cols, w_joined = gate(
                joined_in, kept, got, kept_cols, got_cols, w_joined
            )
            grad_packed = kept[0].astype(f32) + got[0].astype(f32)
            grad_cols = (kept_cols[0].astype(f32) + got_cols[0].astype(f32)).astype(bf16)
        else:
            joined_in = lax.all_to_all(grad_joined, "ctx", 0, 0, tiled=True)
            grad_cols = dot_rows(hidden_one, grad_joined.reshape(total, 3 * LANES)).astype(bf16)
            grad_cols = lax.psum_scatter(grad_cols, "fsdp", scatter_dimension=0, tiled=True)
        input_grad = finish(owners, joined_in, tokens[0], gains, grad_middle, w_joined)
        grad_cols = grad_cols.reshape(ctx, shard, 3 * LANES)
        grad_cols = lax.all_to_all(grad_cols, "ctx", 0, 0, tiled=True).astype(f32)

        sum_w_out = grad_packed[:, :width]
        sum_w_in = grad_packed[:, width : width + w_in.shape[1]]
        sum_w_down = grad_packed[:, width + w_in.shape[1] :].T
        sum_gain_mlp = jnp.sum(w_in.astype(f32) * sum_w_in, axis=1) / gain_mlp.astype(f32)
        pieces = []
        for third in range(3):
            for head in range(heads):
                column = 0.0
                for c, slot in owners[head]:
                    at = third * LANES + slot * HD
                    column = column + grad_cols[c, :, at : at + HD]
                pieces.append(column)
        sum_w_qkv = jnp.concatenate(pieces, axis=1)
        sum_gain_attn = jnp.sum(w_qkv.astype(f32) * sum_w_qkv, axis=1) / gain_attn.astype(f32)
        return (
            output[None],
            input_grad[None],
            sum_gain_attn,
            sum_w_qkv,
            sum_w_out,
            sum_gain_mlp,
            sum_w_in,
            sum_w_down,
        )

    return on_device


def solution(mesh):
    rows = P(AXES, None)
    tokens = P("fsdp", "ctx", None)
    return jax.shard_map(
        program(mesh.shape["fsdp"], mesh.shape["ctx"]),
        mesh=mesh,
        in_specs=(
            tokens,
            P("fsdp", "ctx"),
            P("fsdp", "ctx"),
            P(AXES),
            rows,
            rows,
            P(AXES),
            rows,
            P(None, AXES),
            tokens,
        ),
        out_specs=(tokens, tokens, P(AXES), rows, rows, P(AXES), rows, P(None, AXES)),
        check_vma=False,
    )
```

time: 282 us -> 265 us (0.940)
  waiting for transfers between devices: 107 us -> 70 us
  Pallas kernels: 78 us -> 111 us
  starting transfers between devices: 37.9 us -> 54.2 us
  between operations: 14.5 us -> 1.16 us
  local copies, waits for them, and re-layouts: 20.4 us -> 11 us
  other arithmetic: 23.5 us -> 16 us
    pallas_call x9 -> x16, Pallas kernels: 42.5 us -> 73.9 us  [the longest x4 18.8 us: project(): pl.pallas_call(project_kernel, grid_spec=pltpu.PrefetchScalarGridSpec(num...]
    all_to_all x1, waiting for transfers between devices: 15.2 us -> 0.01 us  [on_device(): grad_heads = lax.all_to_all(grad_heads, 'ctx', 0, 0, tiled=True)]
    ppermute x17 -> x36, waiting for transfers between devices: 66.4 us -> 52.5 us  [the longest x1 13.8 us: on_device(): got_b = lax.ppermute(other_b, 'fsdp', by_y)]
    ppermute x17 -> x36, starting transfers between devices: 20.1 us -> 32 us  [the longest x3 4.89 us: on_device(): lax.ppermute(w_qkv, 'ctx', turn(back))]
    add x6 -> x1, other arithmetic: 10.6 us -> 0.04 us  [on_device(): grad_packed = kept[0].astype(f32) + got[0].astype(f32)]
    all_to_all x1, waiting for transfers between devices: 13 us -> 4.19 us  [on_device(): sent = lax.all_to_all(sent, 'ctx', 0, 0, tiled=True)]
    unnamed x75 -> x73, local copies, waits for them, and re-layouts: 13.5 us -> 6.68 us
    all_to_all x1 -> x2, starting transfers between devices: 3.64 us -> 9.2 us  [the longest x1 5.65 us: on_device(): joined_in = lax.all_to_all(grad_joined, 'ctx', 0, 0, tiled=True)]
  transfers between devices with their start and end apart: 24 -> 43, of which waited for: 16 -> 16; matrix products, arithmetic and copies ran while one was open for 6% -> 5% of each run, Pallas kernels for 22% -> 37%
where the time goes in v3:
time: 265 us; the launch traced here: 264 us
  Pallas kernels  111 us (42%)
  waiting for transfers between devices  70 us (26%)
  starting transfers between devices  54.2 us (20%)
  other arithmetic  16 us (6%)
  local copies, waits for them, and re-layouts  11 us (4%)
    pallas_call x1, Pallas kernels, attend_back(): pl.pallas_call(functools.partial(attend_back_kernel, units, tile), grid_s...  22.2 us
    pallas_call x4, Pallas kernels, project(): pl.pallas_call(project_kernel, grid_spec=pltpu.PrefetchScalarGridSpec(num...  18.8 us
    pallas_call x1, Pallas kernels, attend(): pl.pallas_call(functools.partial(attend_kernel, units, tile), grid_spec=p...  15.3 us
    pallas_call x2, Pallas kernels, weight_grads(): pl.pallas_call(functools.partial(kernel, len(operands) // 2, cut), in_spe...  14.7 us
    ppermute x1, waiting for transfers between devices, on_device(): got_b = lax.ppermute(other_b, 'fsdp', by_y)  13.8 us
    all_to_all x1, waiting for transfers between devices, on_device(): att_in = lax.all_to_all(att_low, 'ctx', 0, 0, tiled=True)  11.4 us
    pallas_call x1, Pallas kernels, middle_stage(): pl.pallas_call(functools.partial(middle_kernel, owners, first, metas, arr...  10.3 us
    pallas_call x4, Pallas kernels, add_halves(): pl.pallas_call(functools.partial(add_halves_kernel, [pair[3] for pair in...  9.64 us
  transfers between devices with their start and end apart: 43, of which 16 were waited for; matrix products, arithmetic and copies ran while one was open for 5% of the time, Pallas kernels for 37%

profile of v3, /device:TPU:0, one launch (start us, length us, event | category | flops | bytes accessed | tf_op | source)
XLA Modules:
  0.0 263.8 jit_solution(17275950391712720566)
XLA Ops:
  0.6 3.0 %collective-permute-start.1 = (bf16[256,768]{1,0:T(8,128)(2,1)}, bf16[256,768]{1,0:T(8,128)(2,1)S(1)}, u32[]{:S(2)}, u32[]{:S(2)}) collective-permute-start(bf16[256,768]{1,0:T(8,128)(2,1)} %bitcast.129), channel_id=1, source_target_pairs={{0,1},{1,0},{2,3},{3,2},{4,5},{5,4},{6,7},{7,6},{8,9},{9,8},{10,11... | collective-permute-start | bytes 1179656 | tf_op jit(solution)/shard_map/ppermute | solution.py:847
  9.6 3.5 %all-to-all-start = ((bf16[8,32,512]{2,1,0:T(8,128)(2,1)}), bf16[8,32,512]{2,1,0:T(8,128)(2,1)S(1)}, u32[]{:S(2)}, u32[]{:S(2)}) async-start(bf16[8,32,512]{2,1,0:T(8,128)(2,1)} %spread.1), calls=%async_computation | async-start | bytes 524288 | tf_op jit(solution)/shard_map/all_to_all | solution.py:839
  15.1 7.1 %collective-permute-done.2 = bf16[2,24,2176]{2,1,0:T(8,128)(2,1)S(1)} collective-permute-done((bf16[2,24,2176]{2,1,0:T(8,128)(2,1)S(1)}, bf16[2,24,2176]{2,1,0:T(8,128)(2,1)S(1)}, u32[]{:S(2)}, u32[]{:S(2)}) %collective-permute-start.2) | collective-permute-done | bytes 208928 | tf_op jit(solution)/shard_map/ppermute | solution.py:848
  22.2 4.2 %all-to-all-done = bf16[8,32,512]{2,1,0:T(8,128)(2,1)S(1)} async-done(((bf16[8,32,512]{2,1,0:T(8,128)(2,1)}), bf16[8,32,512]{2,1,0:T(8,128)(2,1)S(1)}, u32[]{:S(2)}, u32[]{:S(2)}) %all-to-all-start) | async-done | bytes 262176 | tf_op jit(solution)/shard_map/all_to_all | solution.py:839
  29.9 5.6 %multiply_sine_fusion = (f32[2048,128]{1,0:T(8,128)}, f32[2048,128]{1,0:T(8,128)}) fusion(f32[128]{0:T(128)S(1)} %fusion.19, f32[2048]{0:T(1024)S(1)} %bitcast.158), kind=kLoop, calls=%fused_computation.1 | loop fusion | flops 262144 | bytes 2105856 | tf_op jit(solution)/shard_map/sin | solution.py:834
  38.7 5.1 %collective-permute-done.3.own_ref = bf16[256,768]{1,0:T(8,128)(2,1)S(1)} collective-permute-done((bf16[256,768]{1,0:T(8,128)(2,1)S(1)}, bf16[256,768]{1,0:T(8,128)(2,1)S(1)}, u32[]{:S(2)}, u32[]{:S(2)}) %collective-permute-start.3) | collective-permute-done | bytes 393248 | tf_op jit(solution)/shard_map/ppermute | solution.py:860
  48.7 2.1 ready.1
  50.8 4.7 %project.4 = (bf16[2048,768]{1,0:T(8,128)(2,1)}, bf16[2048,384]{1,0:T(8,128)(2,1)}, bf16[256,2048]{1,0:T(8,128)(2,1)}) custom-call(s32[2]{0:T(128)} %get-tuple-element.316.at_ref, bf16[256,768]{1,0:T(8,128)(2,1)} %bitcast.131, bf16[256,768]{1,0:T(8,128)(2,1)} %copy-done.24, bf16[768,512]{1,0:T(8,128)(2,1)} %get-tuple-element.140.w_ref, ...), custom_call_target="tpu_custom_call" | custom-call | flops 301989888 | bytes 6291456 | tf_op jit(solution)/shard_map/project/pallas_call | solution.py:173
  55.5 4.8 %project.5 = (bf16[2048,768]{1,0:T(8,128)(2,1)}, bf16[2048,384]{1,0:T(8,128)(2,1)}, bf16[256,2048]{1,0:T(8,128)(2,1)}) custom-call(s32[2]{0:T(128)} %get-tuple-element.315.at_ref, bf16[256,768]{1,0:T(8,128)(2,1)} %copy-done.17, bf16[256,768]{1,0:T(8,128)(2,1)} %copy-done.20, ...), custom_call_target="tpu_custom_call", output_to_operand_aliasing={{0}: (7, {}), {1}: (8, {}), {2}: (9, {})} | custom-call | flops 301989888 | bytes 6291456 | tf_op jit(solution)/shard_map/project/pallas_call | solution.py:173
  62.0 2.3 collective-permute-start.18
  69.8 4.7 %project.6 = (bf16[2048,768]{1,0:T(8,128)(2,1)}, bf16[2048,384]{1,0:T(8,128)(2,1)}, bf16[256,2048]{1,0:T(8,128)(2,1)}) custom-call(s32[2]{0:T(128)} %get-tuple-element.317.at_ref, bf16[256,768]{1,0:T(8,128)(2,1)} %copy-done.18, bf16[256,768]{1,0:T(8,128)(2,1)} %copy-done.21, ...), custom_call_target="tpu_custom_call", output_to_operand_aliasing={{0}: (7, {}), {1}: (8, {}), {2}: (9, {})} | custom-call | flops 301989888 | bytes 6291456 | tf_op jit(solution)/shard_map/project/pallas_call | solution.py:173
  75.2 5.1 %collective-permute-done.13.other_ref = bf16[256,768]{1,0:T(8,128)(2,1)S(1)} collective-permute-done((bf16[256,768]{1,0:T(8,128)(2,1)S(1)}, bf16[256,768]{1,0:T(8,128)(2,1)S(1)}, u32[]{:S(2)}, u32[]{:S(2)}) %collective-permute-start.13) | collective-permute-done | bytes 393248 | tf_op jit(solution)/shard_map/ppermute | solution.py:889
  81.9 4.7 %project.7 = (bf16[2048,768]{1,0:T(8,128)(2,1)}, bf16[2048,384]{1,0:T(8,128)(2,1)}, bf16[256,2048]{1,0:T(8,128)(2,1)}) custom-call(s32[2]{0:T(128)} %get-tuple-element.314.at_ref, bf16[256,768]{1,0:T(8,128)(2,1)} %copy-done.19, bf16[256,768]{1,0:T(8,128)(2,1)} %copy-done.22, ...), custom_call_target="tpu_custom_call", output_to_operand_aliasing={{0}: (7, {}), {1}: (8, {}), {2}: (9, {})} | custom-call | flops 301989888 | bytes 6291456 | tf_op jit(solution)/shard_map/project/pallas_call | solution.py:173
  86.6 15.3 %attend.1 = (bf16[8,256,128]{2,1,0:T(8,128)(2,1)}, f32[8,128,384]{2,1,0:T(8,128)}, f32[8,1,384]{2,1,0:T(1,128)}) custom-call(s32[8]{0:T(128)} %get-tuple-element.131.base_ref, s32[8]{0:T(128)} %get-tuple-element.132.count_ref, s32[6]{0:T(128)} %pad_add_fusion.1.units_ref, bf16[2048,384]{1,0:T(8,128)(2,1)} %get-tuple-element.164.q_ref.k_ref.v_ref, ...), custom_call_target="tpu_custom_call" | custom-call | flops 3221225472 | bytes 8388608 | tf_op jit(solution)/shard_map/attend/pallas_call | solution.py:280
  103.4 4.2 %all-to-all-start.1 = ((bf16[8,256,128]{2,1,0:T(8,128)(2,1)}), bf16[8,256,128]{2,1,0:T(8,128)(2,1)S(1)}, u32[]{:S(2)}, u32[]{:S(2)}) async-start(bf16[8,256,128]{2,1,0:T(8,128)(2,1)} %get-tuple-element.173), calls=%async_computation.1 | async-start | bytes 1048576 | tf_op jit(solution)/shard_map/all_to_all | solution.py:927
  111.4 11.4 %all-to-all-done.1.att_ref = bf16[8,256,128]{2,1,0:T(8,128)(2,1)S(1)} async-done(((bf16[8,256,128]{2,1,0:T(8,128)(2,1)}), bf16[8,256,128]{2,1,0:T(8,128)(2,1)S(1)}, u32[]{:S(2)}, u32[]{:S(2)}) %all-to-all-start.1) | async-done | bytes 524320 | tf_op jit(solution)/shard_map/all_to_all | solution.py:927
  123.6 10.3 %middle_stage.1 = (bf16[256,768]{1,0:T(8,128)(2,1)}, bf16[8,256,128]{2,1,0:T(8,128)(2,1)}, f32[256,768]{1,0:T(8,128)}, bf16[256,768]{1,0:T(8,128)(2,1)}, bf16[25...) custom-call(s32[4]{0:T(128)} %pad_add_fusion.place_ref, ...), custom_call_target="tpu_custom_call" | custom-call | flops 4982833152 | bytes 10485760 | tf_op jit(solution)/shard_map/middle_stage/pallas_call | solution.py:505
  133.9 4.7 %gone_grads.1 = (bf16[2,192,2176]{2,1,0:T(8,128)(2,1)}, bf16[2,192,2048]{2,1,0:T(8,128)(2,1)}) custom-call(s32[5]{0:T(128)} %stack.119.sides_ref, bf16[256,768]{1,0:T(8,128)(2,1)} %get-tuple-element.189.refs_0_, bf16[256,768]{1,0:T(8,128)(2,1)} %get-tuple-element.190.refs_1_, bf16[256,768]{1,0:T(8,128)(2,1)} %get-tuple-element.191.refs_2_, ...), custom_call_target="tpu_custom_call" | custom-call | flops 830472192 | bytes 9732096 | tf_op jit(solution)/shard_map/gone_grads/pallas_call | solution.py:661
  139.2 3.6 %all-to-all-start.2 = ((bf16[8,256,128]{2,1,0:T(8,128)(2,1)}), bf16[8,256,128]{2,1,0:T(8,128)(2,1)S(1)}, u32[]{:S(2)}, u32[]{:S(2)}) async-start(bf16[8,256,128]{2,1,0:T(8,128)(2,1)} %get-tuple-element.188), calls=%async_computation.2 | async-start | bytes 1048576 | tf_op jit(solution)/shard_map/all_to_all | solution.py:948
  146.0 10.0 %kept_grads.1 = (bf16[1,192,2176]{2,1,0:T(8,128)(2,1)}, bf16[1,192,2176]{2,1,0:T(8,128)(2,1)}, bf16[8,24,2048]{2,1,0:T(8,128)(2,1)}, bf16[8,24,2048]{2,1,0:T(8,128)(2,1)}) custom-call(s32[5]{0:T(128)} %stack.119.sides_ref, bf16[256,768]{1,0:T(8,128)(2,1)} %get-tuple-element.189.refs_0_, bf16[256,768]{1,0:T(8,128)(2,1)} %get-tuple-element.190.refs_1_, ...), custom_call_target="tpu_custom_call" | custom-call | flops 830472192 | bytes 9732096 | tf_op jit(solution)/shard_map/kept_grads/pallas_call | solution.py:661
  155.9 4.5 %collective-permute-done.26 = bf16[4,24,2304]{2,1,0:T(8,128)(2,1)S(1)} collective-permute-done((bf16[4,24,2304]{2,1,0:T(8,128)(2,1)S(1)}, bf16[4,24,2304]{2,1,0:T(8,128)(2,1)S(1)}, u32[]{:S(2)}, u32[]{:S(2)}) %collective-permute-start.26) | collective-permute-done | bytes 442400 | tf_op jit(solution)/shard_map/ppermute | solution.py:930
  163.3 22.2 %attend_back.1.right_ref = bf16[8,256,384]{2,1,0:T(8,128)(2,1)} custom-call(s32[8]{0:T(128)} %get-tuple-element.131.base_ref, s32[8]{0:T(128)} %get-tuple-element.132.count_ref, s32[6]{0:T(128)} %pad_add_fusion.1.units_ref, bf16[2048,384]{1,0:T(8,128)(2,1)} %get-tuple-element.164.q_ref.k_ref.v_ref, bf16[2048,384]{1,0:T(8,128)(2,1)} %get-tuple-element.164.q_ref.k_ref.v_ref, ...), custom_call_target="tpu_custom_call" | custom-call | flops 8053063680 | bytes 12582912 | tf_op jit(solution)/shard_map/attend_back/pallas_call | solution.py:374
  185.5 5.6 %all-to-all-start.3 = ((bf16[8,256,384]{2,1,0:T(8,128)(2,1)}), bf16[8,256,384]{2,1,0:T(8,128)(2,1)S(1)}, u32[]{:S(2)}, u32[]{:S(2)}) async-start(bf16[8,256,384]{2,1,0:T(8,128)(2,1)} %attend_back.1.right_ref), calls=%async_computation.3 | async-start | bytes 3145728 | tf_op jit(solution)/shard_map/all_to_all | solution.py:985
  191.4 3.5 %add_halves.4 = (bf16[4,24,2176]{2,1,0:T(8,128)(2,1)}, bf16[4,24,2176]{2,1,0:T(8,128)(2,1)}, bf16[1,96,2048]{2,1,0:T(8,128)(2,1)}, bf16[1,96,2048]{2,1,0:T(8,128)(2,1)}) custom-call(s32[5]{0:T(128)} %stack.119.sides_ref, bf16[4,2,24,2176]{3,2,1,0:T(8,128)(2,1)} %bitcast.138, bf16[4,2,24,2176]{3,2,1,0:T(8,128)(2,1)} %bitcast.139, ...), custom_call_target="tpu_custom_call" | custom-call | flops 1622016 | bytes 4866048 | tf_op jit(solution)/shard_map/add_halves/pallas_call | solution.py:747
  198.6 6.5 %head_grads.1 = (bf16[2,192,384]{2,1,0:T(8,128)(2,1)}, bf16[2,192,384]{2,1,0:T(8,128)(2,1)}) custom-call(s32[5]{0:T(128)} %stack.119.sides_ref, bf16[2048,768]{1,0:T(8,128)(2,1)} %get-tuple-element.220.left_ref, bf16[8,256,384]{2,1,0:T(8,128)(2,1)} %attend_back.1.right_ref), custom_call_target="tpu_custom_call" | custom-call | flops 1207959552 | bytes 4718592 | tf_op jit(solution)/shard_map/head_grads/pallas_call | solution.py:698
  205.2 13.8 %collective-permute-done.30 = bf16[1,96,2048]{2,1,0:T(8,128)(2,1)S(1)} collective-permute-done((bf16[1,96,2048]{2,1,0:T(8,128)(2,1)}, bf16[1,96,2048]{2,1,0:T(8,128)(2,1)S(1)}, u32[]{:S(2)}, u32[]{:S(2)}) %collective-permute-start.30) | collective-permute-done | bytes 393248 | tf_op jit(solution)/shard_map/ppermute | solution.py:994
  219.9 2.4 add_halves.5
  226.2 8.9 %collective-permute-done.31 = bf16[2,24,4224]{2,1,0:T(8,128)(2,1)S(1)} collective-permute-done((bf16[2,24,4224]{2,1,0:T(8,128)(2,1)}, bf16[2,24,4224]{2,1,0:T(8,128)(2,1)S(1)}, u32[]{:S(2)}, u32[]{:S(2)}) %collective-permute-start.31) | collective-permute-done | bytes 405536 | tf_op jit(solution)/shard_map/ppermute | solution.py:1005
  242.5 4.7 %settle.1.w_ref = bf16[768,2304]{1,0:T(8,128)(2,1)} custom-call(s32[4]{0:T(128)} %pad_add_fusion.place_ref, bf16[4,48,2304]{2,1,0:T(8,128)(2,1)} %copy-done.1, bf16[4,48,2304]{2,1,0:T(8,128)(2,1)} %copy-done.4, bf16[4,48,2304]{2,1,0:T(8,128)(2,1)} %copy-done.5, bf16[4,48,2304]{2,1,0:T(8,128)(2,1)} %copy-done.6), custom_call_target="tpu_custom_call" | custom-call | bytes 8388608 | tf_op jit(solution)/shard_map/settle/pallas_call | solution.py:543
  247.2 2.1 collective-permute-done.34
  251.6 3.5 %all-to-all-start.4 = ((bf16[8,24,384]{2,1,0:T(8,128)(2,1)}), bf16[8,24,384]{2,1,0:T(8,128)(2,1)S(1)}, u32[]{:S(2)}, u32[]{:S(2)}) async-start(bf16[8,24,384]{2,1,0:T(8,128)(2,1)} %bitcast.44), calls=%async_computation.4 | async-start | bytes 294912 | tf_op jit(solution)/shard_map/all_to_all | solution.py:1026
  255.2 5.3 %finish.1 = bf16[256,768]{1,0:T(8,128)(2,1)} custom-call(bf16[8,256,384]{2,1,0:T(8,128)(2,1)} %copy-done, bf16[256,768]{1,0:T(8,128)(2,1)} %bitcast.133, f32[8,768]{1,0:T(8,128)} %get-tuple-element.141.gains_ref.gain_ref, f32[256,768]{1,0:T(8,128)} %get-tuple-element.242.grad_ref, bf16[768,2304]{1,0:T(8,128)(2,1)} %settle.1.w_ref), custom_call_target="tpu_custom_call" | custom-call | flops 905969664 | bytes 6291456 | tf_op jit(solution)/shard_map/finish/pallas_call | solution.py:568
  (195 shorter events, 63.1 us)
Async XLA Ops:
  0.6 21.6 %collective-permute-start.1 = (bf16[256,768]{1,0:T(8,128)(2,1)}, bf16[256,768]{1,0:T(8,128)(2,1)S(1)}, u32[]{:S(2)}, u32[]{:S(2)}) collective-permute-start(bf16[256,768]{1,0:T(8,128)(2,1)} %bitcast.129), channel_id=1, source_target_pairs={{0,1},{1,0},{2,3},{3,2},{4,5},{5,4},{6,7},{7,6},{8,9},{9,8},{10,11... | collective-permute-start | bytes 1179656 | tf_op jit(solution)/shard_map/ppermute | solution.py:847
  3.6 18.6 %collective-permute-start = (bf16[256,768]{1,0:T(8,128)(2,1)}, bf16[256,768]{1,0:T(8,128)(2,1)S(1)}, u32[]{:S(2)}, u32[]{:S(2)}) collective-permute-start(bf16[256,768]{1,0:T(8,128)(2,1)} %bitcast.130), channel_id=1, source_target_pairs={{0,2},{1,3},{2,4},{3,5},{4,6},{5,7},{6,0},{7,1},{8,10},{9,11},{10,... | collective-permute-start | bytes 1179656 | tf_op jit(solution)/shard_map/ppermute | solution.py:846
  6.2 16.0 %collective-permute-start.2 = (bf16[2,24,2176]{2,1,0:T(8,128)(2,1)S(1)}, bf16[2,24,2176]{2,1,0:T(8,128)(2,1)S(1)}, u32[]{:S(2)}, u32[]{:S(2)}) collective-permute-start(bf16[2,24,2176]{2,1,0:T(8,128)(2,1)S(1)} %pad_maximum_fusion.6), channel_id=1, source_target_pairs={{0,2},{1,3},{2,4},{3,5},{4,6},{5,7},{6,0},{7,1},{8,10},{9,11},{10,... | collective-permute-start | bytes 626696 | tf_op jit(solution)/shard_map/ppermute | solution.py:848
  9.6 16.8 %all-to-all-start = ((bf16[8,32,512]{2,1,0:T(8,128)(2,1)}), bf16[8,32,512]{2,1,0:T(8,128)(2,1)S(1)}, u32[]{:S(2)}, u32[]{:S(2)}) async-start(bf16[8,32,512]{2,1,0:T(8,128)(2,1)} %spread.1), calls=%async_computation | async-start | bytes 524288 | tf_op jit(solution)/shard_map/all_to_all | solution.py:839
  26.5 12.3 %collective-permute-start.5 = (bf16[2,24,2176]{2,1,0:T(8,128)(2,1)S(1)}, bf16[2,24,2176]{2,1,0:T(8,128)(2,1)S(1)}, u32[]{:S(2)}, u32[]{:S(2)}) collective-permute-start(bf16[2,24,2176]{2,1,0:T(8,128)(2,1)S(1)} %collective-permute-done.2), channel_id=1, source_target_pairs={{0,2},{1,3},{2,4},{3,5},{4,6},{5,7},{6,0},{7,1},{8,10},{9,11},{10,... | collective-permute-start | bytes 626696 | tf_op jit(solution)/shard_map/ppermute | solution.py:862
  26.5 12.2 %collective-permute-start.4 = (bf16[256,768]{1,0:T(8,128)(2,1)S(1)}, bf16[256,768]{1,0:T(8,128)(2,1)S(1)}, u32[]{:S(2)}, u32[]{:S(2)}) collective-permute-start(bf16[256,768]{1,0:T(8,128)(2,1)S(1)} %collective-permute-done.own_ref), channel_id=1, source_target_pairs={{0,1},{1,0},{2,3},{3,2},{4,5},{5,4},{6,7},{7,6},{8,9},{9,8},{10,11... | collective-permute-start | bytes 1179656 | tf_op jit(solution)/shard_map/ppermute | solution.py:861
  27.5 16.4 %collective-permute-start.3 = (bf16[256,768]{1,0:T(8,128)(2,1)S(1)}, bf16[256,768]{1,0:T(8,128)(2,1)S(1)}, u32[]{:S(2)}, u32[]{:S(2)}) collective-permute-start(bf16[256,768]{1,0:T(8,128)(2,1)S(1)} %collective-permute-done.own_ref), channel_id=1, source_target_pairs={{0,2},{1,3},{2,4},{3,5},{4,6},{5,7},{6,0},{7,1},{8,10},{9,11},{10,... | collective-permute-start | bytes 1179656 | tf_op jit(solution)/shard_map/ppermute | solution.py:860
  45.1 21.7 %collective-permute-start.9 = (bf16[256,768]{1,0:T(8,128)(2,1)S(1)}, bf16[256,768]{1,0:T(8,128)(2,1)S(1)}, u32[]{:S(2)}, u32[]{:S(2)}) collective-permute-start(bf16[256,768]{1,0:T(8,128)(2,1)S(1)} %collective-permute-done.3.own_ref), channel_id=1, source_target_pairs={{0,1},{1,0},{2,3},{3,2},{4,5},{5,4},{6,7},{7,6},{8,9},{9,8},{10,11... | collective-permute-start | bytes 1179656 | tf_op jit(solution)/shard_map/ppermute | solution.py:880
  45.9 21.0 %collective-permute-start.8 = (bf16[256,768]{1,0:T(8,128)(2,1)S(1)}, bf16[256,768]{1,0:T(8,128)(2,1)S(1)}, u32[]{:S(2)}, u32[]{:S(2)}) collective-permute-start(bf16[256,768]{1,0:T(8,128)(2,1)S(1)} %collective-permute-done.3.own_ref), channel_id=1, source_target_pairs={{0,2},{1,3},{2,4},{3,5},{4,6},{5,7},{6,0},{7,1},{8,10},{9,11},{10,... | collective-permute-start | bytes 1179656 | tf_op jit(solution)/shard_map/ppermute | solution.py:879
  45.9 16.1 %collective-permute-start.10 = (bf16[2,24,2176]{2,1,0:T(8,128)(2,1)S(1)}, bf16[2,24,2176]{2,1,0:T(8,128)(2,1)S(1)}, u32[]{:S(2)}, u32[]{:S(2)}) collective-permute-start(bf16[2,24,2176]{2,1,0:T(8,128)(2,1)S(1)} %collective-permute-done.5), channel_id=1, source_target_pairs={{0,2},{1,3},{2,4},{3,5},{4,6},{5,7},{6,0},{7,1},{8,10},{9,11},{10,... | collective-permute-start | bytes 626696 | tf_op jit(solution)/shard_map/ppermute | solution.py:881
  45.9 18.3 %collective-permute-start.11 = (bf16[2,24,2176]{2,1,0:T(8,128)(2,1)S(1)}, bf16[2,24,2176]{2,1,0:T(8,128)(2,1)S(1)}, u32[]{:S(2)}, u32[]{:S(2)}) collective-permute-start(bf16[2,24,2176]{2,1,0:T(8,128)(2,1)S(1)} %get-tuple-element.136), channel_id=1, source_target_pairs={{0,1},{1,0},{2,3},{3,2},{4,5},{5,4},{6,7},{7,6},{8,9},{9,8},{10,11... | collective-permute-start | bytes 626696 | tf_op jit(solution)/shard_map/ppermute | solution.py:882
  47.2 17.8 %collective-permute-start.12 = (bf16[2,24,2176]{2,1,0:T(8,128)(2,1)S(1)}, bf16[2,24,2176]{2,1,0:T(8,128)(2,1)S(1)}, u32[]{:S(2)}, u32[]{:S(2)}) collective-permute-start(bf16[2,24,2176]{2,1,0:T(8,128)(2,1)S(1)} %get-tuple-element.137), channel_id=1, source_target_pairs={{0,16},{8,24},{16,0},{24,8},{1,17},{9,25},{17,1},{25,9},{2,18},{10... | collective-permute-start | bytes 626696 | tf_op jit(solution)/shard_map/ppermute | solution.py:883
  64.3 10.2 %collective-permute-start.17 = (bf16[24,2304]{1,0:T(8,128)(2,1)S(1)}, bf16[24,2304]{1,0:T(8,128)(2,1)S(1)}, u32[]{:S(2)}, u32[]{:S(2)}) collective-permute-start(bf16[24,2304]{1,0:T(8,128)(2,1)S(1)} %copy-done.3), channel_id=1, source_target_pairs={{0,4},{1,5},{2,6},{3,7},{4,0},{5,1},{6,2},{7,3},{8,12},{9,13},{10,... | collective-permute-start | bytes 331784 | tf_op jit(solution)/shard_map/ppermute | solution.py:894
  64.9 9.6 %collective-permute-start.16 = (bf16[24,2304]{1,0:T(8,128)(2,1)S(1)}, bf16[24,2304]{1,0:T(8,128)(2,1)S(1)}, u32[]{:S(2)}, u32[]{:S(2)}) collective-permute-start(bf16[24,2304]{1,0:T(8,128)(2,1)S(1)} %copy-done.3), channel_id=1, source_target_pairs={{0,2},{1,3},{2,4},{3,5},{4,6},{5,7},{6,0},{7,1},{8,10},{9,11},{10,... | collective-permute-start | bytes 331784 | tf_op jit(solution)/shard_map/ppermute | solution.py:894
  67.0 8.2 %collective-permute-start.14 = (bf16[2,24,2176]{2,1,0:T(8,128)(2,1)S(1)}, bf16[2,24,2176]{2,1,0:T(8,128)(2,1)S(1)}, u32[]{:S(2)}, u32[]{:S(2)}) collective-permute-start(bf16[2,24,2176]{2,1,0:T(8,128)(2,1)S(1)} %pad_maximum_fusion.8), channel_id=1, source_target_pairs={{0,1},{1,0},{2,3},{3,2},{4,5},{5,4},{6,7},{7,6},{8,9},{9,8},{10,11... | collective-permute-start | bytes 626696 | tf_op jit(solution)/shard_map/ppermute | solution.py:892
  68.4 11.9 %collective-permute-start.13 = (bf16[256,768]{1,0:T(8,128)(2,1)S(1)}, bf16[256,768]{1,0:T(8,128)(2,1)S(1)}, u32[]{:S(2)}, u32[]{:S(2)}) collective-permute-start(bf16[256,768]{1,0:T(8,128)(2,1)S(1)} %collective-permute-done.8.own_ref), channel_id=1, source_target_pairs={{0,1},{1,0},{2,3},{3,2},{4,5},{5,4},{6,7},{7,6},{8,9},{9,8},{10,11... | collective-permute-start | bytes 1179656 | tf_op jit(solution)/shard_map/ppermute | solution.py:889
  80.5 21.5 %collective-permute-start.19 = (bf16[4,48,2176]{2,1,0:T(8,128)(2,1)S(1)}, bf16[4,48,2176]{2,1,0:T(8,128)(2,1)S(1)}, u32[]{:S(2)}, u32[]{:S(2)}) collective-permute-start(bf16[4,48,2176]{2,1,0:T(8,128)(2,1)S(1)} %maximum_maximum_fusion.refs_0_), channel_id=1, source_target_pairs={{0,16},{8,24},{16,0},{24,8},{1,17},{9,25},{17,1},{25,9},{2,18},{10... | collective-permute-start | bytes 2506760 | tf_op jit(solution)/shard_map/ppermute | solution.py:900
  80.6 21.4 %collective-permute-start.20 = (bf16[8,24,2176]{2,1,0:T(8,128)(2,1)S(1)}, bf16[8,24,2176]{2,1,0:T(8,128)(2,1)S(1)}, u32[]{:S(2)}, u32[]{:S(2)}) collective-permute-start(bf16[8,24,2176]{2,1,0:T(8,128)(2,1)S(1)} %constant_dynamic-update-slice_fusion), channel_id=1, source_target_pairs={{0,1},{1,0},{2,3},{3,2},{4,5},{5,4},{6,7},{7,6},{8,9},{9,8},{10,11... | collective-permute-start | bytes 2506760 | tf_op jit(solution)/shard_map/ppermute | solution.py:901
  103.4 19.3 %collective-permute-start.23 = (bf16[8,48,2176]{2,1,0:T(8,128)(2,1)}, bf16[8,48,2176]{2,1,0:T(8,128)(2,1)}, u32[]{:S(2)}, u32[]{:S(2)}) collective-permute-start(bf16[8,48,2176]{2,1,0:T(8,128)(2,1)} %pad_maximum_fusion.refs_4_), channel_id=1, source_target_pairs={{0,8},{8,0},{16,24},{24,16},{1,9},{9,1},{17,25},{25,17},{2,10},{10... | collective-permute-start | bytes 5013512 | tf_op jit(solution)/shard_map/ppermute | solution.py:921
  103.4 19.3 %all-to-all-start.1 = ((bf16[8,256,128]{2,1,0:T(8,128)(2,1)}), bf16[8,256,128]{2,1,0:T(8,128)(2,1)S(1)}, u32[]{:S(2)}, u32[]{:S(2)}) async-start(bf16[8,256,128]{2,1,0:T(8,128)(2,1)} %get-tuple-element.173), calls=%async_computation.1 | async-start | bytes 1048576 | tf_op jit(solution)/shard_map/all_to_all | solution.py:927
  139.2 21.3 %all-to-all-start.2 = ((bf16[8,256,128]{2,1,0:T(8,128)(2,1)}), bf16[8,256,128]{2,1,0:T(8,128)(2,1)S(1)}, u32[]{:S(2)}, u32[]{:S(2)}) async-start(bf16[8,256,128]{2,1,0:T(8,128)(2,1)} %get-tuple-element.188), calls=%async_computation.2 | async-start | bytes 1048576 | tf_op jit(solution)/shard_map/all_to_all | solution.py:948
  142.8 17.7 %collective-permute-start.26 = (bf16[4,24,2304]{2,1,0:T(8,128)(2,1)S(1)}, bf16[4,24,2304]{2,1,0:T(8,128)(2,1)S(1)}, u32[]{:S(2)}, u32[]{:S(2)}) collective-permute-start(bf16[4,24,2304]{2,1,0:T(8,128)(2,1)S(1)} %pad_maximum_fusion.3), channel_id=1, source_target_pairs={{0,1},{1,0},{2,3},{3,2},{4,5},{5,4},{6,7},{7,6},{8,9},{9,8},{10,11... | collective-permute-start | bytes 1327112 | tf_op jit(solution)/shard_map/ppermute | solution.py:930
  161.2 24.3 %collective-permute-start.27 = (bf16[1,192,2176]{2,1,0:T(8,128)(2,1)}, bf16[1,192,2176]{2,1,0:T(8,128)(2,1)S(1)}, u32[]{:S(2)}, u32[]{:S(2)}) collective-permute-start(bf16[1,192,2176]{2,1,0:T(8,128)(2,1)} %get-tuple-element.205), channel_id=1, source_target_pairs={{0,16},{8,24},{16,0},{24,8},{1,17},{9,25},{17,1},{25,9},{2,18},{10... | collective-permute-start | bytes 2506760 | tf_op jit(solution)/shard_map/ppermute | solution.py:964
  162.7 22.8 %collective-permute-start.28 = (bf16[8,24,2048]{2,1,0:T(8,128)(2,1)}, bf16[8,24,2048]{2,1,0:T(8,128)(2,1)}, u32[]{:S(2)}, u32[]{:S(2)}) collective-permute-start(bf16[8,24,2048]{2,1,0:T(8,128)(2,1)} %get-tuple-element.207), channel_id=1, source_target_pairs={{0,1},{1,0},{2,3},{3,2},{4,5},{5,4},{6,7},{7,6},{8,9},{9,8},{10,11... | collective-permute-start | bytes 2359304 | tf_op jit(solution)/shard_map/ppermute | solution.py:965
  185.5 63.8 %all-to-all-start.3 = ((bf16[8,256,384]{2,1,0:T(8,128)(2,1)}), bf16[8,256,384]{2,1,0:T(8,128)(2,1)S(1)}, u32[]{:S(2)}, u32[]{:S(2)}) async-start(bf16[8,256,384]{2,1,0:T(8,128)(2,1)} %attend_back.1.right_ref), calls=%async_computation.3 | async-start | bytes 3145728 | tf_op jit(solution)/shard_map/all_to_all | solution.py:985
  191.3 33.3 %collective-permute-start.33 = (bf16[4,48,2304]{2,1,0:T(8,128)(2,1)S(1)}, bf16[4,48,2304]{2,1,0:T(8,128)(2,1)S(1)}, u32[]{:S(2)}, u32[]{:S(2)}) collective-permute-start(bf16[4,48,2304]{2,1,0:T(8,128)(2,1)S(1)} %pad_maximum_fusion.1.refs_0_), channel_id=1, source_target_pairs={{0,16},{8,24},{16,0},{24,8},{1,17},{9,25},{17,1},{25,9},{2,18},{10... | collective-permute-start | bytes 2654216 | tf_op jit(solution)/shard_map/ppermute | solution.py:984
  194.9 24.1 %collective-permute-start.29 = (bf16[4,24,2176]{2,1,0:T(8,128)(2,1)}, bf16[4,24,2176]{2,1,0:T(8,128)(2,1)S(1)}, u32[]{:S(2)}, u32[]{:S(2)}) collective-permute-start(bf16[4,24,2176]{2,1,0:T(8,128)(2,1)} %get-tuple-element.216), channel_id=1, source_target_pairs={{0,1},{1,0},{2,3},{3,2},{4,5},{5,4},{6,7},{7,6},{8,9},{9,8},{10,11... | collective-permute-start | bytes 1253384 | tf_op jit(solution)/shard_map/ppermute | solution.py:993
  196.9 22.1 %collective-permute-start.30 = (bf16[1,96,2048]{2,1,0:T(8,128)(2,1)}, bf16[1,96,2048]{2,1,0:T(8,128)(2,1)S(1)}, u32[]{:S(2)}, u32[]{:S(2)}) collective-permute-start(bf16[1,96,2048]{2,1,0:T(8,128)(2,1)} %get-tuple-element.218), channel_id=1, source_target_pairs={{0,16},{8,24},{16,0},{24,8},{1,17},{9,25},{17,1},{25,9},{2,18},{10... | collective-permute-start | bytes 1179656 | tf_op jit(solution)/shard_map/ppermute | solution.py:994
  222.4 12.8 %collective-permute-start.31 = (bf16[2,24,4224]{2,1,0:T(8,128)(2,1)}, bf16[2,24,4224]{2,1,0:T(8,128)(2,1)S(1)}, u32[]{:S(2)}, u32[]{:S(2)}) collective-permute-start(bf16[2,24,4224]{2,1,0:T(8,128)(2,1)} %get-tuple-element.228), channel_id=1, source_target_pairs={{0,2},{1,3},{2,0},{3,1},{4,6},{5,7},{6,4},{7,5},{8,10},{9,11},{10,... | collective-permute-start | bytes 1216520 | tf_op jit(solution)/shard_map/ppermute | solution.py:1005
  224.1 16.5 %collective-permute-start.36 = (bf16[4,48,2304]{2,1,0:T(8,128)(2,1)S(1)}, bf16[4,48,2304]{2,1,0:T(8,128)(2,1)S(1)}, u32[]{:S(2)}, u32[]{:S(2)}) collective-permute-start(bf16[4,48,2304]{2,1,0:T(8,128)(2,1)S(1)} %pad_maximum_fusion.1.refs_0_), channel_id=1, source_target_pairs={{0,8},{8,0},{16,24},{24,16},{1,9},{9,1},{17,25},{25,17},{2,10},{10... | collective-permute-start | bytes 2654216 | tf_op jit(solution)/shard_map/ppermute | solution.py:1012
  237.9 11.5 %collective-permute-start.34 = (bf16[1,24,4224]{2,1,0:T(8,128)(2,1)}, bf16[1,24,4224]{2,1,0:T(8,128)(2,1)S(1)}, u32[]{:S(2)}, u32[]{:S(2)}) collective-permute-start(bf16[1,24,4224]{2,1,0:T(8,128)(2,1)} %get-tuple-element.235), channel_id=1, source_target_pairs={{0,4},{1,5},{2,6},{3,7},{4,0},{5,1},{6,2},{7,3},{8,12},{9,13},{10,... | collective-permute-start | bytes 608264 | tf_op jit(solution)/shard_map/ppermute | solution.py:1009
  251.6 11.0 %all-to-all-start.4 = ((bf16[8,24,384]{2,1,0:T(8,128)(2,1)}), bf16[8,24,384]{2,1,0:T(8,128)(2,1)S(1)}, u32[]{:S(2)}, u32[]{:S(2)}) async-start(bf16[8,24,384]{2,1,0:T(8,128)(2,1)} %bitcast.44), calls=%async_computation.4 | async-start | bytes 294912 | tf_op jit(solution)/shard_map/all_to_all | solution.py:1026
  (44 other events, 287.9 us)

commit v4 on v3

--- a/solution.py
+++ b/solution.py
@@ -11,6 +11,7 @@
 HD = 64
 SLOTS = 2
 LANES = SLOTS * HD
+UNITS = 3
 GRAIN = 128
 KEY_TILE = 512
 CHUNK = 384
@@ -219,6 +220,46 @@
         acc_ref[pl.ds(start, part), :] += jnp.where(lane // HD == units_ref[i], chunk, 0.0)
 
 
+def pack_units(units_ref, acc_ref, part):
+    half = part // 2
+
+    def slab(unit, start, size, want):
+        values = acc_ref[pl.ds(start, size), :]
+        here = jnp.full(values.shape, units_ref[unit], jnp.int32) == want
+        return jnp.where(here, values, pltpu.roll(values, HD, 1))
+
+    def beside(left, right):
+        left_side = lax.broadcasted_iota(jnp.int32, left.shape, 1) < HD
+        return jnp.where(left_side, left, right)
+
+    starts = [pl.multiple_of(units_ref[UNITS + unit] * part, part) for unit in range(UNITS)]
+    top = beside(slab(0, starts[0], part, 0), slab(1, starts[1], part, 1))
+    low = beside(slab(2, starts[2], half, 0), slab(2, starts[2] + half, half, 1))
+    return jnp.concatenate([top, low], axis=0)
+
+
+def unpack_units(units_ref, packed, part):
+    half = part // 2
+    values = packed.astype(f32)
+    turned = pltpu.roll(values, HD, 1)
+    side = lax.broadcasted_iota(jnp.int32, values.shape, 1) // HD
+
+    def piece(unit, home, start, size):
+        slot = jnp.full(values.shape, units_ref[unit], jnp.int32)
+        chosen = jnp.where(slot == home, values, turned)
+        return jnp.where(side == slot, chosen, 0.0)[start : start + size]
+
+    return jnp.concatenate(
+        [
+            piece(0, 0, 0, part),
+            piece(1, 1, 0, part),
+            piece(2, 0, part, half),
+            piece(2, 1, part, half),
+        ],
+        axis=0,
+    ).astype(bf16)
+
+
 def across(slab, wide):
     if wide <= LANES:
         return slab[:, :wide]
@@ -269,7 +310,7 @@
     att_ref[0] = att
     lse_ref[0] = top + jnp.log(total)
     scatter_rows(units_ref, acc_ref, jnp.transpose(att), units, part)
-    low_ref[0] = acc_ref[...].astype(bf16)
+    low_ref[0] = pack_units(units_ref, acc_ref, part).astype(bf16)
 
 
 def attend(base, tiles, unit_places, qkv, turned, doc_slab, doc_q, rows, tile):
@@ -290,14 +331,14 @@
                 pl.BlockSpec((1, 1, wide), lambda i, *s: (i, 0, 0)),
             ],
             out_specs=[
-                pl.BlockSpec((1, rows, LANES), lambda i, *s: (i, 0, 0)),
+                pl.BlockSpec((1, wide // 2, LANES), lambda i, *s: (i, 0, 0)),
                 pl.BlockSpec((1, LANES, wide), lambda i, *s: (i, 0, 0)),
                 pl.BlockSpec((1, 1, wide), lambda i, *s: (i, 0, 0)),
             ],
             scratch_shapes=[pltpu.VMEM((total, wide), f32), pltpu.VMEM((rows, LANES), f32)],
         ),
         out_shape=[
-            jax.ShapeDtypeStruct((count, rows, LANES), bf16),
+            jax.ShapeDtypeStruct((count, wide // 2, LANES), bf16),
             jax.ShapeDtypeStruct((count, LANES, wide), f32),
             jax.ShapeDtypeStruct((count, 1, wide), f32),
         ],
@@ -313,7 +354,7 @@
 
 def attend_back_kernel(units, tile, base_ref, count_ref, units_ref, q_ref, k_ref, v_ref, kt_ref, doc_ref,
                        doc_q_ref, grad_ref, att_ref, lse_ref, cos_ref, sin_ref,
-                       out_ref, dk_ref, dv_ref, acc_ref):
+                       out_ref, send_ref, dk_ref, dv_ref, acc_ref):
     block = pl.program_id(0)
     count = pl.num_programs(0)
     rows = acc_ref.shape[0]
@@ -329,7 +370,7 @@
         return values * cos_ref[span, :] - rotate_half(values * sin_ref[span, :])
 
     queries = gather_rows(units_ref, q_ref, units, part)
-    grads = gather_rows(units_ref, grad_ref.at[0], units, part)
+    grads = unpack_units(units_ref, grad_ref[0], part)
     delta = jnp.sum(jnp.transpose(grads.astype(f32)) * att_ref[0], axis=0, keepdims=True)
     log_sum = lse_ref[0]
     doc_q = doc_q_ref[0]
@@ -350,14 +391,21 @@
     )
     scatter_rows(units_ref, acc_ref, jnp.transpose(grad_query) * HD**-0.5, units, part)
     here = pl.ds(pl.multiple_of(block * rows, rows), rows)
-    out_ref[block, :, :LANES] = turn_back(acc_ref[...], here).astype(bf16)
+    turned = turn_back(acc_ref[...], here)
+    out_ref[block, :, :LANES] = turned.astype(bf16)
+    acc_ref[...] = turned
+    send_ref[block, : wide // 2, :] = pack_units(units_ref, acc_ref, part).astype(bf16)
 
     @pl.when(block == count - 1)
     def _():
         def finish(at, carry):
             span = pl.ds(pl.multiple_of(at * rows, rows), rows)
-            out_ref[at, :, LANES : 2 * LANES] = turn_back(dk_ref[span, :], span).astype(bf16)
-            out_ref[at, :, 2 * LANES :] = dv_ref[span, :].astype(bf16)
+            keys = turn_back(dk_ref[span, :], span).astype(bf16)
+            values = dv_ref[span, :].astype(bf16)
+            out_ref[at, :, LANES : 2 * LANES] = keys
+            out_ref[at, :, 2 * LANES :] = values
+            send_ref[at, wide // 2 : wide // 2 + rows, :] = keys
+            send_ref[at, wide // 2 + rows :, :] = values
             return carry
 
         lax.fori_loop(0, count, finish, 0)
@@ -383,20 +431,26 @@
                 pl.BlockSpec((LANES, total), lambda i, *s: (0, 0)),
                 whole(0),
                 each(1, wide),
-                each(rows, LANES),
+                each(wide // 2, LANES),
                 each(LANES, wide),
                 each(1, wide),
                 whole(0),
                 whole(0),
             ],
-            out_specs=pl.BlockSpec((count, rows, 3 * LANES), lambda i, *s: (0, 0, 0)),
+            out_specs=[
+                pl.BlockSpec((count, rows, 3 * LANES), lambda i, *s: (0, 0, 0)),
+                pl.BlockSpec((count, wide // 2 + 2 * rows, LANES), lambda i, *s: (0, 0, 0)),
+            ],
             scratch_shapes=[
                 pltpu.VMEM((total, LANES), f32),
                 pltpu.VMEM((total, LANES), f32),
                 pltpu.VMEM((rows, LANES), f32),
             ],
         ),
-        out_shape=jax.ShapeDtypeStruct((count, rows, 3 * LANES), bf16),
+        out_shape=[
+            jax.ShapeDtypeStruct((count, rows, 3 * LANES), bf16),
+            jax.ShapeDtypeStruct((count, wide // 2 + 2 * rows, LANES), bf16),
+        ],
         compiler_params=params(),
         cost_estimate=pl.CostEstimate(
             flops=10 * count * wide * total * LANES,
@@ -407,51 +461,98 @@
     )(base, tiles, unit_places, qkv, qkv, qkv, turned, doc_slab, doc_q, grads, att, lse, cosine, sine)
 
 
-def join_heads(parts_ref, at, owners):
-    rows = parts_ref.shape[1]
+def lanes_of(slab, at, want):
+    slab = slab.astype(f32)
+    return slab if at == want else pltpu.roll(slab, HD, 1)
+
+
+def beside(left, right):
+    side = lax.broadcasted_iota(jnp.int32, left.shape, 1) // HD
+    return jnp.where(side == 0, left, right).astype(bf16)
+
+
+def join_packed(parts_ref, heads, splits, part):
+    half = part // 2
+    tiles = []
+    for tile in range(heads // SLOTS):
+        blocks = []
+        for piece in range(splits):
+            for low in range(2):
+                sides = []
+                for want in range(SLOTS):
+                    c, unit = divmod((tile * SLOTS + want) * splits + piece, UNITS)
+                    row, at = (low * half, unit) if unit < 2 else (part, low)
+                    sides.append(lanes_of(parts_ref[c, row : row + half, :], at, want))
+                blocks.append(beside(*sides))
+        tiles.append(jnp.concatenate(blocks, axis=0))
+    return jnp.concatenate(tiles, axis=1)
+
+
+def split_packed(values, out_ref, splits, part):
+    half = part // 2
+
+    def slab(unit, low, want):
+        head, piece = divmod(unit, splits)
+        row = piece * part + low * half
+        at = head // SLOTS * LANES
+        return lanes_of(values[row : row + half, at : at + LANES], head % SLOTS, want)
+
+    for c in range(out_ref.shape[0]):
+        unit = UNITS * c
+        for low in range(2):
+            out_ref[c, low * half : (low + 1) * half, :] = beside(
+                slab(unit, low, 0), slab(unit + 1, low, 1)
+            )
+        out_ref[c, part:, :] = beside(slab(unit + 2, 0, 0), slab(unit + 2, 1, 1))
+
+
+def join_heads(parts_ref, at, rows, owners):
     side = lax.broadcasted_iota(jnp.int32, (rows, LANES), 1) // HD
     tiles = []
     for tile in range(len(owners) // SLOTS):
         column = jnp.zeros((rows, LANES), f32)
         for half in range(SLOTS):
             for c, slot in owners[tile * SLOTS + half]:
-                slab = parts_ref[c, :, at : at + LANES].astype(f32)
-                if slot != half:
-                    slab = pltpu.roll(slab, HD, 1)
+                slab = lanes_of(parts_ref[c, at : at + rows, :], slot, half)
                 column = column + jnp.where(side == half, slab, 0.0)
         tiles.append(column.astype(bf16))
     return jnp.concatenate(tiles, axis=1)
 
 
-def fetch_rows(place_ref, metas, refs, target_ref, at, sems):
+def fetch_rows(place_ref, metas, refs, target_ref, at, sems, span=None):
     copies = []
+    begin, end = span or (0, refs[0].shape[2])
     for ref, blocks in zip(refs, metas):
         for index, (flip, back) in enumerate(blocks):
             count = ref.shape[1]
             turn = lax.rem(place_ref[1] + place_ref[2] - back, place_ref[2])
             row = (place_ref[0] ^ flip) * place_ref[3] + turn * count
             row = pl.multiple_of(row, count) if count < target_ref.shape[0] else 0
-            target = target_ref.at[pl.ds(row, count), pl.ds(at, ref.shape[2])]
-            copies.append(pltpu.make_async_copy(ref.at[index], target, sems.at[len(copies)]))
+            target = target_ref.at[pl.ds(row, count), pl.ds(at + begin, end - begin)]
+            source = ref.at[index, :, pl.ds(begin, end - begin)]
+            copies.append(pltpu.make_async_copy(source, target, sems.at[len(copies)]))
             copies[-1].start()
     return copies
 
 
-def middle_kernel(owners, first, metas, cut, place_ref, att_ref, tokens_ref, gain_ref, cot_ref,
+def middle_kernel(heads, splits, metas, cut, place_ref, att_ref, tokens_ref, gain_ref, cot_ref,
                   *refs):
     count = len(metas[0]) + len(metas[1])
     sources = refs[:count]
     (output_ref, grad_heads_ref, grad_middle_ref, attended_ref, branch_ref, hidden_ref,
-     grad_up_ref, product_ref, w_ref, sems_a, sems_b) = refs[count:]
+     grad_up_ref, product_ref, w_ref, sems_a, sems_b, sems_c) = refs[count:]
     width = tokens_ref.shape[1]
     units = product_ref.shape[1]
-    copies_a = fetch_rows(place_ref, metas[0], sources[: len(metas[0])], w_ref, 0, sems_a)
-    copies_b = fetch_rows(place_ref, metas[1], sources[len(metas[0]) :], w_ref, cut, sems_b)
+    fetch = functools.partial(fetch_rows, place_ref)
+    copies_a = fetch(metas[0], sources[: len(metas[0])], w_ref, 0, sems_a, (0, width))
+    copies_b = fetch(metas[0], sources[: len(metas[0])], w_ref, 0, sems_c, (width, cut))
+    copies_b += fetch(metas[1], sources[len(metas[0]) :], w_ref, cut, sems_b)
     up = width
     down = width + 2 * units
     gain = gain_ref[1:2, :]
     cot = cot_ref[...]
-    attended = join_heads(att_ref, 0, owners)
+    part = tokens_ref.shape[0] // splits
+    attended = join_packed(att_ref, heads, splits, part)
     attended_ref[...] = attended
     for copy in copies_a:
         copy.wait()
@@ -492,25 +593,24 @@
     grad_branch = grad_middle.astype(bf16)
     branch_ref[...] = grad_branch
     grad_attended = dot_tt(grad_branch, w_ref[:, :width])
-    for c, head in enumerate(first):
-        grad_heads_ref[c] = grad_attended[:, head * HD : head * HD + LANES].astype(bf16)
-
-
-def middle_stage(owners, first, place, att_in, tokens, gains, cot, parts_a, parts_b, units):
+    split_packed(grad_attended, grad_heads_ref, splits, part)
+
+
+def middle_stage(heads, splits, place, att_in, tokens, gains, cot, parts_a, parts_b, units):
     rows, width = tokens.shape
     arrays = [[array for array, _ in parts] for parts in (parts_a, parts_b)]
     metas = [[blocks for _, blocks in parts] for parts in (parts_a, parts_b)]
     vmem = pl.BlockSpec(memory_space=pltpu.VMEM)
     shape = jax.ShapeDtypeStruct
     return pl.pallas_call(
-        functools.partial(middle_kernel, owners, first, metas, arrays[0][0].shape[-1]),
+        functools.partial(middle_kernel, heads, splits, metas, arrays[0][0].shape[-1]),
         in_specs=[pl.BlockSpec(memory_space=pltpu.SMEM)]
         + [vmem] * 4
         + [pl.BlockSpec(memory_space=pl.ANY)] * (len(arrays[0]) + len(arrays[1])),
         out_specs=[vmem] * 8,
         out_shape=[
             shape((rows, width), bf16),
-            shape((len(first), rows, LANES), bf16),
+            shape(att_in.shape, bf16),
             shape((rows, width), f32),
             shape((rows, width), bf16),
             shape((rows, width), bf16),
@@ -519,7 +619,10 @@
             shape((rows, units), bf16),
         ],
         scratch_shapes=[pltpu.VMEM((width, 2 * arrays[0][0].shape[-1]), bf16)]
-        + [pltpu.SemaphoreType.DMA((sum(len(b) for b in blocks),)) for blocks in metas],
+        + [
+            pltpu.SemaphoreType.DMA((sum(len(b) for b in blocks),))
+            for blocks in (metas[0], metas[1], metas[0])
+        ],
         compiler_params=pltpu.CompilerParams(vmem_limit_bytes=VMEM_BYTES),
         cost_estimate=pl.CostEstimate(
             flops=6 * rows * width * (width + 3 * units),
@@ -552,9 +655,17 @@
     )(place, *arrays)
 
 
-def finish_kernel(owners, parts_ref, tokens_ref, gain_ref, grad_ref, w_ref, out_ref):
+def finish_kernel(owners, splits, parts_ref, tokens_ref, gain_ref, grad_ref, w_ref, out_ref):
+    rows = tokens_ref.shape[0]
+    part = rows // splits
+    packed = UNITS * part // 2
     joined = jnp.concatenate(
-        [join_heads(parts_ref, part * LANES, owners) for part in range(3)], axis=1
+        [
+            join_packed(parts_ref, len(owners), splits, part),
+            join_heads(parts_ref, packed, rows, owners),
+            join_heads(parts_ref, packed + rows, rows, owners),
+        ],
+        axis=1,
     )
     normed, inverse = norm_rows(tokens_ref[...].astype(f32))
     grad_hidden = dot_tt(joined, w_ref[...])
@@ -562,11 +673,11 @@
     out_ref[...] = (grad_ref[...] + back).astype(bf16)
 
 
-def finish(owners, joined, tokens, gains, grad_middle, w_joined):
+def finish(owners, splits, joined, tokens, gains, grad_middle, w_joined):
     rows, width = tokens.shape
     vmem = pl.BlockSpec(memory_space=pltpu.VMEM)
     return pl.pallas_call(
-        functools.partial(finish_kernel, owners),
+        functools.partial(finish_kernel, owners, splits),
         in_specs=[vmem] * 5,
         out_specs=vmem,
         out_shape=jax.ShapeDtypeStruct((rows, width), bf16),
@@ -620,50 +731,61 @@
 
 
 def kept_grads_kernel(pairs, cut, sides_ref, *refs):
-    gots = refs[2 * pairs : 2 * pairs + 2]
-    mine_a, other_a, mine_b, other_b = refs[2 * pairs + 2 : 2 * pairs + 6]
-    share = gots[0].shape[1]
-    shard = mine_b.shape[1]
+    sources = refs[2 * pairs : 2 * pairs + 2]
+    targets = refs[2 * pairs + 2 : 2 * pairs + 6]
+    lt_ref, got_a, got_b, sum_a, sum_b, sems = refs[2 * pairs + 6 :]
+    gots = (got_a, got_b)
+    copies = [
+        pltpu.make_async_copy(source, got, sems.at[i])
+        for i, (source, got) in enumerate(zip(sources, gots))
+    ]
+    for copy in copies:
+        copy.start()
+    share = got_a.shape[1]
+    shard = sum_b.shape[2]
     outer = share // shard // 2
+    waits = list(copies)
 
     def emit(half, at, value):
+        while waits:
+            waits.pop().wait()
         for which, start, piece in pieces_of(cut, at, value):
             span = slice(start, start + piece.shape[1])
-            total = (piece + gots[which][half, :, span].astype(f32)).astype(bf16)
+            total = piece + gots[which][half, :, span].astype(f32)
             if which == 0:
-
-                @pl.when(sides_ref[1] == half)
-                def _():
-                    mine_a[0, :, span] = total
-
-                @pl.when(sides_ref[1] != half)
-                def _():
-                    other_a[0, :, span] = total
-
+                sum_a[sides_ref[1] ^ half, :, span] = total.astype(bf16)
             else:
-                for x in range(2):
-                    to = (mine_b, other_b)
-
-                    @pl.when(sides_ref[2] == x)
-                    def _():
-                        for z in range(outer):
-                            for flip in range(2):
-                                row = (z * 2 + (x ^ flip)) * shard
-                                to[flip][half * outer + z, :, span] = total[row : row + shard]
-
-    half_rows(pairs, sides_ref[0], share, refs, refs[-1], emit)
-
-
-def weight_grads(kernel, sides, operands, gots, outs, cut, name):
+                for z in range(outer):
+                    for x in range(2):
+                        row = (z * 2 + x) * shard
+                        block = total[row : row + shard].astype(bf16)
+                        sum_b[sides_ref[2] ^ x, half * outer + z, :, span] = block
+
+    half_rows(pairs, sides_ref[0], share, refs, lt_ref, emit)
+    copies = []
+    for i, total in enumerate((sum_a, sum_b)):
+        for flip in range(2):
+            copies.append(
+                pltpu.make_async_copy(total.at[flip], targets[2 * i + flip], sems.at[2 * i + flip])
+            )
+            copies[-1].start()
+    for copy in copies:
+        copy.wait()
+
+
+def weight_grads(kernel, sides, operands, gots, outs, cut, scratch, name):
     vmem = pl.BlockSpec(memory_space=pltpu.VMEM)
+    outside = pl.BlockSpec(memory_space=pl.ANY)
     rows, width = operands[0].shape
     columns = sum(array.shape[1] for array in operands[1::2])
     return pl.pallas_call(
         functools.partial(kernel, len(operands) // 2, cut),
-        in_specs=[pl.BlockSpec(memory_space=pltpu.SMEM)] + [vmem] * (len(operands) + len(gots)),
-        out_specs=[vmem] * len(outs),
+        in_specs=[pl.BlockSpec(memory_space=pltpu.SMEM)]
+        + [vmem] * len(operands)
+        + [outside] * len(gots),
+        out_specs=[outside if gots else vmem] * len(outs),
         out_shape=[jax.ShapeDtypeStruct(shape, bf16) for shape in outs],
-        scratch_shapes=[pltpu.VMEM((len(operands) // 2, width, rows), bf16)],
+        scratch_shapes=[pltpu.VMEM((len(operands) // 2, width, rows), bf16)] + scratch,
         compiler_params=pltpu.CompilerParams(vmem_limit_bytes=VMEM_BYTES),
         cost_estimate=pl.CostEstimate(
             flops=rows * width * columns, bytes_accessed=3 * width * columns, transcendentals=0
@@ -882,8 +1004,8 @@
             next_a = lax.ppermute(low_a, "ctx", swap)
             next_b = lax.ppermute(low_b, "fsdp", by_y)
             held = project_pair(1, project_pair(0, []))
-            own[3], other[2], near[3], next_a, next_b, held = gate(
-                own[3], other[2], near[3], next_a, next_b, held
+            own[3], other[2], near[3], next_a, next_b, held, late = gate(
+                own[3], other[2], near[3], next_a, next_b, held, w_qkv
             )
 
             other.append(lax.ppermute(own[3], "ctx", swap))
@@ -891,9 +1013,10 @@
             high_b = jnp.stack([near[2][1], near[3][1]])
             past_a = lax.ppermute(high_a, "ctx", swap)
             past_b = lax.ppermute(high_b, "fsdp", by_y)
-            ring_c = [w_qkv] + [lax.ppermute(w_qkv, "ctx", turn(back)) for back in range(1, outer)]
             held = project_pair(2, held)
-            other[3], past_a, past_b, ring_c, held = gate(other[3], past_a, past_b, ring_c, held)
+            ring_c = [late, lax.ppermute(late, "ctx", turn(1))]
+            other[3], past_a, past_b, held, ring_c = gate(other[3], past_a, past_b, held, ring_c)
+            ring_c.append(lax.ppermute(ring_c[1], "ctx", turn(1)))
 
             pair_a = jnp.concatenate([weave(low_a, next_a), weave(high_a, past_a)])
             pair_b = jnp.concatenate([low_b, next_b, high_b, past_b])
@@ -914,7 +1037,7 @@
             base, count, unit_places, qkv, turned, doc_slab, doc_q, rows, tile
         )
         if by_hand:
-            att_low, far_a, far_b = gate(att_low, far_a, far_b)
+            att_low, far_a, far_b, ring_c = gate(att_low, far_a, far_b, ring_c)
             pair_b = weave(pair_b, far_b)
             arrays = [pair_a, far_a, lax.ppermute(pair_a, "fsdp", by_core),
                       lax.ppermute(far_a, "fsdp", by_core),
@@ -925,6 +1048,7 @@
                        + [(flip + 2 * near, back) for near in (0, 1) for back in (2, 3)]
                        for flip in range(2)]
             att_in = lax.all_to_all(att_low, "ctx", 0, 0, tiled=True)
+            ring_c.append(lax.ppermute(ring_c[2], "ctx", turn(1)))
             pair_c = jnp.stack(ring_c)
             att_in, arrays, pair_c = gate(att_in, arrays, pair_c)
             near_c = lax.ppermute(pair_c, "ctx", swap)
@@ -940,26 +1064,38 @@
 
         output, grad_heads, grad_middle, attended, grad_branch, hidden_two, grad_up, product = (
             middle_stage(
-                owners, first, place, att_in, tokens[0], gains, cot, parts_a, parts_b,
+                heads, splits, place, att_in, tokens[0], gains, cot, parts_a, parts_b,
                 w_down.shape[0],
             )
         )
         operands = [attended, grad_branch, hidden_two, grad_up, cot, product]
+        if by_hand:
+            grad_heads, operands, near_c = gate(grad_heads, operands, near_c)
+            pair_c = weave(pair_c, near_c)
+            far_c = lax.ppermute(pair_c, "fsdp", by_y)
         grad_heads = lax.all_to_all(grad_heads, "ctx", 0, 0, tiled=True)
         if by_hand:
             rest = columns - cut
             gone_a, gone_b = weight_grads(
                 gone_grads_kernel, sides, operands, [], [(2, share, cut), (2, share, rest)], cut,
-                "gone_grads",
+                [], "gone_grads",
             )
             got_a = lax.ppermute(gone_a, "fsdp", by_core)
             got_b = lax.ppermute(gone_b, "fsdp", by_core)
             mine_a, other_a, mine_b, other_b = weight_grads(
                 kept_grads_kernel, sides, operands, [got_a, got_b],
-                [(1, share, cut)] * 2 + [(2 * outer, shard, rest)] * 2, cut, "kept_grads",
-            )
-            grad_heads, mine_a, other_a, mine_b, other_b, near_c = gate(
-                grad_heads, mine_a, other_a, mine_b, other_b, near_c
+                [(share, cut)] * 2 + [(2 * outer, shard, rest)] * 2, cut,
+                [
+                    pltpu.VMEM((2, share, cut), bf16),
+                    pltpu.VMEM((2, share, rest), bf16),
+                    pltpu.VMEM((2, share, cut), bf16),
+                    pltpu.VMEM((2, 2 * outer, shard, rest), bf16),
+                    pltpu.SemaphoreType.DMA((4,)),
+                ],
+                "kept_grads",
+            )
+            grad_heads, mine_a, other_a, mine_b, other_b = gate(
+                grad_heads, mine_a, other_a, mine_b, other_b
             )
             got_a = lax.ppermute(other_a, "fsdp", by_y)
             got_b = lax.ppermute(other_b, "ctx", swap)
@@ -972,17 +1108,17 @@
             grad_packed = lax.psum_scatter(grad_packed, "ctx", scatter_dimension=0, tiled=True)
             grad_packed = grad_packed.astype(f32)
 
-        grad_joined = attend_back(
+        grad_joined, grad_sent = attend_back(
             base, count, unit_places, qkv, turned, doc_slab, doc_q, grad_heads, att, lse, cosine,
             sine, rows, tile,
         )
         if by_hand:
-            grad_joined, mine_a, got_a, mine_b, got_b = gate(
-                grad_joined, mine_a, got_a, mine_b, got_b
-            )
-            pair_c = weave(pair_c, near_c)
-            far_c = lax.ppermute(pair_c, "fsdp", by_y)
-            joined_in = lax.all_to_all(grad_joined, "ctx", 0, 0, tiled=True)
+            grad_joined, grad_sent, mine_a, got_a, mine_b, got_b, pair_c, far_c = gate(
+                grad_joined, grad_sent, mine_a, got_a, mine_b, got_b, pair_c, far_c
+            )
+            joined_in = lax.all_to_all(grad_sent, "ctx", 0, 0, tiled=True)
+            arrays = [pair_c, far_c, lax.ppermute(pair_c, "fsdp", by_core),
+                      lax.ppermute(far_c, "fsdp", by_core)]
             by_x = lambda array: array.reshape(outer, 2, shard, array.shape[-1])
             mine_a, other_a, mine_b, other_b = add_halves(
                 sides,
@@ -993,9 +1129,11 @@
             got_a = lax.ppermute(other_a, "ctx", swap)
             got_b = lax.ppermute(other_b, "fsdp", by_y)
             kept_cols, gone_cols = head_grads(fsdp, sides_late, hidden_one, grad_joined)
-            mine_a, got_a, mine_b, got_b, kept_cols, gone_cols = gate(
-                mine_a, got_a, mine_b, got_b, kept_cols, gone_cols
-            )
+            got_cols = lax.ppermute(gone_cols, "fsdp", by_core)
+            mine_a, got_a, mine_b, got_b, kept_cols, got_cols, arrays = gate(
+                mine_a, got_a, mine_b, got_b, kept_cols, got_cols, arrays
+            )
+            w_joined = settle(place, list(zip(arrays, metas_a)), width)
             pairs = lambda array: array.reshape(outer // 2, 2, shard, array.shape[-1])
             kept, gone = add_halves(
                 sides,
@@ -1003,25 +1141,21 @@
                 joined=True,
             )
             got = lax.ppermute(gone, "ctx", flips(ctx, 2))
-            got_cols = lax.ppermute(gone_cols, "fsdp", by_core)
-            kept, got, kept_cols, got_cols, far_c = gate(kept, got, kept_cols, got_cols, far_c)
+            kept_cols, gone_cols = add_halves(sides, [(kept_cols, got_cols, 0, 1)])
+            got_cols = lax.ppermute(gone_cols, "fsdp", by_y)
+            joined_in, kept, got, kept_cols, got_cols, w_joined = gate(
+                joined_in, kept, got, kept_cols, got_cols, w_joined
+            )
             kept, gone = add_halves(sides, [(kept, got, 0, 4)])
             got = lax.ppermute(gone, "ctx", flips(ctx, 4))
-            kept_cols, gone_cols = add_halves(sides, [(kept_cols, got_cols, 0, 1)])
-            got_cols = lax.ppermute(gone_cols, "fsdp", by_y)
-            arrays = [pair_c, far_c, lax.ppermute(pair_c, "fsdp", by_core),
-                      lax.ppermute(far_c, "fsdp", by_core)]
-            w_joined = settle(place, list(zip(arrays, metas_a)), width)
-            joined_in, kept, got, kept_cols, got_cols, w_joined = gate(
-                joined_in, kept, got, kept_cols, got_cols, w_joined
-            )
             grad_packed = kept[0].astype(f32) + got[0].astype(f32)
             grad_cols = (kept_cols[0].astype(f32) + got_cols[0].astype(f32)).astype(bf16)
+            grad_cols, _ = gate(grad_cols, gone)
         else:
-            joined_in = lax.all_to_all(grad_joined, "ctx", 0, 0, tiled=True)
+            joined_in = lax.all_to_all(grad_sent, "ctx", 0, 0, tiled=True)
             grad_cols = dot_rows(hidden_one, grad_joined.reshape(total, 3 * LANES)).astype(bf16)
             grad_cols = lax.psum_scatter(grad_cols, "fsdp", scatter_dimension=0, tiled=True)
-        input_grad = finish(owners, joined_in, tokens[0], gains, grad_middle, w_joined)
+        input_grad = finish(owners, splits, joined_in, tokens[0], gains, grad_middle, w_joined)
         grad_cols = grad_cols.reshape(ctx, shard, 3 * LANES)
         grad_cols = lax.all_to_all(grad_cols, "ctx", 0, 0, tiled=True).astype(f32)
 

time: 265 us -> 248 us (0.936)
  waiting for transfers between devices: 70 us -> 59.6 us
  Pallas kernels: 111 us -> 103 us
  starting transfers between devices: 54.2 us -> 61.1 us
  local copies, waits for them, and re-layouts: 11 us -> 6.14 us
    ppermute x1, waiting for transfers between devices: 13.8 us -> 0.97 us  [on_device(): got_b = lax.ppermute(other_b, 'fsdp', by_y)]
    ppermute x3, waiting for transfers between devices: 0.01 us -> 12 us  [the longest x1 10.2 us: on_device(): ring_c.append(lax.ppermute(ring_c[2], 'ctx', turn(1)))]
    all_to_all x1, waiting for transfers between devices: 11.4 us -> 1.23 us  [on_device(): att_in = lax.all_to_all(att_low, 'ctx', 0, 0, tiled=True)]
    ppermute x1, waiting for transfers between devices: 0.01 us -> 9.3 us  [on_device(): got_a = lax.ppermute(other_a, 'ctx', swap)]
    ppermute x1, waiting for transfers between devices: 5.12 us -> 0.01 us  [on_device(): other.append(lax.ppermute(own[3], 'ctx', swap))]
    ppermute x1, waiting for transfers between devices: 5.1 us -> 0.01 us  [on_device(): own.append(lax.ppermute(own[1], 'ctx', turn(1)))]
    unnamed x73 -> x59, local copies, waits for them, and re-layouts: 6.68 us -> 1.85 us
    ppermute x1, waiting for transfers between devices: 0.01 us -> 4.67 us  [on_device(): near.append(lax.ppermute(near[1], 'ctx', turn(1)))]
  transfers between devices with their start and end apart: 43 -> 43, of which waited for: 16 -> 16; matrix products, arithmetic and copies ran while one was open for 5% -> 7% of each run, Pallas kernels for 37% -> 39%
where the time goes in v4:
time: 248 us; the launch traced here: 246 us
  Pallas kernels  103 us (42%)
  starting transfers between devices  61.1 us (25%)
  waiting for transfers between devices  59.6 us (24%)
  other arithmetic  14.9 us (6%)
  local copies, waits for them, and re-layouts  6.14 us (2%)
    pallas_call x1, Pallas kernels, attend_back(): pl.pallas_call(functools.partial(attend_back_kernel, units, tile), grid_s...  20.1 us
    pallas_call x4, Pallas kernels, project(): pl.pallas_call(project_kernel, grid_spec=pltpu.PrefetchScalarGridSpec(num...  18.8 us
    pallas_call x1, Pallas kernels, attend(): pl.pallas_call(functools.partial(attend_kernel, units, tile), grid_spec=p...  12.8 us
    pallas_call x2, Pallas kernels, weight_grads(): pl.pallas_call(functools.partial(kernel, len(operands) // 2, cut), in_spe...  11.4 us
    pallas_call x1, Pallas kernels, middle_stage(): pl.pallas_call(functools.partial(middle_kernel, heads, splits, metas, arr...  10.4 us
    ppermute x1, waiting for transfers between devices, on_device(): ring_c.append(lax.ppermute(ring_c[2], 'ctx', turn(1)))  10.2 us
    pallas_call x4, Pallas kernels, add_halves(): pl.pallas_call(functools.partial(add_halves_kernel, [pair[3] for pair in...  9.39 us
    ppermute x1, waiting for transfers between devices, on_device(): got_a = lax.ppermute(other_a, 'ctx', swap)  9.3 us
  transfers between devices with their start and end apart: 43, of which 16 were waited for; matrix products, arithmetic and copies ran while one was open for 7% of the time, Pallas kernels for 39%

profile of v4, /device:TPU:0, one launch (start us, length us, event | category | flops | bytes accessed | tf_op | source)
XLA Modules:
  0.0 246.1 jit_solution(13765087351586878971)
XLA Ops:
  0.6 3.1 %collective-permute-start = (bf16[256,768]{1,0:T(8,128)(2,1)}, bf16[256,768]{1,0:T(8,128)(2,1)S(1)}, u32[]{:S(2)}, u32[]{:S(2)}) collective-permute-start(bf16[256,768]{1,0:T(8,128)(2,1)} %bitcast.131), channel_id=1, source_target_pairs={{0,2},{1,3},{2,4},{3,5},{4,6},{5,7},{6,0},{7,1},{8,10},{9,11},{10,... | collective-permute-start | bytes 1179656 | tf_op jit(solution)/shard_map/ppermute | solution.py:968
  9.6 3.5 %all-to-all-start = ((bf16[8,32,512]{2,1,0:T(8,128)(2,1)}), bf16[8,32,512]{2,1,0:T(8,128)(2,1)S(1)}, u32[]{:S(2)}, u32[]{:S(2)}) async-start(bf16[8,32,512]{2,1,0:T(8,128)(2,1)} %spread.1), calls=%async_computation | async-start | bytes 524288 | tf_op jit(solution)/shard_map/all_to_all | solution.py:961
  15.2 5.3 %collective-permute-done.2 = bf16[2,24,2176]{2,1,0:T(8,128)(2,1)S(1)} collective-permute-done((bf16[2,24,2176]{2,1,0:T(8,128)(2,1)S(1)}, bf16[2,24,2176]{2,1,0:T(8,128)(2,1)S(1)}, u32[]{:S(2)}, u32[]{:S(2)}) %collective-permute-start.2) | collective-permute-done | bytes 208928 | tf_op jit(solution)/shard_map/ppermute | solution.py:970
  20.4 4.7 %all-to-all-done = bf16[8,32,512]{2,1,0:T(8,128)(2,1)S(1)} async-done(((bf16[8,32,512]{2,1,0:T(8,128)(2,1)}), bf16[8,32,512]{2,1,0:T(8,128)(2,1)S(1)}, u32[]{:S(2)}, u32[]{:S(2)}) %all-to-all-start) | async-done | bytes 262176 | tf_op jit(solution)/shard_map/all_to_all | solution.py:961
  29.0 5.6 %multiply_sine_fusion = (f32[2048,128]{1,0:T(8,128)}, f32[2048,128]{1,0:T(8,128)}) fusion(f32[128]{0:T(128)S(1)} %fusion.20, f32[2048]{0:T(1024)S(1)} %bitcast.159), kind=kLoop, calls=%fused_computation.1 | loop fusion | flops 262144 | bytes 2105856 | tf_op jit(solution)/shard_map/sin | solution.py:956
  37.8 4.7 %collective-permute-done.5 = bf16[2,24,2176]{2,1,0:T(8,128)(2,1)S(1)} collective-permute-done((bf16[2,24,2176]{2,1,0:T(8,128)(2,1)S(1)}, bf16[2,24,2176]{2,1,0:T(8,128)(2,1)S(1)}, u32[]{:S(2)}, u32[]{:S(2)}) %collective-permute-start.5) | collective-permute-done | bytes 208928 | tf_op jit(solution)/shard_map/ppermute | solution.py:984
  49.4 4.7 %project.4 = (bf16[2048,768]{1,0:T(8,128)(2,1)}, bf16[2048,384]{1,0:T(8,128)(2,1)}, bf16[256,2048]{1,0:T(8,128)(2,1)}) custom-call(s32[2]{0:T(128)} %get-tuple-element.344.at_ref, bf16[256,768]{1,0:T(8,128)(2,1)} %bitcast.133, bf16[256,768]{1,0:T(8,128)(2,1)} %copy-done.20, bf16[768,512]{1,0:T(8,128)(2,1)} %get-tuple-element.154.w_ref, ...), custom_call_target="tpu_custom_call" | custom-call | flops 301989888 | bytes 6291456 | tf_op jit(solution)/shard_map/project/pallas_call | solution.py:174
  54.1 4.7 %project.5 = (bf16[2048,768]{1,0:T(8,128)(2,1)}, bf16[2048,384]{1,0:T(8,128)(2,1)}, bf16[256,2048]{1,0:T(8,128)(2,1)}) custom-call(s32[2]{0:T(128)} %get-tuple-element.343.at_ref, bf16[256,768]{1,0:T(8,128)(2,1)} %copy-done.12, bf16[256,768]{1,0:T(8,128)(2,1)} %copy-done.15, ...), custom_call_target="tpu_custom_call", output_to_operand_aliasing={{0}: (7, {}), {1}: (8, {}), {2}: (9, {})} | custom-call | flops 301989888 | bytes 6291456 | tf_op jit(solution)/shard_map/project/pallas_call | solution.py:174
  64.3 4.7 %project.6 = (bf16[2048,768]{1,0:T(8,128)(2,1)}, bf16[2048,384]{1,0:T(8,128)(2,1)}, bf16[256,2048]{1,0:T(8,128)(2,1)}) custom-call(s32[2]{0:T(128)} %get-tuple-element.345.at_ref, bf16[256,768]{1,0:T(8,128)(2,1)} %copy-done.13, bf16[256,768]{1,0:T(8,128)(2,1)} %copy-done.17, ...), custom_call_target="tpu_custom_call", output_to_operand_aliasing={{0}: (7, {}), {1}: (8, {}), {2}: (9, {})} | custom-call | flops 301989888 | bytes 6291456 | tf_op jit(solution)/shard_map/project/pallas_call | solution.py:174
  70.7 3.4 %collective-permute-done.14 = bf16[2,24,2176]{2,1,0:T(8,128)(2,1)S(1)} collective-permute-done((bf16[2,24,2176]{2,1,0:T(8,128)(2,1)S(1)}, bf16[2,24,2176]{2,1,0:T(8,128)(2,1)S(1)}, u32[]{:S(2)}, u32[]{:S(2)}) %collective-permute-start.14) | collective-permute-done | bytes 208928 | tf_op jit(solution)/shard_map/ppermute | solution.py:1014
  78.1 4.7 %project.7 = (bf16[2048,768]{1,0:T(8,128)(2,1)}, bf16[2048,384]{1,0:T(8,128)(2,1)}, bf16[256,2048]{1,0:T(8,128)(2,1)}) custom-call(s32[2]{0:T(128)} %get-tuple-element.342.at_ref, bf16[256,768]{1,0:T(8,128)(2,1)} %copy-done.14, bf16[256,768]{1,0:T(8,128)(2,1)} %copy-done.16, ...), custom_call_target="tpu_custom_call", output_to_operand_aliasing={{0}: (7, {}), {1}: (8, {}), {2}: (9, {})} | custom-call | flops 301989888 | bytes 6291456 | tf_op jit(solution)/shard_map/project/pallas_call | solution.py:174
  82.8 12.8 %attend.1 = (bf16[8,192,128]{2,1,0:T(8,128)(2,1)}, f32[8,128,384]{2,1,0:T(8,128)}, f32[8,1,384]{2,1,0:T(1,128)}) custom-call(s32[8]{0:T(128)} %get-tuple-element.145.base_ref, s32[8]{0:T(128)} %get-tuple-element.146.count_ref, s32[6]{0:T(128)} %pad_add_fusion.1.units_ref, bf16[2048,384]{1,0:T(8,128)(2,1)} %get-tuple-element.179.q_ref.k_ref.v_ref, ...), custom_call_target="tpu_custom_call" | custom-call | flops 3221225472 | bytes 8388608 | tf_op jit(solution)/shard_map/attend/pallas_call | solution.py:321
  96.7 5.1 %all-to-all-start.1 = ((bf16[8,192,128]{2,1,0:T(8,128)(2,1)}), bf16[8,192,128]{2,1,0:T(8,128)(2,1)}, u32[]{:S(2)}, u32[]{:S(2)}) async-start(bf16[8,192,128]{2,1,0:T(8,128)(2,1)} %get-tuple-element.190), calls=%async_computation.1 | async-start | bytes 786432 | tf_op jit(solution)/shard_map/all_to_all | solution.py:1050
  105.0 10.2 %collective-permute-done.23 = bf16[24,2304]{1,0:T(8,128)(2,1)S(1)} collective-permute-done((bf16[24,2304]{1,0:T(8,128)(2,1)S(1)}, bf16[24,2304]{1,0:T(8,128)(2,1)S(1)}, u32[]{:S(2)}, u32[]{:S(2)}) %collective-permute-start.23) | collective-permute-done | bytes 110624 | tf_op jit(solution)/shard_map/ppermute | solution.py:1051
  118.0 10.4 %middle_stage.1 = (bf16[256,768]{1,0:T(8,128)(2,1)}, bf16[8,192,128]{2,1,0:T(8,128)(2,1)}, f32[256,768]{1,0:T(8,128)}, bf16[256,768]{1,0:T(8,128)(2,1)}, bf16[25...) custom-call(s32[4]{0:T(128)} %pad_add_fusion.place_ref, ...), custom_call_target="tpu_custom_call" | custom-call | flops 4982833152 | bytes 10485760 | tf_op jit(solution)/shard_map/middle_stage/pallas_call | solution.py:605
  128.4 4.7 %gone_grads.1 = (bf16[2,192,2176]{2,1,0:T(8,128)(2,1)}, bf16[2,192,2048]{2,1,0:T(8,128)(2,1)}) custom-call(s32[5]{0:T(128)} %stack.119.sides_ref, bf16[256,768]{1,0:T(8,128)(2,1)} %get-tuple-element.212.refs_0_, bf16[256,768]{1,0:T(8,128)(2,1)} %get-tuple-element.213.refs_1_, bf16[256,768]{1,0:T(8,128)(2,1)} %get-tuple-element.214.refs_2_, ...), custom_call_target="tpu_custom_call" | custom-call | flops 830472192 | bytes 9732096 | tf_op jit(solution)/shard_map/gone_grads/pallas_call | solution.py:781
  133.6 3.5 %all-to-all-start.2 = ((bf16[8,192,128]{2,1,0:T(8,128)(2,1)}), bf16[8,192,128]{2,1,0:T(8,128)(2,1)S(1)}, u32[]{:S(2)}, u32[]{:S(2)}) async-start(bf16[8,192,128]{2,1,0:T(8,128)(2,1)} %get-tuple-element.211), calls=%async_computation.2 | async-start | bytes 786432 | tf_op jit(solution)/shard_map/all_to_all | solution.py:1076
  137.2 3.3 %collective-permute-start.29 = (bf16[4,48,2304]{2,1,0:T(8,128)(2,1)S(1)}, bf16[4,48,2304]{2,1,0:T(8,128)(2,1)S(1)}, u32[]{:S(2)}, u32[]{:S(2)}) collective-permute-start(bf16[4,48,2304]{2,1,0:T(8,128)(2,1)S(1)} %pad_maximum_fusion.1.refs_0_), channel_id=1, source_target_pairs={{0,16},{8,24},{16,0},{24,8},{1,17},{9,25},{17,1},{25,9},{2,18},{10... | collective-permute-start | bytes 2654216 | tf_op jit(solution)/shard_map/ppermute | solution.py:1075
  140.6 6.7 %kept_grads.1 = (bf16[192,2176]{1,0:T(8,128)(2,1)}, bf16[192,2176]{1,0:T(8,128)(2,1)}, bf16[8,24,2048]{2,1,0:T(8,128)(2,1)}, bf16[8,24,2048]{2,1,0:T(8,128)(2,1)}) custom-call(s32[5]{0:T(128)} %stack.119.sides_ref, bf16[256,768]{1,0:T(8,128)(2,1)} %get-tuple-element.212.refs_0_, bf16[256,768]{1,0:T(8,128)(2,1)} %get-tuple-element.213.refs_1_, ...), custom_call_target="tpu_custom_call" | custom-call | flops 830472192 | bytes 9732096 | tf_op jit(solution)/shard_map/kept_grads/pallas_call | solution.py:781
  149.1 3.3 %collective-permute-start.27 = (bf16[192,2176]{1,0:T(8,128)(2,1)}, bf16[192,2176]{1,0:T(8,128)(2,1)}, u32[]{:S(2)}, u32[]{:S(2)}) collective-permute-start(bf16[192,2176]{1,0:T(8,128)(2,1)} %get-tuple-element.230), channel_id=1, source_target_pairs={{0,16},{8,24},{16,0},{24,8},{1,17},{9,25},{17,1},{25,9},{2,18},{10... | collective-permute-start | bytes 2506760 | tf_op jit(solution)/shard_map/ppermute | solution.py:1100
  153.9 20.1 %attend_back.1 = (bf16[8,256,384]{2,1,0:T(8,128)(2,1)}, bf16[8,704,128]{2,1,0:T(8,128)(2,1)}) custom-call(s32[8]{0:T(128)} %get-tuple-element.145.base_ref, s32[8]{0:T(128)} %get-tuple-element.146.count_ref, s32[6]{0:T(128)} %pad_add_fusion.1.units_ref, bf16[2048,384]{1,0:T(8,128)(2,1)} %get-tuple-element.179.q_ref.k_ref.v_ref, ...), custom_call_target="tpu_custom_call" | custom-call | flops 8053063680 | bytes 12582912 | tf_op jit(solution)/shard_map/attend_back/pallas_call | solution.py:422
  174.0 4.4 %collective-permute-done.27 = bf16[192,2176]{1,0:T(8,128)(2,1)} collective-permute-done((bf16[192,2176]{1,0:T(8,128)(2,1)}, bf16[192,2176]{1,0:T(8,128)(2,1)}, u32[]{:S(2)}, u32[]{:S(2)}) %collective-permute-start.27) | collective-permute-done | bytes 835616 | tf_op jit(solution)/shard_map/ppermute | solution.py:1100
  178.4 5.6 %all-to-all-start.3 = ((bf16[8,704,128]{2,1,0:T(8,128)(2,1)}), bf16[8,704,128]{2,1,0:T(8,128)(2,1)S(1)}, u32[]{:S(2)}, u32[]{:S(2)}) async-start(bf16[8,704,128]{2,1,0:T(8,128)(2,1)} %get-tuple-element.234), calls=%async_computation.3 | async-start | bytes 2883584 | tf_op jit(solution)/shard_map/all_to_all | solution.py:1119
  184.6 3.2 %add_halves.4 = (bf16[4,24,2176]{2,1,0:T(8,128)(2,1)}, bf16[4,24,2176]{2,1,0:T(8,128)(2,1)}, bf16[1,96,2048]{2,1,0:T(8,128)(2,1)}, bf16[1,96,2048]{2,1,0:T(8,128)(2,1)}) custom-call(s32[5]{0:T(128)} %stack.119.sides_ref, bf16[4,2,24,2176]{3,2,1,0:T(8,128)(2,1)} %bitcast.140, bf16[4,2,24,2176]{3,2,1,0:T(8,128)(2,1)} %bitcast.32.refs_1_, ...), custom_call_target="tpu_custom_call" | custom-call | flops 1622016 | bytes 4866048 | tf_op jit(solution)/shard_map/add_halves/pallas_call | solution.py:869
  191.5 6.5 %head_grads.1 = (bf16[2,192,384]{2,1,0:T(8,128)(2,1)}, bf16[2,192,384]{2,1,0:T(8,128)(2,1)}) custom-call(s32[5]{0:T(128)} %stack.119.sides_ref, bf16[2048,768]{1,0:T(8,128)(2,1)} %get-tuple-element.246.left_ref, bf16[8,256,384]{2,1,0:T(8,128)(2,1)} %get-tuple-element.247.right_ref), custom_call_target="tpu_custom_call" | custom-call | flops 1207959552 | bytes 4718592 | tf_op jit(solution)/shard_map/head_grads/pallas_call | solution.py:820
  200.8 9.3 %collective-permute-done.30 = bf16[4,24,2176]{2,1,0:T(8,128)(2,1)S(1)} collective-permute-done((bf16[4,24,2176]{2,1,0:T(8,128)(2,1)}, bf16[4,24,2176]{2,1,0:T(8,128)(2,1)S(1)}, u32[]{:S(2)}, u32[]{:S(2)}) %collective-permute-start.30) | collective-permute-done | bytes 417824 | tf_op jit(solution)/shard_map/ppermute | solution.py:1129
  210.9 2.4 add_halves.5
  216.6 4.7 %settle.1.w_ref = bf16[768,2304]{1,0:T(8,128)(2,1)} custom-call(s32[4]{0:T(128)} %pad_add_fusion.place_ref, bf16[4,48,2304]{2,1,0:T(8,128)(2,1)} %copy-done.1, bf16[4,48,2304]{2,1,0:T(8,128)(2,1)} %copy-done.4, bf16[4,48,2304]{2,1,0:T(8,128)(2,1)} %copy-done.5, bf16[4,48,2304]{2,1,0:T(8,128)(2,1)} %copy-done.6), custom_call_target="tpu_custom_call" | custom-call | bytes 8388608 | tf_op jit(solution)/shard_map/settle/pallas_call | solution.py:646
  221.2 5.1 %collective-permute-done.35 = bf16[2,24,4224]{2,1,0:T(8,128)(2,1)S(1)} collective-permute-done((bf16[2,24,4224]{2,1,0:T(8,128)(2,1)}, bf16[2,24,4224]{2,1,0:T(8,128)(2,1)S(1)}, u32[]{:S(2)}, u32[]{:S(2)}) %collective-permute-start.35) | collective-permute-done | bytes 405536 | tf_op jit(solution)/shard_map/ppermute | solution.py:1143
  230.6 3.7 %all-to-all-start.4 = ((bf16[8,24,384]{2,1,0:T(8,128)(2,1)}), bf16[8,24,384]{2,1,0:T(8,128)(2,1)S(1)}, u32[]{:S(2)}, u32[]{:S(2)}) async-start(bf16[8,24,384]{2,1,0:T(8,128)(2,1)} %bitcast.45), calls=%async_computation.4 | async-start | bytes 294912 | tf_op jit(solution)/shard_map/all_to_all | solution.py:1160
  234.4 5.2 %finish.1 = bf16[256,768]{1,0:T(8,128)(2,1)} custom-call(bf16[8,704,128]{2,1,0:T(8,128)(2,1)} %copy-done, bf16[256,768]{1,0:T(8,128)(2,1)} %bitcast.135, f32[8,768]{1,0:T(8,128)} %get-tuple-element.155.gains_ref.gain_ref, f32[256,768]{1,0:T(8,128)} %get-tuple-element.267.grad_ref, bf16[768,2304]{1,0:T(8,128)(2,1)} %settle.1.w_ref), custom_call_target="tpu_custom_call" | custom-call | flops 905969664 | bytes 6291456 | tf_op jit(solution)/shard_map/finish/pallas_call | solution.py:679
  239.6 2.7 %collective-permute-done.37 = bf16[1,24,4224]{2,1,0:T(8,128)(2,1)S(1)} collective-permute-done((bf16[1,24,4224]{2,1,0:T(8,128)(2,1)}, bf16[1,24,4224]{2,1,0:T(8,128)(2,1)S(1)}, u32[]{:S(2)}, u32[]{:S(2)}) %collective-permute-start.37) | collective-permute-done | bytes 202784 | tf_op jit(solution)/shard_map/ppermute | solution.py:1150
  (181 shorter events, 63.0 us)
Async XLA Ops:
  0.6 19.8 %collective-permute-start = (bf16[256,768]{1,0:T(8,128)(2,1)}, bf16[256,768]{1,0:T(8,128)(2,1)S(1)}, u32[]{:S(2)}, u32[]{:S(2)}) collective-permute-start(bf16[256,768]{1,0:T(8,128)(2,1)} %bitcast.131), channel_id=1, source_target_pairs={{0,2},{1,3},{2,4},{3,5},{4,6},{5,7},{6,0},{7,1},{8,10},{9,11},{10,... | collective-permute-start | bytes 1179656 | tf_op jit(solution)/shard_map/ppermute | solution.py:968
  3.7 16.7 %collective-permute-start.1 = (bf16[256,768]{1,0:T(8,128)(2,1)}, bf16[256,768]{1,0:T(8,128)(2,1)S(1)}, u32[]{:S(2)}, u32[]{:S(2)}) collective-permute-start(bf16[256,768]{1,0:T(8,128)(2,1)} %bitcast.132), channel_id=1, source_target_pairs={{0,1},{1,0},{2,3},{3,2},{4,5},{5,4},{6,7},{7,6},{8,9},{9,8},{10,11... | collective-permute-start | bytes 1179656 | tf_op jit(solution)/shard_map/ppermute | solution.py:969
  6.2 14.2 %collective-permute-start.2 = (bf16[2,24,2176]{2,1,0:T(8,128)(2,1)S(1)}, bf16[2,24,2176]{2,1,0:T(8,128)(2,1)S(1)}, u32[]{:S(2)}, u32[]{:S(2)}) collective-permute-start(bf16[2,24,2176]{2,1,0:T(8,128)(2,1)S(1)} %pad_maximum_fusion.6), channel_id=1, source_target_pairs={{0,2},{1,3},{2,4},{3,5},{4,6},{5,7},{6,0},{7,1},{8,10},{9,11},{10,... | collective-permute-start | bytes 626696 | tf_op jit(solution)/shard_map/ppermute | solution.py:970
  9.6 15.5 %all-to-all-start = ((bf16[8,32,512]{2,1,0:T(8,128)(2,1)}), bf16[8,32,512]{2,1,0:T(8,128)(2,1)S(1)}, u32[]{:S(2)}, u32[]{:S(2)}) async-start(bf16[8,32,512]{2,1,0:T(8,128)(2,1)} %spread.1), calls=%async_computation | async-start | bytes 524288 | tf_op jit(solution)/shard_map/all_to_all | solution.py:961
  25.2 17.3 %collective-permute-start.3 = (bf16[256,768]{1,0:T(8,128)(2,1)S(1)}, bf16[256,768]{1,0:T(8,128)(2,1)S(1)}, u32[]{:S(2)}, u32[]{:S(2)}) collective-permute-start(bf16[256,768]{1,0:T(8,128)(2,1)S(1)} %collective-permute-done.own_ref), channel_id=1, source_target_pairs={{0,2},{1,3},{2,4},{3,5},{4,6},{5,7},{6,0},{7,1},{8,10},{9,11},{10,... | collective-permute-start | bytes 1179656 | tf_op jit(solution)/shard_map/ppermute | solution.py:982
  26.1 16.4 %collective-permute-start.4 = (bf16[256,768]{1,0:T(8,128)(2,1)S(1)}, bf16[256,768]{1,0:T(8,128)(2,1)S(1)}, u32[]{:S(2)}, u32[]{:S(2)}) collective-permute-start(bf16[256,768]{1,0:T(8,128)(2,1)S(1)} %collective-permute-done.own_ref), channel_id=1, source_target_pairs={{0,1},{1,0},{2,3},{3,2},{4,5},{5,4},{6,7},{7,6},{8,9},{9,8},{10,11... | collective-permute-start | bytes 1179656 | tf_op jit(solution)/shard_map/ppermute | solution.py:983
  26.7 15.8 %collective-permute-start.5 = (bf16[2,24,2176]{2,1,0:T(8,128)(2,1)S(1)}, bf16[2,24,2176]{2,1,0:T(8,128)(2,1)S(1)}, u32[]{:S(2)}, u32[]{:S(2)}) collective-permute-start(bf16[2,24,2176]{2,1,0:T(8,128)(2,1)S(1)} %collective-permute-done.2), channel_id=1, source_target_pairs={{0,2},{1,3},{2,4},{3,5},{4,6},{5,7},{6,0},{7,1},{8,10},{9,11},{10,... | collective-permute-start | bytes 626696 | tf_op jit(solution)/shard_map/ppermute | solution.py:984
  43.8 16.5 %collective-permute-start.8 = (bf16[256,768]{1,0:T(8,128)(2,1)S(1)}, bf16[256,768]{1,0:T(8,128)(2,1)S(1)}, u32[]{:S(2)}, u32[]{:S(2)}) collective-permute-start(bf16[256,768]{1,0:T(8,128)(2,1)S(1)} %collective-permute-done.3.own_ref), channel_id=1, source_target_pairs={{0,2},{1,3},{2,4},{3,5},{4,6},{5,7},{6,0},{7,1},{8,10},{9,11},{10,... | collective-permute-start | bytes 1179656 | tf_op jit(solution)/shard_map/ppermute | solution.py:1001
  43.8 16.5 %collective-permute-start.9 = (bf16[256,768]{1,0:T(8,128)(2,1)S(1)}, bf16[256,768]{1,0:T(8,128)(2,1)S(1)}, u32[]{:S(2)}, u32[]{:S(2)}) collective-permute-start(bf16[256,768]{1,0:T(8,128)(2,1)S(1)} %collective-permute-done.3.own_ref), channel_id=1, source_target_pairs={{0,1},{1,0},{2,3},{3,2},{4,5},{5,4},{6,7},{7,6},{8,9},{9,8},{10,11... | collective-permute-start | bytes 1179656 | tf_op jit(solution)/shard_map/ppermute | solution.py:1002
  45.3 14.9 %collective-permute-start.10 = (bf16[2,24,2176]{2,1,0:T(8,128)(2,1)S(1)}, bf16[2,24,2176]{2,1,0:T(8,128)(2,1)S(1)}, u32[]{:S(2)}, u32[]{:S(2)}) collective-permute-start(bf16[2,24,2176]{2,1,0:T(8,128)(2,1)S(1)} %collective-permute-done.5), channel_id=1, source_target_pairs={{0,2},{1,3},{2,4},{3,5},{4,6},{5,7},{6,0},{7,1},{8,10},{9,11},{10,... | collective-permute-start | bytes 626696 | tf_op jit(solution)/shard_map/ppermute | solution.py:1003
  45.3 14.9 %collective-permute-start.11 = (bf16[2,24,2176]{2,1,0:T(8,128)(2,1)S(1)}, bf16[2,24,2176]{2,1,0:T(8,128)(2,1)S(1)}, u32[]{:S(2)}, u32[]{:S(2)}) collective-permute-start(bf16[2,24,2176]{2,1,0:T(8,128)(2,1)S(1)} %get-tuple-element.150), channel_id=1, source_target_pairs={{0,1},{1,0},{2,3},{3,2},{4,5},{5,4},{6,7},{7,6},{8,9},{9,8},{10,11... | collective-permute-start | bytes 626696 | tf_op jit(solution)/shard_map/ppermute | solution.py:1004
  45.8 14.4 %collective-permute-start.12 = (bf16[2,24,2176]{2,1,0:T(8,128)(2,1)S(1)}, bf16[2,24,2176]{2,1,0:T(8,128)(2,1)S(1)}, u32[]{:S(2)}, u32[]{:S(2)}) collective-permute-start(bf16[2,24,2176]{2,1,0:T(8,128)(2,1)S(1)} %get-tuple-element.151), channel_id=1, source_target_pairs={{0,16},{8,24},{16,0},{24,8},{1,17},{9,25},{17,1},{25,9},{2,18},{10... | collective-permute-start | bytes 626696 | tf_op jit(solution)/shard_map/ppermute | solution.py:1005
  60.3 13.8 %collective-permute-start.13 = (bf16[256,768]{1,0:T(8,128)(2,1)S(1)}, bf16[256,768]{1,0:T(8,128)(2,1)S(1)}, u32[]{:S(2)}, u32[]{:S(2)}) collective-permute-start(bf16[256,768]{1,0:T(8,128)(2,1)S(1)} %collective-permute-done.8.own_ref), channel_id=1, source_target_pairs={{0,1},{1,0},{2,3},{3,2},{4,5},{5,4},{6,7},{7,6},{8,9},{9,8},{10,11... | collective-permute-start | bytes 1179656 | tf_op jit(solution)/shard_map/ppermute | solution.py:1011
  74.3 21.4 %collective-permute-start.17 = (bf16[4,48,2176]{2,1,0:T(8,128)(2,1)S(1)}, bf16[4,48,2176]{2,1,0:T(8,128)(2,1)}, u32[]{:S(2)}, u32[]{:S(2)}) collective-permute-start(bf16[4,48,2176]{2,1,0:T(8,128)(2,1)S(1)} %maximum_maximum_fusion.refs_0_), channel_id=1, source_target_pairs={{0,16},{8,24},{16,0},{24,8},{1,17},{9,25},{17,1},{25,9},{2,18},{10... | collective-permute-start | bytes 2506760 | tf_op jit(solution)/shard_map/ppermute | solution.py:1023
  75.9 19.8 %collective-permute-start.18 = (bf16[8,24,2176]{2,1,0:T(8,128)(2,1)S(1)}, bf16[8,24,2176]{2,1,0:T(8,128)(2,1)S(1)}, u32[]{:S(2)}, u32[]{:S(2)}) collective-permute-start(bf16[8,24,2176]{2,1,0:T(8,128)(2,1)S(1)} %constant_dynamic-update-slice_fusion), channel_id=1, source_target_pairs={{0,1},{1,0},{2,3},{3,2},{4,5},{5,4},{6,7},{7,6},{8,9},{9,8},{10,11... | collective-permute-start | bytes 2506760 | tf_op jit(solution)/shard_map/ppermute | solution.py:1024
  78.1 17.6 %collective-permute-start.19 = (bf16[24,2304]{1,0:T(8,128)(2,1)S(1)}, bf16[24,2304]{1,0:T(8,128)(2,1)S(1)}, u32[]{:S(2)}, u32[]{:S(2)}) collective-permute-start(bf16[24,2304]{1,0:T(8,128)(2,1)S(1)} %collective-permute-done.16), channel_id=1, source_target_pairs={{0,2},{1,3},{2,4},{3,5},{4,6},{5,7},{6,0},{7,1},{8,10},{9,11},{10,... | collective-permute-start | bytes 331784 | tf_op jit(solution)/shard_map/ppermute | solution.py:1019
  96.0 20.5 %collective-permute-start.22 = (bf16[8,48,2176]{2,1,0:T(8,128)(2,1)S(1)}, bf16[8,48,2176]{2,1,0:T(8,128)(2,1)}, u32[]{:S(2)}, u32[]{:S(2)}) collective-permute-start(bf16[8,48,2176]{2,1,0:T(8,128)(2,1)S(1)} %pad_maximum_fusion.refs_4_), channel_id=1, source_target_pairs={{0,8},{8,0},{16,24},{24,16},{1,9},{9,1},{17,25},{25,17},{2,10},{10... | collective-permute-start | bytes 5013512 | tf_op jit(solution)/shard_map/ppermute | solution.py:1044
  96.1 19.1 %collective-permute-start.20 = (bf16[4,48,2176]{2,1,0:T(8,128)(2,1)S(1)}, bf16[4,48,2176]{2,1,0:T(8,128)(2,1)}, u32[]{:S(2)}, u32[]{:S(2)}) collective-permute-start(bf16[4,48,2176]{2,1,0:T(8,128)(2,1)S(1)} %maximum_maximum_fusion.refs_0_), channel_id=1, source_target_pairs={{0,8},{8,0},{16,24},{24,16},{1,9},{9,1},{17,25},{25,17},{2,10},{10... | collective-permute-start | bytes 2506760 | tf_op jit(solution)/shard_map/ppermute | solution.py:1042
  96.6 19.9 %collective-permute-start.21 = (bf16[4,48,2176]{2,1,0:T(8,128)(2,1)}, bf16[4,48,2176]{2,1,0:T(8,128)(2,1)}, u32[]{:S(2)}, u32[]{:S(2)}) collective-permute-start(bf16[4,48,2176]{2,1,0:T(8,128)(2,1)} %collective-permute-done.17.refs_1_), channel_id=1, source_target_pairs={{0,8},{8,0},{16,24},{24,16},{1,9},{9,1},{17,25},{25,17},{2,10},{10... | collective-permute-start | bytes 2506760 | tf_op jit(solution)/shard_map/ppermute | solution.py:1043
  96.7 19.8 %all-to-all-start.1 = ((bf16[8,192,128]{2,1,0:T(8,128)(2,1)}), bf16[8,192,128]{2,1,0:T(8,128)(2,1)}, u32[]{:S(2)}, u32[]{:S(2)}) async-start(bf16[8,192,128]{2,1,0:T(8,128)(2,1)} %get-tuple-element.190), calls=%async_computation.1 | async-start | bytes 786432 | tf_op jit(solution)/shard_map/all_to_all | solution.py:1050
  102.4 12.8 %collective-permute-start.23 = (bf16[24,2304]{1,0:T(8,128)(2,1)S(1)}, bf16[24,2304]{1,0:T(8,128)(2,1)S(1)}, u32[]{:S(2)}, u32[]{:S(2)}) collective-permute-start(bf16[24,2304]{1,0:T(8,128)(2,1)S(1)} %collective-permute-done.19), channel_id=1, source_target_pairs={{0,2},{1,3},{2,4},{3,5},{4,6},{5,7},{6,0},{7,1},{8,10},{9,11},{10,... | collective-permute-start | bytes 331784 | tf_op jit(solution)/shard_map/ppermute | solution.py:1051
  133.6 15.5 %all-to-all-start.2 = ((bf16[8,192,128]{2,1,0:T(8,128)(2,1)}), bf16[8,192,128]{2,1,0:T(8,128)(2,1)S(1)}, u32[]{:S(2)}, u32[]{:S(2)}) async-start(bf16[8,192,128]{2,1,0:T(8,128)(2,1)} %get-tuple-element.211), calls=%async_computation.2 | async-start | bytes 786432 | tf_op jit(solution)/shard_map/all_to_all | solution.py:1076
  137.2 36.7 %collective-permute-start.29 = (bf16[4,48,2304]{2,1,0:T(8,128)(2,1)S(1)}, bf16[4,48,2304]{2,1,0:T(8,128)(2,1)S(1)}, u32[]{:S(2)}, u32[]{:S(2)}) collective-permute-start(bf16[4,48,2304]{2,1,0:T(8,128)(2,1)S(1)} %pad_maximum_fusion.1.refs_0_), channel_id=1, source_target_pairs={{0,16},{8,24},{16,0},{24,8},{1,17},{9,25},{17,1},{25,9},{2,18},{10... | collective-permute-start | bytes 2654216 | tf_op jit(solution)/shard_map/ppermute | solution.py:1075
  149.1 29.3 %collective-permute-start.27 = (bf16[192,2176]{1,0:T(8,128)(2,1)}, bf16[192,2176]{1,0:T(8,128)(2,1)}, u32[]{:S(2)}, u32[]{:S(2)}) collective-permute-start(bf16[192,2176]{1,0:T(8,128)(2,1)} %get-tuple-element.230), channel_id=1, source_target_pairs={{0,16},{8,24},{16,0},{24,8},{1,17},{9,25},{17,1},{25,9},{2,18},{10... | collective-permute-start | bytes 2506760 | tf_op jit(solution)/shard_map/ppermute | solution.py:1100
  152.4 21.6 %collective-permute-start.28 = (bf16[8,24,2048]{2,1,0:T(8,128)(2,1)}, bf16[8,24,2048]{2,1,0:T(8,128)(2,1)}, u32[]{:S(2)}, u32[]{:S(2)}) collective-permute-start(bf16[8,24,2048]{2,1,0:T(8,128)(2,1)} %get-tuple-element.232), channel_id=1, source_target_pairs={{0,1},{1,0},{2,3},{3,2},{4,5},{5,4},{6,7},{7,6},{8,9},{9,8},{10,11... | collective-permute-start | bytes 2359304 | tf_op jit(solution)/shard_map/ppermute | solution.py:1101
  178.4 47.9 %all-to-all-start.3 = ((bf16[8,704,128]{2,1,0:T(8,128)(2,1)}), bf16[8,704,128]{2,1,0:T(8,128)(2,1)S(1)}, u32[]{:S(2)}, u32[]{:S(2)}) async-start(bf16[8,704,128]{2,1,0:T(8,128)(2,1)} %get-tuple-element.234), calls=%async_computation.3 | async-start | bytes 2883584 | tf_op jit(solution)/shard_map/all_to_all | solution.py:1119
  184.0 26.1 %collective-permute-start.33 = (bf16[4,48,2304]{2,1,0:T(8,128)(2,1)S(1)}, bf16[4,48,2304]{2,1,0:T(8,128)(2,1)S(1)}, u32[]{:S(2)}, u32[]{:S(2)}) collective-permute-start(bf16[4,48,2304]{2,1,0:T(8,128)(2,1)S(1)} %pad_maximum_fusion.1.refs_0_), channel_id=1, source_target_pairs={{0,8},{8,0},{16,24},{24,16},{1,9},{9,1},{17,25},{25,17},{2,10},{10... | collective-permute-start | bytes 2654216 | tf_op jit(solution)/shard_map/ppermute | solution.py:1120
  184.1 26.0 %collective-permute-start.34 = (bf16[4,48,2304]{2,1,0:T(8,128)(2,1)S(1)}, bf16[4,48,2304]{2,1,0:T(8,128)(2,1)S(1)}, u32[]{:S(2)}, u32[]{:S(2)}) collective-permute-start(bf16[4,48,2304]{2,1,0:T(8,128)(2,1)S(1)} %collective-permute-done.29.refs_1_), channel_id=1, source_target_pairs={{0,8},{8,0},{16,24},{24,16},{1,9},{9,1},{17,25},{25,17},{2,10},{10... | collective-permute-start | bytes 2654216 | tf_op jit(solution)/shard_map/ppermute | solution.py:1121
  187.8 22.3 %collective-permute-start.30 = (bf16[4,24,2176]{2,1,0:T(8,128)(2,1)}, bf16[4,24,2176]{2,1,0:T(8,128)(2,1)S(1)}, u32[]{:S(2)}, u32[]{:S(2)}) collective-permute-start(bf16[4,24,2176]{2,1,0:T(8,128)(2,1)} %get-tuple-element.242), channel_id=1, source_target_pairs={{0,1},{1,0},{2,3},{3,2},{4,5},{5,4},{6,7},{7,6},{8,9},{9,8},{10,11... | collective-permute-start | bytes 1253384 | tf_op jit(solution)/shard_map/ppermute | solution.py:1129
  213.3 13.0 %collective-permute-start.35 = (bf16[2,24,4224]{2,1,0:T(8,128)(2,1)}, bf16[2,24,4224]{2,1,0:T(8,128)(2,1)S(1)}, u32[]{:S(2)}, u32[]{:S(2)}) collective-permute-start(bf16[2,24,4224]{2,1,0:T(8,128)(2,1)} %get-tuple-element.257), channel_id=1, source_target_pairs={{0,2},{1,3},{2,0},{3,1},{4,6},{5,7},{6,4},{7,5},{8,10},{9,11},{10,... | collective-permute-start | bytes 1216520 | tf_op jit(solution)/shard_map/ppermute | solution.py:1143
  229.0 13.2 %collective-permute-start.37 = (bf16[1,24,4224]{2,1,0:T(8,128)(2,1)}, bf16[1,24,4224]{2,1,0:T(8,128)(2,1)S(1)}, u32[]{:S(2)}, u32[]{:S(2)}) collective-permute-start(bf16[1,24,4224]{2,1,0:T(8,128)(2,1)} %get-tuple-element.273), channel_id=1, source_target_pairs={{0,4},{1,5},{2,6},{3,7},{4,0},{5,1},{6,2},{7,3},{8,12},{9,13},{10,... | collective-permute-start | bytes 608264 | tf_op jit(solution)/shard_map/ppermute | solution.py:1150
  230.6 14.3 %all-to-all-start.4 = ((bf16[8,24,384]{2,1,0:T(8,128)(2,1)}), bf16[8,24,384]{2,1,0:T(8,128)(2,1)S(1)}, u32[]{:S(2)}, u32[]{:S(2)}) async-start(bf16[8,24,384]{2,1,0:T(8,128)(2,1)} %bitcast.45), calls=%async_computation.4 | async-start | bytes 294912 | tf_op jit(solution)/shard_map/all_to_all | solution.py:1160
  (37 other events, 349.4 us)

commit v5 on v4

--- a/solution.py
+++ b/solution.py
@@ -12,6 +12,7 @@
 SLOTS = 2
 LANES = SLOTS * HD
 UNITS = 3
+IDS = 16
 GRAIN = 128
 KEY_TILE = 512
 CHUNK = 384
@@ -139,10 +140,14 @@
     )(at, w_parts)
 
 
-def project_kernel(at_ref, own_ref, other_ref, w_ref, gains_ref, cos_ref, sin_ref, *refs):
+def project_kernel(count, at_ref, *refs):
+    x_refs = refs[:count]
+    w_ref, gains_ref, cos_ref, sin_ref = refs[count : count + 4]
     hidden_ref, qkv_ref, turned_ref = refs[-3:]
-    own = pl.program_id(0) == 0
-    x = jnp.where(own, own_ref[...], other_ref[...]).astype(f32)
+    x = x_refs[0][...]
+    for i in range(1, count):
+        x = jnp.where(pl.program_id(0) == i, x_refs[i][...], x)
+    x = x.astype(f32)
     normed, _ = norm_rows(x)
     hidden = (normed * gains_ref[:1, :]).astype(bf16)
     hidden_ref[...] = hidden
@@ -161,109 +166,68 @@
     turned_ref[LANES:, :] = jnp.transpose(values).astype(bf16)
 
 
-def project(at, own, other, w_heads, gains, cosine, sine, total, held):
-    rows, width = own.shape
+def project(at, blocks, w_heads, gains, cosine, sine, total, held):
+    rows, width = blocks[0].shape
+    count = len(blocks)
     fixed = lambda *shape: pl.BlockSpec(shape, lambda i, at: (0,) * len(shape))
-    block = lambda i, at: at[0] * 2 + (at[1] ^ i)
-    tall = lambda width: pl.BlockSpec((rows, width), lambda i, at: (block(i, at), 0))
+    tall = lambda width: pl.BlockSpec((rows, width), lambda i, at: (at[i], 0))
     shapes = [
         jax.ShapeDtypeStruct((total, width), bf16),
         jax.ShapeDtypeStruct((total, 3 * LANES), bf16),
         jax.ShapeDtypeStruct((2 * LANES, total), bf16),
     ]
     return pl.pallas_call(
-        project_kernel,
+        functools.partial(project_kernel, count),
         grid_spec=pltpu.PrefetchScalarGridSpec(
             num_scalar_prefetch=1,
-            grid=(2,),
-            in_specs=[
-                fixed(rows, width),
-                fixed(rows, width),
-                fixed(width, 3 * LANES),
-                fixed(8, width),
-                tall(LANES),
-                tall(LANES),
-            ]
+            grid=(count,),
+            in_specs=[fixed(rows, width)] * count
+            + [fixed(width, 3 * LANES), fixed(8, width), tall(LANES), tall(LANES)]
             + [pl.BlockSpec(memory_space=pl.ANY) for _ in held],
             out_specs=[
                 tall(width),
                 tall(3 * LANES),
-                pl.BlockSpec((2 * LANES, rows), lambda i, at: (0, block(i, at))),
+                pl.BlockSpec((2 * LANES, rows), lambda i, at: (0, at[i])),
             ],
         ),
         out_shape=shapes,
-        input_output_aliases={7 + i: i for i in range(len(held))},
+        input_output_aliases={count + 5 + i: i for i in range(len(held))},
         compiler_params=params(),
         cost_estimate=pl.CostEstimate(
-            flops=2 * 2 * rows * width * 3 * LANES, bytes_accessed=6 << 20, transcendentals=0
+            flops=2 * count * rows * width * 3 * LANES,
+            bytes_accessed=3 * count << 20,
+            transcendentals=0,
         ),
         name="project",
-    )(at, own, other, w_heads, gains, cosine, sine, *held)
-
-
-def gather_rows(units_ref, ref, units, part):
+    )(at, *blocks, w_heads, gains, cosine, sine, *held)
+
+
+def gather_rows(units_ref, ref, part):
     lane = lax.broadcasted_iota(jnp.int32, (part, LANES), 1)
     chunks = []
-    for i in range(units):
-        start = pl.multiple_of(units_ref[units + i] * part, part)
+    for unit in range(UNITS):
+        start = pl.multiple_of(units_ref[UNITS + unit] * part, part)
         chunk = ref[pl.ds(start, part), :]
-        chunks.append(jnp.where(lane // HD == units_ref[i], chunk, jnp.zeros_like(chunk)))
+        chunks.append(jnp.where(lane // HD == units_ref[unit], chunk, jnp.zeros_like(chunk)))
     return jnp.concatenate(chunks, axis=0)
 
 
-def scatter_rows(units_ref, acc_ref, values, units, part):
-    lane = lax.broadcasted_iota(jnp.int32, (part, LANES), 1)
-    acc_ref[...] = jnp.zeros(acc_ref.shape, f32)
-    for i in range(units):
-        start = pl.multiple_of(units_ref[units + i] * part, part)
-        chunk = values[i * part : (i + 1) * part]
-        acc_ref[pl.ds(start, part), :] += jnp.where(lane // HD == units_ref[i], chunk, 0.0)
-
-
-def pack_units(units_ref, acc_ref, part):
-    half = part // 2
-
-    def slab(unit, start, size, want):
-        values = acc_ref[pl.ds(start, size), :]
-        here = jnp.full(values.shape, units_ref[unit], jnp.int32) == want
-        return jnp.where(here, values, pltpu.roll(values, HD, 1))
-
-    def beside(left, right):
-        left_side = lax.broadcasted_iota(jnp.int32, left.shape, 1) < HD
-        return jnp.where(left_side, left, right)
-
-    starts = [pl.multiple_of(units_ref[UNITS + unit] * part, part) for unit in range(UNITS)]
-    top = beside(slab(0, starts[0], part, 0), slab(1, starts[1], part, 1))
-    low = beside(slab(2, starts[2], half, 0), slab(2, starts[2] + half, half, 1))
-    return jnp.concatenate([top, low], axis=0)
-
-
-def unpack_units(units_ref, packed, part):
-    half = part // 2
+def slot_rows(units_ref, unit):
+    return pl.ds(pl.multiple_of(units_ref[unit] * HD, HD), HD)
+
+
+def pack(pieces):
+    half = pieces[2].shape[1] // 2
+    top = jnp.concatenate(pieces[:2], axis=0)
+    low = jnp.concatenate([pieces[2][:, :half], pieces[2][:, half:]], axis=0)
+    return jnp.concatenate([jnp.transpose(top), jnp.transpose(low)], axis=0).astype(bf16)
+
+
+def unpack(packed, part):
     values = packed.astype(f32)
-    turned = pltpu.roll(values, HD, 1)
-    side = lax.broadcasted_iota(jnp.int32, values.shape, 1) // HD
-
-    def piece(unit, home, start, size):
-        slot = jnp.full(values.shape, units_ref[unit], jnp.int32)
-        chosen = jnp.where(slot == home, values, turned)
-        return jnp.where(side == slot, chosen, 0.0)[start : start + size]
-
-    return jnp.concatenate(
-        [
-            piece(0, 0, 0, part),
-            piece(1, 1, 0, part),
-            piece(2, 0, part, half),
-            piece(2, 1, part, half),
-        ],
-        axis=0,
-    ).astype(bf16)
-
-
-def across(slab, wide):
-    if wide <= LANES:
-        return slab[:, :wide]
-    return jnp.concatenate([slab] * (wide // LANES), axis=1)
+    top = jnp.transpose(values[:part])
+    low = jnp.transpose(values[part:])
+    return [top[:HD], top[HD:], jnp.concatenate([low[:HD], low[HD:]], axis=1)]
 
 
 def fold(values, reduce):
@@ -275,18 +239,22 @@
     return pl.ds(pl.multiple_of(base_ref[block] * GRAIN + at * tile, GRAIN), tile)
 
 
-def attend_kernel(units, tile, base_ref, count_ref, units_ref, q_ref, k_ref, vt_ref, doc_ref, doc_q_ref,
+def masked(scores, base_ref, block, at, tile, range_ref):
+    key = lax.broadcasted_iota(jnp.int32, scores.shape, 0) + (base_ref[block] * GRAIN + at * tile)
+    same = (key >= range_ref[0, :1, :]) & (key < range_ref[0, 1:2, :])
+    return jnp.where(same, scores, NEG)
+
+
+def attend_kernel(tile, base_ref, count_ref, units_ref, q_ref, k_ref, vt_ref, range_ref,
                   low_ref, att_ref, lse_ref, s_ref, acc_ref):
     block = pl.program_id(0)
     wide = s_ref.shape[1]
-    part = wide // units
-    queries = gather_rows(units_ref, q_ref, units, part)
-    doc_q = doc_q_ref[0]
+    part = wide // UNITS
+    queries = gather_rows(units_ref, q_ref, part)
 
     def score(at, top):
         span = tile_span(base_ref, block, at, tile)
-        scores = dot_tt(k_ref[span, :], queries)
-        scores = jnp.where(across(doc_ref[span, :], wide) == doc_q, scores, NEG)
+        scores = masked(dot_tt(k_ref[span, :], queries), base_ref, block, at, tile, range_ref)
         s_ref[span, :] = scores
         return jnp.maximum(top, fold(scores, jnp.max))
 
@@ -306,20 +274,23 @@
         0, count, weigh, (jnp.zeros((8, wide), f32), jnp.zeros((LANES, wide), f32))
     )
     total = jnp.sum(total, axis=0, keepdims=True)
-    att = accum / total
-    att_ref[0] = att
     lse_ref[0] = top + jnp.log(total)
-    scatter_rows(units_ref, acc_ref, jnp.transpose(att), units, part)
-    low_ref[0] = pack_units(units_ref, acc_ref, part).astype(bf16)
-
-
-def attend(base, tiles, unit_places, qkv, turned, doc_slab, doc_q, rows, tile):
+    acc_ref[...] = accum / total
+    pieces = [
+        acc_ref[slot_rows(units_ref, unit), unit * part : (unit + 1) * part]
+        for unit in range(UNITS)
+    ]
+    att_ref[0] = jnp.concatenate(pieces, axis=1)
+    low_ref[0] = pack(pieces)
+
+
+def attend(base, tiles, unit_places, qkv, turned, ranges, rows, tile):
     total = qkv.shape[0]
     count = total // rows
-    units = unit_places.shape[0] // 2
-    wide = doc_q.shape[2]
+    wide = ranges.shape[2]
+    each = lambda *shape: pl.BlockSpec((1,) + shape, lambda i, *s: (i, 0, 0))
     return pl.pallas_call(
-        functools.partial(attend_kernel, units, tile),
+        functools.partial(attend_kernel, tile),
         grid_spec=pltpu.PrefetchScalarGridSpec(
             num_scalar_prefetch=3,
             grid=(count,),
@@ -327,19 +298,14 @@
                 pl.BlockSpec((rows, LANES), lambda i, *s: (i, 0)),
                 pl.BlockSpec((total, LANES), lambda i, *s: (0, 1)),
                 pl.BlockSpec((LANES, total), lambda i, *s: (1, 0)),
-                pl.BlockSpec((total, LANES), lambda i, *s: (0, 0)),
-                pl.BlockSpec((1, 1, wide), lambda i, *s: (i, 0, 0)),
+                each(2, wide),
             ],
-            out_specs=[
-                pl.BlockSpec((1, wide // 2, LANES), lambda i, *s: (i, 0, 0)),
-                pl.BlockSpec((1, LANES, wide), lambda i, *s: (i, 0, 0)),
-                pl.BlockSpec((1, 1, wide), lambda i, *s: (i, 0, 0)),
-            ],
-            scratch_shapes=[pltpu.VMEM((total, wide), f32), pltpu.VMEM((rows, LANES), f32)],
+            out_specs=[each(wide // 2, LANES), each(HD, wide), each(1, wide)],
+            scratch_shapes=[pltpu.VMEM((total, wide), f32), pltpu.VMEM((LANES, wide), f32)],
         ),
         out_shape=[
             jax.ShapeDtypeStruct((count, wide // 2, LANES), bf16),
-            jax.ShapeDtypeStruct((count, LANES, wide), f32),
+            jax.ShapeDtypeStruct((count, HD, wide), f32),
             jax.ShapeDtypeStruct((count, 1, wide), f32),
         ],
         compiler_params=params(),
@@ -349,58 +315,73 @@
             transcendentals=count * wide * total,
         ),
         name="attend",
-    )(base, tiles, unit_places, qkv, qkv, turned, doc_slab, doc_q)
-
-
-def attend_back_kernel(units, tile, base_ref, count_ref, units_ref, q_ref, k_ref, v_ref, kt_ref, doc_ref,
-                       doc_q_ref, grad_ref, att_ref, lse_ref, cos_ref, sin_ref,
-                       out_ref, send_ref, dk_ref, dv_ref, acc_ref):
+    )(base, tiles, unit_places, qkv, qkv, turned, ranges)
+
+
+def attend_back_kernel(tile, base_ref, count_ref, units_ref, q_ref, k_ref, v_ref, kt_ref, range_ref,
+                       grad_ref, att_ref, lse_ref, cos_q_ref, sin_q_ref, cos_hbm, sin_hbm,
+                       out_ref, send_ref, dk_ref, dv_ref, acc_ref, gt_ref, full_ref, cos_ref,
+                       sin_ref, sems):
     block = pl.program_id(0)
     count = pl.num_programs(0)
-    rows = acc_ref.shape[0]
-    wide = att_ref.shape[2]
-    part = wide // units
+    rows = full_ref.shape[1]
+    wide = acc_ref.shape[1]
+    part = wide // UNITS
+    tables = [
+        pltpu.make_async_copy(cos_hbm, cos_ref, sems.at[0]),
+        pltpu.make_async_copy(sin_hbm, sin_ref, sems.at[1]),
+    ]
 
     @pl.when(block == 0)
     def _():
+        for table in tables:
+            table.start()
         dk_ref[...] = jnp.zeros(dk_ref.shape, f32)
         dv_ref[...] = jnp.zeros(dv_ref.shape, f32)
-
-    def turn_back(values, span):
-        return values * cos_ref[span, :] - rotate_half(values * sin_ref[span, :])
-
-    queries = gather_rows(units_ref, q_ref, units, part)
-    grads = unpack_units(units_ref, grad_ref[0], part)
-    delta = jnp.sum(jnp.transpose(grads.astype(f32)) * att_ref[0], axis=0, keepdims=True)
+        gt_ref[...] = jnp.zeros(gt_ref.shape, bf16)
+        full_ref[...] = jnp.zeros(full_ref.shape, f32)
+
+    queries = gather_rows(units_ref, q_ref, part)
+    grads = unpack(grad_ref[0], part)
+    delta = jnp.sum(jnp.concatenate(grads, axis=1) * att_ref[0], axis=0, keepdims=True)
+    for unit, piece in enumerate(grads):
+        columns = slice(unit * part, (unit + 1) * part)
+        gt_ref[slot_rows(units_ref, unit), columns] = piece.astype(bf16)
     log_sum = lse_ref[0]
-    doc_q = doc_q_ref[0]
 
     def step(at, grad_query):
         span = tile_span(base_ref, block, at, tile)
-        scores = dot_tt(k_ref[span, :], queries)
-        grad_probs = dot_tt(v_ref[span, :], grads)
-        scores = jnp.where(across(doc_ref[span, :], wide) == doc_q, scores, NEG)
+        grads_t = gt_ref[...]
+        scores = masked(dot_tt(k_ref[span, :], queries), base_ref, block, at, tile, range_ref)
+        grad_probs = jnp.dot(v_ref[span, :], grads_t, preferred_element_type=f32)
         probs = jnp.exp(scores - log_sum)
-        dv_ref[span, :] += jnp.dot(probs.astype(bf16), grads, preferred_element_type=f32)
+        dv_ref[span, :] += dot_tt(probs.astype(bf16), grads_t)
         grad_scores = (probs * (grad_probs - delta)).astype(bf16)
         dk_ref[span, :] += jnp.dot(grad_scores, queries, preferred_element_type=f32)
         return grad_query + jnp.dot(kt_ref[:, span], grad_scores, preferred_element_type=f32)
 
-    grad_query = lax.fori_loop(
-        0, count_ref[block], step, jnp.zeros((LANES, wide), f32)
-    )
-    scatter_rows(units_ref, acc_ref, jnp.transpose(grad_query) * HD**-0.5, units, part)
-    here = pl.ds(pl.multiple_of(block * rows, rows), rows)
-    turned = turn_back(acc_ref[...], here)
-    out_ref[block, :, :LANES] = turned.astype(bf16)
-    acc_ref[...] = turned
-    send_ref[block, : wide // 2, :] = pack_units(units_ref, acc_ref, part).astype(bf16)
+    acc_ref[...] = lax.fori_loop(0, count_ref[block], step, jnp.zeros((LANES, wide), f32))
+    pieces = []
+    for unit in range(UNITS):
+        columns = slice(unit * part, (unit + 1) * part)
+        piece = acc_ref[slot_rows(units_ref, unit), columns] * HD**-0.5
+        turned = piece * sin_q_ref[0, :, columns]
+        turned = jnp.concatenate([-turned[HD // 2 :], turned[: HD // 2]], axis=0)
+        pieces.append(piece * cos_q_ref[0, :, columns] - turned)
+    send_ref[block, : wide // 2, :] = pack(pieces)
+    place_units(units_ref, full_ref, pieces, part)
+    out_ref[block, :, :LANES] = jnp.transpose(full_ref[...]).astype(bf16)
 
     @pl.when(block == count - 1)
     def _():
+        for table in tables:
+            table.wait()
+
         def finish(at, carry):
             span = pl.ds(pl.multiple_of(at * rows, rows), rows)
-            keys = turn_back(dk_ref[span, :], span).astype(bf16)
+            keys = dk_ref[span, :]
+            keys = keys * cos_ref[span, :] - rotate_half(keys * sin_ref[span, :])
+            keys = keys.astype(bf16)
             values = dv_ref[span, :].astype(bf16)
             out_ref[at, :, LANES : 2 * LANES] = keys
             out_ref[at, :, 2 * LANES :] = values
@@ -411,16 +392,29 @@
         lax.fori_loop(0, count, finish, 0)
 
 
-def attend_back(base, tiles, unit_places, qkv, turned, doc_slab, doc_q, grads, att, lse, cosine, sine,
+def place_units(units_ref, full_ref, pieces, part):
+    rows = full_ref.shape[1]
+    for split in range(rows // part):
+        for unit, piece in enumerate(pieces):
+
+            @pl.when(units_ref[UNITS + unit] == split)
+            def _():
+                columns = slice(split * part, (split + 1) * part)
+                full_ref[slot_rows(units_ref, unit), columns] = piece
+
+
+def attend_back(base, tiles, unit_places, qkv, turned, ranges, grads, att, lse, tables_q, tables,
                 rows, tile):
     total = qkv.shape[0]
     count = total // rows
-    units = unit_places.shape[0] // 2
-    wide = doc_q.shape[2]
+    wide = ranges.shape[2]
     whole = lambda part: pl.BlockSpec((total, LANES), lambda i, *s: (0, part))
     each = lambda *shape: pl.BlockSpec((1,) + shape, lambda i, *s: (i, 0, 0))
+    kept = lambda *shape: pl.BlockSpec(shape, lambda i, *s: (0, 0, 0))
+    outside = pl.BlockSpec(memory_space=pl.ANY)
+    table = pltpu.VMEM((total, LANES), f32)
     return pl.pallas_call(
-        functools.partial(attend_back_kernel, units, tile),
+        functools.partial(attend_back_kernel, tile),
         grid_spec=pltpu.PrefetchScalarGridSpec(
             num_scalar_prefetch=3,
             grid=(count,),
@@ -429,22 +423,28 @@
                 whole(1),
                 whole(2),
                 pl.BlockSpec((LANES, total), lambda i, *s: (0, 0)),
-                whole(0),
+                each(2, wide),
+                each(wide // 2, LANES),
+                each(HD, wide),
                 each(1, wide),
-                each(wide // 2, LANES),
-                each(LANES, wide),
-                each(1, wide),
-                whole(0),
-                whole(0),
+                each(HD, wide),
+                each(HD, wide),
+                outside,
+                outside,
             ],
             out_specs=[
-                pl.BlockSpec((count, rows, 3 * LANES), lambda i, *s: (0, 0, 0)),
-                pl.BlockSpec((count, wide // 2 + 2 * rows, LANES), lambda i, *s: (0, 0, 0)),
+                kept(count, rows, 3 * LANES),
+                kept(count, wide // 2 + 2 * rows, LANES),
             ],
             scratch_shapes=[
-                pltpu.VMEM((total, LANES), f32),
-                pltpu.VMEM((total, LANES), f32),
-                pltpu.VMEM((rows, LANES), f32),
+                table,
+                table,
+                pltpu.VMEM((LANES, wide), f32),
+                pltpu.VMEM((LANES, wide), bf16),
+                pltpu.VMEM((LANES, rows), f32),
+                table,
+                table,
+                pltpu.SemaphoreType.DMA((2,)),
             ],
         ),
         out_shape=[
@@ -458,7 +458,7 @@
             transcendentals=count * wide * total,
         ),
         name="attend_back",
-    )(base, tiles, unit_places, qkv, qkv, qkv, turned, doc_slab, doc_q, grads, att, lse, cosine, sine)
+    )(base, tiles, unit_places, qkv, qkv, qkv, turned, ranges, grads, att, lse, *tables_q, *tables)
 
 
 def lanes_of(slab, at, want):
@@ -939,7 +939,6 @@
             half = jnp.arange(LANES) % (HD // 2)
             rates = THETA ** (-2.0 * half.astype(f32) / HD)
             angles = spots * rates[None, :]
-            doc_slab = jnp.broadcast_to(docs.reshape(total, 1), (total, LANES))
             edges = docs.reshape(total // GRAIN, GRAIN)
             lo = jnp.sum((edges[None, :, -1] < docs[:, :1]).astype(jnp.int32), axis=1)
             hi = jnp.sum((edges[None, :, 0] <= docs[:, rows - 1 :]).astype(jnp.int32), axis=1)
@@ -949,13 +948,27 @@
             first_head = jnp.minimum(units * me // splits, heads - SLOTS)
             unit_places = jnp.concatenate([unit // splits - first_head, unit % splits])
             pick = (unit % splits)[:, None] == jnp.arange(splits, dtype=jnp.int32)[None, :]
-            doc_q = jnp.sum(
-                jnp.where(pick[None, :, :, None], docs.reshape(ctx, 1, splits, part), 0), axis=2
+            own_part = lambda array: jnp.sum(
+                jnp.where(pick[None, :, :, None], array.reshape(ctx, 1, splits, part), 0), axis=2
             ).reshape(ctx, 1, units * part)
+            doc_q = own_part(docs)
+            spot_q = own_part(spots)
+            ids = jnp.arange(IDS + 1, dtype=jnp.int32)
+            before = jnp.sum((docs.reshape(1, total) < ids[:, None]).astype(jnp.int32), axis=1)
+            is_id = doc_q == ids[None, :-1, None]
+            bounds = [
+                jnp.sum(jnp.where(is_id, edge[None, :, None], 0), axis=1, keepdims=True)
+                for edge in (before[:-1], before[1:])
+            ]
             return (
-                jnp.cos(angles), jnp.sin(angles), doc_slab, base, count,
-                unit_places.astype(jnp.int32), doc_q,
-            )
+                jnp.cos(angles), jnp.sin(angles), base, count, unit_places.astype(jnp.int32),
+                jnp.concatenate(bounds, axis=1), spot_q,
+            )
+
+        def query_tables(spot_q):
+            half = jnp.arange(HD) % (HD // 2)
+            angles = THETA ** (-2.0 * half.astype(f32) / HD)[None, :, None] * spot_q
+            return jnp.cos(angles), jnp.sin(angles)
 
         sent = spread(first, w_qkv, gain_attn, gain_mlp, segment_ids, positions)
         sent = lax.all_to_all(sent, "ctx", 0, 0, tiled=True)
@@ -987,15 +1000,16 @@
             own[2], other[1], near[2], low_a, low_b, w_parts, known = gate(
                 own[2], other[1], near[2], low_a, low_b, w_parts, known
             )
-        cosine, sine, doc_slab, base, count, unit_places, doc_q = known
+        cosine, sine, base, count, unit_places, ranges, spot_q = known
 
         w_heads, gains = ready(masks, mine.astype(jnp.int32).reshape(1), w_parts)
 
-        def project_pair(step, held):
-            at = jnp.stack([(me // 2 + outer - step) % outer, me % 2]).astype(jnp.int32)
-            return project(
-                at, own[step], other[step], w_heads, gains, cosine, sine, total, held
-            )
+        def project_some(blocks, places, held):
+            at = jnp.stack(places).astype(jnp.int32)
+            return project(at, blocks, w_heads, gains, cosine, sine, total, held)
+
+        def came_from(step, flip):
+            return (me // 2 + outer - step) % outer * 2 + (me % 2 + flip) % 2
 
         if by_hand:
             own.append(lax.ppermute(own[2], "ctx", turn(1)))
@@ -1003,7 +1017,11 @@
             near.append(lax.ppermute(near[2], "ctx", turn(1)))
             next_a = lax.ppermute(low_a, "ctx", swap)
             next_b = lax.ppermute(low_b, "fsdp", by_y)
-            held = project_pair(1, project_pair(0, []))
+            held = []
+            for step in range(2):
+                held = project_some(
+                    [own[step], other[step]], [came_from(step, 0), came_from(step, 1)], held
+                )
             own[3], other[2], near[3], next_a, next_b, held, late = gate(
                 own[3], other[2], near[3], next_a, next_b, held, w_qkv
             )
@@ -1013,31 +1031,35 @@
             high_b = jnp.stack([near[2][1], near[3][1]])
             past_a = lax.ppermute(high_a, "ctx", swap)
             past_b = lax.ppermute(high_b, "fsdp", by_y)
-            held = project_pair(2, held)
+            held = project_some(
+                [own[2], other[2], own[3]],
+                [came_from(2, 0), came_from(2, 1), came_from(3, 0)], held,
+            )
             ring_c = [late, lax.ppermute(late, "ctx", turn(1))]
             other[3], past_a, past_b, held, ring_c = gate(other[3], past_a, past_b, held, ring_c)
-            ring_c.append(lax.ppermute(ring_c[1], "ctx", turn(1)))
+            ring_c = jnp.stack(ring_c)
+            ring_c = [ring_c, lax.ppermute(ring_c, "ctx", turn(2))]
 
             pair_a = jnp.concatenate([weave(low_a, next_a), weave(high_a, past_a)])
             pair_b = jnp.concatenate([low_b, next_b, high_b, past_b])
             far_a = lax.ppermute(pair_a, "fsdp", by_y)
             far_b = lax.ppermute(pair_b, "ctx", swap)
-            held = project_pair(3, held)
+            held = project_some([other[3]], [came_from(3, 1)], held)
         else:
             blocks = lax.all_gather(tokens[0], "ctx", axis=0, tiled=True)
-            blocks = blocks.reshape(outer, 2, rows, width)
+            blocks = blocks.reshape(ctx, rows, width)
             held = []
-            for step in range(outer):
-                at = jnp.asarray([step, 0], jnp.int32)
-                held = project(
-                    at, blocks[step, 0], blocks[step, 1], w_heads, gains, cosine, sine, total, held
+            for c in range(0, ctx, 2):
+                held = project_some(
+                    [blocks[c], blocks[c + 1]], [jnp.int32(c), jnp.int32(c + 1)], held
                 )
         hidden_one, qkv, turned = held
         att_low, att, lse = attend(
-            base, count, unit_places, qkv, turned, doc_slab, doc_q, rows, tile
+            base, count, unit_places, qkv, turned, ranges, rows, tile
         )
         if by_hand:
-            att_low, far_a, far_b, ring_c = gate(att_low, far_a, far_b, ring_c)
+            att_low, far_a, far_b, ring_c, spot_q = gate(att_low, far_a, far_b, ring_c, spot_q)
+            tables_q = query_tables(spot_q)
             pair_b = weave(pair_b, far_b)
             arrays = [pair_a, far_a, lax.ppermute(pair_a, "fsdp", by_core),
                       lax.ppermute(far_a, "fsdp", by_core),
@@ -1048,12 +1070,12 @@
                        + [(flip + 2 * near, back) for near in (0, 1) for back in (2, 3)]
                        for flip in range(2)]
             att_in = lax.all_to_all(att_low, "ctx", 0, 0, tiled=True)
-            ring_c.append(lax.ppermute(ring_c[2], "ctx", turn(1)))
-            pair_c = jnp.stack(ring_c)
-            att_in, arrays, pair_c = gate(att_in, arrays, pair_c)
+            pair_c = jnp.concatenate(ring_c)
+            att_in, arrays, pair_c, tables_q = gate(att_in, arrays, pair_c, tables_q)
             near_c = lax.ppermute(pair_c, "ctx", swap)
         else:
             att_in = lax.all_to_all(att_low, "ctx", 0, 0, tiled=True)
+            tables_q = query_tables(spot_q)
             every = lax.all_gather(packed, AXES, axis=0, tiled=True)
             arrays = [every[None, :, :cut], every[None, :, cut:]]
             metas_a = metas_b = [[(0, 0)]]
@@ -1109,8 +1131,8 @@
             grad_packed = grad_packed.astype(f32)
 
         grad_joined, grad_sent = attend_back(
-            base, count, unit_places, qkv, turned, doc_slab, doc_q, grad_heads, att, lse, cosine,
-            sine, rows, tile,
+            base, count, unit_places, qkv, turned, ranges, grad_heads, att, lse, tables_q,
+            (cosine, sine), rows, tile,
         )
         if by_hand:
             grad_joined, grad_sent, mine_a, got_a, mine_b, got_b, pair_c, far_c = gate(

time: 248 us -> 243 us (0.980)
  waiting for transfers between devices: 59.6 us -> 50 us
  other arithmetic: 14.9 us -> 21 us
  Pallas kernels: 103 us -> 108 us
  starting transfers between devices: 61.1 us -> 56.5 us
    ppermute x2 -> x1, waiting for transfers between devices: 10.2 us -> 0.01 us  [on_device(): ring_c = [ring_c, lax.ppermute(ring_c, 'ctx', turn(2))]]
    all_to_all x1, waiting for transfers between devices: 1.23 us -> 7.53 us  [on_device(): att_in = lax.all_to_all(att_low, 'ctx', 0, 0, tiled=True)]
    pallas_call x6, Pallas kernels: 51.8 us -> 56.6 us  [the longest x1 23.6 us: attend_back(): pl.pallas_call(functools.partial(attend_back_kernel, tile), grid_spec=plt...]
    sin x0 -> x1, other arithmetic: none -> 3.86 us  [query_tables(): return (jnp.cos(angles), jnp.sin(angles))]
    ppermute x1, waiting for transfers between devices: 4.41 us -> 1.01 us  [on_device(): got_a = lax.ppermute(other_a, 'fsdp', by_y)]
  transfers between devices with their start and end apart: 43 -> 42, of which waited for: 16 -> 16; matrix products, arithmetic and copies ran while one was open for 7% -> 9% of each run, Pallas kernels for 39% -> 42%
where the time goes in v5:
time: 243 us; the launch traced here: 242 us
  Pallas kernels  108 us (44%)
  starting transfers between devices  56.5 us (23%)
  waiting for transfers between devices  50 us (21%)
  other arithmetic  21 us (9%)
  local copies, waits for them, and re-layouts  4.62 us (2%)
    pallas_call x1, Pallas kernels, attend_back(): pl.pallas_call(functools.partial(attend_back_kernel, tile), grid_spec=plt...  23.6 us
    pallas_call x4, Pallas kernels, project(): pl.pallas_call(functools.partial(project_kernel, count), grid_spec=pltpu....  18.1 us
    pallas_call x1, Pallas kernels, attend(): pl.pallas_call(functools.partial(attend_kernel, tile), grid_spec=pltpu.Pr...  14.9 us
    pallas_call x2, Pallas kernels, weight_grads(): pl.pallas_call(functools.partial(kernel, len(operands) // 2, cut), in_spe...  11.4 us
    pallas_call x1, Pallas kernels, middle_stage(): pl.pallas_call(functools.partial(middle_kernel, heads, splits, metas, arr...  10.4 us
    pallas_call x4, Pallas kernels, add_halves(): pl.pallas_call(functools.partial(add_halves_kernel, [pair[3] for pair in...  9.42 us
    ppermute x1, waiting for transfers between devices, on_device(): got_a = lax.ppermute(other_a, 'ctx', swap)  8.67 us
    all_to_all x1, waiting for transfers between devices, on_device(): att_in = lax.all_to_all(att_low, 'ctx', 0, 0, tiled=True)  7.53 us
  transfers between devices with their start and end apart: 42, of which 16 were waited for; matrix products, arithmetic and copies ran while one was open for 9% of the time, Pallas kernels for 42%

profile of v5, /device:TPU:0, one launch (start us, length us, event | category | flops | bytes accessed | tf_op | source)
XLA Modules:
  0.0 241.6 jit_solution(14617180300189889088)
XLA Ops:
  0.6 3.1 %collective-permute-start = (bf16[256,768]{1,0:T(8,128)(2,1)}, bf16[256,768]{1,0:T(8,128)(2,1)S(1)}, u32[]{:S(2)}, u32[]{:S(2)}) collective-permute-start(bf16[256,768]{1,0:T(8,128)(2,1)} %bitcast.137), channel_id=1, source_target_pairs={{0,2},{1,3},{2,4},{3,5},{4,6},{5,7},{6,0},{7,1},{8,10},{9,11},{10,... | collective-permute-start | bytes 1179656 | tf_op jit(solution)/shard_map/ppermute | solution.py:981
  9.6 3.5 %all-to-all-start = ((bf16[8,32,512]{2,1,0:T(8,128)(2,1)}), bf16[8,32,512]{2,1,0:T(8,128)(2,1)S(1)}, u32[]{:S(2)}, u32[]{:S(2)}) async-start(bf16[8,32,512]{2,1,0:T(8,128)(2,1)} %spread.1), calls=%async_computation | async-start | bytes 524288 | tf_op jit(solution)/shard_map/all_to_all | solution.py:974
  15.8 4.6 %collective-permute-done.2 = bf16[2,24,2176]{2,1,0:T(8,128)(2,1)S(1)} collective-permute-done((bf16[2,24,2176]{2,1,0:T(8,128)(2,1)S(1)}, bf16[2,24,2176]{2,1,0:T(8,128)(2,1)S(1)}, u32[]{:S(2)}, u32[]{:S(2)}) %collective-permute-start.2) | collective-permute-done | bytes 208928 | tf_op jit(solution)/shard_map/ppermute | solution.py:983
  20.4 4.7 %all-to-all-done = bf16[8,32,512]{2,1,0:T(8,128)(2,1)S(1)} async-done(((bf16[8,32,512]{2,1,0:T(8,128)(2,1)}), bf16[8,32,512]{2,1,0:T(8,128)(2,1)S(1)}, u32[]{:S(2)}, u32[]{:S(2)}) %all-to-all-start) | async-done | bytes 262176 | tf_op jit(solution)/shard_map/all_to_all | solution.py:974
  29.5 5.6 %multiply_sine_fusion = (f32[2048,128]{1,0:T(8,128)}, f32[2048,128]{1,0:T(8,128)}) fusion(f32[128]{0:T(128)S(1)} %fusion.22, f32[2048]{0:T(1024)S(1)} %bitcast.161), kind=kLoop, calls=%fused_computation.1 | loop fusion | flops 262144 | bytes 2105856 | tf_op jit(solution)/shard_map/sin | solution.py:964
  38.8 3.7 %collective-permute-done.5 = bf16[2,24,2176]{2,1,0:T(8,128)(2,1)S(1)} collective-permute-done((bf16[2,24,2176]{2,1,0:T(8,128)(2,1)S(1)}, bf16[2,24,2176]{2,1,0:T(8,128)(2,1)S(1)}, u32[]{:S(2)}, u32[]{:S(2)}) %collective-permute-start.5) | collective-permute-done | bytes 208928 | tf_op jit(solution)/shard_map/ppermute | solution.py:997
  46.2 2.1 ready.1
  48.2 4.7 %project.4 = (bf16[2048,768]{1,0:T(8,128)(2,1)}, bf16[2048,384]{1,0:T(8,128)(2,1)}, bf16[256,2048]{1,0:T(8,128)(2,1)}) custom-call(s32[2]{0:T(128)} %pad_add_fusion.4.at_ref, bf16[256,768]{1,0:T(8,128)(2,1)} %bitcast.139, bf16[256,768]{1,0:T(8,128)(2,1)} %copy-done.19, bf16[768,512]{1,0:T(8,128)(2,1)} %get-tuple-element.156.refs_2_.refs_3_.refs_1_, ...), custom_call_target="tpu_custom_call" | custom-call | flops 301989888 | bytes 6291456 | tf_op jit(solution)/shard_map/project/pallas_call | solution.py:179
  52.9 4.8 %project.5 = (bf16[2048,768]{1,0:T(8,128)(2,1)}, bf16[2048,384]{1,0:T(8,128)(2,1)}, bf16[256,2048]{1,0:T(8,128)(2,1)}) custom-call(s32[2]{0:T(128)} %pad_add_fusion.3.at_ref, bf16[256,768]{1,0:T(8,128)(2,1)} %copy-done.12, bf16[256,768]{1,0:T(8,128)(2,1)} %copy-done.14, ...), custom_call_target="tpu_custom_call", output_to_operand_aliasing={{0}: (7, {}), {1}: (8, {}), {2}: (9, {})} | custom-call | flops 301989888 | bytes 6291456 | tf_op jit(solution)/shard_map/project/pallas_call | solution.py:179
  63.0 5.9 %project.6 = (bf16[2048,768]{1,0:T(8,128)(2,1)}, bf16[2048,384]{1,0:T(8,128)(2,1)}, bf16[256,2048]{1,0:T(8,128)(2,1)}) custom-call(s32[3]{0:T(128)} %pad_add_fusion.5.at_ref, bf16[256,768]{1,0:T(8,128)(2,1)} %copy-done.13, bf16[256,768]{1,0:T(8,128)(2,1)} %copy-done.16, ...), custom_call_target="tpu_custom_call", output_to_operand_aliasing={{0}: (8, {}), {1}: (9, {}), {2}: (10, {})} | custom-call | flops 452984832 | bytes 9437184 | tf_op jit(solution)/shard_map/project/pallas_call | solution.py:179
  69.5 3.4 %collective-permute-done.14 = bf16[2,24,2176]{2,1,0:T(8,128)(2,1)S(1)} collective-permute-done((bf16[2,24,2176]{2,1,0:T(8,128)(2,1)S(1)}, bf16[2,24,2176]{2,1,0:T(8,128)(2,1)S(1)}, u32[]{:S(2)}, u32[]{:S(2)}) %collective-permute-start.14) | collective-permute-done | bytes 208928 | tf_op jit(solution)/shard_map/ppermute | solution.py:1032
  77.8 2.8 %project.7 = (bf16[2048,768]{1,0:T(8,128)(2,1)}, bf16[2048,384]{1,0:T(8,128)(2,1)}, bf16[256,2048]{1,0:T(8,128)(2,1)}) custom-call(s32[1]{0:T(128)} %bitcast.18.at_ref, bf16[256,768]{1,0:T(8,128)(2,1)} %copy-done.20, bf16[768,512]{1,0:T(8,128)(2,1)} %get-tuple-element.156.refs_2_.refs_3_.refs_1_, ...), custom_call_target="tpu_custom_call", output_to_operand_aliasing={{0}: (6, {}), {1}: (7, {}), {2}: (8, {})} | custom-call | flops 150994944 | bytes 3145728 | tf_op jit(solution)/shard_map/project/pallas_call | solution.py:179
  80.6 14.9 %attend.1 = (bf16[8,192,128]{2,1,0:T(8,128)(2,1)}, f32[8,64,384]{2,1,0:T(8,128)}, f32[8,1,384]{2,1,0:T(1,128)}) custom-call(s32[8]{0:T(128)} %get-tuple-element.147.base_ref, s32[8]{0:T(128)} %get-tuple-element.148.count_ref, s32[6]{0:T(128)} %pad_add_fusion.2.units_ref, bf16[2048,384]{1,0:T(8,128)(2,1)} %get-tuple-element.181.q_ref.k_ref.v_ref, ...), custom_call_target="tpu_custom_call" | custom-call | flops 3221225472 | bytes 8388608 | tf_op jit(solution)/shard_map/attend/pallas_call | solution.py:292
  97.5 4.3 %all-to-all-start.1 = ((bf16[8,192,128]{2,1,0:T(8,128)(2,1)}), bf16[8,192,128]{2,1,0:T(8,128)(2,1)}, u32[]{:S(2)}, u32[]{:S(2)}) async-start(bf16[8,192,128]{2,1,0:T(8,128)(2,1)} %get-tuple-element.192), calls=%async_computation.1 | async-start | bytes 786432 | tf_op jit(solution)/shard_map/all_to_all | solution.py:1072
  102.4 3.9 %multiply_sine_fusion.1 = (f32[8,64,384]{2,1,0:T(8,128)}, f32[8,64,384]{2,1,0:T(8,128)}) fusion(f32[8,384]{1,0:T(8,128)S(1)} %bitcast.164, f32[64]{0:T(128)S(1)} %fusion.25), kind=kLoop, calls=%fused_computation.3 | loop fusion | flops 196608 | bytes 1585408 | tf_op jit(solution)/shard_map/sin | solution.py:971
  106.3 7.5 %all-to-all-done.1.att_ref = bf16[8,192,128]{2,1,0:T(8,128)(2,1)} async-done(((bf16[8,192,128]{2,1,0:T(8,128)(2,1)}), bf16[8,192,128]{2,1,0:T(8,128)(2,1)}, u32[]{:S(2)}, u32[]{:S(2)}) %all-to-all-start.1) | async-done | bytes 393248 | tf_op jit(solution)/shard_map/all_to_all | solution.py:1072
  115.3 10.4 %middle_stage.1 = (bf16[256,768]{1,0:T(8,128)(2,1)}, bf16[8,192,128]{2,1,0:T(8,128)(2,1)}, f32[256,768]{1,0:T(8,128)}, bf16[256,768]{1,0:T(8,128)(2,1)}, bf16[25...) custom-call(s32[4]{0:T(128)} %pad_add_fusion.1.place_ref, ...), custom_call_target="tpu_custom_call" | custom-call | flops 4982833152 | bytes 10485760 | tf_op jit(solution)/shard_map/middle_stage/pallas_call | solution.py:605
  125.8 4.7 %gone_grads.1 = (bf16[2,192,2176]{2,1,0:T(8,128)(2,1)}, bf16[2,192,2048]{2,1,0:T(8,128)(2,1)}) custom-call(s32[5]{0:T(128)} %stack.119.sides_ref, bf16[256,768]{1,0:T(8,128)(2,1)} %get-tuple-element.214.refs_0_, bf16[256,768]{1,0:T(8,128)(2,1)} %get-tuple-element.215.refs_1_, bf16[256,768]{1,0:T(8,128)(2,1)} %get-tuple-element.216.refs_2_, ...), custom_call_target="tpu_custom_call" | custom-call | flops 830472192 | bytes 9732096 | tf_op jit(solution)/shard_map/gone_grads/pallas_call | solution.py:781
  131.0 3.8 %all-to-all-start.2 = ((bf16[8,192,128]{2,1,0:T(8,128)(2,1)}), bf16[8,192,128]{2,1,0:T(8,128)(2,1)S(1)}, u32[]{:S(2)}, u32[]{:S(2)}) async-start(bf16[8,192,128]{2,1,0:T(8,128)(2,1)} %get-tuple-element.213), calls=%async_computation.2 | async-start | bytes 786432 | tf_op jit(solution)/shard_map/all_to_all | solution.py:1098
  136.6 6.7 %kept_grads.1 = (bf16[192,2176]{1,0:T(8,128)(2,1)}, bf16[192,2176]{1,0:T(8,128)(2,1)}, bf16[8,24,2048]{2,1,0:T(8,128)(2,1)}, bf16[8,24,2048]{2,1,0:T(8,128)(2,1)}) custom-call(s32[5]{0:T(128)} %stack.119.sides_ref, bf16[256,768]{1,0:T(8,128)(2,1)} %get-tuple-element.214.refs_0_, bf16[256,768]{1,0:T(8,128)(2,1)} %get-tuple-element.215.refs_1_, ...), custom_call_target="tpu_custom_call" | custom-call | flops 830472192 | bytes 9732096 | tf_op jit(solution)/shard_map/kept_grads/pallas_call | solution.py:781
  143.3 3.3 %all-to-all-done.2.grad_ref = bf16[8,192,128]{2,1,0:T(8,128)(2,1)S(1)} async-done(((bf16[8,192,128]{2,1,0:T(8,128)(2,1)}), bf16[8,192,128]{2,1,0:T(8,128)(2,1)S(1)}, u32[]{:S(2)}, u32[]{:S(2)}) %all-to-all-start.2) | async-done | bytes 393248 | tf_op jit(solution)/shard_map/all_to_all | solution.py:1098
  149.6 23.6 %attend_back.1 = (bf16[8,256,384]{2,1,0:T(8,128)(2,1)}, bf16[8,704,128]{2,1,0:T(8,128)(2,1)}) custom-call(s32[8]{0:T(128)} %get-tuple-element.147.base_ref, s32[8]{0:T(128)} %get-tuple-element.148.count_ref, s32[6]{0:T(128)} %pad_add_fusion.2.units_ref, bf16[2048,384]{1,0:T(8,128)(2,1)} %get-tuple-element.181.q_ref.k_ref.v_ref, ...), custom_call_target="tpu_custom_call" | custom-call | flops 8053063680 | bytes 12582912 | tf_op jit(solution)/shard_map/attend_back/pallas_call | solution.py:416
  174.3 5.7 %all-to-all-start.3 = ((bf16[8,704,128]{2,1,0:T(8,128)(2,1)}), bf16[8,704,128]{2,1,0:T(8,128)(2,1)S(1)}, u32[]{:S(2)}, u32[]{:S(2)}) async-start(bf16[8,704,128]{2,1,0:T(8,128)(2,1)} %get-tuple-element.238), calls=%async_computation.3 | async-start | bytes 2883584 | tf_op jit(solution)/shard_map/all_to_all | solution.py:1141
  180.6 3.2 %add_halves.4 = (bf16[4,24,2176]{2,1,0:T(8,128)(2,1)}, bf16[4,24,2176]{2,1,0:T(8,128)(2,1)}, bf16[1,96,2048]{2,1,0:T(8,128)(2,1)}, bf16[1,96,2048]{2,1,0:T(8,128)(2,1)}) custom-call(s32[5]{0:T(128)} %stack.119.sides_ref, bf16[4,2,24,2176]{3,2,1,0:T(8,128)(2,1)} %bitcast.146, bf16[4,2,24,2176]{3,2,1,0:T(8,128)(2,1)} %bitcast.37.refs_1_, ...), custom_call_target="tpu_custom_call" | custom-call | flops 1622016 | bytes 4866048 | tf_op jit(solution)/shard_map/add_halves/pallas_call | solution.py:869
  187.3 6.5 %head_grads.1 = (bf16[2,192,384]{2,1,0:T(8,128)(2,1)}, bf16[2,192,384]{2,1,0:T(8,128)(2,1)}) custom-call(s32[5]{0:T(128)} %stack.119.sides_ref, bf16[2048,768]{1,0:T(8,128)(2,1)} %get-tuple-element.250.left_ref, bf16[8,256,384]{2,1,0:T(8,128)(2,1)} %get-tuple-element.251.right_ref), custom_call_target="tpu_custom_call" | custom-call | flops 1207959552 | bytes 4718592 | tf_op jit(solution)/shard_map/head_grads/pallas_call | solution.py:820
  196.8 8.7 %collective-permute-done.29 = bf16[4,24,2176]{2,1,0:T(8,128)(2,1)S(1)} collective-permute-done((bf16[4,24,2176]{2,1,0:T(8,128)(2,1)}, bf16[4,24,2176]{2,1,0:T(8,128)(2,1)S(1)}, u32[]{:S(2)}, u32[]{:S(2)}) %collective-permute-start.29) | collective-permute-done | bytes 417824 | tf_op jit(solution)/shard_map/ppermute | solution.py:1151
  206.2 2.5 %add_halves.5 = (bf16[2,24,4224]{2,1,0:T(8,128)(2,1)}, bf16[2,24,4224]{2,1,0:T(8,128)(2,1)}) custom-call(s32[5]{0:T(128)} %stack.119.sides_ref, bf16[2,2,24,2176]{3,2,1,0:T(8,128)(2,1)} %bitcast.148, bf16[2,2,24,2176]{3,2,1,0:T(8,128)(2,1)} %bitcast.149, bf16[2,2,24,2048]{3,2,1,0:T(8,128)(2,1)} %bitcast.153, bf16[2,2,24,2048]{3,2,1,0:T(8,128)(2,1)} %bitcast.154), custom_call_target="tpu_custom_call" | custom-call | flops 811008 | bytes 2433024 | tf_op jit(solution)/shard_map/add_halves/pallas_call | solution.py:869
  212.0 4.7 %settle.1.w_ref = bf16[768,2304]{1,0:T(8,128)(2,1)} custom-call(s32[4]{0:T(128)} %pad_add_fusion.1.place_ref, bf16[4,48,2304]{2,1,0:T(8,128)(2,1)} %copy-done.1, bf16[4,48,2304]{2,1,0:T(8,128)(2,1)} %copy-done.4, bf16[4,48,2304]{2,1,0:T(8,128)(2,1)} %copy-done.5, bf16[4,48,2304]{2,1,0:T(8,128)(2,1)} %copy-done.6), custom_call_target="tpu_custom_call" | custom-call | bytes 8388608 | tf_op jit(solution)/shard_map/settle/pallas_call | solution.py:646
  216.8 5.1 %collective-permute-done.34 = bf16[2,24,4224]{2,1,0:T(8,128)(2,1)S(1)} collective-permute-done((bf16[2,24,4224]{2,1,0:T(8,128)(2,1)}, bf16[2,24,4224]{2,1,0:T(8,128)(2,1)S(1)}, u32[]{:S(2)}, u32[]{:S(2)}) %collective-permute-start.34) | collective-permute-done | bytes 405536 | tf_op jit(solution)/shard_map/ppermute | solution.py:1165
  226.2 3.4 %all-to-all-start.4 = ((bf16[8,24,384]{2,1,0:T(8,128)(2,1)}), bf16[8,24,384]{2,1,0:T(8,128)(2,1)S(1)}, u32[]{:S(2)}, u32[]{:S(2)}) async-start(bf16[8,24,384]{2,1,0:T(8,128)(2,1)} %bitcast.50), calls=%async_computation.4 | async-start | bytes 294912 | tf_op jit(solution)/shard_map/all_to_all | solution.py:1182
  229.6 5.2 %finish.1 = bf16[256,768]{1,0:T(8,128)(2,1)} custom-call(bf16[8,704,128]{2,1,0:T(8,128)(2,1)} %copy-done, bf16[256,768]{1,0:T(8,128)(2,1)} %bitcast.141, f32[8,768]{1,0:T(8,128)} %get-tuple-element.157.refs_3_.refs_4_.refs_2_.gain_ref, f32[256,768]{1,0:T(8,128)} %get-tuple-element.271.grad_ref, bf16[768,2304]{1,0:T(8,128)(2,1)} %settle.1.w_ref), custom_call_target="tpu_custom_call" | custom-call | flops 905969664 | bytes 6291456 | tf_op jit(solution)/shard_map/finish/pallas_call | solution.py:679
  234.8 2.9 %collective-permute-done.36 = bf16[1,24,4224]{2,1,0:T(8,128)(2,1)S(1)} collective-permute-done((bf16[1,24,4224]{2,1,0:T(8,128)(2,1)}, bf16[1,24,4224]{2,1,0:T(8,128)(2,1)S(1)}, u32[]{:S(2)}, u32[]{:S(2)}) %collective-permute-start.36) | collective-permute-done | bytes 202784 | tf_op jit(solution)/shard_map/ppermute | solution.py:1172
  (192 shorter events, 60.5 us)
Async XLA Ops:
  0.6 19.8 %collective-permute-start = (bf16[256,768]{1,0:T(8,128)(2,1)}, bf16[256,768]{1,0:T(8,128)(2,1)S(1)}, u32[]{:S(2)}, u32[]{:S(2)}) collective-permute-start(bf16[256,768]{1,0:T(8,128)(2,1)} %bitcast.137), channel_id=1, source_target_pairs={{0,2},{1,3},{2,4},{3,5},{4,6},{5,7},{6,0},{7,1},{8,10},{9,11},{10,... | collective-permute-start | bytes 1179656 | tf_op jit(solution)/shard_map/ppermute | solution.py:981
  3.7 16.7 %collective-permute-start.1 = (bf16[256,768]{1,0:T(8,128)(2,1)}, bf16[256,768]{1,0:T(8,128)(2,1)S(1)}, u32[]{:S(2)}, u32[]{:S(2)}) collective-permute-start(bf16[256,768]{1,0:T(8,128)(2,1)} %bitcast.138), channel_id=1, source_target_pairs={{0,1},{1,0},{2,3},{3,2},{4,5},{5,4},{6,7},{7,6},{8,9},{9,8},{10,11... | collective-permute-start | bytes 1179656 | tf_op jit(solution)/shard_map/ppermute | solution.py:982
  6.2 14.2 %collective-permute-start.2 = (bf16[2,24,2176]{2,1,0:T(8,128)(2,1)S(1)}, bf16[2,24,2176]{2,1,0:T(8,128)(2,1)S(1)}, u32[]{:S(2)}, u32[]{:S(2)}) collective-permute-start(bf16[2,24,2176]{2,1,0:T(8,128)(2,1)S(1)} %pad_maximum_fusion.6), channel_id=1, source_target_pairs={{0,2},{1,3},{2,4},{3,5},{4,6},{5,7},{6,0},{7,1},{8,10},{9,11},{10,... | collective-permute-start | bytes 626696 | tf_op jit(solution)/shard_map/ppermute | solution.py:983
  9.6 15.5 %all-to-all-start = ((bf16[8,32,512]{2,1,0:T(8,128)(2,1)}), bf16[8,32,512]{2,1,0:T(8,128)(2,1)S(1)}, u32[]{:S(2)}, u32[]{:S(2)}) async-start(bf16[8,32,512]{2,1,0:T(8,128)(2,1)} %spread.1), calls=%async_computation | async-start | bytes 524288 | tf_op jit(solution)/shard_map/all_to_all | solution.py:974
  25.2 17.3 %collective-permute-start.3 = (bf16[256,768]{1,0:T(8,128)(2,1)S(1)}, bf16[256,768]{1,0:T(8,128)(2,1)S(1)}, u32[]{:S(2)}, u32[]{:S(2)}) collective-permute-start(bf16[256,768]{1,0:T(8,128)(2,1)S(1)} %collective-permute-done.refs_0_), channel_id=1, source_target_pairs={{0,2},{1,3},{2,4},{3,5},{4,6},{5,7},{6,0},{7,1},{8,10},{9,11},{10,... | collective-permute-start | bytes 1179656 | tf_op jit(solution)/shard_map/ppermute | solution.py:995
  26.1 16.4 %collective-permute-start.4 = (bf16[256,768]{1,0:T(8,128)(2,1)S(1)}, bf16[256,768]{1,0:T(8,128)(2,1)S(1)}, u32[]{:S(2)}, u32[]{:S(2)}) collective-permute-start(bf16[256,768]{1,0:T(8,128)(2,1)S(1)} %collective-permute-done.refs_0_), channel_id=1, source_target_pairs={{0,1},{1,0},{2,3},{3,2},{4,5},{5,4},{6,7},{7,6},{8,9},{9,8},{10,11... | collective-permute-start | bytes 1179656 | tf_op jit(solution)/shard_map/ppermute | solution.py:996
  26.7 15.8 %collective-permute-start.5 = (bf16[2,24,2176]{2,1,0:T(8,128)(2,1)S(1)}, bf16[2,24,2176]{2,1,0:T(8,128)(2,1)S(1)}, u32[]{:S(2)}, u32[]{:S(2)}) collective-permute-start(bf16[2,24,2176]{2,1,0:T(8,128)(2,1)S(1)} %collective-permute-done.2), channel_id=1, source_target_pairs={{0,2},{1,3},{2,4},{3,5},{4,6},{5,7},{6,0},{7,1},{8,10},{9,11},{10,... | collective-permute-start | bytes 626696 | tf_op jit(solution)/shard_map/ppermute | solution.py:997
  42.5 16.5 %collective-permute-start.8 = (bf16[256,768]{1,0:T(8,128)(2,1)S(1)}, bf16[256,768]{1,0:T(8,128)(2,1)S(1)}, u32[]{:S(2)}, u32[]{:S(2)}) collective-permute-start(bf16[256,768]{1,0:T(8,128)(2,1)S(1)} %collective-permute-done.3.refs_0_), channel_id=1, source_target_pairs={{0,2},{1,3},{2,4},{3,5},{4,6},{5,7},{6,0},{7,1},{8,10},{9,11},{10,... | collective-permute-start | bytes 1179656 | tf_op jit(solution)/shard_map/ppermute | solution.py:1015
  42.6 16.5 %collective-permute-start.9 = (bf16[256,768]{1,0:T(8,128)(2,1)S(1)}, bf16[256,768]{1,0:T(8,128)(2,1)S(1)}, u32[]{:S(2)}, u32[]{:S(2)}) collective-permute-start(bf16[256,768]{1,0:T(8,128)(2,1)S(1)} %collective-permute-done.3.refs_0_), channel_id=1, source_target_pairs={{0,1},{1,0},{2,3},{3,2},{4,5},{5,4},{6,7},{7,6},{8,9},{9,8},{10,11... | collective-permute-start | bytes 1179656 | tf_op jit(solution)/shard_map/ppermute | solution.py:1016
  44.2 14.9 %collective-permute-start.10 = (bf16[2,24,2176]{2,1,0:T(8,128)(2,1)S(1)}, bf16[2,24,2176]{2,1,0:T(8,128)(2,1)S(1)}, u32[]{:S(2)}, u32[]{:S(2)}) collective-permute-start(bf16[2,24,2176]{2,1,0:T(8,128)(2,1)S(1)} %collective-permute-done.5), channel_id=1, source_target_pairs={{0,2},{1,3},{2,4},{3,5},{4,6},{5,7},{6,0},{7,1},{8,10},{9,11},{10,... | collective-permute-start | bytes 626696 | tf_op jit(solution)/shard_map/ppermute | solution.py:1017
  44.2 14.9 %collective-permute-start.11 = (bf16[2,24,2176]{2,1,0:T(8,128)(2,1)S(1)}, bf16[2,24,2176]{2,1,0:T(8,128)(2,1)S(1)}, u32[]{:S(2)}, u32[]{:S(2)}) collective-permute-start(bf16[2,24,2176]{2,1,0:T(8,128)(2,1)S(1)} %get-tuple-element.152), channel_id=1, source_target_pairs={{0,1},{1,0},{2,3},{3,2},{4,5},{5,4},{6,7},{7,6},{8,9},{9,8},{10,11... | collective-permute-start | bytes 626696 | tf_op jit(solution)/shard_map/ppermute | solution.py:1018
  45.3 13.7 %collective-permute-start.12 = (bf16[2,24,2176]{2,1,0:T(8,128)(2,1)S(1)}, bf16[2,24,2176]{2,1,0:T(8,128)(2,1)S(1)}, u32[]{:S(2)}, u32[]{:S(2)}) collective-permute-start(bf16[2,24,2176]{2,1,0:T(8,128)(2,1)S(1)} %get-tuple-element.153), channel_id=1, source_target_pairs={{0,16},{8,24},{16,0},{24,8},{1,17},{9,25},{17,1},{25,9},{2,18},{10... | collective-permute-start | bytes 626696 | tf_op jit(solution)/shard_map/ppermute | solution.py:1019
  59.1 13.8 %collective-permute-start.13 = (bf16[256,768]{1,0:T(8,128)(2,1)S(1)}, bf16[256,768]{1,0:T(8,128)(2,1)S(1)}, u32[]{:S(2)}, u32[]{:S(2)}) collective-permute-start(bf16[256,768]{1,0:T(8,128)(2,1)S(1)} %collective-permute-done.8.refs_2_), channel_id=1, source_target_pairs={{0,1},{1,0},{2,3},{3,2},{4,5},{5,4},{6,7},{7,6},{8,9},{9,8},{10,11... | collective-permute-start | bytes 1179656 | tf_op jit(solution)/shard_map/ppermute | solution.py:1029
  60.8 12.1 %collective-permute-start.14 = (bf16[2,24,2176]{2,1,0:T(8,128)(2,1)S(1)}, bf16[2,24,2176]{2,1,0:T(8,128)(2,1)S(1)}, u32[]{:S(2)}, u32[]{:S(2)}) collective-permute-start(bf16[2,24,2176]{2,1,0:T(8,128)(2,1)S(1)} %pad_maximum_fusion.9), channel_id=1, source_target_pairs={{0,1},{1,0},{2,3},{3,2},{4,5},{5,4},{6,7},{7,6},{8,9},{9,8},{10,11... | collective-permute-start | bytes 626696 | tf_op jit(solution)/shard_map/ppermute | solution.py:1032
  73.0 22.5 %collective-permute-start.17 = (bf16[4,48,2176]{2,1,0:T(8,128)(2,1)S(1)}, bf16[4,48,2176]{2,1,0:T(8,128)(2,1)}, u32[]{:S(2)}, u32[]{:S(2)}) collective-permute-start(bf16[4,48,2176]{2,1,0:T(8,128)(2,1)S(1)} %maximum_maximum_fusion.refs_0_), channel_id=1, source_target_pairs={{0,16},{8,24},{16,0},{24,8},{1,17},{9,25},{17,1},{25,9},{2,18},{10... | collective-permute-start | bytes 2506760 | tf_op jit(solution)/shard_map/ppermute | solution.py:1045
  74.7 20.9 %collective-permute-start.18 = (bf16[8,24,2176]{2,1,0:T(8,128)(2,1)S(1)}, bf16[8,24,2176]{2,1,0:T(8,128)(2,1)S(1)}, u32[]{:S(2)}, u32[]{:S(2)}) collective-permute-start(bf16[8,24,2176]{2,1,0:T(8,128)(2,1)S(1)} %constant_dynamic-update-slice_fusion), channel_id=1, source_target_pairs={{0,1},{1,0},{2,3},{3,2},{4,5},{5,4},{6,7},{7,6},{8,9},{9,8},{10,11... | collective-permute-start | bytes 2506760 | tf_op jit(solution)/shard_map/ppermute | solution.py:1046
  76.3 19.2 %collective-permute-start.19 = (bf16[2,24,2304]{2,1,0:T(8,128)(2,1)S(1)}, bf16[2,24,2304]{2,1,0:T(8,128)(2,1)S(1)}, u32[]{:S(2)}, u32[]{:S(2)}) collective-permute-start(bf16[2,24,2304]{2,1,0:T(8,128)(2,1)S(1)} %pad_maximum_fusion.7), channel_id=1, source_target_pairs={{0,4},{1,5},{2,6},{3,7},{4,0},{5,1},{6,2},{7,3},{8,12},{9,13},{10,... | collective-permute-start | bytes 663560 | tf_op jit(solution)/shard_map/ppermute | solution.py:1041
  95.9 18.0 %collective-permute-start.22 = (bf16[8,48,2176]{2,1,0:T(8,128)(2,1)S(1)}, bf16[8,48,2176]{2,1,0:T(8,128)(2,1)}, u32[]{:S(2)}, u32[]{:S(2)}) collective-permute-start(bf16[8,48,2176]{2,1,0:T(8,128)(2,1)S(1)} %pad_maximum_fusion.refs_4_), channel_id=1, source_target_pairs={{0,8},{8,0},{16,24},{24,16},{1,9},{9,1},{17,25},{25,17},{2,10},{10... | collective-permute-start | bytes 5013512 | tf_op jit(solution)/shard_map/ppermute | solution.py:1066
  97.1 16.7 %collective-permute-start.21 = (bf16[4,48,2176]{2,1,0:T(8,128)(2,1)}, bf16[4,48,2176]{2,1,0:T(8,128)(2,1)}, u32[]{:S(2)}, u32[]{:S(2)}) collective-permute-start(bf16[4,48,2176]{2,1,0:T(8,128)(2,1)} %collective-permute-done.17.refs_1_), channel_id=1, source_target_pairs={{0,8},{8,0},{16,24},{24,16},{1,9},{9,1},{17,25},{25,17},{2,10},{10... | collective-permute-start | bytes 2506760 | tf_op jit(solution)/shard_map/ppermute | solution.py:1065
  97.5 16.4 %all-to-all-start.1 = ((bf16[8,192,128]{2,1,0:T(8,128)(2,1)}), bf16[8,192,128]{2,1,0:T(8,128)(2,1)}, u32[]{:S(2)}, u32[]{:S(2)}) async-start(bf16[8,192,128]{2,1,0:T(8,128)(2,1)} %get-tuple-element.192), calls=%async_computation.1 | async-start | bytes 786432 | tf_op jit(solution)/shard_map/all_to_all | solution.py:1072
  113.9 11.9 %collective-permute-start.23 = (bf16[4,24,2304]{2,1,0:T(8,128)(2,1)S(1)}, bf16[4,24,2304]{2,1,0:T(8,128)(2,1)S(1)}, u32[]{:S(2)}, u32[]{:S(2)}) collective-permute-start(bf16[4,24,2304]{2,1,0:T(8,128)(2,1)S(1)} %pad_maximum_fusion.3), channel_id=1, source_target_pairs={{0,1},{1,0},{2,3},{3,2},{4,5},{5,4},{6,7},{7,6},{8,9},{9,8},{10,11... | collective-permute-start | bytes 1327112 | tf_op jit(solution)/shard_map/ppermute | solution.py:1075
  131.0 15.7 %all-to-all-start.2 = ((bf16[8,192,128]{2,1,0:T(8,128)(2,1)}), bf16[8,192,128]{2,1,0:T(8,128)(2,1)S(1)}, u32[]{:S(2)}, u32[]{:S(2)}) async-start(bf16[8,192,128]{2,1,0:T(8,128)(2,1)} %get-tuple-element.213), calls=%async_computation.2 | async-start | bytes 786432 | tf_op jit(solution)/shard_map/all_to_all | solution.py:1098
  134.9 38.3 %collective-permute-start.28 = (bf16[4,48,2304]{2,1,0:T(8,128)(2,1)S(1)}, bf16[4,48,2304]{2,1,0:T(8,128)(2,1)S(1)}, u32[]{:S(2)}, u32[]{:S(2)}) collective-permute-start(bf16[4,48,2304]{2,1,0:T(8,128)(2,1)S(1)} %pad_maximum_fusion.1.refs_0_), channel_id=1, source_target_pairs={{0,16},{8,24},{16,0},{24,8},{1,17},{9,25},{17,1},{25,9},{2,18},{10... | collective-permute-start | bytes 2654216 | tf_op jit(solution)/shard_map/ppermute | solution.py:1097
  146.6 27.6 %collective-permute-start.26 = (bf16[192,2176]{1,0:T(8,128)(2,1)}, bf16[192,2176]{1,0:T(8,128)(2,1)}, u32[]{:S(2)}, u32[]{:S(2)}) collective-permute-start(bf16[192,2176]{1,0:T(8,128)(2,1)} %get-tuple-element.234), channel_id=1, source_target_pairs={{0,16},{8,24},{16,0},{24,8},{1,17},{9,25},{17,1},{25,9},{2,18},{10... | collective-permute-start | bytes 2506760 | tf_op jit(solution)/shard_map/ppermute | solution.py:1122
  148.2 25.1 %collective-permute-start.27 = (bf16[8,24,2048]{2,1,0:T(8,128)(2,1)}, bf16[8,24,2048]{2,1,0:T(8,128)(2,1)}, u32[]{:S(2)}, u32[]{:S(2)}) collective-permute-start(bf16[8,24,2048]{2,1,0:T(8,128)(2,1)} %get-tuple-element.236), channel_id=1, source_target_pairs={{0,1},{1,0},{2,3},{3,2},{4,5},{5,4},{6,7},{7,6},{8,9},{9,8},{10,11... | collective-permute-start | bytes 2359304 | tf_op jit(solution)/shard_map/ppermute | solution.py:1123
  174.3 47.5 %all-to-all-start.3 = ((bf16[8,704,128]{2,1,0:T(8,128)(2,1)}), bf16[8,704,128]{2,1,0:T(8,128)(2,1)S(1)}, u32[]{:S(2)}, u32[]{:S(2)}) async-start(bf16[8,704,128]{2,1,0:T(8,128)(2,1)} %get-tuple-element.238), calls=%async_computation.3 | async-start | bytes 2883584 | tf_op jit(solution)/shard_map/all_to_all | solution.py:1141
  180.0 25.4 %collective-permute-start.32 = (bf16[4,48,2304]{2,1,0:T(8,128)(2,1)S(1)}, bf16[4,48,2304]{2,1,0:T(8,128)(2,1)S(1)}, u32[]{:S(2)}, u32[]{:S(2)}) collective-permute-start(bf16[4,48,2304]{2,1,0:T(8,128)(2,1)S(1)} %pad_maximum_fusion.1.refs_0_), channel_id=1, source_target_pairs={{0,8},{8,0},{16,24},{24,16},{1,9},{9,1},{17,25},{25,17},{2,10},{10... | collective-permute-start | bytes 2654216 | tf_op jit(solution)/shard_map/ppermute | solution.py:1142
  180.1 25.4 %collective-permute-start.33 = (bf16[4,48,2304]{2,1,0:T(8,128)(2,1)S(1)}, bf16[4,48,2304]{2,1,0:T(8,128)(2,1)S(1)}, u32[]{:S(2)}, u32[]{:S(2)}) collective-permute-start(bf16[4,48,2304]{2,1,0:T(8,128)(2,1)S(1)} %collective-permute-done.28.refs_1_), channel_id=1, source_target_pairs={{0,8},{8,0},{16,24},{24,16},{1,9},{9,1},{17,25},{25,17},{2,10},{10... | collective-permute-start | bytes 2654216 | tf_op jit(solution)/shard_map/ppermute | solution.py:1143
  183.8 21.7 %collective-permute-start.29 = (bf16[4,24,2176]{2,1,0:T(8,128)(2,1)}, bf16[4,24,2176]{2,1,0:T(8,128)(2,1)S(1)}, u32[]{:S(2)}, u32[]{:S(2)}) collective-permute-start(bf16[4,24,2176]{2,1,0:T(8,128)(2,1)} %get-tuple-element.246), channel_id=1, source_target_pairs={{0,1},{1,0},{2,3},{3,2},{4,5},{5,4},{6,7},{7,6},{8,9},{9,8},{10,11... | collective-permute-start | bytes 1253384 | tf_op jit(solution)/shard_map/ppermute | solution.py:1151
  208.7 13.1 %collective-permute-start.34 = (bf16[2,24,4224]{2,1,0:T(8,128)(2,1)}, bf16[2,24,4224]{2,1,0:T(8,128)(2,1)S(1)}, u32[]{:S(2)}, u32[]{:S(2)}) collective-permute-start(bf16[2,24,4224]{2,1,0:T(8,128)(2,1)} %get-tuple-element.261), channel_id=1, source_target_pairs={{0,2},{1,3},{2,0},{3,1},{4,6},{5,7},{6,4},{7,5},{8,10},{9,11},{10,... | collective-permute-start | bytes 1216520 | tf_op jit(solution)/shard_map/ppermute | solution.py:1165
  224.5 13.2 %collective-permute-start.36 = (bf16[1,24,4224]{2,1,0:T(8,128)(2,1)}, bf16[1,24,4224]{2,1,0:T(8,128)(2,1)S(1)}, u32[]{:S(2)}, u32[]{:S(2)}) collective-permute-start(bf16[1,24,4224]{2,1,0:T(8,128)(2,1)} %get-tuple-element.277), channel_id=1, source_target_pairs={{0,4},{1,5},{2,6},{3,7},{4,0},{5,1},{6,2},{7,3},{8,12},{9,13},{10,... | collective-permute-start | bytes 608264 | tf_op jit(solution)/shard_map/ppermute | solution.py:1172
  226.2 14.2 %all-to-all-start.4 = ((bf16[8,24,384]{2,1,0:T(8,128)(2,1)}), bf16[8,24,384]{2,1,0:T(8,128)(2,1)S(1)}, u32[]{:S(2)}, u32[]{:S(2)}) async-start(bf16[8,24,384]{2,1,0:T(8,128)(2,1)} %bitcast.50), calls=%async_computation.4 | async-start | bytes 294912 | tf_op jit(solution)/shard_map/all_to_all | solution.py:1182
  (37 other events, 307.1 us)

commit v6 on v5

--- a/solution.py
+++ b/solution.py
@@ -1097,20 +1097,21 @@
             far_c = lax.ppermute(pair_c, "fsdp", by_y)
         grad_heads = lax.all_to_all(grad_heads, "ctx", 0, 0, tiled=True)
         if by_hand:
-            rest = columns - cut
+            grad_cut = columns // LANES // 2 * LANES
+            rest = columns - grad_cut
             gone_a, gone_b = weight_grads(
-                gone_grads_kernel, sides, operands, [], [(2, share, cut), (2, share, rest)], cut,
-                [], "gone_grads",
+                gone_grads_kernel, sides, operands, [], [(2, share, grad_cut), (2, share, rest)],
+                grad_cut, [], "gone_grads",
             )
             got_a = lax.ppermute(gone_a, "fsdp", by_core)
             got_b = lax.ppermute(gone_b, "fsdp", by_core)
             mine_a, other_a, mine_b, other_b = weight_grads(
                 kept_grads_kernel, sides, operands, [got_a, got_b],
-                [(share, cut)] * 2 + [(2 * outer, shard, rest)] * 2, cut,
+                [(share, grad_cut)] * 2 + [(2 * outer, shard, rest)] * 2, grad_cut,
                 [
-                    pltpu.VMEM((2, share, cut), bf16),
+                    pltpu.VMEM((2, share, grad_cut), bf16),
                     pltpu.VMEM((2, share, rest), bf16),
-                    pltpu.VMEM((2, share, cut), bf16),
+                    pltpu.VMEM((2, share, grad_cut), bf16),
                     pltpu.VMEM((2, 2 * outer, shard, rest), bf16),
                     pltpu.SemaphoreType.DMA((4,)),
                 ],

time: 243 us -> 242 us (level)
  transfers between devices with their start and end apart: 42 -> 42, of which waited for: 16 -> 14; matrix products, arithmetic and copies ran while one was open for 9% -> 9% of each run, Pallas kernels for 42% -> 42%
where the time goes in v6:
time: 242 us; the launch traced here: 241 us
  Pallas kernels  108 us (45%)
  starting transfers between devices  57 us (24%)
  waiting for transfers between devices  48.2 us (20%)
  other arithmetic  21 us (9%)
  local copies, waits for them, and re-layouts  4.78 us (2%)
    pallas_call x1, Pallas kernels, attend_back(): pl.pallas_call(functools.partial(attend_back_kernel, tile), grid_spec=plt...  23.6 us
    pallas_call x4, Pallas kernels, project(): pl.pallas_call(functools.partial(project_kernel, count), grid_spec=pltpu....  18.1 us
    pallas_call x1, Pallas kernels, attend(): pl.pallas_call(functools.partial(attend_kernel, tile), grid_spec=pltpu.Pr...  14.9 us
    pallas_call x2, Pallas kernels, weight_grads(): pl.pallas_call(functools.partial(kernel, len(operands) // 2, cut), in_spe...  11.4 us
    pallas_call x1, Pallas kernels, middle_stage(): pl.pallas_call(functools.partial(middle_kernel, heads, splits, metas, arr...  10.4 us
    pallas_call x4, Pallas kernels, add_halves(): pl.pallas_call(functools.partial(add_halves_kernel, [pair[3] for pair in...  9.49 us
    ppermute x1, waiting for transfers between devices, on_device(): got_a = lax.ppermute(other_a, 'ctx', swap)  8.26 us
    all_to_all x1, waiting for transfers between devices, on_device(): att_in = lax.all_to_all(att_low, 'ctx', 0, 0, tiled=True)  7.53 us
  transfers between devices with their start and end apart: 42, of which 14 were waited for; matrix products, arithmetic and copies ran while one was open for 9% of the time, Pallas kernels for 42%

profile of v6, /device:TPU:0, one launch (start us, length us, event | category | flops | bytes accessed | tf_op | source)
XLA Modules:
  0.0 240.6 jit_solution(10449368849105185453)
XLA Ops:
  0.6 3.1 %collective-permute-start = (bf16[256,768]{1,0:T(8,128)(2,1)}, bf16[256,768]{1,0:T(8,128)(2,1)S(1)}, u32[]{:S(2)}, u32[]{:S(2)}) collective-permute-start(bf16[256,768]{1,0:T(8,128)(2,1)} %bitcast.137), channel_id=1, source_target_pairs={{0,2},{1,3},{2,4},{3,5},{4,6},{5,7},{6,0},{7,1},{8,10},{9,11},{10,... | collective-permute-start | bytes 1179656 | tf_op jit(solution)/shard_map/ppermute | solution.py:981
  9.6 3.5 %all-to-all-start = ((bf16[8,32,512]{2,1,0:T(8,128)(2,1)}), bf16[8,32,512]{2,1,0:T(8,128)(2,1)S(1)}, u32[]{:S(2)}, u32[]{:S(2)}) async-start(bf16[8,32,512]{2,1,0:T(8,128)(2,1)} %spread.1), calls=%async_computation | async-start | bytes 524288 | tf_op jit(solution)/shard_map/all_to_all | solution.py:974
  15.8 4.6 %collective-permute-done.2 = bf16[2,24,2176]{2,1,0:T(8,128)(2,1)S(1)} collective-permute-done((bf16[2,24,2176]{2,1,0:T(8,128)(2,1)S(1)}, bf16[2,24,2176]{2,1,0:T(8,128)(2,1)S(1)}, u32[]{:S(2)}, u32[]{:S(2)}) %collective-permute-start.2) | collective-permute-done | bytes 208928 | tf_op jit(solution)/shard_map/ppermute | solution.py:983
  20.4 4.7 %all-to-all-done = bf16[8,32,512]{2,1,0:T(8,128)(2,1)S(1)} async-done(((bf16[8,32,512]{2,1,0:T(8,128)(2,1)}), bf16[8,32,512]{2,1,0:T(8,128)(2,1)S(1)}, u32[]{:S(2)}, u32[]{:S(2)}) %all-to-all-start) | async-done | bytes 262176 | tf_op jit(solution)/shard_map/all_to_all | solution.py:974
  29.5 5.6 %multiply_sine_fusion = (f32[2048,128]{1,0:T(8,128)}, f32[2048,128]{1,0:T(8,128)}) fusion(f32[128]{0:T(128)S(1)} %fusion.22, f32[2048]{0:T(1024)S(1)} %bitcast.161), kind=kLoop, calls=%fused_computation.1 | loop fusion | flops 262144 | bytes 2105856 | tf_op jit(solution)/shard_map/sin | solution.py:964
  38.8 3.7 %collective-permute-done.5 = bf16[2,24,2176]{2,1,0:T(8,128)(2,1)S(1)} collective-permute-done((bf16[2,24,2176]{2,1,0:T(8,128)(2,1)S(1)}, bf16[2,24,2176]{2,1,0:T(8,128)(2,1)S(1)}, u32[]{:S(2)}, u32[]{:S(2)}) %collective-permute-start.5) | collective-permute-done | bytes 208928 | tf_op jit(solution)/shard_map/ppermute | solution.py:997
  46.2 2.1 ready.1
  48.2 4.7 %project.4 = (bf16[2048,768]{1,0:T(8,128)(2,1)}, bf16[2048,384]{1,0:T(8,128)(2,1)}, bf16[256,2048]{1,0:T(8,128)(2,1)}) custom-call(s32[2]{0:T(128)} %pad_add_fusion.4.at_ref, bf16[256,768]{1,0:T(8,128)(2,1)} %bitcast.139, bf16[256,768]{1,0:T(8,128)(2,1)} %copy-done.19, bf16[768,512]{1,0:T(8,128)(2,1)} %get-tuple-element.156.refs_2_.refs_3_.refs_1_, ...), custom_call_target="tpu_custom_call" | custom-call | flops 301989888 | bytes 6291456 | tf_op jit(solution)/shard_map/project/pallas_call | solution.py:179
  52.9 4.8 %project.5 = (bf16[2048,768]{1,0:T(8,128)(2,1)}, bf16[2048,384]{1,0:T(8,128)(2,1)}, bf16[256,2048]{1,0:T(8,128)(2,1)}) custom-call(s32[2]{0:T(128)} %pad_add_fusion.3.at_ref, bf16[256,768]{1,0:T(8,128)(2,1)} %copy-done.12, bf16[256,768]{1,0:T(8,128)(2,1)} %copy-done.14, ...), custom_call_target="tpu_custom_call", output_to_operand_aliasing={{0}: (7, {}), {1}: (8, {}), {2}: (9, {})} | custom-call | flops 301989888 | bytes 6291456 | tf_op jit(solution)/shard_map/project/pallas_call | solution.py:179
  63.0 5.9 %project.6 = (bf16[2048,768]{1,0:T(8,128)(2,1)}, bf16[2048,384]{1,0:T(8,128)(2,1)}, bf16[256,2048]{1,0:T(8,128)(2,1)}) custom-call(s32[3]{0:T(128)} %pad_add_fusion.5.at_ref, bf16[256,768]{1,0:T(8,128)(2,1)} %copy-done.13, bf16[256,768]{1,0:T(8,128)(2,1)} %copy-done.16, ...), custom_call_target="tpu_custom_call", output_to_operand_aliasing={{0}: (8, {}), {1}: (9, {}), {2}: (10, {})} | custom-call | flops 452984832 | bytes 9437184 | tf_op jit(solution)/shard_map/project/pallas_call | solution.py:179
  69.5 3.4 %collective-permute-done.14 = bf16[2,24,2176]{2,1,0:T(8,128)(2,1)S(1)} collective-permute-done((bf16[2,24,2176]{2,1,0:T(8,128)(2,1)S(1)}, bf16[2,24,2176]{2,1,0:T(8,128)(2,1)S(1)}, u32[]{:S(2)}, u32[]{:S(2)}) %collective-permute-start.14) | collective-permute-done | bytes 208928 | tf_op jit(solution)/shard_map/ppermute | solution.py:1032
  77.8 2.8 %project.7 = (bf16[2048,768]{1,0:T(8,128)(2,1)}, bf16[2048,384]{1,0:T(8,128)(2,1)}, bf16[256,2048]{1,0:T(8,128)(2,1)}) custom-call(s32[1]{0:T(128)} %bitcast.18.at_ref, bf16[256,768]{1,0:T(8,128)(2,1)} %copy-done.20, bf16[768,512]{1,0:T(8,128)(2,1)} %get-tuple-element.156.refs_2_.refs_3_.refs_1_, ...), custom_call_target="tpu_custom_call", output_to_operand_aliasing={{0}: (6, {}), {1}: (7, {}), {2}: (8, {})} | custom-call | flops 150994944 | bytes 3145728 | tf_op jit(solution)/shard_map/project/pallas_call | solution.py:179
  80.6 14.9 %attend.1 = (bf16[8,192,128]{2,1,0:T(8,128)(2,1)}, f32[8,64,384]{2,1,0:T(8,128)}, f32[8,1,384]{2,1,0:T(1,128)}) custom-call(s32[8]{0:T(128)} %get-tuple-element.147.base_ref, s32[8]{0:T(128)} %get-tuple-element.148.count_ref, s32[6]{0:T(128)} %pad_add_fusion.2.units_ref, bf16[2048,384]{1,0:T(8,128)(2,1)} %get-tuple-element.181.q_ref.k_ref.v_ref, ...), custom_call_target="tpu_custom_call" | custom-call | flops 3221225472 | bytes 8388608 | tf_op jit(solution)/shard_map/attend/pallas_call | solution.py:292
  97.5 4.3 %all-to-all-start.1 = ((bf16[8,192,128]{2,1,0:T(8,128)(2,1)}), bf16[8,192,128]{2,1,0:T(8,128)(2,1)}, u32[]{:S(2)}, u32[]{:S(2)}) async-start(bf16[8,192,128]{2,1,0:T(8,128)(2,1)} %get-tuple-element.192), calls=%async_computation.1 | async-start | bytes 786432 | tf_op jit(solution)/shard_map/all_to_all | solution.py:1072
  102.4 3.9 %multiply_sine_fusion.1 = (f32[8,64,384]{2,1,0:T(8,128)}, f32[8,64,384]{2,1,0:T(8,128)}) fusion(f32[8,384]{1,0:T(8,128)S(1)} %bitcast.164, f32[64]{0:T(128)S(1)} %fusion.25), kind=kLoop, calls=%fused_computation.3 | loop fusion | flops 196608 | bytes 1585408 | tf_op jit(solution)/shard_map/sin | solution.py:971
  106.3 7.5 %all-to-all-done.1.att_ref = bf16[8,192,128]{2,1,0:T(8,128)(2,1)} async-done(((bf16[8,192,128]{2,1,0:T(8,128)(2,1)}), bf16[8,192,128]{2,1,0:T(8,128)(2,1)}, u32[]{:S(2)}, u32[]{:S(2)}) %all-to-all-start.1) | async-done | bytes 393248 | tf_op jit(solution)/shard_map/all_to_all | solution.py:1072
  115.3 10.4 %middle_stage.1 = (bf16[256,768]{1,0:T(8,128)(2,1)}, bf16[8,192,128]{2,1,0:T(8,128)(2,1)}, f32[256,768]{1,0:T(8,128)}, bf16[256,768]{1,0:T(8,128)(2,1)}, bf16[25...) custom-call(s32[4]{0:T(128)} %pad_add_fusion.1.place_ref, ...), custom_call_target="tpu_custom_call" | custom-call | flops 4982833152 | bytes 10485760 | tf_op jit(solution)/shard_map/middle_stage/pallas_call | solution.py:605
  125.8 4.7 %gone_grads.1 = (bf16[2,192,2048]{2,1,0:T(8,128)(2,1)}, bf16[2,192,2176]{2,1,0:T(8,128)(2,1)}) custom-call(s32[5]{0:T(128)} %stack.119.sides_ref, bf16[256,768]{1,0:T(8,128)(2,1)} %get-tuple-element.214.refs_0_, bf16[256,768]{1,0:T(8,128)(2,1)} %get-tuple-element.215.refs_1_, bf16[256,768]{1,0:T(8,128)(2,1)} %get-tuple-element.216.refs_2_, ...), custom_call_target="tpu_custom_call" | custom-call | flops 830472192 | bytes 9732096 | tf_op jit(solution)/shard_map/gone_grads/pallas_call | solution.py:781
  131.0 3.8 %all-to-all-start.2 = ((bf16[8,192,128]{2,1,0:T(8,128)(2,1)}), bf16[8,192,128]{2,1,0:T(8,128)(2,1)S(1)}, u32[]{:S(2)}, u32[]{:S(2)}) async-start(bf16[8,192,128]{2,1,0:T(8,128)(2,1)} %get-tuple-element.213), calls=%async_computation.2 | async-start | bytes 786432 | tf_op jit(solution)/shard_map/all_to_all | solution.py:1098
  136.7 6.7 %kept_grads.1 = (bf16[192,2048]{1,0:T(8,128)(2,1)}, bf16[192,2048]{1,0:T(8,128)(2,1)}, bf16[8,24,2176]{2,1,0:T(8,128)(2,1)}, bf16[8,24,2176]{2,1,0:T(8,128)(2,1)}) custom-call(s32[5]{0:T(128)} %stack.119.sides_ref, bf16[256,768]{1,0:T(8,128)(2,1)} %get-tuple-element.214.refs_0_, bf16[256,768]{1,0:T(8,128)(2,1)} %get-tuple-element.215.refs_1_, ...), custom_call_target="tpu_custom_call" | custom-call | flops 830472192 | bytes 9732096 | tf_op jit(solution)/shard_map/kept_grads/pallas_call | solution.py:781
  143.3 3.4 %all-to-all-done.2.grad_ref = bf16[8,192,128]{2,1,0:T(8,128)(2,1)S(1)} async-done(((bf16[8,192,128]{2,1,0:T(8,128)(2,1)}), bf16[8,192,128]{2,1,0:T(8,128)(2,1)S(1)}, u32[]{:S(2)}, u32[]{:S(2)}) %all-to-all-start.2) | async-done | bytes 393248 | tf_op jit(solution)/shard_map/all_to_all | solution.py:1098
  149.7 23.6 %attend_back.1 = (bf16[8,256,384]{2,1,0:T(8,128)(2,1)}, bf16[8,704,128]{2,1,0:T(8,128)(2,1)}) custom-call(s32[8]{0:T(128)} %get-tuple-element.147.base_ref, s32[8]{0:T(128)} %get-tuple-element.148.count_ref, s32[6]{0:T(128)} %pad_add_fusion.2.units_ref, bf16[2048,384]{1,0:T(8,128)(2,1)} %get-tuple-element.181.q_ref.k_ref.v_ref, ...), custom_call_target="tpu_custom_call" | custom-call | flops 8053063680 | bytes 12582912 | tf_op jit(solution)/shard_map/attend_back/pallas_call | solution.py:416
  173.4 5.7 %all-to-all-start.3 = ((bf16[8,704,128]{2,1,0:T(8,128)(2,1)}), bf16[8,704,128]{2,1,0:T(8,128)(2,1)S(1)}, u32[]{:S(2)}, u32[]{:S(2)}) async-start(bf16[8,704,128]{2,1,0:T(8,128)(2,1)} %get-tuple-element.238), calls=%async_computation.3 | async-start | bytes 2883584 | tf_op jit(solution)/shard_map/all_to_all | solution.py:1142
  179.6 3.3 %add_halves.4 = (bf16[4,24,2048]{2,1,0:T(8,128)(2,1)}, bf16[4,24,2048]{2,1,0:T(8,128)(2,1)}, bf16[1,96,2176]{2,1,0:T(8,128)(2,1)}, bf16[1,96,2176]{2,1,0:T(8,128)(2,1)}) custom-call(s32[5]{0:T(128)} %stack.119.sides_ref, bf16[4,2,24,2048]{3,2,1,0:T(8,128)(2,1)} %bitcast.147, bf16[4,2,24,2048]{3,2,1,0:T(8,128)(2,1)} %bitcast.37.refs_1_, ...), custom_call_target="tpu_custom_call" | custom-call | flops 1622016 | bytes 4866048 | tf_op jit(solution)/shard_map/add_halves/pallas_call | solution.py:869
  186.3 6.5 %head_grads.1 = (bf16[2,192,384]{2,1,0:T(8,128)(2,1)}, bf16[2,192,384]{2,1,0:T(8,128)(2,1)}) custom-call(s32[5]{0:T(128)} %stack.119.sides_ref, bf16[2048,768]{1,0:T(8,128)(2,1)} %get-tuple-element.250.left_ref, bf16[8,256,384]{2,1,0:T(8,128)(2,1)} %get-tuple-element.251.right_ref), custom_call_target="tpu_custom_call" | custom-call | flops 1207959552 | bytes 4718592 | tf_op jit(solution)/shard_map/head_grads/pallas_call | solution.py:820
  194.6 8.3 %collective-permute-done.29 = bf16[4,24,2048]{2,1,0:T(8,128)(2,1)S(1)} collective-permute-done((bf16[4,24,2048]{2,1,0:T(8,128)(2,1)}, bf16[4,24,2048]{2,1,0:T(8,128)(2,1)S(1)}, u32[]{:S(2)}, u32[]{:S(2)}) %collective-permute-start.29) | collective-permute-done | bytes 393248 | tf_op jit(solution)/shard_map/ppermute | solution.py:1152
  203.8 2.5 %add_halves.5 = (bf16[2,24,4224]{2,1,0:T(8,128)(2,1)}, bf16[2,24,4224]{2,1,0:T(8,128)(2,1)}) custom-call(s32[5]{0:T(128)} %stack.119.sides_ref, bf16[2,2,24,2048]{3,2,1,0:T(8,128)(2,1)} %bitcast.153, bf16[2,2,24,2048]{3,2,1,0:T(8,128)(2,1)} %bitcast.154, bf16[2,2,24,2176]{3,2,1,0:T(8,128)(2,1)} %bitcast.148, bf16[2,2,24,2176]{3,2,1,0:T(8,128)(2,1)} %bitcast.149), custom_call_target="tpu_custom_call" | custom-call | flops 811008 | bytes 2433024 | tf_op jit(solution)/shard_map/add_halves/pallas_call | solution.py:869
  210.4 4.7 %settle.1.w_ref = bf16[768,2304]{1,0:T(8,128)(2,1)} custom-call(s32[4]{0:T(128)} %pad_add_fusion.1.place_ref, bf16[4,48,2304]{2,1,0:T(8,128)(2,1)} %copy-done.1, bf16[4,48,2304]{2,1,0:T(8,128)(2,1)} %copy-done.4, bf16[4,48,2304]{2,1,0:T(8,128)(2,1)} %copy-done.5, bf16[4,48,2304]{2,1,0:T(8,128)(2,1)} %copy-done.6), custom_call_target="tpu_custom_call" | custom-call | bytes 8388608 | tf_op jit(solution)/shard_map/settle/pallas_call | solution.py:646
  215.1 5.8 %collective-permute-done.34 = bf16[2,24,4224]{2,1,0:T(8,128)(2,1)S(1)} collective-permute-done((bf16[2,24,4224]{2,1,0:T(8,128)(2,1)}, bf16[2,24,4224]{2,1,0:T(8,128)(2,1)S(1)}, u32[]{:S(2)}, u32[]{:S(2)}) %collective-permute-start.34) | collective-permute-done | bytes 405536 | tf_op jit(solution)/shard_map/ppermute | solution.py:1166
  225.1 3.4 %all-to-all-start.4 = ((bf16[8,24,384]{2,1,0:T(8,128)(2,1)}), bf16[8,24,384]{2,1,0:T(8,128)(2,1)S(1)}, u32[]{:S(2)}, u32[]{:S(2)}) async-start(bf16[8,24,384]{2,1,0:T(8,128)(2,1)} %bitcast.50), calls=%async_computation.4 | async-start | bytes 294912 | tf_op jit(solution)/shard_map/all_to_all | solution.py:1183
  228.5 5.2 %finish.1 = bf16[256,768]{1,0:T(8,128)(2,1)} custom-call(bf16[8,704,128]{2,1,0:T(8,128)(2,1)} %copy-done, bf16[256,768]{1,0:T(8,128)(2,1)} %bitcast.141, f32[8,768]{1,0:T(8,128)} %get-tuple-element.157.refs_3_.refs_4_.refs_2_.gain_ref, f32[256,768]{1,0:T(8,128)} %get-tuple-element.271.grad_ref, bf16[768,2304]{1,0:T(8,128)(2,1)} %settle.1.w_ref), custom_call_target="tpu_custom_call" | custom-call | flops 905969664 | bytes 6291456 | tf_op jit(solution)/shard_map/finish/pallas_call | solution.py:679
  233.7 3.0 %collective-permute-done.36 = bf16[1,24,4224]{2,1,0:T(8,128)(2,1)S(1)} collective-permute-done((bf16[1,24,4224]{2,1,0:T(8,128)(2,1)}, bf16[1,24,4224]{2,1,0:T(8,128)(2,1)S(1)}, u32[]{:S(2)}, u32[]{:S(2)}) %collective-permute-start.36) | collective-permute-done | bytes 202784 | tf_op jit(solution)/shard_map/ppermute | solution.py:1173
  (192 shorter events, 59.0 us)
Async XLA Ops:
  0.6 19.8 %collective-permute-start = (bf16[256,768]{1,0:T(8,128)(2,1)}, bf16[256,768]{1,0:T(8,128)(2,1)S(1)}, u32[]{:S(2)}, u32[]{:S(2)}) collective-permute-start(bf16[256,768]{1,0:T(8,128)(2,1)} %bitcast.137), channel_id=1, source_target_pairs={{0,2},{1,3},{2,4},{3,5},{4,6},{5,7},{6,0},{7,1},{8,10},{9,11},{10,... | collective-permute-start | bytes 1179656 | tf_op jit(solution)/shard_map/ppermute | solution.py:981
  3.7 16.7 %collective-permute-start.1 = (bf16[256,768]{1,0:T(8,128)(2,1)}, bf16[256,768]{1,0:T(8,128)(2,1)S(1)}, u32[]{:S(2)}, u32[]{:S(2)}) collective-permute-start(bf16[256,768]{1,0:T(8,128)(2,1)} %bitcast.138), channel_id=1, source_target_pairs={{0,1},{1,0},{2,3},{3,2},{4,5},{5,4},{6,7},{7,6},{8,9},{9,8},{10,11... | collective-permute-start | bytes 1179656 | tf_op jit(solution)/shard_map/ppermute | solution.py:982
  6.2 14.2 %collective-permute-start.2 = (bf16[2,24,2176]{2,1,0:T(8,128)(2,1)S(1)}, bf16[2,24,2176]{2,1,0:T(8,128)(2,1)S(1)}, u32[]{:S(2)}, u32[]{:S(2)}) collective-permute-start(bf16[2,24,2176]{2,1,0:T(8,128)(2,1)S(1)} %pad_maximum_fusion.6), channel_id=1, source_target_pairs={{0,2},{1,3},{2,4},{3,5},{4,6},{5,7},{6,0},{7,1},{8,10},{9,11},{10,... | collective-permute-start | bytes 626696 | tf_op jit(solution)/shard_map/ppermute | solution.py:983
  9.6 15.5 %all-to-all-start = ((bf16[8,32,512]{2,1,0:T(8,128)(2,1)}), bf16[8,32,512]{2,1,0:T(8,128)(2,1)S(1)}, u32[]{:S(2)}, u32[]{:S(2)}) async-start(bf16[8,32,512]{2,1,0:T(8,128)(2,1)} %spread.1), calls=%async_computation | async-start | bytes 524288 | tf_op jit(solution)/shard_map/all_to_all | solution.py:974
  25.2 17.3 %collective-permute-start.3 = (bf16[256,768]{1,0:T(8,128)(2,1)S(1)}, bf16[256,768]{1,0:T(8,128)(2,1)S(1)}, u32[]{:S(2)}, u32[]{:S(2)}) collective-permute-start(bf16[256,768]{1,0:T(8,128)(2,1)S(1)} %collective-permute-done.refs_0_), channel_id=1, source_target_pairs={{0,2},{1,3},{2,4},{3,5},{4,6},{5,7},{6,0},{7,1},{8,10},{9,11},{10,... | collective-permute-start | bytes 1179656 | tf_op jit(solution)/shard_map/ppermute | solution.py:995
  26.1 16.4 %collective-permute-start.4 = (bf16[256,768]{1,0:T(8,128)(2,1)S(1)}, bf16[256,768]{1,0:T(8,128)(2,1)S(1)}, u32[]{:S(2)}, u32[]{:S(2)}) collective-permute-start(bf16[256,768]{1,0:T(8,128)(2,1)S(1)} %collective-permute-done.refs_0_), channel_id=1, source_target_pairs={{0,1},{1,0},{2,3},{3,2},{4,5},{5,4},{6,7},{7,6},{8,9},{9,8},{10,11... | collective-permute-start | bytes 1179656 | tf_op jit(solution)/shard_map/ppermute | solution.py:996
  26.7 15.8 %collective-permute-start.5 = (bf16[2,24,2176]{2,1,0:T(8,128)(2,1)S(1)}, bf16[2,24,2176]{2,1,0:T(8,128)(2,1)S(1)}, u32[]{:S(2)}, u32[]{:S(2)}) collective-permute-start(bf16[2,24,2176]{2,1,0:T(8,128)(2,1)S(1)} %collective-permute-done.2), channel_id=1, source_target_pairs={{0,2},{1,3},{2,4},{3,5},{4,6},{5,7},{6,0},{7,1},{8,10},{9,11},{10,... | collective-permute-start | bytes 626696 | tf_op jit(solution)/shard_map/ppermute | solution.py:997
  42.5 16.5 %collective-permute-start.8 = (bf16[256,768]{1,0:T(8,128)(2,1)S(1)}, bf16[256,768]{1,0:T(8,128)(2,1)S(1)}, u32[]{:S(2)}, u32[]{:S(2)}) collective-permute-start(bf16[256,768]{1,0:T(8,128)(2,1)S(1)} %collective-permute-done.3.refs_0_), channel_id=1, source_target_pairs={{0,2},{1,3},{2,4},{3,5},{4,6},{5,7},{6,0},{7,1},{8,10},{9,11},{10,... | collective-permute-start | bytes 1179656 | tf_op jit(solution)/shard_map/ppermute | solution.py:1015
  42.6 16.5 %collective-permute-start.9 = (bf16[256,768]{1,0:T(8,128)(2,1)S(1)}, bf16[256,768]{1,0:T(8,128)(2,1)S(1)}, u32[]{:S(2)}, u32[]{:S(2)}) collective-permute-start(bf16[256,768]{1,0:T(8,128)(2,1)S(1)} %collective-permute-done.3.refs_0_), channel_id=1, source_target_pairs={{0,1},{1,0},{2,3},{3,2},{4,5},{5,4},{6,7},{7,6},{8,9},{9,8},{10,11... | collective-permute-start | bytes 1179656 | tf_op jit(solution)/shard_map/ppermute | solution.py:1016
  44.2 14.9 %collective-permute-start.10 = (bf16[2,24,2176]{2,1,0:T(8,128)(2,1)S(1)}, bf16[2,24,2176]{2,1,0:T(8,128)(2,1)S(1)}, u32[]{:S(2)}, u32[]{:S(2)}) collective-permute-start(bf16[2,24,2176]{2,1,0:T(8,128)(2,1)S(1)} %collective-permute-done.5), channel_id=1, source_target_pairs={{0,2},{1,3},{2,4},{3,5},{4,6},{5,7},{6,0},{7,1},{8,10},{9,11},{10,... | collective-permute-start | bytes 626696 | tf_op jit(solution)/shard_map/ppermute | solution.py:1017
  44.2 14.9 %collective-permute-start.11 = (bf16[2,24,2176]{2,1,0:T(8,128)(2,1)S(1)}, bf16[2,24,2176]{2,1,0:T(8,128)(2,1)S(1)}, u32[]{:S(2)}, u32[]{:S(2)}) collective-permute-start(bf16[2,24,2176]{2,1,0:T(8,128)(2,1)S(1)} %get-tuple-element.152), channel_id=1, source_target_pairs={{0,1},{1,0},{2,3},{3,2},{4,5},{5,4},{6,7},{7,6},{8,9},{9,8},{10,11... | collective-permute-start | bytes 626696 | tf_op jit(solution)/shard_map/ppermute | solution.py:1018
  45.3 13.7 %collective-permute-start.12 = (bf16[2,24,2176]{2,1,0:T(8,128)(2,1)S(1)}, bf16[2,24,2176]{2,1,0:T(8,128)(2,1)S(1)}, u32[]{:S(2)}, u32[]{:S(2)}) collective-permute-start(bf16[2,24,2176]{2,1,0:T(8,128)(2,1)S(1)} %get-tuple-element.153), channel_id=1, source_target_pairs={{0,16},{8,24},{16,0},{24,8},{1,17},{9,25},{17,1},{25,9},{2,18},{10... | collective-permute-start | bytes 626696 | tf_op jit(solution)/shard_map/ppermute | solution.py:1019
  59.1 13.8 %collective-permute-start.13 = (bf16[256,768]{1,0:T(8,128)(2,1)S(1)}, bf16[256,768]{1,0:T(8,128)(2,1)S(1)}, u32[]{:S(2)}, u32[]{:S(2)}) collective-permute-start(bf16[256,768]{1,0:T(8,128)(2,1)S(1)} %collective-permute-done.8.refs_2_), channel_id=1, source_target_pairs={{0,1},{1,0},{2,3},{3,2},{4,5},{5,4},{6,7},{7,6},{8,9},{9,8},{10,11... | collective-permute-start | bytes 1179656 | tf_op jit(solution)/shard_map/ppermute | solution.py:1029
  60.8 12.1 %collective-permute-start.14 = (bf16[2,24,2176]{2,1,0:T(8,128)(2,1)S(1)}, bf16[2,24,2176]{2,1,0:T(8,128)(2,1)S(1)}, u32[]{:S(2)}, u32[]{:S(2)}) collective-permute-start(bf16[2,24,2176]{2,1,0:T(8,128)(2,1)S(1)} %pad_maximum_fusion.9), channel_id=1, source_target_pairs={{0,1},{1,0},{2,3},{3,2},{4,5},{5,4},{6,7},{7,6},{8,9},{9,8},{10,11... | collective-permute-start | bytes 626696 | tf_op jit(solution)/shard_map/ppermute | solution.py:1032
  73.0 22.5 %collective-permute-start.17 = (bf16[4,48,2176]{2,1,0:T(8,128)(2,1)S(1)}, bf16[4,48,2176]{2,1,0:T(8,128)(2,1)}, u32[]{:S(2)}, u32[]{:S(2)}) collective-permute-start(bf16[4,48,2176]{2,1,0:T(8,128)(2,1)S(1)} %maximum_maximum_fusion.refs_0_), channel_id=1, source_target_pairs={{0,16},{8,24},{16,0},{24,8},{1,17},{9,25},{17,1},{25,9},{2,18},{10... | collective-permute-start | bytes 2506760 | tf_op jit(solution)/shard_map/ppermute | solution.py:1045
  74.7 20.9 %collective-permute-start.18 = (bf16[8,24,2176]{2,1,0:T(8,128)(2,1)S(1)}, bf16[8,24,2176]{2,1,0:T(8,128)(2,1)S(1)}, u32[]{:S(2)}, u32[]{:S(2)}) collective-permute-start(bf16[8,24,2176]{2,1,0:T(8,128)(2,1)S(1)} %constant_dynamic-update-slice_fusion), channel_id=1, source_target_pairs={{0,1},{1,0},{2,3},{3,2},{4,5},{5,4},{6,7},{7,6},{8,9},{9,8},{10,11... | collective-permute-start | bytes 2506760 | tf_op jit(solution)/shard_map/ppermute | solution.py:1046
  76.3 19.2 %collective-permute-start.19 = (bf16[2,24,2304]{2,1,0:T(8,128)(2,1)S(1)}, bf16[2,24,2304]{2,1,0:T(8,128)(2,1)S(1)}, u32[]{:S(2)}, u32[]{:S(2)}) collective-permute-start(bf16[2,24,2304]{2,1,0:T(8,128)(2,1)S(1)} %pad_maximum_fusion.7), channel_id=1, source_target_pairs={{0,4},{1,5},{2,6},{3,7},{4,0},{5,1},{6,2},{7,3},{8,12},{9,13},{10,... | collective-permute-start | bytes 663560 | tf_op jit(solution)/shard_map/ppermute | solution.py:1041
  95.9 18.0 %collective-permute-start.22 = (bf16[8,48,2176]{2,1,0:T(8,128)(2,1)S(1)}, bf16[8,48,2176]{2,1,0:T(8,128)(2,1)}, u32[]{:S(2)}, u32[]{:S(2)}) collective-permute-start(bf16[8,48,2176]{2,1,0:T(8,128)(2,1)S(1)} %pad_maximum_fusion.refs_4_), channel_id=1, source_target_pairs={{0,8},{8,0},{16,24},{24,16},{1,9},{9,1},{17,25},{25,17},{2,10},{10... | collective-permute-start | bytes 5013512 | tf_op jit(solution)/shard_map/ppermute | solution.py:1066
  97.1 16.7 %collective-permute-start.21 = (bf16[4,48,2176]{2,1,0:T(8,128)(2,1)}, bf16[4,48,2176]{2,1,0:T(8,128)(2,1)}, u32[]{:S(2)}, u32[]{:S(2)}) collective-permute-start(bf16[4,48,2176]{2,1,0:T(8,128)(2,1)} %collective-permute-done.17.refs_1_), channel_id=1, source_target_pairs={{0,8},{8,0},{16,24},{24,16},{1,9},{9,1},{17,25},{25,17},{2,10},{10... | collective-permute-start | bytes 2506760 | tf_op jit(solution)/shard_map/ppermute | solution.py:1065
  97.5 16.4 %all-to-all-start.1 = ((bf16[8,192,128]{2,1,0:T(8,128)(2,1)}), bf16[8,192,128]{2,1,0:T(8,128)(2,1)}, u32[]{:S(2)}, u32[]{:S(2)}) async-start(bf16[8,192,128]{2,1,0:T(8,128)(2,1)} %get-tuple-element.192), calls=%async_computation.1 | async-start | bytes 786432 | tf_op jit(solution)/shard_map/all_to_all | solution.py:1072
  131.0 15.7 %all-to-all-start.2 = ((bf16[8,192,128]{2,1,0:T(8,128)(2,1)}), bf16[8,192,128]{2,1,0:T(8,128)(2,1)S(1)}, u32[]{:S(2)}, u32[]{:S(2)}) async-start(bf16[8,192,128]{2,1,0:T(8,128)(2,1)} %get-tuple-element.213), calls=%async_computation.2 | async-start | bytes 786432 | tf_op jit(solution)/shard_map/all_to_all | solution.py:1098
  135.0 38.3 %collective-permute-start.28 = (bf16[4,48,2304]{2,1,0:T(8,128)(2,1)S(1)}, bf16[4,48,2304]{2,1,0:T(8,128)(2,1)S(1)}, u32[]{:S(2)}, u32[]{:S(2)}) collective-permute-start(bf16[4,48,2304]{2,1,0:T(8,128)(2,1)S(1)} %pad_maximum_fusion.1.refs_0_), channel_id=1, source_target_pairs={{0,16},{8,24},{16,0},{24,8},{1,17},{9,25},{17,1},{25,9},{2,18},{10... | collective-permute-start | bytes 2654216 | tf_op jit(solution)/shard_map/ppermute | solution.py:1097
  146.7 26.6 %collective-permute-start.27 = (bf16[8,24,2176]{2,1,0:T(8,128)(2,1)}, bf16[8,24,2176]{2,1,0:T(8,128)(2,1)}, u32[]{:S(2)}, u32[]{:S(2)}) collective-permute-start(bf16[8,24,2176]{2,1,0:T(8,128)(2,1)} %get-tuple-element.236), channel_id=1, source_target_pairs={{0,1},{1,0},{2,3},{3,2},{4,5},{5,4},{6,7},{7,6},{8,9},{9,8},{10,11... | collective-permute-start | bytes 2506760 | tf_op jit(solution)/shard_map/ppermute | solution.py:1124
  148.2 25.2 %collective-permute-start.26 = (bf16[192,2048]{1,0:T(8,128)(2,1)}, bf16[192,2048]{1,0:T(8,128)(2,1)}, u32[]{:S(2)}, u32[]{:S(2)}) collective-permute-start(bf16[192,2048]{1,0:T(8,128)(2,1)} %get-tuple-element.234), channel_id=1, source_target_pairs={{0,16},{8,24},{16,0},{24,8},{1,17},{9,25},{17,1},{25,9},{2,18},{10... | collective-permute-start | bytes 2359304 | tf_op jit(solution)/shard_map/ppermute | solution.py:1123
  173.4 47.5 %all-to-all-start.3 = ((bf16[8,704,128]{2,1,0:T(8,128)(2,1)}), bf16[8,704,128]{2,1,0:T(8,128)(2,1)S(1)}, u32[]{:S(2)}, u32[]{:S(2)}) async-start(bf16[8,704,128]{2,1,0:T(8,128)(2,1)} %get-tuple-element.238), calls=%async_computation.3 | async-start | bytes 2883584 | tf_op jit(solution)/shard_map/all_to_all | solution.py:1142
  179.0 23.9 %collective-permute-start.32 = (bf16[4,48,2304]{2,1,0:T(8,128)(2,1)S(1)}, bf16[4,48,2304]{2,1,0:T(8,128)(2,1)S(1)}, u32[]{:S(2)}, u32[]{:S(2)}) collective-permute-start(bf16[4,48,2304]{2,1,0:T(8,128)(2,1)S(1)} %pad_maximum_fusion.1.refs_0_), channel_id=1, source_target_pairs={{0,8},{8,0},{16,24},{24,16},{1,9},{9,1},{17,25},{25,17},{2,10},{10... | collective-permute-start | bytes 2654216 | tf_op jit(solution)/shard_map/ppermute | solution.py:1143
  179.1 23.8 %collective-permute-start.33 = (bf16[4,48,2304]{2,1,0:T(8,128)(2,1)S(1)}, bf16[4,48,2304]{2,1,0:T(8,128)(2,1)S(1)}, u32[]{:S(2)}, u32[]{:S(2)}) collective-permute-start(bf16[4,48,2304]{2,1,0:T(8,128)(2,1)S(1)} %collective-permute-done.28.refs_1_), channel_id=1, source_target_pairs={{0,8},{8,0},{16,24},{24,16},{1,9},{9,1},{17,25},{25,17},{2,10},{10... | collective-permute-start | bytes 2654216 | tf_op jit(solution)/shard_map/ppermute | solution.py:1144
  182.9 20.0 %collective-permute-start.30 = (bf16[1,96,2176]{2,1,0:T(8,128)(2,1)}, bf16[1,96,2176]{2,1,0:T(8,128)(2,1)S(1)}, u32[]{:S(2)}, u32[]{:S(2)}) collective-permute-start(bf16[1,96,2176]{2,1,0:T(8,128)(2,1)} %get-tuple-element.248), channel_id=1, source_target_pairs={{0,16},{8,24},{16,0},{24,8},{1,17},{9,25},{17,1},{25,9},{2,18},{10... | collective-permute-start | bytes 1253384 | tf_op jit(solution)/shard_map/ppermute | solution.py:1153
  184.4 18.5 %collective-permute-start.29 = (bf16[4,24,2048]{2,1,0:T(8,128)(2,1)}, bf16[4,24,2048]{2,1,0:T(8,128)(2,1)S(1)}, u32[]{:S(2)}, u32[]{:S(2)}) collective-permute-start(bf16[4,24,2048]{2,1,0:T(8,128)(2,1)} %get-tuple-element.246), channel_id=1, source_target_pairs={{0,1},{1,0},{2,3},{3,2},{4,5},{5,4},{6,7},{7,6},{8,9},{9,8},{10,11... | collective-permute-start | bytes 1179656 | tf_op jit(solution)/shard_map/ppermute | solution.py:1152
  206.3 14.5 %collective-permute-start.34 = (bf16[2,24,4224]{2,1,0:T(8,128)(2,1)}, bf16[2,24,4224]{2,1,0:T(8,128)(2,1)S(1)}, u32[]{:S(2)}, u32[]{:S(2)}) collective-permute-start(bf16[2,24,4224]{2,1,0:T(8,128)(2,1)} %get-tuple-element.261), channel_id=1, source_target_pairs={{0,2},{1,3},{2,0},{3,1},{4,6},{5,7},{6,4},{7,5},{8,10},{9,11},{10,... | collective-permute-start | bytes 1216520 | tf_op jit(solution)/shard_map/ppermute | solution.py:1166
  223.5 13.2 %collective-permute-start.36 = (bf16[1,24,4224]{2,1,0:T(8,128)(2,1)}, bf16[1,24,4224]{2,1,0:T(8,128)(2,1)S(1)}, u32[]{:S(2)}, u32[]{:S(2)}) collective-permute-start(bf16[1,24,4224]{2,1,0:T(8,128)(2,1)} %get-tuple-element.277), channel_id=1, source_target_pairs={{0,4},{1,5},{2,6},{3,7},{4,0},{5,1},{6,2},{7,3},{8,12},{9,13},{10,... | collective-permute-start | bytes 608264 | tf_op jit(solution)/shard_map/ppermute | solution.py:1173
  225.1 14.4 %all-to-all-start.4 = ((bf16[8,24,384]{2,1,0:T(8,128)(2,1)}), bf16[8,24,384]{2,1,0:T(8,128)(2,1)S(1)}, u32[]{:S(2)}, u32[]{:S(2)}) async-start(bf16[8,24,384]{2,1,0:T(8,128)(2,1)} %bitcast.50), calls=%async_computation.4 | async-start | bytes 294912 | tf_op jit(solution)/shard_map/all_to_all | solution.py:1183
  (37 other events, 299.2 us)

commit v7 on v6

--- a/solution.py
+++ b/solution.py
@@ -202,14 +202,22 @@
     )(at, *blocks, w_heads, gains, cosine, sine, *held)
 
 
-def gather_rows(units_ref, ref, part):
+def unit_rows(units_ref, ref, unit, first, part):
     lane = lax.broadcasted_iota(jnp.int32, (part, LANES), 1)
-    chunks = []
-    for unit in range(UNITS):
-        start = pl.multiple_of(units_ref[UNITS + unit] * part, part)
-        chunk = ref[pl.ds(start, part), :]
-        chunks.append(jnp.where(lane // HD == units_ref[unit], chunk, jnp.zeros_like(chunk)))
-    return jnp.concatenate(chunks, axis=0)
+    start = pl.multiple_of(first + units_ref[UNITS + unit] * part, part)
+    chunk = ref[pl.ds(start, part), :]
+    return jnp.where(lane // HD == units_ref[unit], chunk, jnp.zeros_like(chunk))
+
+
+def jobs(step, part):
+    every = slice(0, UNITS * part)
+    return [
+        (2 * step + at, [(at, unit) for unit in range(UNITS)], [(at, every)]) for at in range(2)
+    ]
+
+
+def row_of(ref, row, where):
+    return jnp.concatenate([ref[at, row : row + 1, columns] for at, columns in where], axis=1)
 
 
 def slot_rows(units_ref, unit):
@@ -235,73 +243,84 @@
     return reduce(values.reshape(rows // 8, 8, wide), axis=0)
 
 
-def tile_span(base_ref, block, at, tile):
-    return pl.ds(pl.multiple_of(base_ref[block] * GRAIN + at * tile, GRAIN), tile)
-
-
-def masked(scores, base_ref, block, at, tile, range_ref):
-    key = lax.broadcasted_iota(jnp.int32, scores.shape, 0) + (base_ref[block] * GRAIN + at * tile)
-    same = (key >= range_ref[0, :1, :]) & (key < range_ref[0, 1:2, :])
-    return jnp.where(same, scores, NEG)
+def tile_span(first, at, tile):
+    return pl.ds(pl.multiple_of(first + at * tile, GRAIN), tile)
+
+
+def masked(scores, first, at, tile, low, high):
+    key = lax.broadcasted_iota(jnp.int32, scores.shape, 0) + (first + at * tile)
+    return jnp.where((key >= low) & (key < high), scores, NEG)
 
 
 def attend_kernel(tile, base_ref, count_ref, units_ref, q_ref, k_ref, vt_ref, range_ref,
                   low_ref, att_ref, lse_ref, s_ref, acc_ref):
-    block = pl.program_id(0)
     wide = s_ref.shape[1]
     part = wide // UNITS
-    queries = gather_rows(units_ref, q_ref, part)
-
-    def score(at, top):
-        span = tile_span(base_ref, block, at, tile)
-        scores = masked(dot_tt(k_ref[span, :], queries), base_ref, block, at, tile, range_ref)
-        s_ref[span, :] = scores
-        return jnp.maximum(top, fold(scores, jnp.max))
-
-    count = count_ref[block]
-    top = lax.fori_loop(0, count, score, jnp.full((8, wide), NEG, f32))
-    top = jnp.max(top, axis=0, keepdims=True)
-
-    def weigh(at, carry):
-        total, accum = carry
-        span = tile_span(base_ref, block, at, tile)
-        expo = jnp.exp(s_ref[span, :] - top)
-        total = total + fold(expo, jnp.sum)
-        accum = accum + jnp.dot(vt_ref[:, span], expo.astype(bf16), preferred_element_type=f32)
-        return (total, accum)
-
-    total, accum = lax.fori_loop(
-        0, count, weigh, (jnp.zeros((8, wide), f32), jnp.zeros((LANES, wide), f32))
-    )
-    total = jnp.sum(total, axis=0, keepdims=True)
-    lse_ref[0] = top + jnp.log(total)
-    acc_ref[...] = accum / total
-    pieces = [
-        acc_ref[slot_rows(units_ref, unit), unit * part : (unit + 1) * part]
-        for unit in range(UNITS)
-    ]
-    att_ref[0] = jnp.concatenate(pieces, axis=1)
-    low_ref[0] = pack(pieces)
+    rows = q_ref.shape[0] // 2
+    pieces = {}
+    for job, places, where in jobs(pl.program_id(0), part):
+        queries = jnp.concatenate(
+            [unit_rows(units_ref, q_ref, unit, at * rows, part) for at, unit in places], axis=0
+        )
+        low = row_of(range_ref, 0, where)
+        high = row_of(range_ref, 1, where)
+        first = base_ref[job] * GRAIN
+        count = count_ref[job]
+
+        def score(at, top):
+            span = tile_span(first, at, tile)
+            scores = masked(dot_tt(k_ref[span, :], queries), first, at, tile, low, high)
+            s_ref[span, :] = scores
+            return jnp.maximum(top, fold(scores, jnp.max))
+
+        top = lax.fori_loop(0, count, score, jnp.full((8, wide), NEG, f32))
+        top = jnp.max(top, axis=0, keepdims=True)
+
+        def weigh(at, carry):
+            total, accum = carry
+            span = tile_span(first, at, tile)
+            expo = jnp.exp(s_ref[span, :] - top)
+            total = total + fold(expo, jnp.sum)
+            accum = accum + jnp.dot(vt_ref[:, span], expo.astype(bf16), preferred_element_type=f32)
+            return (total, accum)
+
+        total, accum = lax.fori_loop(
+            0, count, weigh, (jnp.zeros((8, wide), f32), jnp.zeros((LANES, wide), f32))
+        )
+        total = jnp.sum(total, axis=0, keepdims=True)
+        log_sum = top + jnp.log(total)
+        acc_ref[...] = accum / total
+        for i, (at, unit) in enumerate(places):
+            source = slice(i * part, (i + 1) * part)
+            target = slice(unit * part, (unit + 1) * part)
+            lse_ref[at, :, target] = log_sum[:, source]
+            pieces[at, unit] = acc_ref[slot_rows(units_ref, unit), source]
+            att_ref[at, :, target] = pieces[at, unit]
+    for at in range(2):
+        low_ref[at] = pack([pieces[at, unit] for unit in range(UNITS)])
 
 
 def attend(base, tiles, unit_places, qkv, turned, ranges, rows, tile):
     total = qkv.shape[0]
     count = total // rows
     wide = ranges.shape[2]
-    each = lambda *shape: pl.BlockSpec((1,) + shape, lambda i, *s: (i, 0, 0))
+    two = lambda *shape: pl.BlockSpec((2,) + shape, lambda i, *s: (i, 0, 0))
     return pl.pallas_call(
         functools.partial(attend_kernel, tile),
         grid_spec=pltpu.PrefetchScalarGridSpec(
             num_scalar_prefetch=3,
-            grid=(count,),
+            grid=(count // 2,),
             in_specs=[
-                pl.BlockSpec((rows, LANES), lambda i, *s: (i, 0)),
+                pl.BlockSpec((2 * rows, LANES), lambda i, *s: (i, 0)),
                 pl.BlockSpec((total, LANES), lambda i, *s: (0, 1)),
                 pl.BlockSpec((LANES, total), lambda i, *s: (1, 0)),
-                each(2, wide),
+                two(2, wide),
             ],
-            out_specs=[each(wide // 2, LANES), each(HD, wide), each(1, wide)],
-            scratch_shapes=[pltpu.VMEM((total, wide), f32), pltpu.VMEM((LANES, wide), f32)],
+            out_specs=[two(wide // 2, LANES), two(HD, wide), two(1, wide)],
+            scratch_shapes=[
+                pltpu.VMEM((total, wide), f32),
+                pltpu.VMEM((LANES, wide), f32),
+            ],
         ),
         out_shape=[
             jax.ShapeDtypeStruct((count, wide // 2, LANES), bf16),
@@ -322,57 +341,73 @@
                        grad_ref, att_ref, lse_ref, cos_q_ref, sin_q_ref, cos_hbm, sin_hbm,
                        out_ref, send_ref, dk_ref, dv_ref, acc_ref, gt_ref, full_ref, cos_ref,
                        sin_ref, sems):
-    block = pl.program_id(0)
-    count = pl.num_programs(0)
+    step = pl.program_id(0)
+    steps = pl.num_programs(0)
     rows = full_ref.shape[1]
     wide = acc_ref.shape[1]
     part = wide // UNITS
+    packed = UNITS * part // 2
     tables = [
         pltpu.make_async_copy(cos_hbm, cos_ref, sems.at[0]),
         pltpu.make_async_copy(sin_hbm, sin_ref, sems.at[1]),
     ]
 
-    @pl.when(block == 0)
+    @pl.when(step == 0)
     def _():
         for table in tables:
             table.start()
         dk_ref[...] = jnp.zeros(dk_ref.shape, f32)
         dv_ref[...] = jnp.zeros(dv_ref.shape, f32)
+        full_ref[...] = jnp.zeros(full_ref.shape, f32)
+
+    grads = [unpack(grad_ref[at], part) for at in range(2)]
+    deltas = [
+        jnp.sum(jnp.concatenate(grads[at], axis=1) * att_ref[at], axis=0, keepdims=True)
+        for at in range(2)
+    ]
+    pieces = {}
+    for job, places, where in jobs(step, part):
+        queries = jnp.concatenate(
+            [unit_rows(units_ref, q_ref, unit, at * rows, part) for at, unit in places], axis=0
+        )
+        low = row_of(range_ref, 0, where)
+        high = row_of(range_ref, 1, where)
+        log_sum = row_of(lse_ref, 0, where)
+        delta = jnp.concatenate([deltas[at][:, columns] for at, columns in where], axis=1)
+        first = base_ref[job] * GRAIN
         gt_ref[...] = jnp.zeros(gt_ref.shape, bf16)
-        full_ref[...] = jnp.zeros(full_ref.shape, f32)
-
-    queries = gather_rows(units_ref, q_ref, part)
-    grads = unpack(grad_ref[0], part)
-    delta = jnp.sum(jnp.concatenate(grads, axis=1) * att_ref[0], axis=0, keepdims=True)
-    for unit, piece in enumerate(grads):
-        columns = slice(unit * part, (unit + 1) * part)
-        gt_ref[slot_rows(units_ref, unit), columns] = piece.astype(bf16)
-    log_sum = lse_ref[0]
-
-    def step(at, grad_query):
-        span = tile_span(base_ref, block, at, tile)
-        grads_t = gt_ref[...]
-        scores = masked(dot_tt(k_ref[span, :], queries), base_ref, block, at, tile, range_ref)
-        grad_probs = jnp.dot(v_ref[span, :], grads_t, preferred_element_type=f32)
-        probs = jnp.exp(scores - log_sum)
-        dv_ref[span, :] += dot_tt(probs.astype(bf16), grads_t)
-        grad_scores = (probs * (grad_probs - delta)).astype(bf16)
-        dk_ref[span, :] += jnp.dot(grad_scores, queries, preferred_element_type=f32)
-        return grad_query + jnp.dot(kt_ref[:, span], grad_scores, preferred_element_type=f32)
-
-    acc_ref[...] = lax.fori_loop(0, count_ref[block], step, jnp.zeros((LANES, wide), f32))
-    pieces = []
-    for unit in range(UNITS):
-        columns = slice(unit * part, (unit + 1) * part)
-        piece = acc_ref[slot_rows(units_ref, unit), columns] * HD**-0.5
-        turned = piece * sin_q_ref[0, :, columns]
-        turned = jnp.concatenate([-turned[HD // 2 :], turned[: HD // 2]], axis=0)
-        pieces.append(piece * cos_q_ref[0, :, columns] - turned)
-    send_ref[block, : wide // 2, :] = pack(pieces)
-    place_units(units_ref, full_ref, pieces, part)
-    out_ref[block, :, :LANES] = jnp.transpose(full_ref[...]).astype(bf16)
-
-    @pl.when(block == count - 1)
+        for i, (at, unit) in enumerate(places):
+            columns = slice(i * part, (i + 1) * part)
+            gt_ref[slot_rows(units_ref, unit), columns] = grads[at][unit].astype(bf16)
+
+        def one_tile(at, grad_query):
+            span = tile_span(first, at, tile)
+            grads_t = gt_ref[...]
+            scores = masked(dot_tt(k_ref[span, :], queries), first, at, tile, low, high)
+            grad_probs = jnp.dot(v_ref[span, :], grads_t, preferred_element_type=f32)
+            probs = jnp.exp(scores - log_sum)
+            dv_ref[span, :] += dot_tt(probs.astype(bf16), grads_t)
+            grad_scores = (probs * (grad_probs - delta)).astype(bf16)
+            dk_ref[span, :] += jnp.dot(grad_scores, queries, preferred_element_type=f32)
+            return grad_query + jnp.dot(kt_ref[:, span], grad_scores, preferred_element_type=f32)
+
+        acc_ref[...] = lax.fori_loop(
+            0, count_ref[job], one_tile, jnp.zeros((LANES, wide), f32)
+        )
+        for i, (at, unit) in enumerate(places):
+            source = slice(i * part, (i + 1) * part)
+            target = slice(unit * part, (unit + 1) * part)
+            piece = acc_ref[slot_rows(units_ref, unit), source] * HD**-0.5
+            turned = piece * sin_q_ref[at, :, target]
+            turned = jnp.concatenate([-turned[HD // 2 :], turned[: HD // 2]], axis=0)
+            pieces[at, unit] = piece * cos_q_ref[at, :, target] - turned
+    for at in range(2):
+        found = [pieces[at, unit] for unit in range(UNITS)]
+        send_ref[2 * step + at, :packed, :] = pack(found)
+        place_units(units_ref, full_ref, found, part)
+        out_ref[2 * step + at, :, :LANES] = jnp.transpose(full_ref[...]).astype(bf16)
+
+    @pl.when(step == steps - 1)
     def _():
         for table in tables:
             table.wait()
@@ -385,11 +420,11 @@
             values = dv_ref[span, :].astype(bf16)
             out_ref[at, :, LANES : 2 * LANES] = keys
             out_ref[at, :, 2 * LANES :] = values
-            send_ref[at, wide // 2 : wide // 2 + rows, :] = keys
-            send_ref[at, wide // 2 + rows :, :] = values
+            send_ref[at, packed : packed + rows, :] = keys
+            send_ref[at, packed + rows :, :] = values
             return carry
 
-        lax.fori_loop(0, count, finish, 0)
+        lax.fori_loop(0, 2 * steps, finish, 0)
 
 
 def place_units(units_ref, full_ref, pieces, part):
@@ -409,7 +444,7 @@
     count = total // rows
     wide = ranges.shape[2]
     whole = lambda part: pl.BlockSpec((total, LANES), lambda i, *s: (0, part))
-    each = lambda *shape: pl.BlockSpec((1,) + shape, lambda i, *s: (i, 0, 0))
+    two = lambda *shape: pl.BlockSpec((2,) + shape, lambda i, *s: (i, 0, 0))
     kept = lambda *shape: pl.BlockSpec(shape, lambda i, *s: (0, 0, 0))
     outside = pl.BlockSpec(memory_space=pl.ANY)
     table = pltpu.VMEM((total, LANES), f32)
@@ -417,18 +452,18 @@
         functools.partial(attend_back_kernel, tile),
         grid_spec=pltpu.PrefetchScalarGridSpec(
             num_scalar_prefetch=3,
-            grid=(count,),
+            grid=(count // 2,),
             in_specs=[
-                pl.BlockSpec((rows, LANES), lambda i, *s: (i, 0)),
+                pl.BlockSpec((2 * rows, LANES), lambda i, *s: (i, 0)),
                 whole(1),
                 whole(2),
                 pl.BlockSpec((LANES, total), lambda i, *s: (0, 0)),
-                each(2, wide),
-                each(wide // 2, LANES),
-                each(HD, wide),
-                each(1, wide),
-                each(HD, wide),
-                each(HD, wide),
+                two(2, wide),
+                two(wide // 2, LANES),
+                two(HD, wide),
+                two(1, wide),
+                two(HD, wide),
+                two(HD, wide),
                 outside,
                 outside,
             ],
@@ -1097,7 +1132,7 @@
             far_c = lax.ppermute(pair_c, "fsdp", by_y)
         grad_heads = lax.all_to_all(grad_heads, "ctx", 0, 0, tiled=True)
         if by_hand:
-            grad_cut = columns // LANES // 2 * LANES
+            grad_cut = columns // LANES * 5 // 11 * LANES
             rest = columns - grad_cut
             gone_a, gone_b = weight_grads(
                 gone_grads_kernel, sides, operands, [], [(2, share, grad_cut), (2, share, rest)],

time: 242 us -> 241 us (level)
  starting transfers between devices: 57 us -> 54.4 us
  transfers between devices with their start and end apart: 42 -> 42, of which waited for: 14 -> 15; matrix products, arithmetic and copies ran while one was open for 9% -> 9% of each run, Pallas kernels for 42% -> 42%
where the time goes in v7:
time: 241 us; the launch traced here: 240 us
  Pallas kernels  108 us (45%)
  starting transfers between devices  54.4 us (23%)
  waiting for transfers between devices  50.6 us (21%)
  other arithmetic  21 us (9%)
  local copies, waits for them, and re-layouts  4.76 us (2%)
    pallas_call x1, Pallas kernels, attend_back(): pl.pallas_call(functools.partial(attend_back_kernel, tile), grid_spec=plt...  22.8 us
    pallas_call x4, Pallas kernels, project(): pl.pallas_call(functools.partial(project_kernel, count), grid_spec=pltpu....  18.1 us
    pallas_call x1, Pallas kernels, attend(): pl.pallas_call(functools.partial(attend_kernel, tile), grid_spec=pltpu.Pr...  15.1 us
    pallas_call x2, Pallas kernels, weight_grads(): pl.pallas_call(functools.partial(kernel, len(operands) // 2, cut), in_spe...  11.5 us
    pallas_call x1, Pallas kernels, middle_stage(): pl.pallas_call(functools.partial(middle_kernel, heads, splits, metas, arr...  10.4 us
    pallas_call x4, Pallas kernels, add_halves(): pl.pallas_call(functools.partial(add_halves_kernel, [pair[3] for pair in...  9.49 us
    ppermute x1, waiting for transfers between devices, on_device(): got_a = lax.ppermute(other_a, 'ctx', swap)  7.78 us
    ppermute x1, waiting for transfers between devices, on_device(): got = lax.ppermute(gone, 'ctx', flips(ctx, 2))  7.64 us
  transfers between devices with their start and end apart: 42, of which 15 were waited for; matrix products, arithmetic and copies ran while one was open for 9% of the time, Pallas kernels for 42%

profile of v7, /device:TPU:0, one launch (start us, length us, event | category | flops | bytes accessed | tf_op | source)
XLA Modules:
  0.0 239.7 jit_solution(7933343002252651944)
XLA Ops:
  0.6 3.1 %collective-permute-start = (bf16[256,768]{1,0:T(8,128)(2,1)}, bf16[256,768]{1,0:T(8,128)(2,1)S(1)}, u32[]{:S(2)}, u32[]{:S(2)}) collective-permute-start(bf16[256,768]{1,0:T(8,128)(2,1)} %bitcast.137), channel_id=1, source_target_pairs={{0,2},{1,3},{2,4},{3,5},{4,6},{5,7},{6,0},{7,1},{8,10},{9,11},{10,... | collective-permute-start | bytes 1179656 | tf_op jit(solution)/shard_map/ppermute | solution.py:1016
  9.6 3.5 %all-to-all-start = ((bf16[8,32,512]{2,1,0:T(8,128)(2,1)}), bf16[8,32,512]{2,1,0:T(8,128)(2,1)S(1)}, u32[]{:S(2)}, u32[]{:S(2)}) async-start(bf16[8,32,512]{2,1,0:T(8,128)(2,1)} %spread.1), calls=%async_computation | async-start | bytes 524288 | tf_op jit(solution)/shard_map/all_to_all | solution.py:1009
  15.8 4.6 %collective-permute-done.2 = bf16[2,24,2176]{2,1,0:T(8,128)(2,1)S(1)} collective-permute-done((bf16[2,24,2176]{2,1,0:T(8,128)(2,1)S(1)}, bf16[2,24,2176]{2,1,0:T(8,128)(2,1)S(1)}, u32[]{:S(2)}, u32[]{:S(2)}) %collective-permute-start.2) | collective-permute-done | bytes 208928 | tf_op jit(solution)/shard_map/ppermute | solution.py:1018
  20.4 4.7 %all-to-all-done = bf16[8,32,512]{2,1,0:T(8,128)(2,1)S(1)} async-done(((bf16[8,32,512]{2,1,0:T(8,128)(2,1)}), bf16[8,32,512]{2,1,0:T(8,128)(2,1)S(1)}, u32[]{:S(2)}, u32[]{:S(2)}) %all-to-all-start) | async-done | bytes 262176 | tf_op jit(solution)/shard_map/all_to_all | solution.py:1009
  29.5 5.6 %multiply_sine_fusion = (f32[2048,128]{1,0:T(8,128)}, f32[2048,128]{1,0:T(8,128)}) fusion(f32[128]{0:T(128)S(1)} %fusion.22, f32[2048]{0:T(1024)S(1)} %bitcast.161), kind=kLoop, calls=%fused_computation.1 | loop fusion | flops 262144 | bytes 2105856 | tf_op jit(solution)/shard_map/sin | solution.py:999
  38.8 3.7 %collective-permute-done.5 = bf16[2,24,2176]{2,1,0:T(8,128)(2,1)S(1)} collective-permute-done((bf16[2,24,2176]{2,1,0:T(8,128)(2,1)S(1)}, bf16[2,24,2176]{2,1,0:T(8,128)(2,1)S(1)}, u32[]{:S(2)}, u32[]{:S(2)}) %collective-permute-start.5) | collective-permute-done | bytes 208928 | tf_op jit(solution)/shard_map/ppermute | solution.py:1032
  46.2 2.1 ready.1
  48.2 4.7 %project.4 = (bf16[2048,768]{1,0:T(8,128)(2,1)}, bf16[2048,384]{1,0:T(8,128)(2,1)}, bf16[256,2048]{1,0:T(8,128)(2,1)}) custom-call(s32[2]{0:T(128)} %pad_add_fusion.4.at_ref, bf16[256,768]{1,0:T(8,128)(2,1)} %bitcast.139, bf16[256,768]{1,0:T(8,128)(2,1)} %copy-done.18, bf16[768,512]{1,0:T(8,128)(2,1)} %get-tuple-element.156.refs_2_.refs_3_.refs_1_, ...), custom_call_target="tpu_custom_call" | custom-call | flops 301989888 | bytes 6291456 | tf_op jit(solution)/shard_map/project/pallas_call | solution.py:179
  52.9 4.8 %project.5 = (bf16[2048,768]{1,0:T(8,128)(2,1)}, bf16[2048,384]{1,0:T(8,128)(2,1)}, bf16[256,2048]{1,0:T(8,128)(2,1)}) custom-call(s32[2]{0:T(128)} %pad_add_fusion.3.at_ref, bf16[256,768]{1,0:T(8,128)(2,1)} %copy-done.12, bf16[256,768]{1,0:T(8,128)(2,1)} %copy-done.14, ...), custom_call_target="tpu_custom_call", output_to_operand_aliasing={{0}: (7, {}), {1}: (8, {}), {2}: (9, {})} | custom-call | flops 301989888 | bytes 6291456 | tf_op jit(solution)/shard_map/project/pallas_call | solution.py:179
  63.0 5.9 %project.6 = (bf16[2048,768]{1,0:T(8,128)(2,1)}, bf16[2048,384]{1,0:T(8,128)(2,1)}, bf16[256,2048]{1,0:T(8,128)(2,1)}) custom-call(s32[3]{0:T(128)} %pad_add_fusion.5.at_ref, bf16[256,768]{1,0:T(8,128)(2,1)} %copy-done.13, bf16[256,768]{1,0:T(8,128)(2,1)} %copy-done.16, ...), custom_call_target="tpu_custom_call", output_to_operand_aliasing={{0}: (8, {}), {1}: (9, {}), {2}: (10, {})} | custom-call | flops 452984832 | bytes 9437184 | tf_op jit(solution)/shard_map/project/pallas_call | solution.py:179
  69.5 3.4 %collective-permute-done.14 = bf16[2,24,2176]{2,1,0:T(8,128)(2,1)S(1)} collective-permute-done((bf16[2,24,2176]{2,1,0:T(8,128)(2,1)S(1)}, bf16[2,24,2176]{2,1,0:T(8,128)(2,1)S(1)}, u32[]{:S(2)}, u32[]{:S(2)}) %collective-permute-start.14) | collective-permute-done | bytes 208928 | tf_op jit(solution)/shard_map/ppermute | solution.py:1067
  77.8 2.8 %project.7 = (bf16[2048,768]{1,0:T(8,128)(2,1)}, bf16[2048,384]{1,0:T(8,128)(2,1)}, bf16[256,2048]{1,0:T(8,128)(2,1)}) custom-call(s32[1]{0:T(128)} %bitcast.18.at_ref, bf16[256,768]{1,0:T(8,128)(2,1)} %copy-done.19, bf16[768,512]{1,0:T(8,128)(2,1)} %get-tuple-element.156.refs_2_.refs_3_.refs_1_, ...), custom_call_target="tpu_custom_call", output_to_operand_aliasing={{0}: (6, {}), {1}: (7, {}), {2}: (8, {})} | custom-call | flops 150994944 | bytes 3145728 | tf_op jit(solution)/shard_map/project/pallas_call | solution.py:179
  80.6 15.1 %attend.1 = (bf16[8,192,128]{2,1,0:T(8,128)(2,1)}, f32[8,64,384]{2,1,0:T(8,128)}, f32[8,1,384]{2,1,0:T(1,128)}) custom-call(s32[8]{0:T(128)} %get-tuple-element.147.base_ref, s32[8]{0:T(128)} %get-tuple-element.148.count_ref, s32[6]{0:T(128)} %pad_add_fusion.2.units_ref, bf16[2048,384]{1,0:T(8,128)(2,1)} %get-tuple-element.181.q_ref.k_ref.v_ref, ...), custom_call_target="tpu_custom_call" | custom-call | flops 3221225472 | bytes 8388608 | tf_op jit(solution)/shard_map/attend/pallas_call | solution.py:308
  97.6 4.3 %all-to-all-start.1 = ((bf16[8,192,128]{2,1,0:T(8,128)(2,1)}), bf16[8,192,128]{2,1,0:T(8,128)(2,1)}, u32[]{:S(2)}, u32[]{:S(2)}) async-start(bf16[8,192,128]{2,1,0:T(8,128)(2,1)} %get-tuple-element.192), calls=%async_computation.1 | async-start | bytes 786432 | tf_op jit(solution)/shard_map/all_to_all | solution.py:1107
  102.5 3.9 %multiply_sine_fusion.1 = (f32[8,64,384]{2,1,0:T(8,128)}, f32[8,64,384]{2,1,0:T(8,128)}) fusion(f32[8,384]{1,0:T(8,128)S(1)} %bitcast.164, f32[64]{0:T(128)S(1)} %fusion.25), kind=kLoop, calls=%fused_computation.3 | loop fusion | flops 196608 | bytes 1585408 | tf_op jit(solution)/shard_map/sin | solution.py:1006
  106.4 7.5 %all-to-all-done.1.att_ref = bf16[8,192,128]{2,1,0:T(8,128)(2,1)} async-done(((bf16[8,192,128]{2,1,0:T(8,128)(2,1)}), bf16[8,192,128]{2,1,0:T(8,128)(2,1)}, u32[]{:S(2)}, u32[]{:S(2)}) %all-to-all-start.1) | async-done | bytes 393248 | tf_op jit(solution)/shard_map/all_to_all | solution.py:1107
  115.5 10.4 %middle_stage.1 = (bf16[256,768]{1,0:T(8,128)(2,1)}, bf16[8,192,128]{2,1,0:T(8,128)(2,1)}, f32[256,768]{1,0:T(8,128)}, bf16[256,768]{1,0:T(8,128)(2,1)}, bf16[25...) custom-call(s32[4]{0:T(128)} %pad_add_fusion.1.place_ref, ...), custom_call_target="tpu_custom_call" | custom-call | flops 4982833152 | bytes 10485760 | tf_op jit(solution)/shard_map/middle_stage/pallas_call | solution.py:640
  125.9 4.8 %gone_grads.1 = (bf16[2,192,1920]{2,1,0:T(8,128)(2,1)}, bf16[2,192,2304]{2,1,0:T(8,128)(2,1)}) custom-call(s32[5]{0:T(128)} %stack.119.sides_ref, bf16[256,768]{1,0:T(8,128)(2,1)} %get-tuple-element.214.refs_0_, bf16[256,768]{1,0:T(8,128)(2,1)} %get-tuple-element.215.refs_1_, bf16[256,768]{1,0:T(8,128)(2,1)} %get-tuple-element.216.refs_2_, ...), custom_call_target="tpu_custom_call" | custom-call | flops 830472192 | bytes 9732096 | tf_op jit(solution)/shard_map/gone_grads/pallas_call | solution.py:816
  131.2 3.8 %all-to-all-start.2 = ((bf16[8,192,128]{2,1,0:T(8,128)(2,1)}), bf16[8,192,128]{2,1,0:T(8,128)(2,1)S(1)}, u32[]{:S(2)}, u32[]{:S(2)}) async-start(bf16[8,192,128]{2,1,0:T(8,128)(2,1)} %get-tuple-element.213), calls=%async_computation.2 | async-start | bytes 786432 | tf_op jit(solution)/shard_map/all_to_all | solution.py:1133
  136.8 6.7 %kept_grads.1 = (bf16[192,1920]{1,0:T(8,128)(2,1)}, bf16[192,1920]{1,0:T(8,128)(2,1)}, bf16[8,24,2304]{2,1,0:T(8,128)(2,1)}, bf16[8,24,2304]{2,1,0:T(8,128)(2,1)}) custom-call(s32[5]{0:T(128)} %stack.119.sides_ref, bf16[256,768]{1,0:T(8,128)(2,1)} %get-tuple-element.214.refs_0_, bf16[256,768]{1,0:T(8,128)(2,1)} %get-tuple-element.215.refs_1_, ...), custom_call_target="tpu_custom_call" | custom-call | flops 830472192 | bytes 9732096 | tf_op jit(solution)/shard_map/kept_grads/pallas_call | solution.py:816
  143.5 3.3 %all-to-all-done.2.grad_ref = bf16[8,192,128]{2,1,0:T(8,128)(2,1)S(1)} async-done(((bf16[8,192,128]{2,1,0:T(8,128)(2,1)}), bf16[8,192,128]{2,1,0:T(8,128)(2,1)S(1)}, u32[]{:S(2)}, u32[]{:S(2)}) %all-to-all-start.2) | async-done | bytes 393248 | tf_op jit(solution)/shard_map/all_to_all | solution.py:1133
  149.3 22.8 %attend_back.1 = (bf16[8,256,384]{2,1,0:T(8,128)(2,1)}, bf16[8,704,128]{2,1,0:T(8,128)(2,1)}) custom-call(s32[8]{0:T(128)} %get-tuple-element.147.base_ref, s32[8]{0:T(128)} %get-tuple-element.148.count_ref, s32[6]{0:T(128)} %pad_add_fusion.2.units_ref, bf16[2048,384]{1,0:T(8,128)(2,1)} %get-tuple-element.181.q_ref.k_ref.v_ref, ...), custom_call_target="tpu_custom_call" | custom-call | flops 8053063680 | bytes 12582912 | tf_op jit(solution)/shard_map/attend_back/pallas_call | solution.py:451
  172.5 5.6 %all-to-all-start.3 = ((bf16[8,704,128]{2,1,0:T(8,128)(2,1)}), bf16[8,704,128]{2,1,0:T(8,128)(2,1)S(1)}, u32[]{:S(2)}, u32[]{:S(2)}) async-start(bf16[8,704,128]{2,1,0:T(8,128)(2,1)} %get-tuple-element.238), calls=%async_computation.3 | async-start | bytes 2883584 | tf_op jit(solution)/shard_map/all_to_all | solution.py:1177
  178.7 3.3 %add_halves.4 = (bf16[4,24,1920]{2,1,0:T(8,128)(2,1)}, bf16[4,24,1920]{2,1,0:T(8,128)(2,1)}, bf16[1,96,2304]{2,1,0:T(8,128)(2,1)}, bf16[1,96,2304]{2,1,0:T(8,128)(2,1)}) custom-call(s32[5]{0:T(128)} %stack.119.sides_ref, bf16[4,2,24,1920]{3,2,1,0:T(8,128)(2,1)} %bitcast.147, bf16[4,2,24,1920]{3,2,1,0:T(8,128)(2,1)} %bitcast.37.refs_1_, ...), custom_call_target="tpu_custom_call" | custom-call | flops 1622016 | bytes 4866048 | tf_op jit(solution)/shard_map/add_halves/pallas_call | solution.py:904
  184.9 6.5 %head_grads.1 = (bf16[2,192,384]{2,1,0:T(8,128)(2,1)}, bf16[2,192,384]{2,1,0:T(8,128)(2,1)}) custom-call(s32[5]{0:T(128)} %stack.119.sides_ref, bf16[2048,768]{1,0:T(8,128)(2,1)} %get-tuple-element.250.left_ref, bf16[8,256,384]{2,1,0:T(8,128)(2,1)} %get-tuple-element.251.right_ref), custom_call_target="tpu_custom_call" | custom-call | flops 1207959552 | bytes 4718592 | tf_op jit(solution)/shard_map/head_grads/pallas_call | solution.py:855
  193.2 7.8 %collective-permute-done.29 = bf16[4,24,1920]{2,1,0:T(8,128)(2,1)S(1)} collective-permute-done((bf16[4,24,1920]{2,1,0:T(8,128)(2,1)}, bf16[4,24,1920]{2,1,0:T(8,128)(2,1)S(1)}, u32[]{:S(2)}, u32[]{:S(2)}) %collective-permute-start.29) | collective-permute-done | bytes 368672 | tf_op jit(solution)/shard_map/ppermute | solution.py:1187
  201.8 2.5 %add_halves.5 = (bf16[2,24,4224]{2,1,0:T(8,128)(2,1)}, bf16[2,24,4224]{2,1,0:T(8,128)(2,1)}) custom-call(s32[5]{0:T(128)} %stack.119.sides_ref, bf16[2,2,24,1920]{3,2,1,0:T(8,128)(2,1)} %bitcast.153, bf16[2,2,24,1920]{3,2,1,0:T(8,128)(2,1)} %bitcast.154, bf16[2,2,24,2304]{3,2,1,0:T(8,128)(2,1)} %bitcast.148, bf16[2,2,24,2304]{3,2,1,0:T(8,128)(2,1)} %bitcast.149), custom_call_target="tpu_custom_call" | custom-call | flops 811008 | bytes 2433024 | tf_op jit(solution)/shard_map/add_halves/pallas_call | solution.py:904
  207.6 4.7 %settle.1.w_ref = bf16[768,2304]{1,0:T(8,128)(2,1)} custom-call(s32[4]{0:T(128)} %pad_add_fusion.1.place_ref, bf16[4,48,2304]{2,1,0:T(8,128)(2,1)} %copy-done.1, bf16[4,48,2304]{2,1,0:T(8,128)(2,1)} %copy-done.4, bf16[4,48,2304]{2,1,0:T(8,128)(2,1)} %copy-done.5, bf16[4,48,2304]{2,1,0:T(8,128)(2,1)} %copy-done.6), custom_call_target="tpu_custom_call" | custom-call | bytes 8388608 | tf_op jit(solution)/shard_map/settle/pallas_call | solution.py:681
  212.3 7.6 %collective-permute-done.34 = bf16[2,24,4224]{2,1,0:T(8,128)(2,1)S(1)} collective-permute-done((bf16[2,24,4224]{2,1,0:T(8,128)(2,1)}, bf16[2,24,4224]{2,1,0:T(8,128)(2,1)S(1)}, u32[]{:S(2)}, u32[]{:S(2)}) %collective-permute-start.34) | collective-permute-done | bytes 405536 | tf_op jit(solution)/shard_map/ppermute | solution.py:1201
  223.3 4.2 %all-to-all-start.4 = ((bf16[8,24,384]{2,1,0:T(8,128)(2,1)}), bf16[8,24,384]{2,1,0:T(8,128)(2,1)S(1)}, u32[]{:S(2)}, u32[]{:S(2)}) async-start(bf16[8,24,384]{2,1,0:T(8,128)(2,1)} %bitcast.50), calls=%async_computation.4 | async-start | bytes 294912 | tf_op jit(solution)/shard_map/all_to_all | solution.py:1218
  227.6 5.2 %finish.1 = bf16[256,768]{1,0:T(8,128)(2,1)} custom-call(bf16[8,704,128]{2,1,0:T(8,128)(2,1)} %copy-done, bf16[256,768]{1,0:T(8,128)(2,1)} %bitcast.141, f32[8,768]{1,0:T(8,128)} %get-tuple-element.157.refs_3_.refs_4_.refs_2_.gain_ref, f32[256,768]{1,0:T(8,128)} %get-tuple-element.271.grad_ref, bf16[768,2304]{1,0:T(8,128)(2,1)} %settle.1.w_ref), custom_call_target="tpu_custom_call" | custom-call | flops 905969664 | bytes 6291456 | tf_op jit(solution)/shard_map/finish/pallas_call | solution.py:714
  232.8 3.1 %collective-permute-done.36 = bf16[1,24,4224]{2,1,0:T(8,128)(2,1)S(1)} collective-permute-done((bf16[1,24,4224]{2,1,0:T(8,128)(2,1)}, bf16[1,24,4224]{2,1,0:T(8,128)(2,1)S(1)}, u32[]{:S(2)}, u32[]{:S(2)}) %collective-permute-start.36) | collective-permute-done | bytes 202784 | tf_op jit(solution)/shard_map/ppermute | solution.py:1208
  (192 shorter events, 56.6 us)
Async XLA Ops:
  0.6 19.8 %collective-permute-start = (bf16[256,768]{1,0:T(8,128)(2,1)}, bf16[256,768]{1,0:T(8,128)(2,1)S(1)}, u32[]{:S(2)}, u32[]{:S(2)}) collective-permute-start(bf16[256,768]{1,0:T(8,128)(2,1)} %bitcast.137), channel_id=1, source_target_pairs={{0,2},{1,3},{2,4},{3,5},{4,6},{5,7},{6,0},{7,1},{8,10},{9,11},{10,... | collective-permute-start | bytes 1179656 | tf_op jit(solution)/shard_map/ppermute | solution.py:1016
  3.7 16.7 %collective-permute-start.1 = (bf16[256,768]{1,0:T(8,128)(2,1)}, bf16[256,768]{1,0:T(8,128)(2,1)S(1)}, u32[]{:S(2)}, u32[]{:S(2)}) collective-permute-start(bf16[256,768]{1,0:T(8,128)(2,1)} %bitcast.138), channel_id=1, source_target_pairs={{0,1},{1,0},{2,3},{3,2},{4,5},{5,4},{6,7},{7,6},{8,9},{9,8},{10,11... | collective-permute-start | bytes 1179656 | tf_op jit(solution)/shard_map/ppermute | solution.py:1017
  6.2 14.2 %collective-permute-start.2 = (bf16[2,24,2176]{2,1,0:T(8,128)(2,1)S(1)}, bf16[2,24,2176]{2,1,0:T(8,128)(2,1)S(1)}, u32[]{:S(2)}, u32[]{:S(2)}) collective-permute-start(bf16[2,24,2176]{2,1,0:T(8,128)(2,1)S(1)} %pad_maximum_fusion.6), channel_id=1, source_target_pairs={{0,2},{1,3},{2,4},{3,5},{4,6},{5,7},{6,0},{7,1},{8,10},{9,11},{10,... | collective-permute-start | bytes 626696 | tf_op jit(solution)/shard_map/ppermute | solution.py:1018
  9.6 15.5 %all-to-all-start = ((bf16[8,32,512]{2,1,0:T(8,128)(2,1)}), bf16[8,32,512]{2,1,0:T(8,128)(2,1)S(1)}, u32[]{:S(2)}, u32[]{:S(2)}) async-start(bf16[8,32,512]{2,1,0:T(8,128)(2,1)} %spread.1), calls=%async_computation | async-start | bytes 524288 | tf_op jit(solution)/shard_map/all_to_all | solution.py:1009
  25.2 17.3 %collective-permute-start.3 = (bf16[256,768]{1,0:T(8,128)(2,1)S(1)}, bf16[256,768]{1,0:T(8,128)(2,1)S(1)}, u32[]{:S(2)}, u32[]{:S(2)}) collective-permute-start(bf16[256,768]{1,0:T(8,128)(2,1)S(1)} %collective-permute-done.refs_0_), channel_id=1, source_target_pairs={{0,2},{1,3},{2,4},{3,5},{4,6},{5,7},{6,0},{7,1},{8,10},{9,11},{10,... | collective-permute-start | bytes 1179656 | tf_op jit(solution)/shard_map/ppermute | solution.py:1030
  26.1 16.4 %collective-permute-start.4 = (bf16[256,768]{1,0:T(8,128)(2,1)S(1)}, bf16[256,768]{1,0:T(8,128)(2,1)S(1)}, u32[]{:S(2)}, u32[]{:S(2)}) collective-permute-start(bf16[256,768]{1,0:T(8,128)(2,1)S(1)} %collective-permute-done.refs_0_), channel_id=1, source_target_pairs={{0,1},{1,0},{2,3},{3,2},{4,5},{5,4},{6,7},{7,6},{8,9},{9,8},{10,11... | collective-permute-start | bytes 1179656 | tf_op jit(solution)/shard_map/ppermute | solution.py:1031
  26.7 15.8 %collective-permute-start.5 = (bf16[2,24,2176]{2,1,0:T(8,128)(2,1)S(1)}, bf16[2,24,2176]{2,1,0:T(8,128)(2,1)S(1)}, u32[]{:S(2)}, u32[]{:S(2)}) collective-permute-start(bf16[2,24,2176]{2,1,0:T(8,128)(2,1)S(1)} %collective-permute-done.2), channel_id=1, source_target_pairs={{0,2},{1,3},{2,4},{3,5},{4,6},{5,7},{6,0},{7,1},{8,10},{9,11},{10,... | collective-permute-start | bytes 626696 | tf_op jit(solution)/shard_map/ppermute | solution.py:1032
  42.5 16.5 %collective-permute-start.8 = (bf16[256,768]{1,0:T(8,128)(2,1)S(1)}, bf16[256,768]{1,0:T(8,128)(2,1)S(1)}, u32[]{:S(2)}, u32[]{:S(2)}) collective-permute-start(bf16[256,768]{1,0:T(8,128)(2,1)S(1)} %collective-permute-done.3.refs_0_), channel_id=1, source_target_pairs={{0,2},{1,3},{2,4},{3,5},{4,6},{5,7},{6,0},{7,1},{8,10},{9,11},{10,... | collective-permute-start | bytes 1179656 | tf_op jit(solution)/shard_map/ppermute | solution.py:1050
  42.6 16.5 %collective-permute-start.9 = (bf16[256,768]{1,0:T(8,128)(2,1)S(1)}, bf16[256,768]{1,0:T(8,128)(2,1)S(1)}, u32[]{:S(2)}, u32[]{:S(2)}) collective-permute-start(bf16[256,768]{1,0:T(8,128)(2,1)S(1)} %collective-permute-done.3.refs_0_), channel_id=1, source_target_pairs={{0,1},{1,0},{2,3},{3,2},{4,5},{5,4},{6,7},{7,6},{8,9},{9,8},{10,11... | collective-permute-start | bytes 1179656 | tf_op jit(solution)/shard_map/ppermute | solution.py:1051
  44.2 14.9 %collective-permute-start.10 = (bf16[2,24,2176]{2,1,0:T(8,128)(2,1)S(1)}, bf16[2,24,2176]{2,1,0:T(8,128)(2,1)S(1)}, u32[]{:S(2)}, u32[]{:S(2)}) collective-permute-start(bf16[2,24,2176]{2,1,0:T(8,128)(2,1)S(1)} %collective-permute-done.5), channel_id=1, source_target_pairs={{0,2},{1,3},{2,4},{3,5},{4,6},{5,7},{6,0},{7,1},{8,10},{9,11},{10,... | collective-permute-start | bytes 626696 | tf_op jit(solution)/shard_map/ppermute | solution.py:1052
  44.2 14.9 %collective-permute-start.11 = (bf16[2,24,2176]{2,1,0:T(8,128)(2,1)S(1)}, bf16[2,24,2176]{2,1,0:T(8,128)(2,1)S(1)}, u32[]{:S(2)}, u32[]{:S(2)}) collective-permute-start(bf16[2,24,2176]{2,1,0:T(8,128)(2,1)S(1)} %get-tuple-element.152), channel_id=1, source_target_pairs={{0,1},{1,0},{2,3},{3,2},{4,5},{5,4},{6,7},{7,6},{8,9},{9,8},{10,11... | collective-permute-start | bytes 626696 | tf_op jit(solution)/shard_map/ppermute | solution.py:1053
  45.3 13.7 %collective-permute-start.12 = (bf16[2,24,2176]{2,1,0:T(8,128)(2,1)S(1)}, bf16[2,24,2176]{2,1,0:T(8,128)(2,1)S(1)}, u32[]{:S(2)}, u32[]{:S(2)}) collective-permute-start(bf16[2,24,2176]{2,1,0:T(8,128)(2,1)S(1)} %get-tuple-element.153), channel_id=1, source_target_pairs={{0,16},{8,24},{16,0},{24,8},{1,17},{9,25},{17,1},{25,9},{2,18},{10... | collective-permute-start | bytes 626696 | tf_op jit(solution)/shard_map/ppermute | solution.py:1054
  59.1 13.8 %collective-permute-start.13 = (bf16[256,768]{1,0:T(8,128)(2,1)S(1)}, bf16[256,768]{1,0:T(8,128)(2,1)S(1)}, u32[]{:S(2)}, u32[]{:S(2)}) collective-permute-start(bf16[256,768]{1,0:T(8,128)(2,1)S(1)} %collective-permute-done.8.refs_2_), channel_id=1, source_target_pairs={{0,1},{1,0},{2,3},{3,2},{4,5},{5,4},{6,7},{7,6},{8,9},{9,8},{10,11... | collective-permute-start | bytes 1179656 | tf_op jit(solution)/shard_map/ppermute | solution.py:1064
  60.8 12.1 %collective-permute-start.14 = (bf16[2,24,2176]{2,1,0:T(8,128)(2,1)S(1)}, bf16[2,24,2176]{2,1,0:T(8,128)(2,1)S(1)}, u32[]{:S(2)}, u32[]{:S(2)}) collective-permute-start(bf16[2,24,2176]{2,1,0:T(8,128)(2,1)S(1)} %pad_maximum_fusion.9), channel_id=1, source_target_pairs={{0,1},{1,0},{2,3},{3,2},{4,5},{5,4},{6,7},{7,6},{8,9},{9,8},{10,11... | collective-permute-start | bytes 626696 | tf_op jit(solution)/shard_map/ppermute | solution.py:1067
  73.0 22.6 %collective-permute-start.17 = (bf16[4,48,2176]{2,1,0:T(8,128)(2,1)S(1)}, bf16[4,48,2176]{2,1,0:T(8,128)(2,1)}, u32[]{:S(2)}, u32[]{:S(2)}) collective-permute-start(bf16[4,48,2176]{2,1,0:T(8,128)(2,1)S(1)} %maximum_maximum_fusion.refs_0_), channel_id=1, source_target_pairs={{0,16},{8,24},{16,0},{24,8},{1,17},{9,25},{17,1},{25,9},{2,18},{10... | collective-permute-start | bytes 2506760 | tf_op jit(solution)/shard_map/ppermute | solution.py:1080
  74.7 21.0 %collective-permute-start.18 = (bf16[8,24,2176]{2,1,0:T(8,128)(2,1)S(1)}, bf16[8,24,2176]{2,1,0:T(8,128)(2,1)S(1)}, u32[]{:S(2)}, u32[]{:S(2)}) collective-permute-start(bf16[8,24,2176]{2,1,0:T(8,128)(2,1)S(1)} %constant_dynamic-update-slice_fusion), channel_id=1, source_target_pairs={{0,1},{1,0},{2,3},{3,2},{4,5},{5,4},{6,7},{7,6},{8,9},{9,8},{10,11... | collective-permute-start | bytes 2506760 | tf_op jit(solution)/shard_map/ppermute | solution.py:1081
  76.3 19.4 %collective-permute-start.19 = (bf16[2,24,2304]{2,1,0:T(8,128)(2,1)S(1)}, bf16[2,24,2304]{2,1,0:T(8,128)(2,1)S(1)}, u32[]{:S(2)}, u32[]{:S(2)}) collective-permute-start(bf16[2,24,2304]{2,1,0:T(8,128)(2,1)S(1)} %pad_maximum_fusion.7), channel_id=1, source_target_pairs={{0,4},{1,5},{2,6},{3,7},{4,0},{5,1},{6,2},{7,3},{8,12},{9,13},{10,... | collective-permute-start | bytes 663560 | tf_op jit(solution)/shard_map/ppermute | solution.py:1076
  96.0 18.0 %collective-permute-start.22 = (bf16[8,48,2176]{2,1,0:T(8,128)(2,1)S(1)}, bf16[8,48,2176]{2,1,0:T(8,128)(2,1)}, u32[]{:S(2)}, u32[]{:S(2)}) collective-permute-start(bf16[8,48,2176]{2,1,0:T(8,128)(2,1)S(1)} %pad_maximum_fusion.refs_4_), channel_id=1, source_target_pairs={{0,8},{8,0},{16,24},{24,16},{1,9},{9,1},{17,25},{25,17},{2,10},{10... | collective-permute-start | bytes 5013512 | tf_op jit(solution)/shard_map/ppermute | solution.py:1101
  97.2 16.7 %collective-permute-start.21 = (bf16[4,48,2176]{2,1,0:T(8,128)(2,1)}, bf16[4,48,2176]{2,1,0:T(8,128)(2,1)}, u32[]{:S(2)}, u32[]{:S(2)}) collective-permute-start(bf16[4,48,2176]{2,1,0:T(8,128)(2,1)} %collective-permute-done.17.refs_1_), channel_id=1, source_target_pairs={{0,8},{8,0},{16,24},{24,16},{1,9},{9,1},{17,25},{25,17},{2,10},{10... | collective-permute-start | bytes 2506760 | tf_op jit(solution)/shard_map/ppermute | solution.py:1100
  97.6 16.4 %all-to-all-start.1 = ((bf16[8,192,128]{2,1,0:T(8,128)(2,1)}), bf16[8,192,128]{2,1,0:T(8,128)(2,1)}, u32[]{:S(2)}, u32[]{:S(2)}) async-start(bf16[8,192,128]{2,1,0:T(8,128)(2,1)} %get-tuple-element.192), calls=%async_computation.1 | async-start | bytes 786432 | tf_op jit(solution)/shard_map/all_to_all | solution.py:1107
  131.2 15.7 %all-to-all-start.2 = ((bf16[8,192,128]{2,1,0:T(8,128)(2,1)}), bf16[8,192,128]{2,1,0:T(8,128)(2,1)S(1)}, u32[]{:S(2)}, u32[]{:S(2)}) async-start(bf16[8,192,128]{2,1,0:T(8,128)(2,1)} %get-tuple-element.213), calls=%async_computation.2 | async-start | bytes 786432 | tf_op jit(solution)/shard_map/all_to_all | solution.py:1133
  135.1 37.0 %collective-permute-start.28 = (bf16[4,48,2304]{2,1,0:T(8,128)(2,1)S(1)}, bf16[4,48,2304]{2,1,0:T(8,128)(2,1)S(1)}, u32[]{:S(2)}, u32[]{:S(2)}) collective-permute-start(bf16[4,48,2304]{2,1,0:T(8,128)(2,1)S(1)} %pad_maximum_fusion.1.refs_0_), channel_id=1, source_target_pairs={{0,16},{8,24},{16,0},{24,8},{1,17},{9,25},{17,1},{25,9},{2,18},{10... | collective-permute-start | bytes 2654216 | tf_op jit(solution)/shard_map/ppermute | solution.py:1132
  146.8 25.7 %collective-permute-start.27 = (bf16[8,24,2304]{2,1,0:T(8,128)(2,1)}, bf16[8,24,2304]{2,1,0:T(8,128)(2,1)}, u32[]{:S(2)}, u32[]{:S(2)}) collective-permute-start(bf16[8,24,2304]{2,1,0:T(8,128)(2,1)} %get-tuple-element.236), channel_id=1, source_target_pairs={{0,1},{1,0},{2,3},{3,2},{4,5},{5,4},{6,7},{7,6},{8,9},{9,8},{10,11... | collective-permute-start | bytes 2654216 | tf_op jit(solution)/shard_map/ppermute | solution.py:1159
  148.3 24.2 %collective-permute-start.26 = (bf16[192,1920]{1,0:T(8,128)(2,1)}, bf16[192,1920]{1,0:T(8,128)(2,1)}, u32[]{:S(2)}, u32[]{:S(2)}) collective-permute-start(bf16[192,1920]{1,0:T(8,128)(2,1)} %get-tuple-element.234), channel_id=1, source_target_pairs={{0,16},{8,24},{16,0},{24,8},{1,17},{9,25},{17,1},{25,9},{2,18},{10... | collective-permute-start | bytes 2211848 | tf_op jit(solution)/shard_map/ppermute | solution.py:1158
  172.5 47.4 %all-to-all-start.3 = ((bf16[8,704,128]{2,1,0:T(8,128)(2,1)}), bf16[8,704,128]{2,1,0:T(8,128)(2,1)S(1)}, u32[]{:S(2)}, u32[]{:S(2)}) async-start(bf16[8,704,128]{2,1,0:T(8,128)(2,1)} %get-tuple-element.238), calls=%async_computation.3 | async-start | bytes 2883584 | tf_op jit(solution)/shard_map/all_to_all | solution.py:1177
  178.1 22.8 %collective-permute-start.32 = (bf16[4,48,2304]{2,1,0:T(8,128)(2,1)S(1)}, bf16[4,48,2304]{2,1,0:T(8,128)(2,1)S(1)}, u32[]{:S(2)}, u32[]{:S(2)}) collective-permute-start(bf16[4,48,2304]{2,1,0:T(8,128)(2,1)S(1)} %pad_maximum_fusion.1.refs_0_), channel_id=1, source_target_pairs={{0,8},{8,0},{16,24},{24,16},{1,9},{9,1},{17,25},{25,17},{2,10},{10... | collective-permute-start | bytes 2654216 | tf_op jit(solution)/shard_map/ppermute | solution.py:1178
  178.2 22.8 %collective-permute-start.33 = (bf16[4,48,2304]{2,1,0:T(8,128)(2,1)S(1)}, bf16[4,48,2304]{2,1,0:T(8,128)(2,1)S(1)}, u32[]{:S(2)}, u32[]{:S(2)}) collective-permute-start(bf16[4,48,2304]{2,1,0:T(8,128)(2,1)S(1)} %collective-permute-done.28.refs_1_), channel_id=1, source_target_pairs={{0,8},{8,0},{16,24},{24,16},{1,9},{9,1},{17,25},{25,17},{2,10},{10... | collective-permute-start | bytes 2654216 | tf_op jit(solution)/shard_map/ppermute | solution.py:1179
  182.0 19.0 %collective-permute-start.30 = (bf16[1,96,2304]{2,1,0:T(8,128)(2,1)}, bf16[1,96,2304]{2,1,0:T(8,128)(2,1)S(1)}, u32[]{:S(2)}, u32[]{:S(2)}) collective-permute-start(bf16[1,96,2304]{2,1,0:T(8,128)(2,1)} %get-tuple-element.248), channel_id=1, source_target_pairs={{0,16},{8,24},{16,0},{24,8},{1,17},{9,25},{17,1},{25,9},{2,18},{10... | collective-permute-start | bytes 1327112 | tf_op jit(solution)/shard_map/ppermute | solution.py:1188
  182.9 18.0 %collective-permute-start.29 = (bf16[4,24,1920]{2,1,0:T(8,128)(2,1)}, bf16[4,24,1920]{2,1,0:T(8,128)(2,1)S(1)}, u32[]{:S(2)}, u32[]{:S(2)}) collective-permute-start(bf16[4,24,1920]{2,1,0:T(8,128)(2,1)} %get-tuple-element.246), channel_id=1, source_target_pairs={{0,1},{1,0},{2,3},{3,2},{4,5},{5,4},{6,7},{7,6},{8,9},{9,8},{10,11... | collective-permute-start | bytes 1105928 | tf_op jit(solution)/shard_map/ppermute | solution.py:1187
  204.3 15.6 %collective-permute-start.34 = (bf16[2,24,4224]{2,1,0:T(8,128)(2,1)}, bf16[2,24,4224]{2,1,0:T(8,128)(2,1)S(1)}, u32[]{:S(2)}, u32[]{:S(2)}) collective-permute-start(bf16[2,24,4224]{2,1,0:T(8,128)(2,1)} %get-tuple-element.261), channel_id=1, source_target_pairs={{0,2},{1,3},{2,0},{3,1},{4,6},{5,7},{6,4},{7,5},{8,10},{9,11},{10,... | collective-permute-start | bytes 1216520 | tf_op jit(solution)/shard_map/ppermute | solution.py:1201
  222.6 13.2 %collective-permute-start.36 = (bf16[1,24,4224]{2,1,0:T(8,128)(2,1)}, bf16[1,24,4224]{2,1,0:T(8,128)(2,1)S(1)}, u32[]{:S(2)}, u32[]{:S(2)}) collective-permute-start(bf16[1,24,4224]{2,1,0:T(8,128)(2,1)} %get-tuple-element.277), channel_id=1, source_target_pairs={{0,4},{1,5},{2,6},{3,7},{4,0},{5,1},{6,2},{7,3},{8,12},{9,13},{10,... | collective-permute-start | bytes 608264 | tf_op jit(solution)/shard_map/ppermute | solution.py:1208
  223.3 15.2 %all-to-all-start.4 = ((bf16[8,24,384]{2,1,0:T(8,128)(2,1)}), bf16[8,24,384]{2,1,0:T(8,128)(2,1)S(1)}, u32[]{:S(2)}, u32[]{:S(2)}) async-start(bf16[8,24,384]{2,1,0:T(8,128)(2,1)} %bitcast.50), calls=%async_computation.4 | async-start | bytes 294912 | tf_op jit(solution)/shard_map/all_to_all | solution.py:1218
  (37 other events, 295.7 us)

commit v8 on v7

--- a/solution.py
+++ b/solution.py
@@ -16,6 +16,7 @@
 GRAIN = 128
 KEY_TILE = 512
 CHUNK = 384
+MIDDLE_CHUNK = 1152
 EPS = 1e-05
 THETA = 160000.0
 NEG = -1e30
@@ -601,12 +602,12 @@
         copy.wait()
     result = middle
     grad_hidden = jnp.zeros(middle.shape, f32)
-    for at in range(0, units, CHUNK):
-        one = slice(at, at + CHUNK)
-        two = slice(units + at, units + at + CHUNK)
-        w_one = w_ref[:, up + at : up + at + CHUNK]
-        w_two = w_ref[:, up + units + at : up + units + at + CHUNK]
-        w_down = w_ref[:, down + at : down + at + CHUNK]
+    for at in range(0, units, MIDDLE_CHUNK):
+        one = slice(at, at + MIDDLE_CHUNK)
+        two = slice(units + at, units + at + MIDDLE_CHUNK)
+        w_one = w_ref[:, up + at : up + at + MIDDLE_CHUNK]
+        w_two = w_ref[:, up + units + at : up + units + at + MIDDLE_CHUNK]
+        w_down = w_ref[:, down + at : down + at + MIDDLE_CHUNK]
         inner = jnp.dot(hidden, w_one, preferred_element_type=f32)
         gate = jnp.dot(hidden, w_two, preferred_element_type=f32)
         grad_product = jnp.dot(cot, w_down, preferred_element_type=f32)

time: 241 us -> 241 us (level)
  transfers between devices with their start and end apart: 42 -> 42, of which waited for: 15 -> 13; matrix products, arithmetic and copies ran while one was open for 9% -> 9% of each run, Pallas kernels for 42% -> 42%
where the time goes in v8:
time: 241 us; the launch traced here: 240 us
  Pallas kernels  107 us (44%)
  starting transfers between devices  56.7 us (24%)
  waiting for transfers between devices  48.5 us (20%)
  other arithmetic  21 us (9%)
  local copies, waits for them, and re-layouts  4.76 us (2%)
    pallas_call x1, Pallas kernels, attend_back(): pl.pallas_call(functools.partial(attend_back_kernel, tile), grid_spec=plt...  22.8 us
    pallas_call x4, Pallas kernels, project(): pl.pallas_call(functools.partial(project_kernel, count), grid_spec=pltpu....  18.1 us
    pallas_call x1, Pallas kernels, attend(): pl.pallas_call(functools.partial(attend_kernel, tile), grid_spec=pltpu.Pr...  15.1 us
    pallas_call x2, Pallas kernels, weight_grads(): pl.pallas_call(functools.partial(kernel, len(operands) // 2, cut), in_spe...  11.5 us
    pallas_call x1, Pallas kernels, middle_stage(): pl.pallas_call(functools.partial(middle_kernel, heads, splits, metas, arr...  10.1 us
    pallas_call x4, Pallas kernels, add_halves(): pl.pallas_call(functools.partial(add_halves_kernel, [pair[3] for pair in...  9.49 us
    all_to_all x1, waiting for transfers between devices, on_device(): att_in = lax.all_to_all(att_low, 'ctx', 0, 0, tiled=True)  7.53 us
    ppermute x1, waiting for transfers between devices, on_device(): got_a = lax.ppermute(other_a, 'ctx', swap)  7.22 us
  transfers between devices with their start and end apart: 42, of which 13 were waited for; matrix products, arithmetic and copies ran while one was open for 9% of the time, Pallas kernels for 42%

profile of v8, /device:TPU:0, one launch (start us, length us, event | category | flops | bytes accessed | tf_op | source)
XLA Modules:
  0.0 239.7 jit_solution(4152950916865624052)
XLA Ops:
  0.6 3.1 %collective-permute-start = (bf16[256,768]{1,0:T(8,128)(2,1)}, bf16[256,768]{1,0:T(8,128)(2,1)S(1)}, u32[]{:S(2)}, u32[]{:S(2)}) collective-permute-start(bf16[256,768]{1,0:T(8,128)(2,1)} %bitcast.137), channel_id=1, source_target_pairs={{0,2},{1,3},{2,4},{3,5},{4,6},{5,7},{6,0},{7,1},{8,10},{9,11},{10,... | collective-permute-start | bytes 1179656 | tf_op jit(solution)/shard_map/ppermute | solution.py:1017
  9.6 3.5 %all-to-all-start = ((bf16[8,32,512]{2,1,0:T(8,128)(2,1)}), bf16[8,32,512]{2,1,0:T(8,128)(2,1)S(1)}, u32[]{:S(2)}, u32[]{:S(2)}) async-start(bf16[8,32,512]{2,1,0:T(8,128)(2,1)} %spread.1), calls=%async_computation | async-start | bytes 524288 | tf_op jit(solution)/shard_map/all_to_all | solution.py:1010
  15.8 4.6 %collective-permute-done.2 = bf16[2,24,2176]{2,1,0:T(8,128)(2,1)S(1)} collective-permute-done((bf16[2,24,2176]{2,1,0:T(8,128)(2,1)S(1)}, bf16[2,24,2176]{2,1,0:T(8,128)(2,1)S(1)}, u32[]{:S(2)}, u32[]{:S(2)}) %collective-permute-start.2) | collective-permute-done | bytes 208928 | tf_op jit(solution)/shard_map/ppermute | solution.py:1019
  20.4 4.7 %all-to-all-done = bf16[8,32,512]{2,1,0:T(8,128)(2,1)S(1)} async-done(((bf16[8,32,512]{2,1,0:T(8,128)(2,1)}), bf16[8,32,512]{2,1,0:T(8,128)(2,1)S(1)}, u32[]{:S(2)}, u32[]{:S(2)}) %all-to-all-start) | async-done | bytes 262176 | tf_op jit(solution)/shard_map/all_to_all | solution.py:1010
  29.5 5.6 %multiply_sine_fusion = (f32[2048,128]{1,0:T(8,128)}, f32[2048,128]{1,0:T(8,128)}) fusion(f32[128]{0:T(128)S(1)} %fusion.22, f32[2048]{0:T(1024)S(1)} %bitcast.161), kind=kLoop, calls=%fused_computation.1 | loop fusion | flops 262144 | bytes 2105856 | tf_op jit(solution)/shard_map/sin | solution.py:1000
  38.8 3.7 %collective-permute-done.5 = bf16[2,24,2176]{2,1,0:T(8,128)(2,1)S(1)} collective-permute-done((bf16[2,24,2176]{2,1,0:T(8,128)(2,1)S(1)}, bf16[2,24,2176]{2,1,0:T(8,128)(2,1)S(1)}, u32[]{:S(2)}, u32[]{:S(2)}) %collective-permute-start.5) | collective-permute-done | bytes 208928 | tf_op jit(solution)/shard_map/ppermute | solution.py:1033
  46.2 2.1 ready.1
  48.2 4.7 %project.4 = (bf16[2048,768]{1,0:T(8,128)(2,1)}, bf16[2048,384]{1,0:T(8,128)(2,1)}, bf16[256,2048]{1,0:T(8,128)(2,1)}) custom-call(s32[2]{0:T(128)} %pad_add_fusion.4.at_ref, bf16[256,768]{1,0:T(8,128)(2,1)} %bitcast.139, bf16[256,768]{1,0:T(8,128)(2,1)} %copy-done.18, bf16[768,512]{1,0:T(8,128)(2,1)} %get-tuple-element.156.refs_2_.refs_3_.refs_1_, ...), custom_call_target="tpu_custom_call" | custom-call | flops 301989888 | bytes 6291456 | tf_op jit(solution)/shard_map/project/pallas_call | solution.py:180
  52.9 4.8 %project.5 = (bf16[2048,768]{1,0:T(8,128)(2,1)}, bf16[2048,384]{1,0:T(8,128)(2,1)}, bf16[256,2048]{1,0:T(8,128)(2,1)}) custom-call(s32[2]{0:T(128)} %pad_add_fusion.3.at_ref, bf16[256,768]{1,0:T(8,128)(2,1)} %copy-done.12, bf16[256,768]{1,0:T(8,128)(2,1)} %copy-done.14, ...), custom_call_target="tpu_custom_call", output_to_operand_aliasing={{0}: (7, {}), {1}: (8, {}), {2}: (9, {})} | custom-call | flops 301989888 | bytes 6291456 | tf_op jit(solution)/shard_map/project/pallas_call | solution.py:180
  63.0 5.9 %project.6 = (bf16[2048,768]{1,0:T(8,128)(2,1)}, bf16[2048,384]{1,0:T(8,128)(2,1)}, bf16[256,2048]{1,0:T(8,128)(2,1)}) custom-call(s32[3]{0:T(128)} %pad_add_fusion.5.at_ref, bf16[256,768]{1,0:T(8,128)(2,1)} %copy-done.13, bf16[256,768]{1,0:T(8,128)(2,1)} %copy-done.16, ...), custom_call_target="tpu_custom_call", output_to_operand_aliasing={{0}: (8, {}), {1}: (9, {}), {2}: (10, {})} | custom-call | flops 452984832 | bytes 9437184 | tf_op jit(solution)/shard_map/project/pallas_call | solution.py:180
  69.5 3.4 %collective-permute-done.14 = bf16[2,24,2176]{2,1,0:T(8,128)(2,1)S(1)} collective-permute-done((bf16[2,24,2176]{2,1,0:T(8,128)(2,1)S(1)}, bf16[2,24,2176]{2,1,0:T(8,128)(2,1)S(1)}, u32[]{:S(2)}, u32[]{:S(2)}) %collective-permute-start.14) | collective-permute-done | bytes 208928 | tf_op jit(solution)/shard_map/ppermute | solution.py:1068
  77.8 2.8 %project.7 = (bf16[2048,768]{1,0:T(8,128)(2,1)}, bf16[2048,384]{1,0:T(8,128)(2,1)}, bf16[256,2048]{1,0:T(8,128)(2,1)}) custom-call(s32[1]{0:T(128)} %bitcast.18.at_ref, bf16[256,768]{1,0:T(8,128)(2,1)} %copy-done.19, bf16[768,512]{1,0:T(8,128)(2,1)} %get-tuple-element.156.refs_2_.refs_3_.refs_1_, ...), custom_call_target="tpu_custom_call", output_to_operand_aliasing={{0}: (6, {}), {1}: (7, {}), {2}: (8, {})} | custom-call | flops 150994944 | bytes 3145728 | tf_op jit(solution)/shard_map/project/pallas_call | solution.py:180
  80.6 15.1 %attend.1 = (bf16[8,192,128]{2,1,0:T(8,128)(2,1)}, f32[8,64,384]{2,1,0:T(8,128)}, f32[8,1,384]{2,1,0:T(1,128)}) custom-call(s32[8]{0:T(128)} %get-tuple-element.147.base_ref, s32[8]{0:T(128)} %get-tuple-element.148.count_ref, s32[6]{0:T(128)} %pad_add_fusion.2.units_ref, bf16[2048,384]{1,0:T(8,128)(2,1)} %get-tuple-element.181.q_ref.k_ref.v_ref, ...), custom_call_target="tpu_custom_call" | custom-call | flops 3221225472 | bytes 8388608 | tf_op jit(solution)/shard_map/attend/pallas_call | solution.py:309
  97.6 4.3 %all-to-all-start.1 = ((bf16[8,192,128]{2,1,0:T(8,128)(2,1)}), bf16[8,192,128]{2,1,0:T(8,128)(2,1)}, u32[]{:S(2)}, u32[]{:S(2)}) async-start(bf16[8,192,128]{2,1,0:T(8,128)(2,1)} %get-tuple-element.192), calls=%async_computation.1 | async-start | bytes 786432 | tf_op jit(solution)/shard_map/all_to_all | solution.py:1108
  102.5 3.9 %multiply_sine_fusion.1 = (f32[8,64,384]{2,1,0:T(8,128)}, f32[8,64,384]{2,1,0:T(8,128)}) fusion(f32[8,384]{1,0:T(8,128)S(1)} %bitcast.164, f32[64]{0:T(128)S(1)} %fusion.25), kind=kLoop, calls=%fused_computation.3 | loop fusion | flops 196608 | bytes 1585408 | tf_op jit(solution)/shard_map/sin | solution.py:1007
  106.5 7.5 %all-to-all-done.1.att_ref = bf16[8,192,128]{2,1,0:T(8,128)(2,1)} async-done(((bf16[8,192,128]{2,1,0:T(8,128)(2,1)}), bf16[8,192,128]{2,1,0:T(8,128)(2,1)}, u32[]{:S(2)}, u32[]{:S(2)}) %all-to-all-start.1) | async-done | bytes 393248 | tf_op jit(solution)/shard_map/all_to_all | solution.py:1108
  115.5 10.1 %middle_stage.1 = (bf16[256,768]{1,0:T(8,128)(2,1)}, bf16[8,192,128]{2,1,0:T(8,128)(2,1)}, f32[256,768]{1,0:T(8,128)}, bf16[256,768]{1,0:T(8,128)(2,1)}, bf16[25...) custom-call(s32[4]{0:T(128)} %pad_add_fusion.1.place_ref, ...), custom_call_target="tpu_custom_call" | custom-call | flops 4982833152 | bytes 10485760 | tf_op jit(solution)/shard_map/middle_stage/pallas_call | solution.py:641
  125.6 4.8 %gone_grads.1 = (bf16[2,192,1920]{2,1,0:T(8,128)(2,1)}, bf16[2,192,2304]{2,1,0:T(8,128)(2,1)}) custom-call(s32[5]{0:T(128)} %stack.119.sides_ref, bf16[256,768]{1,0:T(8,128)(2,1)} %get-tuple-element.214.refs_0_, bf16[256,768]{1,0:T(8,128)(2,1)} %get-tuple-element.215.refs_1_, bf16[256,768]{1,0:T(8,128)(2,1)} %get-tuple-element.216.refs_2_, ...), custom_call_target="tpu_custom_call" | custom-call | flops 830472192 | bytes 9732096 | tf_op jit(solution)/shard_map/gone_grads/pallas_call | solution.py:817
  130.9 4.1 %all-to-all-start.2 = ((bf16[8,192,128]{2,1,0:T(8,128)(2,1)}), bf16[8,192,128]{2,1,0:T(8,128)(2,1)S(1)}, u32[]{:S(2)}, u32[]{:S(2)}) async-start(bf16[8,192,128]{2,1,0:T(8,128)(2,1)} %get-tuple-element.213), calls=%async_computation.2 | async-start | bytes 786432 | tf_op jit(solution)/shard_map/all_to_all | solution.py:1134
  136.7 6.7 %kept_grads.1 = (bf16[192,1920]{1,0:T(8,128)(2,1)}, bf16[192,1920]{1,0:T(8,128)(2,1)}, bf16[8,24,2304]{2,1,0:T(8,128)(2,1)}, bf16[8,24,2304]{2,1,0:T(8,128)(2,1)}) custom-call(s32[5]{0:T(128)} %stack.119.sides_ref, bf16[256,768]{1,0:T(8,128)(2,1)} %get-tuple-element.214.refs_0_, bf16[256,768]{1,0:T(8,128)(2,1)} %get-tuple-element.215.refs_1_, ...), custom_call_target="tpu_custom_call" | custom-call | flops 830472192 | bytes 9732096 | tf_op jit(solution)/shard_map/kept_grads/pallas_call | solution.py:817
  143.4 3.4 %all-to-all-done.2.grad_ref = bf16[8,192,128]{2,1,0:T(8,128)(2,1)S(1)} async-done(((bf16[8,192,128]{2,1,0:T(8,128)(2,1)}), bf16[8,192,128]{2,1,0:T(8,128)(2,1)S(1)}, u32[]{:S(2)}, u32[]{:S(2)}) %all-to-all-start.2) | async-done | bytes 393248 | tf_op jit(solution)/shard_map/all_to_all | solution.py:1134
  149.8 22.8 %attend_back.1 = (bf16[8,256,384]{2,1,0:T(8,128)(2,1)}, bf16[8,704,128]{2,1,0:T(8,128)(2,1)}) custom-call(s32[8]{0:T(128)} %get-tuple-element.147.base_ref, s32[8]{0:T(128)} %get-tuple-element.148.count_ref, s32[6]{0:T(128)} %pad_add_fusion.2.units_ref, bf16[2048,384]{1,0:T(8,128)(2,1)} %get-tuple-element.181.q_ref.k_ref.v_ref, ...), custom_call_target="tpu_custom_call" | custom-call | flops 8053063680 | bytes 12582912 | tf_op jit(solution)/shard_map/attend_back/pallas_call | solution.py:452
  172.7 5.4 %all-to-all-start.3 = ((bf16[8,704,128]{2,1,0:T(8,128)(2,1)}), bf16[8,704,128]{2,1,0:T(8,128)(2,1)S(1)}, u32[]{:S(2)}, u32[]{:S(2)}) async-start(bf16[8,704,128]{2,1,0:T(8,128)(2,1)} %get-tuple-element.238), calls=%async_computation.3 | async-start | bytes 2883584 | tf_op jit(solution)/shard_map/all_to_all | solution.py:1178
  178.7 3.3 %add_halves.4 = (bf16[4,24,1920]{2,1,0:T(8,128)(2,1)}, bf16[4,24,1920]{2,1,0:T(8,128)(2,1)}, bf16[1,96,2304]{2,1,0:T(8,128)(2,1)}, bf16[1,96,2304]{2,1,0:T(8,128)(2,1)}) custom-call(s32[5]{0:T(128)} %stack.119.sides_ref, bf16[4,2,24,1920]{3,2,1,0:T(8,128)(2,1)} %bitcast.147, bf16[4,2,24,1920]{3,2,1,0:T(8,128)(2,1)} %bitcast.37.refs_1_, ...), custom_call_target="tpu_custom_call" | custom-call | flops 1622016 | bytes 4866048 | tf_op jit(solution)/shard_map/add_halves/pallas_call | solution.py:905
  185.4 6.5 %head_grads.1 = (bf16[2,192,384]{2,1,0:T(8,128)(2,1)}, bf16[2,192,384]{2,1,0:T(8,128)(2,1)}) custom-call(s32[5]{0:T(128)} %stack.119.sides_ref, bf16[2048,768]{1,0:T(8,128)(2,1)} %get-tuple-element.250.left_ref, bf16[8,256,384]{2,1,0:T(8,128)(2,1)} %get-tuple-element.251.right_ref), custom_call_target="tpu_custom_call" | custom-call | flops 1207959552 | bytes 4718592 | tf_op jit(solution)/shard_map/head_grads/pallas_call | solution.py:856
  193.7 7.2 %collective-permute-done.29 = bf16[4,24,1920]{2,1,0:T(8,128)(2,1)S(1)} collective-permute-done((bf16[4,24,1920]{2,1,0:T(8,128)(2,1)}, bf16[4,24,1920]{2,1,0:T(8,128)(2,1)S(1)}, u32[]{:S(2)}, u32[]{:S(2)}) %collective-permute-start.29) | collective-permute-done | bytes 368672 | tf_op jit(solution)/shard_map/ppermute | solution.py:1188
  201.8 2.5 %add_halves.5 = (bf16[2,24,4224]{2,1,0:T(8,128)(2,1)}, bf16[2,24,4224]{2,1,0:T(8,128)(2,1)}) custom-call(s32[5]{0:T(128)} %stack.119.sides_ref, bf16[2,2,24,1920]{3,2,1,0:T(8,128)(2,1)} %bitcast.153, bf16[2,2,24,1920]{3,2,1,0:T(8,128)(2,1)} %bitcast.154, bf16[2,2,24,2304]{3,2,1,0:T(8,128)(2,1)} %bitcast.148, bf16[2,2,24,2304]{3,2,1,0:T(8,128)(2,1)} %bitcast.149), custom_call_target="tpu_custom_call" | custom-call | flops 811008 | bytes 2433024 | tf_op jit(solution)/shard_map/add_halves/pallas_call | solution.py:905
  208.1 4.7 %settle.1.w_ref = bf16[768,2304]{1,0:T(8,128)(2,1)} custom-call(s32[4]{0:T(128)} %pad_add_fusion.1.place_ref, bf16[4,48,2304]{2,1,0:T(8,128)(2,1)} %copy-done.1, bf16[4,48,2304]{2,1,0:T(8,128)(2,1)} %copy-done.4, bf16[4,48,2304]{2,1,0:T(8,128)(2,1)} %copy-done.5, bf16[4,48,2304]{2,1,0:T(8,128)(2,1)} %copy-done.6), custom_call_target="tpu_custom_call" | custom-call | bytes 8388608 | tf_op jit(solution)/shard_map/settle/pallas_call | solution.py:682
  212.9 7.1 %collective-permute-done.34 = bf16[2,24,4224]{2,1,0:T(8,128)(2,1)S(1)} collective-permute-done((bf16[2,24,4224]{2,1,0:T(8,128)(2,1)}, bf16[2,24,4224]{2,1,0:T(8,128)(2,1)S(1)}, u32[]{:S(2)}, u32[]{:S(2)}) %collective-permute-start.34) | collective-permute-done | bytes 405536 | tf_op jit(solution)/shard_map/ppermute | solution.py:1202
  223.6 3.9 %all-to-all-start.4 = ((bf16[8,24,384]{2,1,0:T(8,128)(2,1)}), bf16[8,24,384]{2,1,0:T(8,128)(2,1)S(1)}, u32[]{:S(2)}, u32[]{:S(2)}) async-start(bf16[8,24,384]{2,1,0:T(8,128)(2,1)} %bitcast.50), calls=%async_computation.4 | async-start | bytes 294912 | tf_op jit(solution)/shard_map/all_to_all | solution.py:1219
  227.6 5.2 %finish.1 = bf16[256,768]{1,0:T(8,128)(2,1)} custom-call(bf16[8,704,128]{2,1,0:T(8,128)(2,1)} %copy-done, bf16[256,768]{1,0:T(8,128)(2,1)} %bitcast.141, f32[8,768]{1,0:T(8,128)} %get-tuple-element.157.refs_3_.refs_4_.refs_2_.gain_ref, f32[256,768]{1,0:T(8,128)} %get-tuple-element.271.grad_ref, bf16[768,2304]{1,0:T(8,128)(2,1)} %settle.1.w_ref), custom_call_target="tpu_custom_call" | custom-call | flops 905969664 | bytes 6291456 | tf_op jit(solution)/shard_map/finish/pallas_call | solution.py:715
  232.8 3.1 %collective-permute-done.36 = bf16[1,24,4224]{2,1,0:T(8,128)(2,1)S(1)} collective-permute-done((bf16[1,24,4224]{2,1,0:T(8,128)(2,1)}, bf16[1,24,4224]{2,1,0:T(8,128)(2,1)S(1)}, u32[]{:S(2)}, u32[]{:S(2)}) %collective-permute-start.36) | collective-permute-done | bytes 202784 | tf_op jit(solution)/shard_map/ppermute | solution.py:1209
  (192 shorter events, 58.1 us)
Async XLA Ops:
  0.6 19.8 %collective-permute-start = (bf16[256,768]{1,0:T(8,128)(2,1)}, bf16[256,768]{1,0:T(8,128)(2,1)S(1)}, u32[]{:S(2)}, u32[]{:S(2)}) collective-permute-start(bf16[256,768]{1,0:T(8,128)(2,1)} %bitcast.137), channel_id=1, source_target_pairs={{0,2},{1,3},{2,4},{3,5},{4,6},{5,7},{6,0},{7,1},{8,10},{9,11},{10,... | collective-permute-start | bytes 1179656 | tf_op jit(solution)/shard_map/ppermute | solution.py:1017
  3.7 16.7 %collective-permute-start.1 = (bf16[256,768]{1,0:T(8,128)(2,1)}, bf16[256,768]{1,0:T(8,128)(2,1)S(1)}, u32[]{:S(2)}, u32[]{:S(2)}) collective-permute-start(bf16[256,768]{1,0:T(8,128)(2,1)} %bitcast.138), channel_id=1, source_target_pairs={{0,1},{1,0},{2,3},{3,2},{4,5},{5,4},{6,7},{7,6},{8,9},{9,8},{10,11... | collective-permute-start | bytes 1179656 | tf_op jit(solution)/shard_map/ppermute | solution.py:1018
  6.2 14.2 %collective-permute-start.2 = (bf16[2,24,2176]{2,1,0:T(8,128)(2,1)S(1)}, bf16[2,24,2176]{2,1,0:T(8,128)(2,1)S(1)}, u32[]{:S(2)}, u32[]{:S(2)}) collective-permute-start(bf16[2,24,2176]{2,1,0:T(8,128)(2,1)S(1)} %pad_maximum_fusion.6), channel_id=1, source_target_pairs={{0,2},{1,3},{2,4},{3,5},{4,6},{5,7},{6,0},{7,1},{8,10},{9,11},{10,... | collective-permute-start | bytes 626696 | tf_op jit(solution)/shard_map/ppermute | solution.py:1019
  9.6 15.5 %all-to-all-start = ((bf16[8,32,512]{2,1,0:T(8,128)(2,1)}), bf16[8,32,512]{2,1,0:T(8,128)(2,1)S(1)}, u32[]{:S(2)}, u32[]{:S(2)}) async-start(bf16[8,32,512]{2,1,0:T(8,128)(2,1)} %spread.1), calls=%async_computation | async-start | bytes 524288 | tf_op jit(solution)/shard_map/all_to_all | solution.py:1010
  25.2 17.3 %collective-permute-start.3 = (bf16[256,768]{1,0:T(8,128)(2,1)S(1)}, bf16[256,768]{1,0:T(8,128)(2,1)S(1)}, u32[]{:S(2)}, u32[]{:S(2)}) collective-permute-start(bf16[256,768]{1,0:T(8,128)(2,1)S(1)} %collective-permute-done.refs_0_), channel_id=1, source_target_pairs={{0,2},{1,3},{2,4},{3,5},{4,6},{5,7},{6,0},{7,1},{8,10},{9,11},{10,... | collective-permute-start | bytes 1179656 | tf_op jit(solution)/shard_map/ppermute | solution.py:1031
  26.1 16.4 %collective-permute-start.4 = (bf16[256,768]{1,0:T(8,128)(2,1)S(1)}, bf16[256,768]{1,0:T(8,128)(2,1)S(1)}, u32[]{:S(2)}, u32[]{:S(2)}) collective-permute-start(bf16[256,768]{1,0:T(8,128)(2,1)S(1)} %collective-permute-done.refs_0_), channel_id=1, source_target_pairs={{0,1},{1,0},{2,3},{3,2},{4,5},{5,4},{6,7},{7,6},{8,9},{9,8},{10,11... | collective-permute-start | bytes 1179656 | tf_op jit(solution)/shard_map/ppermute | solution.py:1032
  26.7 15.8 %collective-permute-start.5 = (bf16[2,24,2176]{2,1,0:T(8,128)(2,1)S(1)}, bf16[2,24,2176]{2,1,0:T(8,128)(2,1)S(1)}, u32[]{:S(2)}, u32[]{:S(2)}) collective-permute-start(bf16[2,24,2176]{2,1,0:T(8,128)(2,1)S(1)} %collective-permute-done.2), channel_id=1, source_target_pairs={{0,2},{1,3},{2,4},{3,5},{4,6},{5,7},{6,0},{7,1},{8,10},{9,11},{10,... | collective-permute-start | bytes 626696 | tf_op jit(solution)/shard_map/ppermute | solution.py:1033
  42.5 16.5 %collective-permute-start.8 = (bf16[256,768]{1,0:T(8,128)(2,1)S(1)}, bf16[256,768]{1,0:T(8,128)(2,1)S(1)}, u32[]{:S(2)}, u32[]{:S(2)}) collective-permute-start(bf16[256,768]{1,0:T(8,128)(2,1)S(1)} %collective-permute-done.3.refs_0_), channel_id=1, source_target_pairs={{0,2},{1,3},{2,4},{3,5},{4,6},{5,7},{6,0},{7,1},{8,10},{9,11},{10,... | collective-permute-start | bytes 1179656 | tf_op jit(solution)/shard_map/ppermute | solution.py:1051
  42.6 16.5 %collective-permute-start.9 = (bf16[256,768]{1,0:T(8,128)(2,1)S(1)}, bf16[256,768]{1,0:T(8,128)(2,1)S(1)}, u32[]{:S(2)}, u32[]{:S(2)}) collective-permute-start(bf16[256,768]{1,0:T(8,128)(2,1)S(1)} %collective-permute-done.3.refs_0_), channel_id=1, source_target_pairs={{0,1},{1,0},{2,3},{3,2},{4,5},{5,4},{6,7},{7,6},{8,9},{9,8},{10,11... | collective-permute-start | bytes 1179656 | tf_op jit(solution)/shard_map/ppermute | solution.py:1052
  44.2 14.9 %collective-permute-start.10 = (bf16[2,24,2176]{2,1,0:T(8,128)(2,1)S(1)}, bf16[2,24,2176]{2,1,0:T(8,128)(2,1)S(1)}, u32[]{:S(2)}, u32[]{:S(2)}) collective-permute-start(bf16[2,24,2176]{2,1,0:T(8,128)(2,1)S(1)} %collective-permute-done.5), channel_id=1, source_target_pairs={{0,2},{1,3},{2,4},{3,5},{4,6},{5,7},{6,0},{7,1},{8,10},{9,11},{10,... | collective-permute-start | bytes 626696 | tf_op jit(solution)/shard_map/ppermute | solution.py:1053
  44.2 14.9 %collective-permute-start.11 = (bf16[2,24,2176]{2,1,0:T(8,128)(2,1)S(1)}, bf16[2,24,2176]{2,1,0:T(8,128)(2,1)S(1)}, u32[]{:S(2)}, u32[]{:S(2)}) collective-permute-start(bf16[2,24,2176]{2,1,0:T(8,128)(2,1)S(1)} %get-tuple-element.152), channel_id=1, source_target_pairs={{0,1},{1,0},{2,3},{3,2},{4,5},{5,4},{6,7},{7,6},{8,9},{9,8},{10,11... | collective-permute-start | bytes 626696 | tf_op jit(solution)/shard_map/ppermute | solution.py:1054
  45.3 13.7 %collective-permute-start.12 = (bf16[2,24,2176]{2,1,0:T(8,128)(2,1)S(1)}, bf16[2,24,2176]{2,1,0:T(8,128)(2,1)S(1)}, u32[]{:S(2)}, u32[]{:S(2)}) collective-permute-start(bf16[2,24,2176]{2,1,0:T(8,128)(2,1)S(1)} %get-tuple-element.153), channel_id=1, source_target_pairs={{0,16},{8,24},{16,0},{24,8},{1,17},{9,25},{17,1},{25,9},{2,18},{10... | collective-permute-start | bytes 626696 | tf_op jit(solution)/shard_map/ppermute | solution.py:1055
  59.1 13.8 %collective-permute-start.13 = (bf16[256,768]{1,0:T(8,128)(2,1)S(1)}, bf16[256,768]{1,0:T(8,128)(2,1)S(1)}, u32[]{:S(2)}, u32[]{:S(2)}) collective-permute-start(bf16[256,768]{1,0:T(8,128)(2,1)S(1)} %collective-permute-done.8.refs_2_), channel_id=1, source_target_pairs={{0,1},{1,0},{2,3},{3,2},{4,5},{5,4},{6,7},{7,6},{8,9},{9,8},{10,11... | collective-permute-start | bytes 1179656 | tf_op jit(solution)/shard_map/ppermute | solution.py:1065
  60.8 12.1 %collective-permute-start.14 = (bf16[2,24,2176]{2,1,0:T(8,128)(2,1)S(1)}, bf16[2,24,2176]{2,1,0:T(8,128)(2,1)S(1)}, u32[]{:S(2)}, u32[]{:S(2)}) collective-permute-start(bf16[2,24,2176]{2,1,0:T(8,128)(2,1)S(1)} %pad_maximum_fusion.9), channel_id=1, source_target_pairs={{0,1},{1,0},{2,3},{3,2},{4,5},{5,4},{6,7},{7,6},{8,9},{9,8},{10,11... | collective-permute-start | bytes 626696 | tf_op jit(solution)/shard_map/ppermute | solution.py:1068
  73.0 22.6 %collective-permute-start.17 = (bf16[4,48,2176]{2,1,0:T(8,128)(2,1)S(1)}, bf16[4,48,2176]{2,1,0:T(8,128)(2,1)}, u32[]{:S(2)}, u32[]{:S(2)}) collective-permute-start(bf16[4,48,2176]{2,1,0:T(8,128)(2,1)S(1)} %maximum_maximum_fusion.refs_0_), channel_id=1, source_target_pairs={{0,16},{8,24},{16,0},{24,8},{1,17},{9,25},{17,1},{25,9},{2,18},{10... | collective-permute-start | bytes 2506760 | tf_op jit(solution)/shard_map/ppermute | solution.py:1081
  74.7 21.0 %collective-permute-start.18 = (bf16[8,24,2176]{2,1,0:T(8,128)(2,1)S(1)}, bf16[8,24,2176]{2,1,0:T(8,128)(2,1)S(1)}, u32[]{:S(2)}, u32[]{:S(2)}) collective-permute-start(bf16[8,24,2176]{2,1,0:T(8,128)(2,1)S(1)} %constant_dynamic-update-slice_fusion), channel_id=1, source_target_pairs={{0,1},{1,0},{2,3},{3,2},{4,5},{5,4},{6,7},{7,6},{8,9},{9,8},{10,11... | collective-permute-start | bytes 2506760 | tf_op jit(solution)/shard_map/ppermute | solution.py:1082
  76.3 19.4 %collective-permute-start.19 = (bf16[2,24,2304]{2,1,0:T(8,128)(2,1)S(1)}, bf16[2,24,2304]{2,1,0:T(8,128)(2,1)S(1)}, u32[]{:S(2)}, u32[]{:S(2)}) collective-permute-start(bf16[2,24,2304]{2,1,0:T(8,128)(2,1)S(1)} %pad_maximum_fusion.7), channel_id=1, source_target_pairs={{0,4},{1,5},{2,6},{3,7},{4,0},{5,1},{6,2},{7,3},{8,12},{9,13},{10,... | collective-permute-start | bytes 663560 | tf_op jit(solution)/shard_map/ppermute | solution.py:1077
  96.0 18.0 %collective-permute-start.22 = (bf16[8,48,2176]{2,1,0:T(8,128)(2,1)S(1)}, bf16[8,48,2176]{2,1,0:T(8,128)(2,1)}, u32[]{:S(2)}, u32[]{:S(2)}) collective-permute-start(bf16[8,48,2176]{2,1,0:T(8,128)(2,1)S(1)} %pad_maximum_fusion.refs_4_), channel_id=1, source_target_pairs={{0,8},{8,0},{16,24},{24,16},{1,9},{9,1},{17,25},{25,17},{2,10},{10... | collective-permute-start | bytes 5013512 | tf_op jit(solution)/shard_map/ppermute | solution.py:1102
  97.2 16.7 %collective-permute-start.21 = (bf16[4,48,2176]{2,1,0:T(8,128)(2,1)}, bf16[4,48,2176]{2,1,0:T(8,128)(2,1)}, u32[]{:S(2)}, u32[]{:S(2)}) collective-permute-start(bf16[4,48,2176]{2,1,0:T(8,128)(2,1)} %collective-permute-done.17.refs_1_), channel_id=1, source_target_pairs={{0,8},{8,0},{16,24},{24,16},{1,9},{9,1},{17,25},{25,17},{2,10},{10... | collective-permute-start | bytes 2506760 | tf_op jit(solution)/shard_map/ppermute | solution.py:1101
  97.6 16.4 %all-to-all-start.1 = ((bf16[8,192,128]{2,1,0:T(8,128)(2,1)}), bf16[8,192,128]{2,1,0:T(8,128)(2,1)}, u32[]{:S(2)}, u32[]{:S(2)}) async-start(bf16[8,192,128]{2,1,0:T(8,128)(2,1)} %get-tuple-element.192), calls=%async_computation.1 | async-start | bytes 786432 | tf_op jit(solution)/shard_map/all_to_all | solution.py:1108
  130.9 16.0 %all-to-all-start.2 = ((bf16[8,192,128]{2,1,0:T(8,128)(2,1)}), bf16[8,192,128]{2,1,0:T(8,128)(2,1)S(1)}, u32[]{:S(2)}, u32[]{:S(2)}) async-start(bf16[8,192,128]{2,1,0:T(8,128)(2,1)} %get-tuple-element.213), calls=%async_computation.2 | async-start | bytes 786432 | tf_op jit(solution)/shard_map/all_to_all | solution.py:1134
  135.1 37.5 %collective-permute-start.28 = (bf16[4,48,2304]{2,1,0:T(8,128)(2,1)S(1)}, bf16[4,48,2304]{2,1,0:T(8,128)(2,1)S(1)}, u32[]{:S(2)}, u32[]{:S(2)}) collective-permute-start(bf16[4,48,2304]{2,1,0:T(8,128)(2,1)S(1)} %pad_maximum_fusion.1.refs_0_), channel_id=1, source_target_pairs={{0,16},{8,24},{16,0},{24,8},{1,17},{9,25},{17,1},{25,9},{2,18},{10... | collective-permute-start | bytes 2654216 | tf_op jit(solution)/shard_map/ppermute | solution.py:1133
  146.8 25.9 %collective-permute-start.27 = (bf16[8,24,2304]{2,1,0:T(8,128)(2,1)}, bf16[8,24,2304]{2,1,0:T(8,128)(2,1)}, u32[]{:S(2)}, u32[]{:S(2)}) collective-permute-start(bf16[8,24,2304]{2,1,0:T(8,128)(2,1)} %get-tuple-element.236), channel_id=1, source_target_pairs={{0,1},{1,0},{2,3},{3,2},{4,5},{5,4},{6,7},{7,6},{8,9},{9,8},{10,11... | collective-permute-start | bytes 2654216 | tf_op jit(solution)/shard_map/ppermute | solution.py:1160
  148.3 24.4 %collective-permute-start.26 = (bf16[192,1920]{1,0:T(8,128)(2,1)}, bf16[192,1920]{1,0:T(8,128)(2,1)}, u32[]{:S(2)}, u32[]{:S(2)}) collective-permute-start(bf16[192,1920]{1,0:T(8,128)(2,1)} %get-tuple-element.234), channel_id=1, source_target_pairs={{0,16},{8,24},{16,0},{24,8},{1,17},{9,25},{17,1},{25,9},{2,18},{10... | collective-permute-start | bytes 2211848 | tf_op jit(solution)/shard_map/ppermute | solution.py:1159
  172.7 47.2 %all-to-all-start.3 = ((bf16[8,704,128]{2,1,0:T(8,128)(2,1)}), bf16[8,704,128]{2,1,0:T(8,128)(2,1)S(1)}, u32[]{:S(2)}, u32[]{:S(2)}) async-start(bf16[8,704,128]{2,1,0:T(8,128)(2,1)} %get-tuple-element.238), calls=%async_computation.3 | async-start | bytes 2883584 | tf_op jit(solution)/shard_map/all_to_all | solution.py:1178
  178.1 22.8 %collective-permute-start.32 = (bf16[4,48,2304]{2,1,0:T(8,128)(2,1)S(1)}, bf16[4,48,2304]{2,1,0:T(8,128)(2,1)S(1)}, u32[]{:S(2)}, u32[]{:S(2)}) collective-permute-start(bf16[4,48,2304]{2,1,0:T(8,128)(2,1)S(1)} %pad_maximum_fusion.1.refs_0_), channel_id=1, source_target_pairs={{0,8},{8,0},{16,24},{24,16},{1,9},{9,1},{17,25},{25,17},{2,10},{10... | collective-permute-start | bytes 2654216 | tf_op jit(solution)/shard_map/ppermute | solution.py:1179
  178.2 22.8 %collective-permute-start.33 = (bf16[4,48,2304]{2,1,0:T(8,128)(2,1)S(1)}, bf16[4,48,2304]{2,1,0:T(8,128)(2,1)S(1)}, u32[]{:S(2)}, u32[]{:S(2)}) collective-permute-start(bf16[4,48,2304]{2,1,0:T(8,128)(2,1)S(1)} %collective-permute-done.28.refs_1_), channel_id=1, source_target_pairs={{0,8},{8,0},{16,24},{24,16},{1,9},{9,1},{17,25},{25,17},{2,10},{10... | collective-permute-start | bytes 2654216 | tf_op jit(solution)/shard_map/ppermute | solution.py:1180
  182.0 19.0 %collective-permute-start.30 = (bf16[1,96,2304]{2,1,0:T(8,128)(2,1)}, bf16[1,96,2304]{2,1,0:T(8,128)(2,1)S(1)}, u32[]{:S(2)}, u32[]{:S(2)}) collective-permute-start(bf16[1,96,2304]{2,1,0:T(8,128)(2,1)} %get-tuple-element.248), channel_id=1, source_target_pairs={{0,16},{8,24},{16,0},{24,8},{1,17},{9,25},{17,1},{25,9},{2,18},{10... | collective-permute-start | bytes 1327112 | tf_op jit(solution)/shard_map/ppermute | solution.py:1189
  183.5 17.5 %collective-permute-start.29 = (bf16[4,24,1920]{2,1,0:T(8,128)(2,1)}, bf16[4,24,1920]{2,1,0:T(8,128)(2,1)S(1)}, u32[]{:S(2)}, u32[]{:S(2)}) collective-permute-start(bf16[4,24,1920]{2,1,0:T(8,128)(2,1)} %get-tuple-element.246), channel_id=1, source_target_pairs={{0,1},{1,0},{2,3},{3,2},{4,5},{5,4},{6,7},{7,6},{8,9},{9,8},{10,11... | collective-permute-start | bytes 1105928 | tf_op jit(solution)/shard_map/ppermute | solution.py:1188
  204.3 15.6 %collective-permute-start.34 = (bf16[2,24,4224]{2,1,0:T(8,128)(2,1)}, bf16[2,24,4224]{2,1,0:T(8,128)(2,1)S(1)}, u32[]{:S(2)}, u32[]{:S(2)}) collective-permute-start(bf16[2,24,4224]{2,1,0:T(8,128)(2,1)} %get-tuple-element.261), channel_id=1, source_target_pairs={{0,2},{1,3},{2,0},{3,1},{4,6},{5,7},{6,4},{7,5},{8,10},{9,11},{10,... | collective-permute-start | bytes 1216520 | tf_op jit(solution)/shard_map/ppermute | solution.py:1202
  222.6 13.2 %collective-permute-start.36 = (bf16[1,24,4224]{2,1,0:T(8,128)(2,1)}, bf16[1,24,4224]{2,1,0:T(8,128)(2,1)S(1)}, u32[]{:S(2)}, u32[]{:S(2)}) collective-permute-start(bf16[1,24,4224]{2,1,0:T(8,128)(2,1)} %get-tuple-element.277), channel_id=1, source_target_pairs={{0,4},{1,5},{2,6},{3,7},{4,0},{5,1},{6,2},{7,3},{8,12},{9,13},{10,... | collective-permute-start | bytes 608264 | tf_op jit(solution)/shard_map/ppermute | solution.py:1209
  223.6 14.9 %all-to-all-start.4 = ((bf16[8,24,384]{2,1,0:T(8,128)(2,1)}), bf16[8,24,384]{2,1,0:T(8,128)(2,1)S(1)}, u32[]{:S(2)}, u32[]{:S(2)}) async-start(bf16[8,24,384]{2,1,0:T(8,128)(2,1)} %bitcast.50), calls=%async_computation.4 | async-start | bytes 294912 | tf_op jit(solution)/shard_map/all_to_all | solution.py:1219
  (37 other events, 297.3 us)
